TPU v7x, 256 devices: a whole 4x4x8 slice. The times are simulated.
256 devices in a mesh: ctx: 32 (over x, y, core), tp: 8 (over z).
Axes of the slice: x: 4, y: 4, z: 8, core: 2. Of those that a mesh axis runs over, the one named last changes fastest.
Arguments:
- upstream: bfloat16 [32768, 4096], P('ctx', 'tp'), may hold values from -0.75 to 0.75
- out_weight: bfloat16 [4096, 4096], P('tp'), may hold values from -0.125 to 0.125
- inner_act: bfloat16 [32768, 4096], P('ctx', 'tp'), may hold values from -6 to 6
- head_bc: bfloat16 [32768, 4096], P('ctx', 'tp'), may hold values from -0.75 to 0.75
- log_decay: float32 [32, 32768], P('tp', 'ctx'), may hold values from -1 to 0, as said below
- states: float32 [128, 32, 64, 128], P('ctx', 'tp'), may hold values from -3 to 3
- skip: float32 [32], P('tp'), may hold values from 0.1 to 1.9
Outputs:
- grad_inner: bfloat16 [32768, 4096], P('ctx', 'tp')
- grad_bc: float32 [32768, 4096], P('ctx', 'tp')
- grad_log: float32 [32, 32768], P('tp', 'ctx')
Inputs may be any that keep to these rules, and one draw needn't show every extreme that they name: `log_decay`: every entry is negative.
All inputs are finite; a program needn't handle non-finite values.
Results may differ from a plain program's by a relative error of at most 0.0049.
Values may be sent and summed in bfloat16 or wider, within the bound.
No kernel may reach another device: no remote copies, remote signals or barrier semaphores. Data moves between devices by JAX's collectives and lax.ppermute only.
A program may use at most 128 MiB of HBM per device.

v0:
```python
import jax
import jax.numpy as jnp
from jax import lax
from jax.sharding import PartitionSpec as P

HEAD_DIM = 128
STATE = 64
BLOCK = 256


def carried_in(part, axis, combine, identity):
    count = lax.axis_size(axis)
    place = lax.axis_index(axis)
    ahead = count - 1 - place
    gathered = jax.tree.map(lambda a: lax.all_gather(a, axis), part)
    state = jax.tree.map(lambda a, e: jnp.zeros_like(a) + jnp.asarray(e, a.dtype), part, identity)

    def one(turn, state):
        source = count - 1 - turn
        return combine(
            state, jax.tree.map(lambda a: lax.dynamic_index_in_dim(a, source, 0, False), gathered)
        )

    return lax.fori_loop(0, ahead, one, state)


def state_end(values, b_rows, log_rate, start_state):
    cumlog = jnp.cumsum(log_rate)
    tail_decay = jnp.exp(cumlog[-1] - cumlog)
    weighted = b_rows * tail_decay[:, None]
    return jnp.exp(cumlog[-1]) * start_state + jnp.dot(
        weighted.T, values, precision=lax.Precision.HIGHEST
    )


def block_forward(values, b_rows, c_rows, log_rate, start_state):
    cumlog = jnp.cumsum(log_rate)
    log_gap = cumlog[:, None] - cumlog[None, :]
    row_ids = lax.broadcasted_iota(jnp.int32, log_gap.shape, 0)
    col_ids = lax.broadcasted_iota(jnp.int32, log_gap.shape, 1)
    decays = jnp.where(row_ids >= col_ids, jnp.exp(jnp.minimum(log_gap, 0.0)), 0.0)
    scores = jnp.dot(c_rows, b_rows.T, precision=lax.Precision.HIGHEST) * decays
    output = jnp.dot(scores, values, precision=lax.Precision.HIGHEST)
    output = output + jnp.exp(cumlog)[:, None] * jnp.dot(
        c_rows, start_state, precision=lax.Precision.HIGHEST
    )
    return (output, state_end(values, b_rows, log_rate, start_state))


def block_gradient_pass(values, b_rows, c_rows, log_rate, start_state, out_grad, carried_state):
    unused, pullback = jax.vjp(block_forward, values, b_rows, c_rows, log_rate, start_state)
    return pullback((out_grad, carried_state))


def per_device(upstream, out_weight, inner_act, head_bc, log_decay, states, skip):
    tokens_here = inner_act.shape[0]
    heads_here = log_decay.shape[0]
    block_count = tokens_here // BLOCK
    out_grad = lax.dot_general(
        lax.all_gather(upstream, "tp", axis=1, tiled=True),
        out_weight,
        (((1,), (1,)), ((), ())),
        preferred_element_type=jnp.float32,
    ).astype(jnp.bfloat16)
    grad_vals = (
        out_grad.astype(jnp.float32)
        .reshape(block_count, BLOCK, heads_here, HEAD_DIM)
        .transpose(0, 2, 1, 3)
    )
    inner_vals = (
        inner_act.astype(jnp.float32)
        .reshape(block_count, BLOCK, heads_here, HEAD_DIM)
        .transpose(0, 2, 1, 3)
    )
    bc_vals = (
        head_bc.astype(jnp.float32)
        .reshape(block_count, BLOCK, heads_here, 2, STATE)
        .transpose(0, 2, 1, 3, 4)
    )
    b_vals = bc_vals[:, :, :, 0, :]
    c_vals = bc_vals[:, :, :, 1, :]
    log_vals = log_decay.reshape(heads_here, block_count, BLOCK).transpose(1, 0, 2)
    cumlog = jnp.cumsum(log_vals, axis=-1)
    weighted_c = c_vals * jnp.exp(cumlog)[..., None]
    block_terms = jnp.einsum(
        "khqn,khqp->khnp", weighted_c, grad_vals, precision=lax.Precision.HIGHEST
    )
    block_logs = cumlog[..., -1]
    before_logs = jnp.cumsum(block_logs, axis=0) - block_logs
    part_terms = jnp.einsum(
        "kh,khnp->hnp", jnp.exp(before_logs), block_terms, precision=lax.Precision.HIGHEST
    )
    part_log = jnp.sum(block_logs, axis=0)

    def combine(earlier, later):
        return (later[0] * earlier[0], later[1] + later[0][:, None, None] * earlier[1])

    identity_pair = (jnp.ones((heads_here,), jnp.float32), jnp.zeros(part_terms.shape, jnp.float32))
    prefix = carried_in((jnp.exp(part_log), part_terms), "ctx", combine, identity_pair)
    incoming = prefix[1]
    head_backward = jax.vmap(block_gradient_pass, in_axes=(0, 0, 0, 0, 0, 0, 0))

    def step(carried_state, block_entries):
        (
            input_value,
            input_proj_value,
            output_proj_value,
            log_decay_value,
            state_value,
            output_gradient_value,
        ) = block_entries
        (
            input_gradient,
            input_proj_gradient,
            output_proj_gradient,
            log_decay_gradient,
            state_gradient,
        ) = head_backward(
            input_value,
            input_proj_value,
            output_proj_value,
            log_decay_value,
            state_value,
            output_gradient_value,
            carried_state,
        )
        return (
            state_gradient,
            (input_gradient, input_proj_gradient, output_proj_gradient, log_decay_gradient),
        )

    block_entries = (inner_vals, b_vals, c_vals, log_vals, states, grad_vals)
    unused, outputs = lax.scan(step, incoming, block_entries, reverse=True)
    input_gradient, input_proj_gradient, output_proj_gradient, log_decay_gradient = outputs
    input_gradient = input_gradient + skip[None, :, None, None] * grad_vals
    grad_inner = (
        input_gradient.transpose(0, 2, 1, 3)
        .reshape(tokens_here, heads_here * HEAD_DIM)
        .astype(jnp.bfloat16)
    )
    grad_pair = jnp.stack([input_proj_gradient, output_proj_gradient], axis=3)
    grad_bc = grad_pair.transpose(0, 2, 1, 3, 4).reshape(tokens_here, heads_here * 2 * STATE)
    grad_log = log_decay_gradient.transpose(1, 0, 2).reshape(heads_here, tokens_here)
    return (grad_inner, grad_bc, grad_log)


def solution(mesh):
    return jax.shard_map(
        per_device,
        mesh=mesh,
        in_specs=(
            P("ctx", "tp"),
            P("tp", None),
            P("ctx", "tp"),
            P("ctx", "tp"),
            P("tp", "ctx"),
            P("ctx", "tp", None, None),
            P("tp"),
        ),
        out_specs=(P("ctx", "tp"), P("ctx", "tp"), P("tp", "ctx")),
        check_vma=False,
    )
```

profile of v0, /device:TPU:96, one launch (start us, length us, event | category | flops | bytes accessed | tf_op | source)
XLA Modules:
  0.0 397.5 jit_solution(13955768038466922143)
XLA Ops:
  8.7 4.8 %reduce-window.76 = f32[4,4,2,128]{3,2,1,0:T(2,128)S(1)} reduce-window(f32[4,4,2,128]{3,2,1,0:T(2,128)S(1)} %reshape.354, f32[]{:T(128)} %constant.136.clone.1), window={size=1x1x1x128 pad=0_0x0_0x0_0x127_0}, to_apply=%region_0.0 | reduce-window | flops 520192 | bytes 32772 | tf_op jit(solution)/shard_map/reduce-window.6
  14.5 1.6 copy.93
  16.1 2.2 reshape.361
  19.5 85.8 %all-gather.5.cloned.1.call-done = bf16[1024,4096]{1,0:T(8,128)(2,1)} async-done(((bf16[1024,512]{1,0:T(8,128)(2,1)}), bf16[1024,4096]{1,0:T(8,128)(2,1)}) %all-gather.5.cloned.1.call-update) | async-done | bytes 8388624 | tf_op jit(solution)/shard_map/all_gather | solution.py:60
  105.3 10.1 %convolution_convert_fusion = bf16[1024,512]{1,0:T(8,128)(2,1)} fusion(bf16[1024,4096]{1,0:T(8,128)(2,1)} %all-gather.5.cloned.1.call-done, bf16[512,4096]{1,0:T(8,128)(2,1)} %param.12), kind=kOutput, calls=%fused_computation.87 | convolution fusion | flops 4295491584 | bytes 13631488 | tf_op jit(solution)/shard_map/dot_general | solution.py:59
  116.7 2.4 fusion.58
  119.1 1.9 fusion.62
  122.4 67.1 %all-reduce.2 = f32[128]{0:T(128)S(1)} all-reduce(f32[128]{0:T(128)S(1)} %exponential_dynamic-update-slice_fusion), channel_id=3, replica_groups=mesh['ctx'=32,'tp'=8] {'ctx'}, use_global_device_ids=true, to_apply=%add.2 | all-reduce | flops 128 | bytes 1024
  189.6 2.7 reshape.362
  192.3 1.7 slice_bitcast_fusion
  194.3 32.1 %while.36 = (s32[]{:T(128)}, f32[4,64,128]{2,1,0:T(8,128)S(1)}, s32[]{:T(128)}, f32[32,4,64,128]{3,2,1,0:T(8,128)}, f32[32,4]{1,0:T(8,128)S(1)}, /*index=5*/s32[]{:T(128)}, s32[]{:T(128)}, s32[]{:T(128)}, s32[]{:T(128)}) while((s32[]{:T(128)}, f32[4,64,128]{2,1,0:T(8,128)S(1)}, s32[]{:T(128)}, f32[32,4,64,128]{3,2,1,0:T(8,128)}, ...), condition=%wide.region_5.6_spmd, body=%wide.region_4.5_spmd.sunk | while | flops 65542 | bytes 393419 | solution.py:24
  228.6 1.5 broadcast_in_dim.78
  230.2 145.2 %while.37 = (s32[]{:T(128)}, f32[4,64,128]{2,1,0:T(8,128)S(1)}, f32[4,4,256,128]{3,2,1,0:T(8,128)}, f32[4,4,256,64]{2,3,1,0:T(8,128)}, f32[4,4,256,64]{2,3,1,0:T...) while((s32[]{:T(128)}, f32[4,64,128]{2,1,0:T(8,128)S(1)}, ...), condition=%wide.region_19.20_spmd, body=%wide.region_6.19_spmd.sunk | while | flops 1920542720 | bytes 28358164 | solution.py:133
  234.9 2.1 constant_dynamic-slice_fusion.9
  237.0 2.1 fusion.103
  243.0 2.4 fusion.102
  245.8 3.1 fusion.107
  248.9 5.0 %reduce-window.88 = f32[4,2,128]{2,1,0:T(2,128)S(1)} reduce-window(f32[4,2,128]{2,1,0:T(2,128)S(1)} %reshape.377, f32[]{:T(128)} %constant.136.clone.1..sunk), window={size=1x1x128 pad=0_0x0_0x0_127}, to_apply=%region_12.12 | reduce-window | flops 130048 | bytes 8196 | tf_op jit(solution)/shard_map/reduce-window.40
  254.2 5.0 %reduce-window.87 = f32[4,2,128]{2,1,0:T(2,128)S(1)} reduce-window(f32[4,2,128]{2,1,0:T(2,128)S(1)} %get-tuple-element.561, f32[]{:T(128)} %constant.136.clone.1..sunk), window={size=1x1x128 pad=0_0x0_0x0_127}, to_apply=%region_17.17 | reduce-window | flops 130048 | bytes 8196 | tf_op jit(solution)/shard_map/reduce-window.42
  261.2 2.9 fusion.106
  264.1 2.4 fusion.109
  271.2 2.1 constant_dynamic-slice_fusion.9
  273.3 2.1 fusion.103
  279.3 2.4 fusion.102
  282.1 3.0 fusion.107
  285.2 5.0 %reduce-window.88 = f32[4,2,128]{2,1,0:T(2,128)S(1)} reduce-window(f32[4,2,128]{2,1,0:T(2,128)S(1)} %reshape.377, f32[]{:T(128)} %constant.136.clone.1..sunk), window={size=1x1x128 pad=0_0x0_0x0_127}, to_apply=%region_12.12 | reduce-window | flops 130048 | bytes 8196 | tf_op jit(solution)/shard_map/reduce-window.40
  290.5 5.0 %reduce-window.87 = f32[4,2,128]{2,1,0:T(2,128)S(1)} reduce-window(f32[4,2,128]{2,1,0:T(2,128)S(1)} %get-tuple-element.561, f32[]{:T(128)} %constant.136.clone.1..sunk), window={size=1x1x128 pad=0_0x0_0x0_127}, to_apply=%region_17.17 | reduce-window | flops 130048 | bytes 8196 | tf_op jit(solution)/shard_map/reduce-window.42
  297.5 2.9 fusion.106
  300.3 2.4 fusion.109
  307.5 2.1 constant_dynamic-slice_fusion.9
  309.6 2.1 fusion.103
  315.6 2.4 fusion.102
  318.4 3.0 fusion.107
  321.5 5.0 %reduce-window.88 = f32[4,2,128]{2,1,0:T(2,128)S(1)} reduce-window(f32[4,2,128]{2,1,0:T(2,128)S(1)} %reshape.377, f32[]{:T(128)} %constant.136.clone.1..sunk), window={size=1x1x128 pad=0_0x0_0x0_127}, to_apply=%region_12.12 | reduce-window | flops 130048 | bytes 8196 | tf_op jit(solution)/shard_map/reduce-window.40
  326.7 5.0 %reduce-window.87 = f32[4,2,128]{2,1,0:T(2,128)S(1)} reduce-window(f32[4,2,128]{2,1,0:T(2,128)S(1)} %get-tuple-element.561, f32[]{:T(128)} %constant.136.clone.1..sunk), window={size=1x1x128 pad=0_0x0_0x0_127}, to_apply=%region_17.17 | reduce-window | flops 130048 | bytes 8196 | tf_op jit(solution)/shard_map/reduce-window.42
  333.8 2.9 fusion.106
  336.6 2.4 fusion.109
  343.8 2.1 constant_dynamic-slice_fusion.9
  345.9 2.1 fusion.103
  351.9 2.4 fusion.102
  354.7 3.1 fusion.107
  357.8 5.0 %reduce-window.88 = f32[4,2,128]{2,1,0:T(2,128)S(1)} reduce-window(f32[4,2,128]{2,1,0:T(2,128)S(1)} %reshape.377, f32[]{:T(128)} %constant.136.clone.1..sunk), window={size=1x1x128 pad=0_0x0_0x0_127}, to_apply=%region_12.12 | reduce-window | flops 130048 | bytes 8196 | tf_op jit(solution)/shard_map/reduce-window.40
  363.1 5.0 %reduce-window.87 = f32[4,2,128]{2,1,0:T(2,128)S(1)} reduce-window(f32[4,2,128]{2,1,0:T(2,128)S(1)} %get-tuple-element.561, f32[]{:T(128)} %constant.136.clone.1..sunk), window={size=1x1x128 pad=0_0x0_0x0_127}, to_apply=%region_17.17 | reduce-window | flops 130048 | bytes 8196 | tf_op jit(solution)/shard_map/reduce-window.42
  370.1 2.9 fusion.106
  372.9 2.4 fusion.109
  375.4 2.2 fusion.57
  379.9 4.4 %copy.109 = f32[4,256,4,2,64]{4,3,2,1,0:T(2,128)} copy(f32[4,256,4,2,64]{1,4,2,0,3:T(8,128)S(1)} %maximum_bitcast_fusion) | data formatting | bytes 4194304
  384.3 6.4 %reshape.372 = f32[1024,512]{1,0:T(8,128)} reshape(f32[4,256,4,2,64]{4,3,2,1,0:T(2,128)} %copy.109) | data formatting | bytes 4194304
  (298 shorter events, 86.5 us)
Async XLA Ops:
  7.2 7.3 %copy-start.6 = (bf16[1024,512]{1,0:T(8,128)(2,1)S(1)}, bf16[1024,512]{1,0:T(8,128)(2,1)}, u32[]{:S(2)}) copy-start(bf16[1024,512]{1,0:T(8,128)(2,1)} %param.14) | copy-start | bytes 3145732
  7.2 98.1 %all-gather.5.cloned.1.call-start = ((), (), s32[]{:S(2)}) async-start(), calls=%async_computation | async-start | bytes 9437184 | tf_op jit(solution)/shard_map/all_gather | solution.py:60
  7.9 186.4 %all-gather.7.cloned.1.call-start = ((), (), s32[]{:S(2)}) async-start(), calls=%async_computation.1 | async-start | bytes 4325376 | tf_op jit(solution)/shard_map/all_gather | solution.py:15
  116.7 77.3 %copy-start.2 = (bf16[4,256,4,128]{3,2,1,0:T(4,128)(2,1)}, bf16[4,256,4,128]{3,2,1,0:T(4,128)(2,1)S(1)}, u32[]{:S(2)}) copy-start(bf16[4,256,4,128]{3,2,1,0:T(4,128)(2,1)S(1)} %reshape.357) | copy-start | bytes 3145732
  116.7 4.3 %copy-start.9 = (u32[256]{0:T(256)S(1)}, u32[256]{0:T(256)}, u32[]{:S(2)}) copy-start(u32[256]{0:T(256)} %constant.149) | copy-start | bytes 3076
  230.2 145.2 %copy-start.8 = (f32[4]{0:T(128)S(1)}, f32[4]{0:T(128)}, u32[]{:S(2)}) copy-start(f32[4]{0:T(128)} %param.17) | copy-start | bytes 52
  241.6 3.8 copy-start.1
  243.0 2.8 copy-start.3
  259.6 1.6 copy-start
  277.9 3.8 copy-start.1
  279.3 2.8 copy-start.3
  295.9 1.6 copy-start
  314.2 3.8 copy-start.1
  315.6 2.8 copy-start.3
  332.1 1.6 copy-start
  350.5 3.8 copy-start.1
  351.9 2.8 copy-start.3
  368.4 1.6 copy-start
  375.4 2.2 copy-start.7
  377.6 2.0 copy-start.4
  377.6 2.0 copy-start.5
Sparse Core Ops, SparseCore 0:
  9.8 95.4 all-gather.4
  121.2 50.3 all-gather.6
where the time goes:
time: 399 us; the launch traced here: 398 us
  other arithmetic  92.1 us (23%)
  matrix products  87.4 us (22%)
  waiting for transfers between devices  86.5 us (22%)
  blocking collectives  67.1 us (17%)
  local copies, waits for them, and re-layouts  48.1 us (12%)
  between operations  14.9 us (4%)
    all_gather x1, waiting for transfers between devices, per_device(): lax.all_gather(upstream, 'tp', axis=1, tiled=True)  85.8 us
    unnamed x1, blocking collectives  67.1 us
    another operation x27, other arithmetic  50.5 us
    add x31, other arithmetic, combine(): later[1] + later[0][:, None, None] * earlier[1]  30.9 us
    dot_general x12, matrix products, block_forward(): scores = jnp.dot(c_rows, b_rows.T, precision=lax.Precision.HIGHEST) * decays  27.5 us
    dot_general x12, matrix products, block_forward(): jnp.dot(c_rows, start_state, precision=lax.Precision.HIGHEST)  20.3 us
    dynamic_slice x12, local copies, waits for them, and re-layouts, per_device(): unused, outputs = lax.scan(step, incoming, block_entries, reverse=True)  15.4 us
    dot_general x8, matrix products, block_forward(): output = jnp.dot(scores, values, precision=lax.Precision.HIGHEST)  15.4 us
  transfers between devices with their start and end apart: 2, of which 1 were waited for; matrix products, arithmetic and copies ran while one was open for 4% of the time, Pallas kernels for 0%

commit v1 on v0

v1 whole, which is shorter than its diff:
```python
import jax
import jax.numpy as jnp
from jax import lax
from jax.experimental import pallas as pl
from jax.experimental.pallas import tpu as pltpu
from jax.sharding import PartitionSpec as P

HEAD_DIM = 128
STATE = 64
BLOCK = 256
F32 = jnp.float32
BF16 = jnp.bfloat16
VMEM_LIMIT = 48 << 20


def dot(a, b, dims):
    return lax.dot_general(a, b, (dims, ((), ())), preferred_element_type=F32)


NN = ((1,), (0,))
NT = ((1,), (1,))
TN = ((0,), (0,))


def low_lanes(shape):
    return lax.broadcasted_iota(jnp.int32, shape, len(shape) - 1) < STATE


def prepare_kernel(heads, a_last, bc_ref, sw_ref, arow_ref, acol_ref, dec_ref, sct_ref, wct_ref, wb_ref):
    b = pl.program_id(0)
    rows = lax.broadcasted_iota(jnp.int32, (BLOCK, BLOCK), 0)
    cols = lax.broadcasted_iota(jnp.int32, (BLOCK, BLOCK), 1)
    low = low_lanes((BLOCK, HEAD_DIM))
    for h in range(heads):
        lanes = slice(h * HEAD_DIM, (h + 1) * HEAD_DIM)
        row = arow_ref[h : h + 1, :]
        col1 = acol_ref[:, lanes]
        col = jnp.concatenate([col1, col1], axis=1)
        gap = col - row
        dec_ref[0, h] = jnp.where(rows >= cols, jnp.exp(jnp.minimum(gap, 0.0)), 0.0).astype(BF16)
        bc = bc_ref[:, lanes]
        sw = sw_ref[:, lanes]
        zero = jnp.zeros_like(bc)
        c_low = jnp.where(low, sw, zero)
        b_low = jnp.where(low, bc, zero)
        scores = dot(b_low, c_low, NT)
        back = jnp.where(cols >= rows, jnp.exp(jnp.minimum(-gap, 0.0)), 0.0)
        sct_ref[0, h] = (scores * back).astype(BF16)
        weighted = c_low.astype(F32) * jnp.exp(col1)
        wct_ref[0, h] = weighted.T[:STATE, :].astype(BF16)
        tail = jnp.exp(a_last[b, h] - col1)
        wb_ref[:, lanes] = (b_low.astype(F32) * tail).astype(BF16)


def prepare_body(heads):
    def body(a_last, bc_ref, sw_ref, arow_ref, acol_ref, dec_ref, sct_ref, wct_ref, wb_ref):
        prepare_kernel(heads, a_last, bc_ref, sw_ref, arow_ref, acol_ref, dec_ref, sct_ref, wct_ref, wb_ref)

    return body


def prepare(a_last, bc, sw, arow, acol):
    tokens, width = bc.shape
    heads = width // HEAD_DIM
    blocks = tokens // BLOCK
    wide = pl.BlockSpec((BLOCK, width), lambda b: (b, 0))
    square = pl.BlockSpec((1, heads, BLOCK, BLOCK), lambda b: (b, 0, 0, 0))
    return pl.pallas_call(
        prepare_body(heads),
        name="prepare",
        grid=(blocks,),
        in_specs=[
            pl.BlockSpec(memory_space=pltpu.SMEM),
            wide,
            wide,
            pl.BlockSpec((heads, BLOCK), lambda b: (0, b)),
            wide,
        ],
        out_specs=[
            square,
            square,
            pl.BlockSpec((1, heads, STATE, BLOCK), lambda b: (b, 0, 0, 0)),
            wide,
        ],
        out_shape=[
            jax.ShapeDtypeStruct((blocks, heads, BLOCK, BLOCK), BF16),
            jax.ShapeDtypeStruct((blocks, heads, BLOCK, BLOCK), BF16),
            jax.ShapeDtypeStruct((blocks, heads, STATE, BLOCK), BF16),
            jax.ShapeDtypeStruct((tokens, width), BF16),
        ],
        cost_estimate=pl.CostEstimate(flops=4_000_000_000, bytes_accessed=9_000_000, transcendentals=0),
        compiler_params=pltpu.CompilerParams(vmem_limit_bytes=VMEM_LIMIT),
    )(a_last, bc, sw, arow, acol)


def close_chunk(first, acc, up, down, weight, wct, scale, earlier):
    tokens, width = acc.shape
    heads = width // HEAD_DIM
    last = earlier is not None

    def body(*refs):
        scale_ref, acc_ref, up_ref, down_ref, weight_ref, wct_ref = refs[:6]
        if last:
            earlier_ref, dy_ref, terms_ref, part_ref = refs[6:]
        else:
            dy_ref, terms_ref = refs[6:]
        sums = [jnp.zeros((STATE, HEAD_DIM), F32) for _ in range(heads)]
        if last:
            for b in range(2):
                for h in range(heads):
                    sums[h] = sums[h] + scale_ref[b, h] * earlier_ref[b, h]
        for b, piece in enumerate((up_ref, down_ref)):
            rows = slice(b * BLOCK, (b + 1) * BLOCK)
            dy = (acc_ref[rows, :] + dot(piece[...], weight_ref[...], NT)).astype(BF16)
            dy_ref[rows, :] = dy
            for h in range(heads):
                term = dot(wct_ref[b, h], dy[:, h * HEAD_DIM : (h + 1) * HEAD_DIM], NN)
                terms_ref[b, h] = term
                if last:
                    sums[h] = sums[h] + scale_ref[b + first, h] * term
        if last:
            for h in range(heads):
                part_ref[h] = sums[h]

    vmem = pl.BlockSpec(memory_space=pltpu.VMEM)
    wct = wct[first : first + 2]
    out_shape = [
        jax.ShapeDtypeStruct((tokens, width), BF16),
        jax.ShapeDtypeStruct((2, heads, STATE, HEAD_DIM), F32),
    ]
    in_specs = [pl.BlockSpec(memory_space=pltpu.SMEM)] + [vmem] * 5
    operands = [scale, acc, up, down, weight, wct]
    if last:
        out_shape.append(jax.ShapeDtypeStruct((heads, STATE, HEAD_DIM), F32))
        in_specs.append(vmem)
        operands.append(earlier)
    return pl.pallas_call(
        body,
        name="close_chunk",
        in_specs=in_specs,
        out_specs=[vmem] * len(out_shape),
        out_shape=out_shape,
        cost_estimate=pl.CostEstimate(flops=600_000_000, bytes_accessed=4_000_000, transcendentals=0),
        compiler_params=pltpu.CompilerParams(vmem_limit_bytes=VMEM_LIMIT),
    )(*operands)


def inside(first, dy, x, bc, sw, acol, dec, sct, spad, before):
    width = x.shape[1]
    tokens = x.shape[0]
    heads = width // HEAD_DIM

    def body(dy_ref, x_ref, bc_ref, sw_ref, acol_ref, dec_ref, sct_ref, spad_ref, *rest):
        dx_ref, dbc_ref, dlog_ref = rest[-3:]
        rows = lax.broadcasted_iota(jnp.int32, (BLOCK, BLOCK), 0)
        cols = lax.broadcasted_iota(jnp.int32, (BLOCK, BLOCK), 1)
        low = low_lanes((BLOCK, HEAD_DIM))
        for h in range(heads):
            lanes = slice(h * HEAD_DIM, (h + 1) * HEAD_DIM)
            dy_h = dy_ref[:, lanes]
            x_h = x_ref[:, lanes]
            bc_h = bc_ref[:, lanes]
            sw_h = sw_ref[:, lanes]
            zero = jnp.zeros_like(sw_h)
            gaps = dot(dy_h, x_h, NT)
            mixed = (gaps * dec_ref[0, h].astype(F32)).astype(BF16)
            dx_ref[:, lanes] = dot(sct_ref[0, h], dy_h, NN)
            grad = dot(mixed, jnp.where(low, zero, sw_h), NN)
            grad = grad + dot(mixed, jnp.where(low, sw_h, zero), TN)
            grad = grad + jnp.exp(acol_ref[:, lanes]) * dot(dy_h, spad_ref[0, h], NT)
            dbc_ref[:, lanes] = grad
            signed = grad * bc_h.astype(F32)
            moved = jnp.sum(jnp.where(low, -signed, signed), axis=1, keepdims=True)
            dlog_ref[h : h + 1, :] = jnp.sum(
                jnp.where(rows >= cols, moved, 0.0), axis=0, keepdims=True
            )

    def at(b):
        return (b + first, 0)

    def at4(b):
        return (b + first, 0, 0, 0)

    wide = pl.BlockSpec((BLOCK, width), at)
    square = pl.BlockSpec((1, heads, BLOCK, BLOCK), at4)
    in_specs = [
        pl.BlockSpec((BLOCK, width), lambda b: (b, 0)),
        wide,
        wide,
        wide,
        wide,
        square,
        square,
        pl.BlockSpec((1, heads, HEAD_DIM, HEAD_DIM), at4),
    ]
    operands = [dy, x, bc, sw, acol, dec, sct, spad]
    aliases = {}
    if before is not None:
        for place, array in enumerate(before):
            aliases[len(operands)] = place
            operands.append(array)
            in_specs.append(pl.BlockSpec(memory_space=pl.ANY))
    return pl.pallas_call(
        body,
        name="inside",
        grid=(2,),
        in_specs=in_specs,
        out_specs=[wide, wide, pl.BlockSpec((heads, BLOCK), lambda b: (0, b + first))],
        out_shape=[
            jax.ShapeDtypeStruct((tokens, width), F32),
            jax.ShapeDtypeStruct((tokens, width), F32),
            jax.ShapeDtypeStruct((heads, tokens), F32),
        ],
        input_output_aliases=aliases,
        cost_estimate=pl.CostEstimate(flops=2_000_000_000, bytes_accessed=7_000_000, transcendentals=0),
        compiler_params=pltpu.CompilerParams(vmem_limit_bytes=VMEM_LIMIT),
    )(*operands)


def finish(coefs, skip, a_last, received, dys, x, bc, acol, wb, terms, states, dx, dbc, dlog):
    tokens, width = x.shape
    heads = width // HEAD_DIM
    blocks = tokens // BLOCK
    count = len(received)

    def body(coefs_ref, skip_ref, last_ref, *refs):
        got = refs[:count]
        (dy0_ref, dy1_ref, x_ref, bc_ref, acol_ref, wb_ref, terms0_ref, terms1_ref, states_ref, dx_ref, dbc_ref,
         dlog_ref, out_ref, outbc_ref, outlog_ref, carry_ref) = refs[count:]
        step = pl.program_id(0)
        b = blocks - 1 - step

        @pl.when(step == 0)
        def _():
            for h in range(heads):
                total = coefs_ref[0, h] * got[0][h].astype(F32)
                for i in range(1, count):
                    total = total + coefs_ref[i, h] * got[i][h].astype(F32)
                carry_ref[h] = total

        rows = lax.broadcasted_iota(jnp.int32, (BLOCK, BLOCK), 0)
        cols = lax.broadcasted_iota(jnp.int32, (BLOCK, BLOCK), 1)
        late = step < 2
        for h in range(heads):
            lanes = slice(h * HEAD_DIM, (h + 1) * HEAD_DIM)
            carry = carry_ref[h]
            carry16 = carry.astype(BF16)
            dy_h = jnp.where(late, dy1_ref[:, lanes], dy0_ref[:, lanes]).astype(F32)
            grad = dx_ref[:, lanes] + dot(wb_ref[:, lanes][:, :STATE], carry16, NN)
            out_ref[:, lanes] = (grad + skip_ref[0, h] * dy_h).astype(BF16)
            padded = jnp.concatenate([carry16, jnp.zeros_like(carry16)], axis=0)
            last = last_ref[b, h]
            extra = jnp.exp(last - acol_ref[:, lanes]) * dot(x_ref[:, lanes], padded, NT)
            outbc_ref[:, lanes] = dbc_ref[:, lanes] + extra
            moved = jnp.sum(extra * bc_ref[:, lanes].astype(F32), axis=1, keepdims=True)
            ends = jnp.exp(jnp.full((1, HEAD_DIM), last, F32))
            whole = jnp.sum(jnp.sum(states_ref[0, h] * carry, axis=0, keepdims=True) * ends)
            outlog_ref[h : h + 1, :] = (
                dlog_ref[h : h + 1, :]
                + jnp.sum(jnp.where(rows < cols, moved, 0.0), axis=0, keepdims=True)
                + whole
            )
            carry_ref[h] = ends * carry + jnp.where(late, terms1_ref[0, h], terms0_ref[0, h])

    def at(i):
        return (blocks - 1 - i, 0)

    def at4(i):
        return (blocks - 1 - i, 0, 0, 0)

    wide = pl.BlockSpec((BLOCK, width), at)
    smem = pl.BlockSpec(memory_space=pltpu.SMEM)
    state_block = (1, heads, STATE, HEAD_DIM)
    line = pl.BlockSpec((heads, BLOCK), lambda i: (0, blocks - 1 - i))
    return pl.pallas_call(
        body,
        name="finish",
        grid=(blocks,),
        in_specs=[smem, smem, smem]
        + [pl.BlockSpec((heads, STATE, HEAD_DIM), lambda i: (0, 0, 0)) for _ in received]
        + [
            pl.BlockSpec((BLOCK, width), lambda i: (jnp.clip(3 - i, 0, 1), 0)),
            pl.BlockSpec((BLOCK, width), lambda i: (jnp.clip(1 - i, 0, 1), 0)),
            wide,
            wide,
            wide,
            wide,
            pl.BlockSpec(state_block, lambda i: (jnp.clip(3 - i, 0, 1), 0, 0, 0)),
            pl.BlockSpec(state_block, lambda i: (jnp.clip(1 - i, 0, 1), 0, 0, 0)),
            pl.BlockSpec(state_block, at4),
            wide,
            wide,
            line,
        ],
        out_specs=[wide, wide, line],
        out_shape=[
            jax.ShapeDtypeStruct((tokens, width), BF16),
            jax.ShapeDtypeStruct((tokens, width), F32),
            jax.ShapeDtypeStruct((heads, tokens), F32),
        ],
        scratch_shapes=[pltpu.VMEM((heads, STATE, HEAD_DIM), F32)],
        cost_estimate=pl.CostEstimate(flops=600_000_000, bytes_accessed=14_000_000, transcendentals=0),
        compiler_params=pltpu.CompilerParams(vmem_limit_bytes=VMEM_LIMIT),
    )(coefs, skip, a_last, *received, dys[0], dys[1], x, bc, acol, wb, terms[0], terms[1], states, dx, dbc, dlog)


def shift(count, by):
    return [(i, (i + by) % count) for i in range(count)]


def per_device(upstream, out_weight, inner_act, head_bc, log_decay, states, skip):
    tokens, width = inner_act.shape
    heads = log_decay.shape[0]
    blocks = tokens // BLOCK
    tp = lax.axis_size("tp")
    me = lax.axis_index("tp")
    ctx = lax.axis_index("ctx")
    feats = upstream.shape[1]
    px, py, pc = ctx // 8, (ctx // 2) % 4, ctx % 2

    logs = log_decay.reshape(heads, blocks, BLOCK)
    cum = jnp.cumsum(logs, axis=-1)
    last = cum[:, :, -1].T
    total = jnp.sum(last, axis=0)
    all_logs = lax.all_gather(jnp.zeros((8, 128), F32).at[0, :heads].set(total), "ctx")[:, 0, :heads]

    def weight_of(source):
        return lax.dynamic_slice_in_dim(out_weight, (source % tp) * feats, feats, 1)

    half = tokens // 2
    accs, lasts = [], []
    for c in range(2):
        own = upstream[c * half : (c + 1) * half]
        right = left = own
        acc = dot(own, weight_of(me), NT)
        for k in range(1, tp // 2):
            right = lax.ppermute(right, "tp", shift(tp, 1))
            left = lax.ppermute(left, "tp", shift(tp, -1))
            acc = acc + dot(right, weight_of(me - k + tp), NT) + dot(left, weight_of(me + k), NT)
        up = lax.ppermute(right[:BLOCK], "tp", shift(tp, 1))
        down = lax.ppermute(left[BLOCK:], "tp", shift(tp, -1))
        accs.append(acc)
        lasts.append((up, down))
    weight_last = weight_of(me + tp // 2)

    arow = cum.reshape(heads, tokens)
    acol = jnp.repeat(arow.T, HEAD_DIM, axis=1)
    swapped = head_bc.reshape(tokens, heads, 2, STATE)[:, :, ::-1, :].reshape(tokens, width)
    dec, sct, wct, wb = prepare(last, head_bc, swapped, arow, acol)
    spad = jnp.pad(states, ((0, 0), (0, 0), (STATE, 0), (0, 0))).astype(BF16)
    ahead = jnp.exp(jnp.cumsum(last, axis=0) - last)

    ids = jnp.arange(32)
    ix, iy, ic = ids // 8, (ids // 2) % 4, ids % 2
    row = ix == px
    chip = row & (iy == py)
    none = ids < 0
    after_core = chip & (ic > pc)
    after_y = row & (iy > py)
    yes = jnp.bool_(True)
    entries = [(chip & (ic == 0) & (pc == 1), yes), (chip & (ic == 0) & (pc == 0), yes)]
    entries.append((row & (iy < py), yes))
    for s in (1, 2, 3):
        sy = (py - s) % 4
        entries.append((row & (iy < sy), yes))
    finals = [(none, pc == 0)]
    for s in (1, 2, 3):
        sy = (py - s) % 4
        finals.append((after_core | (row & (iy > py) & (iy < sy)), sy > py))
    for s in (1, 2, 3):
        sx = (px - s) % 4
        finals.append((after_core | after_y | ((ix > px) & (ix < sx)), sx > px))
    entries = entries + finals
    masks = jnp.stack([m for m, _ in entries])
    valid = jnp.stack([v for _, v in entries])
    sums = jnp.sum(jnp.where(masks[:, :, None], all_logs[None], 0.0), axis=1)
    coefs = jnp.where(valid[:, None], jnp.exp(sums), 0.0)

    dy0, terms0 = close_chunk(0, accs[0], *lasts[0], weight_last, wct, ahead, None)
    dy1, terms1, part = close_chunk(2, accs[1], *lasts[1], weight_last, wct, ahead, terms0)

    def by(i):
        return coefs[i][:, None, None]

    places = [(x, y, c) for x in range(4) for y in range(4) for c in range(2)]

    def perm(dx, dy, dc):
        return [(x * 8 + y * 2 + c, ((x + dx) % 4) * 8 + ((y + dy) % 4) * 2 + (c ^ dc)) for x, y, c in places]

    part16 = part.astype(BF16)
    other = lax.ppermute(part16, "ctx", perm(0, 0, 1))
    chip_sum = (by(0) * part + by(1) * other.astype(F32)).astype(BF16)
    ys = [lax.ppermute(chip_sum, "ctx", perm(0, s, 0)) for s in (1, 2, 3)]
    dy0, chip_sum = lax.optimization_barrier((dy0, chip_sum))
    grads = inside(0, dy0, inner_act, head_bc, swapped, acol, dec, sct, spad, None)
    row_sum = by(2) * chip_sum.astype(F32)
    for s in range(3):
        row_sum = row_sum + by(3 + s) * ys[s].astype(F32)
    row_sum = row_sum.astype(BF16)
    xs = [lax.ppermute(row_sum, "ctx", perm(s, 0, 0)) for s in (1, 2, 3)]
    dy1, row_sum = lax.optimization_barrier((dy1, row_sum))
    dx, dbc, dlog = inside(2, dy1, inner_act, head_bc, swapped, acol, dec, sct, spad, grads)
    return finish(
        coefs[6:], skip[None], last, [other] + ys + xs, (dy0, dy1), inner_act, head_bc, acol, wb,
        (terms0, terms1), states, dx, dbc, dlog,
    )


def solution(mesh):
    return jax.shard_map(
        per_device,
        mesh=mesh,
        in_specs=(
            P("ctx", "tp"),
            P("tp", None),
            P("ctx", "tp"),
            P("ctx", "tp"),
            P("tp", "ctx"),
            P("ctx", "tp", None, None),
            P("tp"),
        ),
        out_specs=(P("ctx", "tp"), P("ctx", "tp"), P("tp", "ctx")),
        check_vma=False,
    )
```

time: 399 us -> 149 us (0.37)
  the two profiles are of different devices: /device:TPU:96 before, /device:TPU:2 now
where the time goes in v1:
time: 149 us
  starting transfers between devices  34.8 us (23%)
  waiting for transfers between devices  34.2 us (23%)
  blocking collectives  24.6 us (17%)
  Pallas kernels  23.2 us (16%)
  matrix products  13.4 us (9%)
  local copies, waits for them, and re-layouts  11.8 us (8%)
  other arithmetic  5.63 us (4%)
    all_gather x1, blocking collectives, per_device(): lax.all_gather(jnp.zeros((8, 128), F32).at[0, :heads].set(total), 'ctx')  24.6 us
    ppermute x6, waiting for transfers between devices, per_device(): right = lax.ppermute(right, 'tp', shift(tp, 1))  17.1 us
    ppermute x6, starting transfers between devices, per_device(): left = lax.ppermute(left, 'tp', shift(tp, -1))  15.5 us
    dot_general x14, matrix products, dot(): return lax.dot_general(a, b, (dims, ((), ())), preferred_element_type=F32)  13.4 us
    ppermute x6, waiting for transfers between devices, per_device(): left = lax.ppermute(left, 'tp', shift(tp, -1))  12.5 us
    pallas_call x2, Pallas kernels, inside(): pl.pallas_call(body, name='inside', grid=(2,), in_specs=in_specs, out_spe...  9.45 us
    ppermute x2, starting transfers between devices, per_device(): down = lax.ppermute(left[BLOCK:], 'tp', shift(tp, -1))  6.57 us
    pallas_call x1, Pallas kernels, finish(): pl.pallas_call(body, name='finish', grid=(blocks,), in_specs=[smem, smem,...  5.76 us
  transfers between devices with their start and end apart: 23, of which 7 were waited for; matrix products, arithmetic and copies ran while one was open for 17% of the time, Pallas kernels for 11%

profile of v1, /device:TPU:2, one launch (start us, length us, event | category | flops | bytes accessed | tf_op | source)
XLA Modules:
  0.0 149.0 jit_solution(38568757259401288)
XLA Ops:
  0.6 2.2 %fusion.45 = (bf16[512,512]{1,0:T(8,128)(2,1)}, bf16[512,512]{1,0:T(8,128)(2,1)}) fusion(bf16[1024,512]{1,0:T(8,128)(2,1)} %param.9), kind=kLoop, calls=%fused_computation.98 | loop fusion | bytes 2097152 | tf_op jit(solution)/shard_map/slice | solution.py:333
  2.9 1.9 %collective-permute-start.8 = (bf16[512,512]{1,0:T(8,128)(2,1)}, bf16[512,512]{1,0:T(8,128)(2,1)}, u32[]{:S(2)}, u32[]{:S(2)}) collective-permute-start(bf16[512,512]{1,0:T(8,128)(2,1)} %get-tuple-element.53), channel_id=1, source_target_pairs={{0,1},{1,2},{2,3},{3,4},{4,5},{5,6},{6,7},{7,0},{8,9},{9,10},{10,1... | collective-permute-start | bytes 1572872 | tf_op jit(solution)/shard_map/ppermute | solution.py:337
  4.8 3.9 %collective-permute-start.9 = (bf16[512,512]{1,0:T(8,128)(2,1)}, bf16[512,512]{1,0:T(8,128)(2,1)}, u32[]{:S(2)}, u32[]{:S(2)}) collective-permute-start(bf16[512,512]{1,0:T(8,128)(2,1)} %get-tuple-element.53), channel_id=1, source_target_pairs={{0,7},{1,0},{2,1},{3,2},{4,3},{5,4},{6,5},{7,6},{8,15},{9,8},{10,9... | collective-permute-start | bytes 1572872 | tf_op jit(solution)/shard_map/ppermute | solution.py:338
  8.7 3.2 %collective-permute-start.1 = (bf16[512,512]{1,0:T(8,128)(2,1)}, bf16[512,512]{1,0:T(8,128)(2,1)}, u32[]{:S(2)}, u32[]{:S(2)}) collective-permute-start(bf16[512,512]{1,0:T(8,128)(2,1)} %get-tuple-element.54), channel_id=1, source_target_pairs={{0,7},{1,0},{2,1},{3,2},{4,3},{5,4},{6,5},{7,6},{8,15},{9,8},{10,9... | collective-permute-start | bytes 1572872 | tf_op jit(solution)/shard_map/ppermute | solution.py:338
  12.0 0.8 reshape.297
  12.8 4.8 %reduce-window.6 = f32[4,4,2,128]{3,2,1,0:T(2,128)S(1)} reduce-window(f32[4,4,2,128]{3,2,1,0:T(2,128)S(1)} %reshape.297, f32[]{:T(128)} %constant.270.clone.1), window={size=1x1x1x128 pad=0_0x0_0x0_0x127_0}, to_apply=%region_0.1 | reduce-window | flops 520192 | bytes 32772 | tf_op jit(solution)/shard_map/reduce-window
  18.9 1.2 broadcast_in_dim.50
  20.1 1.5 %copy.125 = f32[128,8,4,128]{3,1,2,0:T(8,128)} copy(f32[128,8,4,128]{3,2,1,0:T(4,128)S(1)} %bitcast.62) | data formatting | bytes 4194304
  21.8 0.5 copy.96
  22.5 0.5 copy.98.sw_ref
  23.1 5.1 %prepare.1 = (bf16[4,4,256,256]{3,2,1,0:T(8,128)(2,1)S(1)}, bf16[4,4,256,256]{3,2,1,0:T(8,128)(2,1)}, bf16[4,4,64,256]{3,2,1,0:T(8,128)(2,1)S(1)}, bf16[1024,512]{1,0:T(8,128)(2,1)S(1)}) custom-call(f32[4,4]{1,0:T(4,128)S(1)} %bitcast.55, bf16[1024,512]{1,0:T(8,128)(2,1)S(1)} %copy-done, bf16[1024,512]{1,0:T(8,128)(2,1)S(1)} %copy.98.sw_ref, ...), custom_call_target="tpu_custom_call" | custom-call | flops 4000000000 | bytes 9000000 | tf_op jit(solution)/shard_map/prepare/pallas_call | solution.py:68
  28.2 1.3 copy-done.2
  29.5 1.0 copy-done.4
  30.6 24.6 %all_gather.7 = f32[32,8,128]{2,1,0:T(8,128)S(1)} all-gather(f32[1,8,128]{2,1,0:T(8,128)S(1)} %scatter.4), channel_id=1, replica_groups=mesh['ctx'=32,'tp'=8] {'ctx'}, dimensions={0}, use_global_device_ids=true | all-gather | bytes 135168 | tf_op jit(solution)/shard_map/all_gather | solution.py:325
  55.3 1.1 constant_dynamic-slice_fusion.refs_4_
  56.8 1.8 %fusion.22 = f32[512,512]{0,1:T(8,128)S(1)} fusion(bf16[512,4096]{1,0:T(8,128)(2,1)} %param.10, s32[]{:T(128)S(6)} %select_n.386, bf16[1024,512]{1,0:T(8,128)(2,1)} %param.9), kind=kOutput, calls=%fused_computation.31 | convolution fusion | flops 268435456 | bytes 2097156 | tf_op jit(solution)/shard_map/dot_general | solution.py:17
  58.6 1.7 %fusion.24 = f32[512,512]{0,1:T(8,128)S(1)} fusion(bf16[512,4096]{1,0:T(8,128)(2,1)} %param.10, s32[]{:T(128)S(6)} %select_n.386, bf16[1024,512]{1,0:T(8,128)(2,1)} %param.9), kind=kOutput, calls=%fused_computation.33 | convolution fusion | flops 268435456 | bytes 2097156 | tf_op jit(solution)/shard_map/dot_general | solution.py:17
  60.3 0.9 collective-permute-start.11
  61.2 1.2 collective-permute-start.10
  62.5 1.5 %convolution_add_fusion.3 = f32[512,512]{0,1:T(8,128)S(1)} fusion(f32[512,512]{0,1:T(8,128)S(1)} %fusion.22, bf16[512,512]{1,0:T(8,128)(2,1)} %collective-permute-done.8, bf16[512,4096]{1,0:T(8,128)(2,1)S(1)} %copy-done.7, s32[]{:T(128)S(6)} %select_n.388), kind=kOutput, calls=%fused_computation.7 | convolution fusion | flops 268697600 | bytes 3145732 | tf_op jit(solution)/shard_map/dot_general | solution.py:17
  64.0 1.5 %convolution_add_fusion.7 = f32[512,512]{0,1:T(8,128)S(1)} fusion(f32[512,512]{0,1:T(8,128)S(1)} %fusion.24, bf16[512,512]{1,0:T(8,128)(2,1)} %collective-permute-done, bf16[512,4096]{1,0:T(8,128)(2,1)S(1)} %copy-done.7, s32[]{:T(128)S(6)} %select_n.388), kind=kOutput, calls=%fused_computation.14 | convolution fusion | flops 268697600 | bytes 3145732 | tf_op jit(solution)/shard_map/dot_general | solution.py:17
  65.6 3.4 %collective-permute-start.3 = (bf16[512,512]{1,0:T(8,128)(2,1)}, bf16[512,512]{1,0:T(8,128)(2,1)S(1)}, u32[]{:S(2)}, u32[]{:S(2)}) collective-permute-start(bf16[512,512]{1,0:T(8,128)(2,1)} %collective-permute-done.1), channel_id=1, source_target_pairs={{0,7},{1,0},{2,1},{3,2},{4,3},{5,4},{6,5},{7,6},{8,15},{9,8},{10,9... | collective-permute-start | bytes 1572872 | tf_op jit(solution)/shard_map/ppermute | solution.py:338
  69.0 1.5 %convolution_add_fusion.2 = f32[512,512]{0,1:T(8,128)S(1)} fusion(f32[512,512]{0,1:T(8,128)S(1)} %convolution_add_fusion.3, bf16[512,512]{1,0:T(8,128)(2,1)} %collective-permute-done.9, bf16[512,4096]{1,0:T(8,128)(2,1)S(1)} %copy-done.7, s32[]{:T(128)S(6)} %select_n.390), kind=kOutput, calls=%fused_computation.6 | convolution fusion | flops 268697600 | bytes 3145732 | tf_op jit(solution)/shard_map/dot_general | solution.py:17
  70.5 1.5 %convolution_add_fusion.6 = f32[512,512]{0,1:T(8,128)S(1)} fusion(f32[512,512]{0,1:T(8,128)S(1)} %convolution_add_fusion.7, bf16[512,512]{1,0:T(8,128)(2,1)} %collective-permute-done.1, bf16[512,4096]{1,0:T(8,128)(2,1)S(1)} %copy-done.7, s32[]{:T(128)S(6)} %select_n.390), kind=kOutput, calls=%fused_computation.13 | convolution fusion | flops 268697600 | bytes 3145732 | tf_op jit(solution)/shard_map/dot_general | solution.py:17
  72.0 3.3 %collective-permute-done.11 = bf16[512,512]{1,0:T(8,128)(2,1)S(1)} collective-permute-done((bf16[512,512]{1,0:T(8,128)(2,1)}, bf16[512,512]{1,0:T(8,128)(2,1)S(1)}, u32[]{:S(2)}, u32[]{:S(2)}) %collective-permute-start.11) | collective-permute-done | bytes 524320 | tf_op jit(solution)/shard_map/ppermute | solution.py:338
  75.3 2.0 %collective-permute-start.13 = (bf16[512,512]{1,0:T(8,128)(2,1)S(1)}, bf16[512,512]{1,0:T(8,128)(2,1)S(1)}, u32[]{:S(2)}, u32[]{:S(2)}) collective-permute-start(bf16[512,512]{1,0:T(8,128)(2,1)S(1)} %collective-permute-done.11), channel_id=1, source_target_pairs={{0,7},{1,0},{2,1},{3,2},{4,3},{5,4},{6,5},{7,6},{8,15},{9,8},{10,9... | collective-permute-start | bytes 1572872 | tf_op jit(solution)/shard_map/ppermute | solution.py:338
  77.4 9.2 %collective-permute-done.3 = bf16[512,512]{1,0:T(8,128)(2,1)S(1)} collective-permute-done((bf16[512,512]{1,0:T(8,128)(2,1)}, bf16[512,512]{1,0:T(8,128)(2,1)S(1)}, u32[]{:S(2)}, u32[]{:S(2)}) %collective-permute-start.3) | collective-permute-done | bytes 524320 | tf_op jit(solution)/shard_map/ppermute | solution.py:338
  86.6 2.0 %collective-permute-start.5 = (bf16[512,512]{1,0:T(8,128)(2,1)S(1)}, bf16[512,512]{1,0:T(8,128)(2,1)S(1)}, u32[]{:S(2)}, u32[]{:S(2)}) collective-permute-start(bf16[512,512]{1,0:T(8,128)(2,1)S(1)} %collective-permute-done.3), channel_id=1, source_target_pairs={{0,7},{1,0},{2,1},{3,2},{4,3},{5,4},{6,5},{7,6},{8,15},{9,8},{10,9... | collective-permute-start | bytes 1572872 | tf_op jit(solution)/shard_map/ppermute | solution.py:338
  89.2 0.5 fusion.2
  90.2 0.5 fusion.5
  90.6 9.2 %collective-permute-done.12 = bf16[512,512]{1,0:T(8,128)(2,1)S(1)} collective-permute-done((bf16[512,512]{1,0:T(8,128)(2,1)S(1)}, bf16[512,512]{1,0:T(8,128)(2,1)S(1)}, u32[]{:S(2)}, u32[]{:S(2)}) %collective-permute-start.12) | collective-permute-done | bytes 524320 | tf_op jit(solution)/shard_map/ppermute | solution.py:337
  100.0 3.3 %collective-permute-start.15 = (bf16[256,512]{1,0:T(8,128)(2,1)S(1)}, bf16[256,512]{1,0:T(8,128)(2,1)S(1)}, u32[]{:S(2)}, u32[]{:S(2)}) collective-permute-start(bf16[256,512]{1,0:T(8,128)(2,1)S(1)} %slice.100), channel_id=1, source_target_pairs={{0,7},{1,0},{2,1},{3,2},{4,3},{5,4},{6,5},{7,6},{8,15},{9,8},{10,9... | collective-permute-start | bytes 786440 | tf_op jit(solution)/shard_map/ppermute | solution.py:341
  103.3 7.8 %collective-permute-done.4 = bf16[512,512]{1,0:T(8,128)(2,1)S(1)} collective-permute-done((bf16[512,512]{1,0:T(8,128)(2,1)S(1)}, bf16[512,512]{1,0:T(8,128)(2,1)S(1)}, u32[]{:S(2)}, u32[]{:S(2)}) %collective-permute-start.4) | collective-permute-done | bytes 524320 | tf_op jit(solution)/shard_map/ppermute | solution.py:337
  111.3 3.3 %collective-permute-start.7 = (bf16[256,512]{1,0:T(8,128)(2,1)S(1)}, bf16[256,512]{1,0:T(8,128)(2,1)S(1)}, u32[]{:S(2)}, u32[]{:S(2)}) collective-permute-start(bf16[256,512]{1,0:T(8,128)(2,1)S(1)} %slice.98), channel_id=1, source_target_pairs={{0,7},{1,0},{2,1},{3,2},{4,3},{5,4},{6,5},{7,6},{8,15},{9,8},{10,9... | collective-permute-start | bytes 786440 | tf_op jit(solution)/shard_map/ppermute | solution.py:341
  115.0 0.5 fusion.8
  115.5 0.5 fusion.1.refs_1_
  116.0 0.5 fusion.4.refs_1_
  116.7 1.4 close_chunk.2
  118.2 3.3 %collective-permute-done.6.refs_2_ = bf16[256,512]{1,0:T(8,128)(2,1)S(1)} collective-permute-done((bf16[256,512]{1,0:T(8,128)(2,1)S(1)}, bf16[256,512]{1,0:T(8,128)(2,1)S(1)}, u32[]{:S(2)}, u32[]{:S(2)}) %collective-permute-start.6) | collective-permute-done | bytes 262176 | tf_op jit(solution)/shard_map/ppermute | solution.py:340
  121.5 1.4 close_chunk.3
  123.2 1.1 collective-permute-done.16.refs_0_
  124.7 2.3 %collective-permute-start.18 = (bf16[4,64,128]{2,1,0:T(8,128)(2,1)S(1)}, bf16[4,64,128]{2,1,0:T(8,128)(2,1)S(1)}, u32[]{:S(2)}, u32[]{:S(2)}) collective-permute-start(bf16[4,64,128]{2,1,0:T(8,128)(2,1)S(1)} %add_convert_fusion.1), channel_id=1, source_target_pairs={{0,32},{8,40},{16,48},{24,56},{32,0},{40,8},{48,16},{56,24},{64,96... | collective-permute-start | bytes 196616 | tf_op jit(solution)/shard_map/ppermute | solution.py:393
  126.9 1.8 %collective-permute-start.19 = (bf16[4,64,128]{2,1,0:T(8,128)(2,1)S(1)}, bf16[4,64,128]{2,1,0:T(8,128)(2,1)S(1)}, u32[]{:S(2)}, u32[]{:S(2)}) collective-permute-start(bf16[4,64,128]{2,1,0:T(8,128)(2,1)S(1)} %add_convert_fusion.1), channel_id=1, source_target_pairs={{0,48},{8,56},{16,0},{24,8},{32,16},{40,24},{48,32},{56,40},{64,11... | collective-permute-start | bytes 196616 | tf_op jit(solution)/shard_map/ppermute | solution.py:393
  128.8 4.6 %inside.2 = (f32[1024,512]{1,0:T(8,128)}, f32[1024,512]{1,0:T(8,128)}, f32[4,1024]{1,0:T(4,128)S(1)}) custom-call(bf16[512,512]{1,0:T(8,128)(2,1)S(1)} %get-tuple-element.38.dy_ref.refs_7_, bf16[1024,512]{1,0:T(8,128)(2,1)S(1)} %copy-done.1, bf16[1024,512]{1,0:T(8,128)(2,1)S(1)} %copy-done, bf16[1024,512]{1,0:T(8,128)(2,1)S(1)} %copy.98.sw_ref, ...), custom_call_target="tpu_custom_call" | custom-call | flops 2000000000 | bytes 7000000 | tf_op jit(solution)/shard_map/inside/pallas_call | solution.py:203
  133.9 2.7 %collective-permute-start.21 = (bf16[4,64,128]{2,1,0:T(8,128)(2,1)S(1)}, bf16[4,64,128]{2,1,0:T(8,128)(2,1)S(1)}, u32[]{:S(2)}, u32[]{:S(2)}) collective-permute-start(bf16[4,64,128]{2,1,0:T(8,128)(2,1)S(1)} %add_convert_fusion), channel_id=1, source_target_pairs={{0,128},{8,136},{16,144},{24,152},{32,160},{40,168},{48,176},{56,1... | collective-permute-start | bytes 196616 | tf_op jit(solution)/shard_map/ppermute | solution.py:400
  136.5 1.8 %collective-permute-start.22 = (bf16[4,64,128]{2,1,0:T(8,128)(2,1)S(1)}, bf16[4,64,128]{2,1,0:T(8,128)(2,1)S(1)}, u32[]{:S(2)}, u32[]{:S(2)}) collective-permute-start(bf16[4,64,128]{2,1,0:T(8,128)(2,1)S(1)} %add_convert_fusion), channel_id=1, source_target_pairs={{0,192},{8,200},{16,208},{24,216},{32,224},{40,232},{48,240},{56,2... | collective-permute-start | bytes 196616 | tf_op jit(solution)/shard_map/ppermute | solution.py:400
  138.3 4.8 %inside.3 = (f32[1024,512]{1,0:T(8,128)}, f32[1024,512]{1,0:T(8,128)}, f32[4,1024]{1,0:T(4,128)S(1)}) custom-call(bf16[512,512]{1,0:T(8,128)(2,1)S(1)} %get-tuple-element.40.dy_ref.refs_8_, bf16[1024,512]{1,0:T(8,128)(2,1)S(1)} %copy-done.1, bf16[1024,512]{1,0:T(8,128)(2,1)S(1)} %copy-done, ...), custom_call_target="tpu_custom_call", output_to_operand_aliasing={{0}: (8, {}), {1}: (9, {}), {2}: (10, {})} | custom-call | flops 2000000000 | bytes 7000000 | tf_op jit(solution)/shard_map/inside/pallas_call | solution.py:203
  143.2 5.8 %finish.1 = (bf16[1024,512]{1,0:T(8,128)(2,1)}, f32[1024,512]{1,0:T(8,128)}, f32[4,1024]{1,0:T(4,128)}) custom-call(f32[7,4]{1,0:T(8,128)S(1)} %slice.96.coefs_ref, f32[1,4]{1,0:T(1,128)S(1)} %bitcast.57, f32[4,4]{1,0:T(4,128)S(1)} %bitcast.56, bf16[4,64,128]{2,1,0:T(8,128)(2,1)S(1)} %collective-permute-done.16.refs_0_, ...), custom_call_target="tpu_custom_call" | custom-call | flops 600000000 | bytes 14000000 | tf_op jit(solution)/shard_map/finish/pallas_call | solution.py:275
  (84 shorter events, 5.1 us)
Async XLA Ops:
  2.9 58.3 %collective-permute-start.8 = (bf16[512,512]{1,0:T(8,128)(2,1)}, bf16[512,512]{1,0:T(8,128)(2,1)}, u32[]{:S(2)}, u32[]{:S(2)}) collective-permute-start(bf16[512,512]{1,0:T(8,128)(2,1)} %get-tuple-element.53), channel_id=1, source_target_pairs={{0,1},{1,2},{2,3},{3,4},{4,5},{5,6},{6,7},{7,0},{8,9},{9,10},{10,1... | collective-permute-start | bytes 1572872 | tf_op jit(solution)/shard_map/ppermute | solution.py:337
  4.8 55.5 %collective-permute-start.9 = (bf16[512,512]{1,0:T(8,128)(2,1)}, bf16[512,512]{1,0:T(8,128)(2,1)}, u32[]{:S(2)}, u32[]{:S(2)}) collective-permute-start(bf16[512,512]{1,0:T(8,128)(2,1)} %get-tuple-element.53), channel_id=1, source_target_pairs={{0,7},{1,0},{2,1},{3,2},{4,3},{5,4},{6,5},{7,6},{8,15},{9,8},{10,9... | collective-permute-start | bytes 1572872 | tf_op jit(solution)/shard_map/ppermute | solution.py:338
  8.7 53.7 %collective-permute-start = (bf16[512,512]{1,0:T(8,128)(2,1)}, bf16[512,512]{1,0:T(8,128)(2,1)}, u32[]{:S(2)}, u32[]{:S(2)}) collective-permute-start(bf16[512,512]{1,0:T(8,128)(2,1)} %get-tuple-element.54), channel_id=1, source_target_pairs={{0,1},{1,2},{2,3},{3,4},{4,5},{5,6},{6,7},{7,0},{8,9},{9,10},{10,1... | collective-permute-start | bytes 1572872 | tf_op jit(solution)/shard_map/ppermute | solution.py:337
  8.7 56.8 %collective-permute-start.1 = (bf16[512,512]{1,0:T(8,128)(2,1)}, bf16[512,512]{1,0:T(8,128)(2,1)}, u32[]{:S(2)}, u32[]{:S(2)}) collective-permute-start(bf16[512,512]{1,0:T(8,128)(2,1)} %get-tuple-element.54), channel_id=1, source_target_pairs={{0,7},{1,0},{2,1},{3,2},{4,3},{5,4},{6,5},{7,6},{8,15},{9,8},{10,9... | collective-permute-start | bytes 1572872 | tf_op jit(solution)/shard_map/ppermute | solution.py:338
  12.0 9.9 %copy-start = (bf16[1024,512]{1,0:T(8,128)(2,1)S(1)}, bf16[1024,512]{1,0:T(8,128)(2,1)}, u32[]{:S(2)}) copy-start(bf16[1024,512]{1,0:T(8,128)(2,1)} %refs_10_.1) | copy-start | bytes 3145732
  28.2 1.3 copy-start.2
  29.5 1.0 copy-start.4
  56.7 5.8 %copy-start.7 = (bf16[512,4096]{1,0:T(8,128)(2,1)S(1)}, bf16[512,4096]{1,0:T(8,128)(2,1)}, u32[]{:S(2)}) copy-start(bf16[512,4096]{1,0:T(8,128)(2,1)} %param.10) | copy-start | bytes 12582916
  60.3 15.0 %collective-permute-start.11 = (bf16[512,512]{1,0:T(8,128)(2,1)}, bf16[512,512]{1,0:T(8,128)(2,1)S(1)}, u32[]{:S(2)}, u32[]{:S(2)}) collective-permute-start(bf16[512,512]{1,0:T(8,128)(2,1)} %collective-permute-done.9), channel_id=1, source_target_pairs={{0,7},{1,0},{2,1},{3,2},{4,3},{5,4},{6,5},{7,6},{8,15},{9,8},{10,9... | collective-permute-start | bytes 1572872 | tf_op jit(solution)/shard_map/ppermute | solution.py:338
  61.2 16.2 %collective-permute-start.10 = (bf16[512,512]{1,0:T(8,128)(2,1)}, bf16[512,512]{1,0:T(8,128)(2,1)S(1)}, u32[]{:S(2)}, u32[]{:S(2)}) collective-permute-start(bf16[512,512]{1,0:T(8,128)(2,1)} %collective-permute-done.8), channel_id=1, source_target_pairs={{0,1},{1,2},{2,3},{3,4},{4,5},{5,6},{6,7},{7,0},{8,9},{9,10},{10,1... | collective-permute-start | bytes 1572872 | tf_op jit(solution)/shard_map/ppermute | solution.py:337
  62.4 26.7 %collective-permute-start.2 = (bf16[512,512]{1,0:T(8,128)(2,1)}, bf16[512,512]{1,0:T(8,128)(2,1)S(1)}, u32[]{:S(2)}, u32[]{:S(2)}) collective-permute-start(bf16[512,512]{1,0:T(8,128)(2,1)} %collective-permute-done), channel_id=1, source_target_pairs={{0,1},{1,2},{2,3},{3,4},{4,5},{5,6},{6,7},{7,0},{8,9},{9,10},{10,1... | collective-permute-start | bytes 1572872 | tf_op jit(solution)/shard_map/ppermute | solution.py:337
  65.6 21.0 %collective-permute-start.3 = (bf16[512,512]{1,0:T(8,128)(2,1)}, bf16[512,512]{1,0:T(8,128)(2,1)S(1)}, u32[]{:S(2)}, u32[]{:S(2)}) collective-permute-start(bf16[512,512]{1,0:T(8,128)(2,1)} %collective-permute-done.1), channel_id=1, source_target_pairs={{0,7},{1,0},{2,1},{3,2},{4,3},{5,4},{6,5},{7,6},{8,15},{9,8},{10,9... | collective-permute-start | bytes 1572872 | tf_op jit(solution)/shard_map/ppermute | solution.py:338
  75.3 24.7 %collective-permute-start.13 = (bf16[512,512]{1,0:T(8,128)(2,1)S(1)}, bf16[512,512]{1,0:T(8,128)(2,1)S(1)}, u32[]{:S(2)}, u32[]{:S(2)}) collective-permute-start(bf16[512,512]{1,0:T(8,128)(2,1)S(1)} %collective-permute-done.11), channel_id=1, source_target_pairs={{0,7},{1,0},{2,1},{3,2},{4,3},{5,4},{6,5},{7,6},{8,15},{9,8},{10,9... | collective-permute-start | bytes 1572872 | tf_op jit(solution)/shard_map/ppermute | solution.py:338
  77.4 22.5 %collective-permute-start.12 = (bf16[512,512]{1,0:T(8,128)(2,1)S(1)}, bf16[512,512]{1,0:T(8,128)(2,1)S(1)}, u32[]{:S(2)}, u32[]{:S(2)}) collective-permute-start(bf16[512,512]{1,0:T(8,128)(2,1)S(1)} %collective-permute-done.10), channel_id=1, source_target_pairs={{0,1},{1,2},{2,3},{3,4},{4,5},{5,6},{6,7},{7,0},{8,9},{9,10},{10,1... | collective-permute-start | bytes 1572872 | tf_op jit(solution)/shard_map/ppermute | solution.py:337
  86.6 24.7 %collective-permute-start.5 = (bf16[512,512]{1,0:T(8,128)(2,1)S(1)}, bf16[512,512]{1,0:T(8,128)(2,1)S(1)}, u32[]{:S(2)}, u32[]{:S(2)}) collective-permute-start(bf16[512,512]{1,0:T(8,128)(2,1)S(1)} %collective-permute-done.3), channel_id=1, source_target_pairs={{0,7},{1,0},{2,1},{3,2},{4,3},{5,4},{6,5},{7,6},{8,15},{9,8},{10,9... | collective-permute-start | bytes 1572872 | tf_op jit(solution)/shard_map/ppermute | solution.py:338
  89.1 22.0 %collective-permute-start.4 = (bf16[512,512]{1,0:T(8,128)(2,1)S(1)}, bf16[512,512]{1,0:T(8,128)(2,1)S(1)}, u32[]{:S(2)}, u32[]{:S(2)}) collective-permute-start(bf16[512,512]{1,0:T(8,128)(2,1)S(1)} %collective-permute-done.2), channel_id=1, source_target_pairs={{0,1},{1,2},{2,3},{3,4},{4,5},{5,6},{6,7},{7,0},{8,9},{9,10},{10,1... | collective-permute-start | bytes 1572872 | tf_op jit(solution)/shard_map/ppermute | solution.py:337
  99.9 16.8 %collective-permute-start.14 = (bf16[256,512]{1,0:T(8,128)(2,1)S(1)}, bf16[256,512]{1,0:T(8,128)(2,1)S(1)}, u32[]{:S(2)}, u32[]{:S(2)}) collective-permute-start(bf16[256,512]{1,0:T(8,128)(2,1)S(1)} %slice.99), channel_id=1, source_target_pairs={{0,1},{1,2},{2,3},{3,4},{4,5},{5,6},{6,7},{7,0},{8,9},{9,10},{10,1... | collective-permute-start | bytes 786440 | tf_op jit(solution)/shard_map/ppermute | solution.py:340
  100.0 16.7 %collective-permute-start.15 = (bf16[256,512]{1,0:T(8,128)(2,1)S(1)}, bf16[256,512]{1,0:T(8,128)(2,1)S(1)}, u32[]{:S(2)}, u32[]{:S(2)}) collective-permute-start(bf16[256,512]{1,0:T(8,128)(2,1)S(1)} %slice.100), channel_id=1, source_target_pairs={{0,7},{1,0},{2,1},{3,2},{4,3},{5,4},{6,5},{7,6},{8,15},{9,8},{10,9... | collective-permute-start | bytes 786440 | tf_op jit(solution)/shard_map/ppermute | solution.py:341
  111.1 10.3 %collective-permute-start.6 = (bf16[256,512]{1,0:T(8,128)(2,1)S(1)}, bf16[256,512]{1,0:T(8,128)(2,1)S(1)}, u32[]{:S(2)}, u32[]{:S(2)}) collective-permute-start(bf16[256,512]{1,0:T(8,128)(2,1)S(1)} %slice.97), channel_id=1, source_target_pairs={{0,1},{1,2},{2,3},{3,4},{4,5},{5,6},{6,7},{7,0},{8,9},{9,10},{10,1... | collective-permute-start | bytes 786440 | tf_op jit(solution)/shard_map/ppermute | solution.py:340
  111.3 10.2 %collective-permute-start.7 = (bf16[256,512]{1,0:T(8,128)(2,1)S(1)}, bf16[256,512]{1,0:T(8,128)(2,1)S(1)}, u32[]{:S(2)}, u32[]{:S(2)}) collective-permute-start(bf16[256,512]{1,0:T(8,128)(2,1)S(1)} %slice.98), channel_id=1, source_target_pairs={{0,7},{1,0},{2,1},{3,2},{4,3},{5,4},{6,5},{7,6},{8,15},{9,8},{10,9... | collective-permute-start | bytes 786440 | tf_op jit(solution)/shard_map/ppermute | solution.py:341
  116.0 7.0 %copy-start.3 = (f32[4,4,64,128]{3,2,1,0:T(8,128)S(1)}, f32[4,4,64,128]{3,2,1,0:T(8,128)}, u32[]{:S(2)}) copy-start(f32[4,4,64,128]{3,2,1,0:T(8,128)} %refs_15_.1) | copy-start | bytes 1572868
  116.5 12.2 %copy-start.1 = (bf16[1024,512]{1,0:T(8,128)(2,1)S(1)}, bf16[1024,512]{1,0:T(8,128)(2,1)}, u32[]{:S(2)}) copy-start(bf16[1024,512]{1,0:T(8,128)(2,1)} %refs_9_.1) | copy-start | bytes 3145732
  122.9 1.3 collective-permute-start.16
  124.4 9.0 %collective-permute-start.17 = (bf16[4,64,128]{2,1,0:T(8,128)(2,1)S(1)}, bf16[4,64,128]{2,1,0:T(8,128)(2,1)S(1)}, u32[]{:S(2)}, u32[]{:S(2)}) collective-permute-start(bf16[4,64,128]{2,1,0:T(8,128)(2,1)S(1)} %add_convert_fusion.1), channel_id=1, source_target_pairs={{0,16},{8,24},{16,32},{24,40},{32,48},{40,56},{48,0},{56,8},{64,80... | collective-permute-start | bytes 196616 | tf_op jit(solution)/shard_map/ppermute | solution.py:393
  124.7 8.7 %collective-permute-start.18 = (bf16[4,64,128]{2,1,0:T(8,128)(2,1)S(1)}, bf16[4,64,128]{2,1,0:T(8,128)(2,1)S(1)}, u32[]{:S(2)}, u32[]{:S(2)}) collective-permute-start(bf16[4,64,128]{2,1,0:T(8,128)(2,1)S(1)} %add_convert_fusion.1), channel_id=1, source_target_pairs={{0,32},{8,40},{16,48},{24,56},{32,0},{40,8},{48,16},{56,24},{64,96... | collective-permute-start | bytes 196616 | tf_op jit(solution)/shard_map/ppermute | solution.py:393
  126.9 6.5 %collective-permute-start.19 = (bf16[4,64,128]{2,1,0:T(8,128)(2,1)S(1)}, bf16[4,64,128]{2,1,0:T(8,128)(2,1)S(1)}, u32[]{:S(2)}, u32[]{:S(2)}) collective-permute-start(bf16[4,64,128]{2,1,0:T(8,128)(2,1)S(1)} %add_convert_fusion.1), channel_id=1, source_target_pairs={{0,48},{8,56},{16,0},{24,8},{32,16},{40,24},{48,32},{56,40},{64,11... | collective-permute-start | bytes 196616 | tf_op jit(solution)/shard_map/ppermute | solution.py:393
  133.5 9.6 %collective-permute-start.20 = (bf16[4,64,128]{2,1,0:T(8,128)(2,1)S(1)}, bf16[4,64,128]{2,1,0:T(8,128)(2,1)S(1)}, u32[]{:S(2)}, u32[]{:S(2)}) collective-permute-start(bf16[4,64,128]{2,1,0:T(8,128)(2,1)S(1)} %add_convert_fusion), channel_id=1, source_target_pairs={{0,64},{8,72},{16,80},{24,88},{32,96},{40,104},{48,112},{56,120},{... | collective-permute-start | bytes 196616 | tf_op jit(solution)/shard_map/ppermute | solution.py:400
  133.9 9.3 %collective-permute-start.21 = (bf16[4,64,128]{2,1,0:T(8,128)(2,1)S(1)}, bf16[4,64,128]{2,1,0:T(8,128)(2,1)S(1)}, u32[]{:S(2)}, u32[]{:S(2)}) collective-permute-start(bf16[4,64,128]{2,1,0:T(8,128)(2,1)S(1)} %add_convert_fusion), channel_id=1, source_target_pairs={{0,128},{8,136},{16,144},{24,152},{32,160},{40,168},{48,176},{56,1... | collective-permute-start | bytes 196616 | tf_op jit(solution)/shard_map/ppermute | solution.py:400
  136.5 6.6 %collective-permute-start.22 = (bf16[4,64,128]{2,1,0:T(8,128)(2,1)S(1)}, bf16[4,64,128]{2,1,0:T(8,128)(2,1)S(1)}, u32[]{:S(2)}, u32[]{:S(2)}) collective-permute-start(bf16[4,64,128]{2,1,0:T(8,128)(2,1)S(1)} %add_convert_fusion), channel_id=1, source_target_pairs={{0,192},{8,200},{16,208},{24,216},{32,224},{40,232},{48,240},{56,2... | collective-permute-start | bytes 196616 | tf_op jit(solution)/shard_map/ppermute | solution.py:400
  138.3 4.8 %copy-start.5 = (bf16[1024,512]{1,0:T(8,128)(2,1)S(1)}, bf16[1024,512]{1,0:T(8,128)(2,1)}, u32[]{:S(2)}) copy-start(bf16[1024,512]{1,0:T(8,128)(2,1)} %copy-done.4) | copy-start | bytes 3145732
  138.3 4.8 %copy-start.6 = (f32[4]{0:T(128)S(1)}, f32[4]{0:T(128)}, u32[]{:S(2)}) copy-start(f32[4]{0:T(128)} %param.15) | copy-start | bytes 52

commit v2 on v1

--- a/solution.py
+++ b/solution.py
@@ -10,7 +10,7 @@
 BLOCK = 256
 F32 = jnp.float32
 BF16 = jnp.bfloat16
-VMEM_LIMIT = 48 << 20
+VMEM_LIMIT = 20 << 20
 
 
 def dot(a, b, dims):
@@ -26,8 +26,7 @@
     return lax.broadcasted_iota(jnp.int32, shape, len(shape) - 1) < STATE
 
 
-def prepare_kernel(heads, a_last, bc_ref, sw_ref, arow_ref, acol_ref, dec_ref, sct_ref, wct_ref, wb_ref):
-    b = pl.program_id(0)
+def prepare_kernel(heads, bc_ref, sw_ref, arow_ref, acol_ref, dec_ref, sct_ref, wct_ref):
     rows = lax.broadcasted_iota(jnp.int32, (BLOCK, BLOCK), 0)
     cols = lax.broadcasted_iota(jnp.int32, (BLOCK, BLOCK), 1)
     low = low_lanes((BLOCK, HEAD_DIM))
@@ -48,18 +47,16 @@
         sct_ref[0, h] = (scores * back).astype(BF16)
         weighted = c_low.astype(F32) * jnp.exp(col1)
         wct_ref[0, h] = weighted.T[:STATE, :].astype(BF16)
-        tail = jnp.exp(a_last[b, h] - col1)
-        wb_ref[:, lanes] = (b_low.astype(F32) * tail).astype(BF16)
 
 
 def prepare_body(heads):
-    def body(a_last, bc_ref, sw_ref, arow_ref, acol_ref, dec_ref, sct_ref, wct_ref, wb_ref):
-        prepare_kernel(heads, a_last, bc_ref, sw_ref, arow_ref, acol_ref, dec_ref, sct_ref, wct_ref, wb_ref)
+    def body(*refs):
+        prepare_kernel(heads, *refs)
 
     return body
 
 
-def prepare(a_last, bc, sw, arow, acol):
+def prepare(bc, sw, arow, acol):
     tokens, width = bc.shape
     heads = width // HEAD_DIM
     blocks = tokens // BLOCK
@@ -70,7 +67,6 @@
         name="prepare",
         grid=(blocks,),
         in_specs=[
-            pl.BlockSpec(memory_space=pltpu.SMEM),
             wide,
             wide,
             pl.BlockSpec((heads, BLOCK), lambda b: (0, b)),
@@ -80,17 +76,15 @@
             square,
             square,
             pl.BlockSpec((1, heads, STATE, BLOCK), lambda b: (b, 0, 0, 0)),
-            wide,
         ],
         out_shape=[
             jax.ShapeDtypeStruct((blocks, heads, BLOCK, BLOCK), BF16),
             jax.ShapeDtypeStruct((blocks, heads, BLOCK, BLOCK), BF16),
             jax.ShapeDtypeStruct((blocks, heads, STATE, BLOCK), BF16),
-            jax.ShapeDtypeStruct((tokens, width), BF16),
         ],
         cost_estimate=pl.CostEstimate(flops=4_000_000_000, bytes_accessed=9_000_000, transcendentals=0),
         compiler_params=pltpu.CompilerParams(vmem_limit_bytes=VMEM_LIMIT),
-    )(a_last, bc, sw, arow, acol)
+    )(bc, sw, arow, acol)
 
 
 def close_chunk(first, acc, up, down, weight, wct, scale, earlier):
@@ -145,17 +139,18 @@
     )(*operands)
 
 
-def inside(first, dy, x, bc, sw, acol, dec, sct, spad, before):
-    width = x.shape[1]
-    tokens = x.shape[0]
+def inside(first, count, dy_first, dy, skip, x, bc, sw, acol, dec, sct, spad, before):
+    tokens, width = x.shape
     heads = width // HEAD_DIM
-
-    def body(dy_ref, x_ref, bc_ref, sw_ref, acol_ref, dec_ref, sct_ref, spad_ref, *rest):
+    group = heads // 2
+
+    def body(skip_ref, dy_ref, x_ref, bc_ref, sw_ref, acol_ref, dec_ref, sct_ref, spad_ref, *rest):
         dx_ref, dbc_ref, dlog_ref = rest[-3:]
+        base = pl.program_id(1) * group
         rows = lax.broadcasted_iota(jnp.int32, (BLOCK, BLOCK), 0)
         cols = lax.broadcasted_iota(jnp.int32, (BLOCK, BLOCK), 1)
         low = low_lanes((BLOCK, HEAD_DIM))
-        for h in range(heads):
+        for h in range(group):
             lanes = slice(h * HEAD_DIM, (h + 1) * HEAD_DIM)
             dy_h = dy_ref[:, lanes]
             x_h = x_ref[:, lanes]
@@ -164,36 +159,29 @@
             zero = jnp.zeros_like(sw_h)
             gaps = dot(dy_h, x_h, NT)
             mixed = (gaps * dec_ref[0, h].astype(F32)).astype(BF16)
-            dx_ref[:, lanes] = dot(sct_ref[0, h], dy_h, NN)
+            dx_ref[:, lanes] = dot(sct_ref[0, h], dy_h, NN) + skip_ref[0, base + h] * dy_h.astype(F32)
             grad = dot(mixed, jnp.where(low, zero, sw_h), NN)
             grad = grad + dot(mixed, jnp.where(low, sw_h, zero), TN)
             grad = grad + jnp.exp(acol_ref[:, lanes]) * dot(dy_h, spad_ref[0, h], NT)
             dbc_ref[:, lanes] = grad
             signed = grad * bc_h.astype(F32)
             moved = jnp.sum(jnp.where(low, -signed, signed), axis=1, keepdims=True)
-            dlog_ref[h : h + 1, :] = jnp.sum(
-                jnp.where(rows >= cols, moved, 0.0), axis=0, keepdims=True
-            )
-
-    def at(b):
-        return (b + first, 0)
-
-    def at4(b):
-        return (b + first, 0, 0, 0)
-
-    wide = pl.BlockSpec((BLOCK, width), at)
-    square = pl.BlockSpec((1, heads, BLOCK, BLOCK), at4)
+            dlog_ref[h] = jnp.sum(jnp.where(rows >= cols, moved, 0.0), axis=0, keepdims=True)
+
+    wide = pl.BlockSpec((BLOCK, group * HEAD_DIM), lambda b, g: (b + first, g))
+    square = pl.BlockSpec((1, group, BLOCK, BLOCK), lambda b, g: (b + first, g, 0, 0))
     in_specs = [
-        pl.BlockSpec((BLOCK, width), lambda b: (b, 0)),
+        pl.BlockSpec(memory_space=pltpu.SMEM),
+        pl.BlockSpec((BLOCK, group * HEAD_DIM), lambda b, g: (b + dy_first, g)),
         wide,
         wide,
         wide,
         wide,
         square,
         square,
-        pl.BlockSpec((1, heads, HEAD_DIM, HEAD_DIM), at4),
+        pl.BlockSpec((1, group, HEAD_DIM, HEAD_DIM), lambda b, g: (b + first, g, 0, 0)),
     ]
-    operands = [dy, x, bc, sw, acol, dec, sct, spad]
+    operands = [skip, dy, x, bc, sw, acol, dec, sct, spad]
     aliases = {}
     if before is not None:
         for place, array in enumerate(before):
@@ -203,30 +191,32 @@
     return pl.pallas_call(
         body,
         name="inside",
-        grid=(2,),
+        grid=(count, 2),
         in_specs=in_specs,
-        out_specs=[wide, wide, pl.BlockSpec((heads, BLOCK), lambda b: (0, b + first))],
+        out_specs=[wide, wide, pl.BlockSpec((group, 1, BLOCK), lambda b, g: (g, 0, b + first))],
         out_shape=[
             jax.ShapeDtypeStruct((tokens, width), F32),
             jax.ShapeDtypeStruct((tokens, width), F32),
-            jax.ShapeDtypeStruct((heads, tokens), F32),
+            jax.ShapeDtypeStruct((heads, 1, tokens), F32),
         ],
         input_output_aliases=aliases,
-        cost_estimate=pl.CostEstimate(flops=2_000_000_000, bytes_accessed=7_000_000, transcendentals=0),
+        cost_estimate=pl.CostEstimate(
+            flops=1_000_000_000 * count, bytes_accessed=3_500_000 * count, transcendentals=0
+        ),
         compiler_params=pltpu.CompilerParams(vmem_limit_bytes=VMEM_LIMIT),
     )(*operands)
 
 
-def finish(coefs, skip, a_last, received, dys, x, bc, acol, wb, terms, states, dx, dbc, dlog):
+def finish(coefs, a_last, received, x, bc, aline, terms, states, dx, dbc, dlog):
     tokens, width = x.shape
     heads = width // HEAD_DIM
     blocks = tokens // BLOCK
     count = len(received)
 
-    def body(coefs_ref, skip_ref, last_ref, *refs):
+    def body(coefs_ref, last_ref, *refs):
         got = refs[:count]
-        (dy0_ref, dy1_ref, x_ref, bc_ref, acol_ref, wb_ref, terms0_ref, terms1_ref, states_ref, dx_ref, dbc_ref,
-         dlog_ref, out_ref, outbc_ref, outlog_ref, carry_ref) = refs[count:]
+        (x_ref, bc_ref, aline_ref, terms0_ref, terms1_ref, states_ref, dx_ref, dbc_ref, dlog_ref, out_ref,
+         outbc_ref, outlog_ref, carry_ref) = refs[count:]
         step = pl.program_id(0)
         b = blocks - 1 - step
 
@@ -240,68 +230,58 @@
 
         rows = lax.broadcasted_iota(jnp.int32, (BLOCK, BLOCK), 0)
         cols = lax.broadcasted_iota(jnp.int32, (BLOCK, BLOCK), 1)
-        late = step < 2
+        late = step < blocks // 2
         for h in range(heads):
             lanes = slice(h * HEAD_DIM, (h + 1) * HEAD_DIM)
             carry = carry_ref[h]
             carry16 = carry.astype(BF16)
-            dy_h = jnp.where(late, dy1_ref[:, lanes], dy0_ref[:, lanes]).astype(F32)
-            grad = dx_ref[:, lanes] + dot(wb_ref[:, lanes][:, :STATE], carry16, NN)
-            out_ref[:, lanes] = (grad + skip_ref[0, h] * dy_h).astype(BF16)
+            last = last_ref[b, h]
+            tail = jnp.exp(last - aline_ref[:, h : h + 1])
+            bc_h = bc_ref[:, lanes].astype(F32)
+            weighted = (bc_h * tail).astype(BF16)[:, :STATE]
+            out_ref[:, lanes] = (dx_ref[:, lanes] + dot(weighted, carry16, NN)).astype(BF16)
             padded = jnp.concatenate([carry16, jnp.zeros_like(carry16)], axis=0)
-            last = last_ref[b, h]
-            extra = jnp.exp(last - acol_ref[:, lanes]) * dot(x_ref[:, lanes], padded, NT)
+            extra = tail * dot(x_ref[:, lanes], padded, NT)
             outbc_ref[:, lanes] = dbc_ref[:, lanes] + extra
-            moved = jnp.sum(extra * bc_ref[:, lanes].astype(F32), axis=1, keepdims=True)
+            moved = jnp.sum(extra * bc_h, axis=1, keepdims=True)
             ends = jnp.exp(jnp.full((1, HEAD_DIM), last, F32))
             whole = jnp.sum(jnp.sum(states_ref[0, h] * carry, axis=0, keepdims=True) * ends)
             outlog_ref[h : h + 1, :] = (
-                dlog_ref[h : h + 1, :]
-                + jnp.sum(jnp.where(rows < cols, moved, 0.0), axis=0, keepdims=True)
-                + whole
+                dlog_ref[h] + jnp.sum(jnp.where(rows < cols, moved, 0.0), axis=0, keepdims=True) + whole
             )
             carry_ref[h] = ends * carry + jnp.where(late, terms1_ref[0, h], terms0_ref[0, h])
 
-    def at(i):
-        return (blocks - 1 - i, 0)
-
-    def at4(i):
-        return (blocks - 1 - i, 0, 0, 0)
-
-    wide = pl.BlockSpec((BLOCK, width), at)
+    wide = pl.BlockSpec((BLOCK, width), lambda i: (blocks - 1 - i, 0))
     smem = pl.BlockSpec(memory_space=pltpu.SMEM)
     state_block = (1, heads, STATE, HEAD_DIM)
-    line = pl.BlockSpec((heads, BLOCK), lambda i: (0, blocks - 1 - i))
+    half = blocks // 2
     return pl.pallas_call(
         body,
         name="finish",
         grid=(blocks,),
-        in_specs=[smem, smem, smem]
+        in_specs=[smem, smem]
         + [pl.BlockSpec((heads, STATE, HEAD_DIM), lambda i: (0, 0, 0)) for _ in received]
         + [
-            pl.BlockSpec((BLOCK, width), lambda i: (jnp.clip(3 - i, 0, 1), 0)),
-            pl.BlockSpec((BLOCK, width), lambda i: (jnp.clip(1 - i, 0, 1), 0)),
-            wide,
-            wide,
-            wide,
-            wide,
-            pl.BlockSpec(state_block, lambda i: (jnp.clip(3 - i, 0, 1), 0, 0, 0)),
-            pl.BlockSpec(state_block, lambda i: (jnp.clip(1 - i, 0, 1), 0, 0, 0)),
-            pl.BlockSpec(state_block, at4),
-            wide,
-            wide,
-            line,
-        ],
-        out_specs=[wide, wide, line],
+            wide,
+            wide,
+            pl.BlockSpec((BLOCK, heads), lambda i: (blocks - 1 - i, 0)),
+            pl.BlockSpec(state_block, lambda i: (jnp.clip(blocks - 1 - i, 0, half - 1), 0, 0, 0)),
+            pl.BlockSpec(state_block, lambda i: (jnp.clip(half - 1 - i, 0, half - 1), 0, 0, 0)),
+            pl.BlockSpec(state_block, lambda i: (blocks - 1 - i, 0, 0, 0)),
+            wide,
+            wide,
+            pl.BlockSpec((heads, 1, BLOCK), lambda i: (0, 0, blocks - 1 - i)),
+        ],
+        out_specs=[wide, wide, pl.BlockSpec((heads, BLOCK), lambda i: (0, blocks - 1 - i))],
         out_shape=[
             jax.ShapeDtypeStruct((tokens, width), BF16),
             jax.ShapeDtypeStruct((tokens, width), F32),
             jax.ShapeDtypeStruct((heads, tokens), F32),
         ],
         scratch_shapes=[pltpu.VMEM((heads, STATE, HEAD_DIM), F32)],
-        cost_estimate=pl.CostEstimate(flops=600_000_000, bytes_accessed=14_000_000, transcendentals=0),
+        cost_estimate=pl.CostEstimate(flops=600_000_000, bytes_accessed=11_000_000, transcendentals=0),
         compiler_params=pltpu.CompilerParams(vmem_limit_bytes=VMEM_LIMIT),
-    )(coefs, skip, a_last, *received, dys[0], dys[1], x, bc, acol, wb, terms[0], terms[1], states, dx, dbc, dlog)
+    )(coefs, a_last, *received, x, bc, aline, terms[0], terms[1], states, dx, dbc, dlog)
 
 
 def shift(count, by):
@@ -322,7 +302,7 @@
     cum = jnp.cumsum(logs, axis=-1)
     last = cum[:, :, -1].T
     total = jnp.sum(last, axis=0)
-    all_logs = lax.all_gather(jnp.zeros((8, 128), F32).at[0, :heads].set(total), "ctx")[:, 0, :heads]
+    all_logs = lax.all_gather(jnp.zeros((64, 128), F32).at[0, :heads].set(total), "ctx")[:, 0, :heads]
 
     def weight_of(source):
         return lax.dynamic_slice_in_dim(out_weight, (source % tp) * feats, feats, 1)
@@ -331,6 +311,8 @@
     accs, lasts = [], []
     for c in range(2):
         own = upstream[c * half : (c + 1) * half]
+        if c == 0:
+            upstream, _ = lax.optimization_barrier((upstream, own))
         right = left = own
         acc = dot(own, weight_of(me), NT)
         for k in range(1, tp // 2):
@@ -344,9 +326,10 @@
     weight_last = weight_of(me + tp // 2)
 
     arow = cum.reshape(heads, tokens)
-    acol = jnp.repeat(arow.T, HEAD_DIM, axis=1)
+    aline = arow.T
+    acol = jnp.repeat(aline, HEAD_DIM, axis=1)
     swapped = head_bc.reshape(tokens, heads, 2, STATE)[:, :, ::-1, :].reshape(tokens, width)
-    dec, sct, wct, wb = prepare(last, head_bc, swapped, arow, acol)
+    dec, sct, wct = prepare(head_bc, swapped, arow, acol)
     spad = jnp.pad(states, ((0, 0), (0, 0), (STATE, 0), (0, 0))).astype(BF16)
     ahead = jnp.exp(jnp.cumsum(last, axis=0) - last)
 
@@ -376,7 +359,16 @@
     sums = jnp.sum(jnp.where(masks[:, :, None], all_logs[None], 0.0), axis=1)
     coefs = jnp.where(valid[:, None], jnp.exp(sums), 0.0)
 
+    skips = skip[None]
+
+    def within(first, count, dy_first, dy, before):
+        return inside(
+            first, count, dy_first, dy, skips, inner_act, head_bc, swapped, acol, dec, sct, spad, before
+        )
+
     dy0, terms0 = close_chunk(0, accs[0], *lasts[0], weight_last, wct, ahead, None)
+    grads = within(0, 2, 0, dy0, None)
+    lasts[1], coefs, grads = lax.optimization_barrier((lasts[1], coefs, grads))
     dy1, terms1, part = close_chunk(2, accs[1], *lasts[1], weight_last, wct, ahead, terms0)
 
     def by(i):
@@ -391,18 +383,17 @@
     other = lax.ppermute(part16, "ctx", perm(0, 0, 1))
     chip_sum = (by(0) * part + by(1) * other.astype(F32)).astype(BF16)
     ys = [lax.ppermute(chip_sum, "ctx", perm(0, s, 0)) for s in (1, 2, 3)]
-    dy0, chip_sum = lax.optimization_barrier((dy0, chip_sum))
-    grads = inside(0, dy0, inner_act, head_bc, swapped, acol, dec, sct, spad, None)
+    dy1, chip_sum = lax.optimization_barrier((dy1, chip_sum))
+    grads = within(2, 1, 0, dy1, grads)
     row_sum = by(2) * chip_sum.astype(F32)
     for s in range(3):
         row_sum = row_sum + by(3 + s) * ys[s].astype(F32)
     row_sum = row_sum.astype(BF16)
     xs = [lax.ppermute(row_sum, "ctx", perm(s, 0, 0)) for s in (1, 2, 3)]
     dy1, row_sum = lax.optimization_barrier((dy1, row_sum))
-    dx, dbc, dlog = inside(2, dy1, inner_act, head_bc, swapped, acol, dec, sct, spad, grads)
+    dx, dbc, dlog = within(3, 1, 1, dy1, grads)
     return finish(
-        coefs[6:], skip[None], last, [other] + ys + xs, (dy0, dy1), inner_act, head_bc, acol, wb,
-        (terms0, terms1), states, dx, dbc, dlog,
+        coefs[6:], last, [other] + ys + xs, inner_act, head_bc, aline, (terms0, terms1), states, dx, dbc, dlog
     )
 
 

time: 149 us -> 160 us (1.074); the launches traced: 149 us -> 157 us
  blocking collectives: 24.6 us -> 0 us
  local copies, waits for them, and re-layouts: 11.8 us -> 35 us
  between operations: 1.32 us -> 14.9 us
  Pallas kernels: 23.2 us -> 18.7 us
  waiting for transfers between devices: 34.2 us -> 30.9 us
  starting transfers between devices: 34.8 us -> 37.3 us
    all_gather x1 -> x0, blocking collectives: 24.6 us -> none  [per_device(): lax.all_gather(jnp.zeros((8, 128), F32).at[0, :heads].set(total), 'ctx')]
    unnamed x18 -> x60, local copies, waits for them, and re-layouts: 4.35 us -> 18.5 us
    ppermute x6, waiting for transfers between devices: 12.5 us -> 6.35 us  [per_device(): left = lax.ppermute(left, 'tp', shift(tp, -1))]
    ppermute x6, starting transfers between devices: 15.5 us -> 20.9 us  [per_device(): left = lax.ppermute(left, 'tp', shift(tp, -1))]
    ppermute x6, waiting for transfers between devices: 17.1 us -> 21 us  [per_device(): right = lax.ppermute(right, 'tp', shift(tp, 1))]
    ppermute x6, starting transfers between devices: 3.3 us -> 0.12 us  [per_device(): right = lax.ppermute(right, 'tp', shift(tp, 1))]
    pallas_call x1, Pallas kernels: 5.14 us -> 2.29 us  [prepare(): pl.pallas_call(prepare_body(heads), name='prepare', grid=(blocks,), in_sp...]
    pallas_call x3 -> x4, Pallas kernels: 15.2 us -> 13.1 us  [the longest x3 8.82 us: inside(): pl.pallas_call(body, name='inside', grid=(count, 2), in_specs=in_specs, o...]
  transfers between devices with their start and end apart: 23 -> 24, of which waited for: 7 -> 7; matrix products, arithmetic and copies ran while one was open for 17% -> 22% of each run, Pallas kernels for 11% -> 8%
where the time goes in v2:
time: 160 us; the launch traced here: 157 us
  starting transfers between devices  37.3 us (23%)
  local copies, waits for them, and re-layouts  35 us (22%)
  waiting for transfers between devices  30.9 us (19%)
  Pallas kernels  18.7 us (12%)
  between operations  14.9 us (9%)
  matrix products  14.5 us (9%)
  other arithmetic  5.63 us (4%)
    ppermute x6, waiting for transfers between devices, per_device(): right = lax.ppermute(right, 'tp', shift(tp, 1))  21 us
    ppermute x6, starting transfers between devices, per_device(): left = lax.ppermute(left, 'tp', shift(tp, -1))  20.9 us
    unnamed x60, local copies, waits for them, and re-layouts  18.5 us
    dot_general x14, matrix products, dot(): return lax.dot_general(a, b, (dims, ((), ())), preferred_element_type=F32)  14.5 us
    pallas_call x3, Pallas kernels, inside(): pl.pallas_call(body, name='inside', grid=(count, 2), in_specs=in_specs, o...  8.82 us
    ppermute x2, starting transfers between devices, per_device(): down = lax.ppermute(left[BLOCK:], 'tp', shift(tp, -1))  6.5 us
    ppermute x6, waiting for transfers between devices, per_device(): left = lax.ppermute(left, 'tp', shift(tp, -1))  6.35 us
    another operation x4, other arithmetic  4.97 us
  transfers between devices with their start and end apart: 24, of which 7 were waited for; matrix products, arithmetic and copies ran while one was open for 22% of the time, Pallas kernels for 8%

profile of v2, /device:TPU:2, one launch (start us, length us, event | category | flops | bytes accessed | tf_op | source)
XLA Modules:
  0.0 156.9 jit_solution(1750840890310933252)
XLA Ops:
  7.2 2.0 %slice.73 = bf16[512,512]{1,0:T(8,128)(2,1)} slice(bf16[1024,512]{1,0:T(8,128)(2,1)} %param.9), slice={[0:512], [0:512]} | slice | bytes 1048576 | tf_op jit(solution)/shard_map/slice | solution.py:313
  9.2 1.9 %slice.74 = bf16[512,512]{1,0:T(8,128)(2,1)} slice(bf16[1024,512]{1,0:T(8,128)(2,1)} %param.9), slice={[512:1024], [0:512]} | slice | bytes 1048576 | tf_op jit(solution)/shard_map/slice | solution.py:313
  11.1 5.9 %collective-permute-start.4 = (bf16[512,512]{1,0:T(8,128)(2,1)}, bf16[512,512]{1,0:T(8,128)(2,1)}, u32[]{:S(2)}, u32[]{:S(2)}) collective-permute-start(bf16[512,512]{1,0:T(8,128)(2,1)} %slice.74), channel_id=1, source_target_pairs={{0,7},{1,0},{2,1},{3,2},{4,3},{5,4},{6,5},{7,6},{8,15},{9,8},{10,9... | collective-permute-start | bytes 1572872 | tf_op jit(solution)/shard_map/ppermute | solution.py:320
  16.9 3.3 %collective-permute-start.9 = (bf16[512,512]{1,0:T(8,128)(2,1)}, bf16[512,512]{1,0:T(8,128)(2,1)}, u32[]{:S(2)}, u32[]{:S(2)}) collective-permute-start(bf16[512,512]{1,0:T(8,128)(2,1)} %slice.73), channel_id=1, source_target_pairs={{0,7},{1,0},{2,1},{3,2},{4,3},{5,4},{6,5},{7,6},{8,15},{9,8},{10,9... | collective-permute-start | bytes 1572872 | tf_op jit(solution)/shard_map/ppermute | solution.py:320
  21.0 4.8 %reduce-window.6 = f32[4,4,2,128]{3,2,1,0:T(2,128)S(1)} reduce-window(f32[4,4,2,128]{3,2,1,0:T(2,128)S(1)} %reshape.297, f32[]{:T(128)} %constant.270.clone.1), window={size=1x1x1x128 pad=0_0x0_0x0_0x127_0}, to_apply=%region_0.1 | reduce-window | flops 520192 | bytes 32772 | tf_op jit(solution)/shard_map/reduce-window
  28.3 1.3 copy.83
  29.6 1.3 rev.3
  31.0 1.3 copy.85.refs_1_.sw_ref
  32.3 1.2 broadcast_in_dim.50
  33.7 2.3 %prepare.1 = (bf16[4,4,256,256]{3,2,1,0:T(8,128)(2,1)S(1)}, bf16[4,4,256,256]{3,2,1,0:T(8,128)(2,1)S(1)}, bf16[4,4,64,256]{3,2,1,0:T(8,128)(2,1)S(1)}) custom-call(bf16[1024,512]{1,0:T(8,128)(2,1)S(1)} %copy-done, bf16[1024,512]{1,0:T(8,128)(2,1)S(1)} %copy-done.13, f32[4,1024]{1,0:T(4,128)S(1)} %copy.86.refs_2_, f32[1024,512]{1,0:T(8,128)S(1)} %bitcast.53), custom_call_target="tpu_custom_call" | custom-call | flops 4000000000 | bytes 9000000 | tf_op jit(solution)/shard_map/prepare/pallas_call | solution.py:65
  36.0 1.3 copy-done.1
  37.3 1.3 copy-done.4
  40.4 1.9 %constant_dynamic-slice_fusion.refs_4_ = bf16[512,512]{1,0:T(8,128)(2,1)} fusion(bf16[512,4096]{1,0:T(8,128)(2,1)} %param.10, s32[]{:T(128)S(6)} %select_n.400), kind=kLoop, calls=%fused_computation.51 | loop fusion | bytes 1048580 | tf_op jit(solution)/shard_map/dynamic_slice | solution.py:308
  42.5 1.8 %fusion.21 = f32[512,512]{1,0:T(8,128)S(1)} fusion(bf16[512,4096]{1,0:T(8,128)(2,1)} %param.10, s32[]{:T(128)S(6)} %select_n.386, bf16[1024,512]{1,0:T(8,128)(2,1)} %param.9), kind=kOutput, calls=%fused_computation.30 | convolution fusion | flops 268435456 | bytes 2097156 | tf_op jit(solution)/shard_map/dot_general | solution.py:17
  44.4 1.7 %fusion.23 = f32[512,512]{0,1:T(8,128)S(1)} fusion(bf16[512,4096]{1,0:T(8,128)(2,1)} %param.10, s32[]{:T(128)S(6)} %select_n.386, bf16[1024,512]{1,0:T(8,128)(2,1)} %param.9), kind=kOutput, calls=%fused_computation.32 | convolution fusion | flops 268435456 | bytes 2097156 | tf_op jit(solution)/shard_map/dot_general | solution.py:17
  46.1 2.1 %collective-permute-start.5 = (bf16[512,512]{1,0:T(8,128)(2,1)}, bf16[512,512]{1,0:T(8,128)(2,1)S(1)}, u32[]{:S(2)}, u32[]{:S(2)}) collective-permute-start(bf16[512,512]{1,0:T(8,128)(2,1)} %collective-permute-done.4), channel_id=1, source_target_pairs={{0,7},{1,0},{2,1},{3,2},{4,3},{5,4},{6,5},{7,6},{8,15},{9,8},{10,9... | collective-permute-start | bytes 1572872 | tf_op jit(solution)/shard_map/ppermute | solution.py:320
  48.3 3.2 %collective-permute-start.11 = (bf16[512,512]{1,0:T(8,128)(2,1)}, bf16[512,512]{1,0:T(8,128)(2,1)S(1)}, u32[]{:S(2)}, u32[]{:S(2)}) collective-permute-start(bf16[512,512]{1,0:T(8,128)(2,1)} %collective-permute-done.9), channel_id=1, source_target_pairs={{0,7},{1,0},{2,1},{3,2},{4,3},{5,4},{6,5},{7,6},{8,15},{9,8},{10,9... | collective-permute-start | bytes 1572872 | tf_op jit(solution)/shard_map/ppermute | solution.py:320
  51.5 1.5 convolution_add_fusion.3
  53.0 1.5 convolution_add_fusion.7
  54.5 1.5 convolution_add_fusion.2
  56.1 1.5 convolution_add_fusion.6
  57.6 3.6 %collective-permute-done.5 = bf16[512,512]{1,0:T(8,128)(2,1)S(1)} collective-permute-done((bf16[512,512]{1,0:T(8,128)(2,1)}, bf16[512,512]{1,0:T(8,128)(2,1)S(1)}, u32[]{:S(2)}, u32[]{:S(2)}) %collective-permute-start.5) | collective-permute-done | bytes 524320 | tf_op jit(solution)/shard_map/ppermute | solution.py:320
  61.2 3.2 %collective-permute-start.6 = (bf16[512,512]{1,0:T(8,128)(2,1)S(1)}, bf16[512,512]{1,0:T(8,128)(2,1)S(1)}, u32[]{:S(2)}, u32[]{:S(2)}) collective-permute-start(bf16[512,512]{1,0:T(8,128)(2,1)S(1)} %collective-permute-done.5), channel_id=1, source_target_pairs={{0,7},{1,0},{2,1},{3,2},{4,3},{5,4},{6,5},{7,6},{8,15},{9,8},{10,9... | collective-permute-start | bytes 1572872 | tf_op jit(solution)/shard_map/ppermute | solution.py:320
  64.4 11.2 %collective-permute-done.10 = bf16[512,512]{1,0:T(8,128)(2,1)S(1)} collective-permute-done((bf16[512,512]{1,0:T(8,128)(2,1)}, bf16[512,512]{1,0:T(8,128)(2,1)S(1)}, u32[]{:S(2)}, u32[]{:S(2)}) %collective-permute-start.10) | collective-permute-done | bytes 524320 | tf_op jit(solution)/shard_map/ppermute | solution.py:319
  76.2 3.3 %collective-permute-start.13 = (bf16[512,512]{1,0:T(8,128)(2,1)S(1)}, bf16[512,512]{1,0:T(8,128)(2,1)S(1)}, u32[]{:S(2)}, u32[]{:S(2)}) collective-permute-start(bf16[512,512]{1,0:T(8,128)(2,1)S(1)} %collective-permute-done.11), channel_id=1, source_target_pairs={{0,7},{1,0},{2,1},{3,2},{4,3},{5,4},{6,5},{7,6},{8,15},{9,8},{10,9... | collective-permute-start | bytes 1572872 | tf_op jit(solution)/shard_map/ppermute | solution.py:320
  80.9 2.7 %collective-permute-done.6 = bf16[512,512]{1,0:T(8,128)(2,1)S(1)} collective-permute-done((bf16[512,512]{1,0:T(8,128)(2,1)S(1)}, bf16[512,512]{1,0:T(8,128)(2,1)S(1)}, u32[]{:S(2)}, u32[]{:S(2)}) %collective-permute-start.6) | collective-permute-done | bytes 524320 | tf_op jit(solution)/shard_map/ppermute | solution.py:320
  84.4 3.2 %collective-permute-start.7 = (bf16[256,512]{1,0:T(8,128)(2,1)}, bf16[256,512]{1,0:T(8,128)(2,1)}, u32[]{:S(2)}, u32[]{:S(2)}) collective-permute-start(bf16[256,512]{1,0:T(8,128)(2,1)} %slice.93), channel_id=1, source_target_pairs={{0,7},{1,0},{2,1},{3,2},{4,3},{5,4},{6,5},{7,6},{8,15},{9,8},{10,9... | collective-permute-start | bytes 786440 | tf_op jit(solution)/shard_map/ppermute | solution.py:323
  88.3 9.8 %collective-permute-done.12 = bf16[512,512]{1,0:T(8,128)(2,1)S(1)} collective-permute-done((bf16[512,512]{1,0:T(8,128)(2,1)S(1)}, bf16[512,512]{1,0:T(8,128)(2,1)S(1)}, u32[]{:S(2)}, u32[]{:S(2)}) %collective-permute-start.12) | collective-permute-done | bytes 524320 | tf_op jit(solution)/shard_map/ppermute | solution.py:319
  98.3 3.3 %collective-permute-start.15 = (bf16[256,512]{1,0:T(8,128)(2,1)S(1)}, bf16[256,512]{1,0:T(8,128)(2,1)S(1)}, u32[]{:S(2)}, u32[]{:S(2)}) collective-permute-start(bf16[256,512]{1,0:T(8,128)(2,1)S(1)} %slice.99), channel_id=1, source_target_pairs={{0,7},{1,0},{2,1},{3,2},{4,3},{5,4},{6,5},{7,6},{8,15},{9,8},{10,9... | collective-permute-start | bytes 786440 | tf_op jit(solution)/shard_map/ppermute | solution.py:323
  102.6 1.5 fusion.refs_1_
  104.6 2.2 %collective-permute-done.14.refs_2_ = bf16[256,512]{1,0:T(8,128)(2,1)S(1)} collective-permute-done((bf16[256,512]{1,0:T(8,128)(2,1)S(1)}, bf16[256,512]{1,0:T(8,128)(2,1)S(1)}, u32[]{:S(2)}, u32[]{:S(2)}) %collective-permute-start.14) | collective-permute-done | bytes 262176 | tf_op jit(solution)/shard_map/ppermute | solution.py:322
  106.8 1.4 close_chunk.2
  108.3 4.2 %inside.3 = (f32[1024,512]{1,0:T(8,128)S(1)}, f32[1024,512]{1,0:T(8,128)S(1)}, f32[4,1,1024]{2,1,0:T(1,128)S(1)}) custom-call(f32[1,4]{1,0:T(1,128)S(1)} %bitcast.62, bf16[512,512]{1,0:T(8,128)(2,1)S(1)} %get-tuple-element.44.dy_ref, bf16[1024,512]{1,0:T(8,128)(2,1)S(1)} %copy-done.11, bf16[1024,512]{1,0:T(8,128)(2,1)S(1)} %copy-done, ...), custom_call_target="tpu_custom_call" | custom-call | flops 2000000000 | bytes 7000000 | tf_op jit(solution)/shard_map/inside/pallas_call | solution.py:191
  112.5 1.4 copy-done.7
  113.9 1.4 copy-done.9
  117.6 1.2 copy-done.22
  119.7 1.9 %close_chunk.3 = (bf16[512,512]{1,0:T(8,128)(2,1)S(1)}, f32[2,4,64,128]{3,2,1,0:T(8,128)S(1)}, f32[4,64,128]{2,1,0:T(8,128)S(1)}) custom-call(f32[4,4]{1,0:T(4,128)S(1)} %subtract_exponential_fusion.refs_0_, f32[512,512]{1,0:T(8,128)S(1)} %copy-done.22, bf16[256,512]{1,0:T(8,128)(2,1)} %collective-permute-done.3.refs_2_, ...), custom_call_target="tpu_custom_call" | custom-call | flops 600000000 | bytes 4000000 | tf_op jit(solution)/shard_map/close_chunk/pallas_call | solution.py:131
  123.1 3.1 %collective-permute-start.19 = (bf16[4,64,128]{2,1,0:T(8,128)(2,1)S(1)}, bf16[4,64,128]{2,1,0:T(8,128)(2,1)S(1)}, u32[]{:S(2)}, u32[]{:S(2)}) collective-permute-start(bf16[4,64,128]{2,1,0:T(8,128)(2,1)S(1)} %add_convert_fusion.1), channel_id=1, source_target_pairs={{0,48},{8,56},{16,0},{24,8},{32,16},{40,24},{48,32},{56,40},{64,11... | collective-permute-start | bytes 196616 | tf_op jit(solution)/shard_map/ppermute | solution.py:385
  127.8 1.6 %copy-done.6 = bf16[4,4,256,256]{3,2,1,0:T(8,128)(2,1)S(1)} copy-done((bf16[4,4,256,256]{3,2,1,0:T(8,128)(2,1)S(1)}, bf16[4,4,256,256]{3,2,1,0:T(8,128)(2,1)}, u32[]{:S(2)}) %copy-start.6) | copy-done | bytes 2097176
  129.4 1.6 %copy-done.8 = f32[1024,512]{1,0:T(8,128)S(1)} copy-done((f32[1024,512]{1,0:T(8,128)S(1)}, f32[1024,512]{1,0:T(8,128)}, u32[]{:S(2)}) %copy-start.8) | copy-done | bytes 2097176
  131.0 1.6 %copy-done.10 = f32[1024,512]{1,0:T(8,128)S(1)} copy-done((f32[1024,512]{1,0:T(8,128)S(1)}, f32[1024,512]{1,0:T(8,128)}, u32[]{:S(2)}) %copy-start.10) | copy-done | bytes 2097176
  132.6 1.2 copy-done.12
  133.8 1.2 copy-done.15
  136.1 2.3 %inside.4 = (f32[1024,512]{1,0:T(8,128)S(1)}, f32[1024,512]{1,0:T(8,128)S(1)}, f32[4,1,1024]{2,1,0:T(1,128)S(1)}) custom-call(f32[1,4]{1,0:T(1,128)S(1)} %bitcast.63, bf16[512,512]{1,0:T(8,128)(2,1)S(1)} %get-tuple-element.59.dy_ref, bf16[1024,512]{1,0:T(8,128)(2,1)S(1)} %copy-done.12, ...), custom_call_target="tpu_custom_call", output_to_operand_aliasing={{0}: (9, {}), {1}: (10, {}), {2}: (11, {})} | custom-call | flops 1000000000 | bytes 3500000 | tf_op jit(solution)/shard_map/inside/pallas_call | solution.py:191
  139.2 2.4 %collective-permute-start.21 = (bf16[4,64,128]{2,1,0:T(8,128)(2,1)S(1)}, bf16[4,64,128]{2,1,0:T(8,128)(2,1)S(1)}, u32[]{:S(2)}, u32[]{:S(2)}) collective-permute-start(bf16[4,64,128]{2,1,0:T(8,128)(2,1)S(1)} %add_convert_fusion), channel_id=1, source_target_pairs={{0,128},{8,136},{16,144},{24,152},{32,160},{40,168},{48,176},{56,1... | collective-permute-start | bytes 196616 | tf_op jit(solution)/shard_map/ppermute | solution.py:392
  141.6 1.8 %collective-permute-start.20 = (bf16[4,64,128]{2,1,0:T(8,128)(2,1)S(1)}, bf16[4,64,128]{2,1,0:T(8,128)(2,1)S(1)}, u32[]{:S(2)}, u32[]{:S(2)}) collective-permute-start(bf16[4,64,128]{2,1,0:T(8,128)(2,1)S(1)} %add_convert_fusion), channel_id=1, source_target_pairs={{0,64},{8,72},{16,80},{24,88},{32,96},{40,104},{48,112},{56,120},{... | collective-permute-start | bytes 196616 | tf_op jit(solution)/shard_map/ppermute | solution.py:392
  143.4 2.3 %inside.5 = (f32[1024,512]{1,0:T(8,128)S(1)}, f32[1024,512]{1,0:T(8,128)S(1)}, f32[4,1,1024]{2,1,0:T(1,128)S(1)}) custom-call(f32[1,4]{1,0:T(1,128)S(1)} %bitcast.64, bf16[512,512]{1,0:T(8,128)(2,1)S(1)} %get-tuple-element.59.dy_ref, bf16[1024,512]{1,0:T(8,128)(2,1)S(1)} %copy-done.12, ...), custom_call_target="tpu_custom_call", output_to_operand_aliasing={{0}: (9, {}), {1}: (10, {}), {2}: (11, {})} | custom-call | flops 1000000000 | bytes 3500000 | tf_op jit(solution)/shard_map/inside/pallas_call | solution.py:191
  145.8 4.2 %finish.1 = (bf16[1024,512]{1,0:T(8,128)(2,1)}, f32[1024,512]{1,0:T(8,128)}, f32[4,1024]{1,0:T(4,128)}) custom-call(f32[7,4]{1,0:T(8,128)S(1)} %slice.84.coefs_ref, f32[4,4]{1,0:T(4,128)S(1)} %bitcast.61, bf16[4,64,128]{2,1,0:T(8,128)(2,1)S(1)} %collective-permute-done.16.refs_0_, bf16[4,64,128]{2,1,0:T(8,128)(2,1)S(1)} %collective-permute-done.17.refs_1_, ...), custom_call_target="tpu_custom_call" | custom-call | flops 600000000 | bytes 11000000 | tf_op jit(solution)/shard_map/finish/pallas_call | solution.py:258
  (130 shorter events, 18.4 us)
Async XLA Ops:
  7.2 20.8 %copy-start.23 = (f32[4,4,64,128]{3,2,1,0:T(8,128)S(1)}, f32[4,4,64,128]{3,2,1,0:T(8,128)}, u32[]{:S(2)}) copy-start(f32[4,4,64,128]{3,2,1,0:T(8,128)} %refs_12_.1) | copy-start | bytes 1572868
  7.2 21.1 %copy-start = (bf16[1024,512]{1,0:T(8,128)(2,1)S(1)}, bf16[1024,512]{1,0:T(8,128)(2,1)}, u32[]{:S(2)}) copy-start(bf16[1024,512]{1,0:T(8,128)(2,1)} %refs_8_.1) | copy-start | bytes 3145732
  7.2 108.0 %all-gather.2.cloned.1.call-start = ((), (), s32[]{:S(2)}) async-start(), calls=%async_computation | async-start | bytes 1081344 | tf_op jit(solution)/shard_map/all_gather | solution.py:305
  11.1 35.0 %collective-permute-start.4 = (bf16[512,512]{1,0:T(8,128)(2,1)}, bf16[512,512]{1,0:T(8,128)(2,1)}, u32[]{:S(2)}, u32[]{:S(2)}) collective-permute-start(bf16[512,512]{1,0:T(8,128)(2,1)} %slice.74), channel_id=1, source_target_pairs={{0,7},{1,0},{2,1},{3,2},{4,3},{5,4},{6,5},{7,6},{8,15},{9,8},{10,9... | collective-permute-start | bytes 1572872 | tf_op jit(solution)/shard_map/ppermute | solution.py:320
  16.9 31.2 %collective-permute-start = (bf16[512,512]{1,0:T(8,128)(2,1)}, bf16[512,512]{1,0:T(8,128)(2,1)}, u32[]{:S(2)}, u32[]{:S(2)}) collective-permute-start(bf16[512,512]{1,0:T(8,128)(2,1)} %slice.74), channel_id=1, source_target_pairs={{0,1},{1,2},{2,3},{3,4},{4,5},{5,6},{6,7},{7,0},{8,9},{9,10},{10,1... | collective-permute-start | bytes 1572872 | tf_op jit(solution)/shard_map/ppermute | solution.py:319
  16.9 31.2 %collective-permute-start.8 = (bf16[512,512]{1,0:T(8,128)(2,1)}, bf16[512,512]{1,0:T(8,128)(2,1)}, u32[]{:S(2)}, u32[]{:S(2)}) collective-permute-start(bf16[512,512]{1,0:T(8,128)(2,1)} %slice.73), channel_id=1, source_target_pairs={{0,1},{1,2},{2,3},{3,4},{4,5},{5,6},{6,7},{7,0},{8,9},{9,10},{10,1... | collective-permute-start | bytes 1572872 | tf_op jit(solution)/shard_map/ppermute | solution.py:319
  16.9 31.3 %collective-permute-start.9 = (bf16[512,512]{1,0:T(8,128)(2,1)}, bf16[512,512]{1,0:T(8,128)(2,1)}, u32[]{:S(2)}, u32[]{:S(2)}) collective-permute-start(bf16[512,512]{1,0:T(8,128)(2,1)} %slice.73), channel_id=1, source_target_pairs={{0,7},{1,0},{2,1},{3,2},{4,3},{5,4},{6,5},{7,6},{8,15},{9,8},{10,9... | collective-permute-start | bytes 1572872 | tf_op jit(solution)/shard_map/ppermute | solution.py:320
  27.9 5.7 %copy-start.16 = (f32[4,4,2,128]{0,3,2,1:T(8,128)}, f32[4,4,2,128]{0,3,2,1:T(8,128)S(1)}, u32[]{:S(2)}) copy-start(f32[4,4,2,128]{0,3,2,1:T(8,128)S(1)} %copy.84) | copy-start | bytes 49156
  32.3 1.4 copy-start.13
  36.0 1.3 copy-start.1
  37.3 1.3 copy-start.4
  42.5 8.9 %copy-start.28 = (bf16[512,4096]{1,0:T(8,128)(2,1)S(1)}, bf16[512,4096]{1,0:T(8,128)(2,1)}, u32[]{:S(2)}) copy-start(bf16[512,4096]{1,0:T(8,128)(2,1)} %param.10) | copy-start | bytes 12582916
  46.1 15.1 %collective-permute-start.5 = (bf16[512,512]{1,0:T(8,128)(2,1)}, bf16[512,512]{1,0:T(8,128)(2,1)S(1)}, u32[]{:S(2)}, u32[]{:S(2)}) collective-permute-start(bf16[512,512]{1,0:T(8,128)(2,1)} %collective-permute-done.4), channel_id=1, source_target_pairs={{0,7},{1,0},{2,1},{3,2},{4,3},{5,4},{6,5},{7,6},{8,15},{9,8},{10,9... | collective-permute-start | bytes 1572872 | tf_op jit(solution)/shard_map/ppermute | solution.py:320
  48.1 16.3 %collective-permute-start.1 = (bf16[512,512]{1,0:T(8,128)(2,1)}, bf16[512,512]{1,0:T(8,128)(2,1)S(1)}, u32[]{:S(2)}, u32[]{:S(2)}) collective-permute-start(bf16[512,512]{1,0:T(8,128)(2,1)} %collective-permute-done), channel_id=1, source_target_pairs={{0,1},{1,2},{2,3},{3,4},{4,5},{5,6},{6,7},{7,0},{8,9},{9,10},{10,1... | collective-permute-start | bytes 1572872 | tf_op jit(solution)/shard_map/ppermute | solution.py:319
  48.2 27.5 %collective-permute-start.10 = (bf16[512,512]{1,0:T(8,128)(2,1)}, bf16[512,512]{1,0:T(8,128)(2,1)S(1)}, u32[]{:S(2)}, u32[]{:S(2)}) collective-permute-start(bf16[512,512]{1,0:T(8,128)(2,1)} %collective-permute-done.8), channel_id=1, source_target_pairs={{0,1},{1,2},{2,3},{3,4},{4,5},{5,6},{6,7},{7,0},{8,9},{9,10},{10,1... | collective-permute-start | bytes 1572872 | tf_op jit(solution)/shard_map/ppermute | solution.py:319
  48.3 27.9 %collective-permute-start.11 = (bf16[512,512]{1,0:T(8,128)(2,1)}, bf16[512,512]{1,0:T(8,128)(2,1)S(1)}, u32[]{:S(2)}, u32[]{:S(2)}) collective-permute-start(bf16[512,512]{1,0:T(8,128)(2,1)} %collective-permute-done.9), channel_id=1, source_target_pairs={{0,7},{1,0},{2,1},{3,2},{4,3},{5,4},{6,5},{7,6},{8,15},{9,8},{10,9... | collective-permute-start | bytes 1572872 | tf_op jit(solution)/shard_map/ppermute | solution.py:320
  61.2 22.5 %collective-permute-start.6 = (bf16[512,512]{1,0:T(8,128)(2,1)S(1)}, bf16[512,512]{1,0:T(8,128)(2,1)S(1)}, u32[]{:S(2)}, u32[]{:S(2)}) collective-permute-start(bf16[512,512]{1,0:T(8,128)(2,1)S(1)} %collective-permute-done.5), channel_id=1, source_target_pairs={{0,7},{1,0},{2,1},{3,2},{4,3},{5,4},{6,5},{7,6},{8,15},{9,8},{10,9... | collective-permute-start | bytes 1572872 | tf_op jit(solution)/shard_map/ppermute | solution.py:320
  64.4 23.2 %collective-permute-start.2 = (bf16[512,512]{1,0:T(8,128)(2,1)S(1)}, bf16[512,512]{1,0:T(8,128)(2,1)S(1)}, u32[]{:S(2)}, u32[]{:S(2)}) collective-permute-start(bf16[512,512]{1,0:T(8,128)(2,1)S(1)} %collective-permute-done.1), channel_id=1, source_target_pairs={{0,1},{1,2},{2,3},{3,4},{4,5},{5,6},{6,7},{7,0},{8,9},{9,10},{10,1... | collective-permute-start | bytes 1572872 | tf_op jit(solution)/shard_map/ppermute | solution.py:319
  75.7 22.5 %collective-permute-start.12 = (bf16[512,512]{1,0:T(8,128)(2,1)S(1)}, bf16[512,512]{1,0:T(8,128)(2,1)S(1)}, u32[]{:S(2)}, u32[]{:S(2)}) collective-permute-start(bf16[512,512]{1,0:T(8,128)(2,1)S(1)} %collective-permute-done.10), channel_id=1, source_target_pairs={{0,1},{1,2},{2,3},{3,4},{4,5},{5,6},{6,7},{7,0},{8,9},{9,10},{10,1... | collective-permute-start | bytes 1572872 | tf_op jit(solution)/shard_map/ppermute | solution.py:319
  76.2 22.1 %collective-permute-start.13 = (bf16[512,512]{1,0:T(8,128)(2,1)S(1)}, bf16[512,512]{1,0:T(8,128)(2,1)S(1)}, u32[]{:S(2)}, u32[]{:S(2)}) collective-permute-start(bf16[512,512]{1,0:T(8,128)(2,1)S(1)} %collective-permute-done.11), channel_id=1, source_target_pairs={{0,7},{1,0},{2,1},{3,2},{4,3},{5,4},{6,5},{7,6},{8,15},{9,8},{10,9... | collective-permute-start | bytes 1572872 | tf_op jit(solution)/shard_map/ppermute | solution.py:320
  84.4 32.0 %collective-permute-start.7 = (bf16[256,512]{1,0:T(8,128)(2,1)}, bf16[256,512]{1,0:T(8,128)(2,1)}, u32[]{:S(2)}, u32[]{:S(2)}) collective-permute-start(bf16[256,512]{1,0:T(8,128)(2,1)} %slice.93), channel_id=1, source_target_pairs={{0,7},{1,0},{2,1},{3,2},{4,3},{5,4},{6,5},{7,6},{8,15},{9,8},{10,9... | collective-permute-start | bytes 786440 | tf_op jit(solution)/shard_map/ppermute | solution.py:323
  88.3 28.1 %collective-permute-start.3 = (bf16[256,512]{1,0:T(8,128)(2,1)}, bf16[256,512]{1,0:T(8,128)(2,1)}, u32[]{:S(2)}, u32[]{:S(2)}) collective-permute-start(bf16[256,512]{1,0:T(8,128)(2,1)} %slice.92), channel_id=1, source_target_pairs={{0,1},{1,2},{2,3},{3,4},{4,5},{5,6},{6,7},{7,0},{8,9},{9,10},{10,1... | collective-permute-start | bytes 786440 | tf_op jit(solution)/shard_map/ppermute | solution.py:322
  98.1 8.6 %collective-permute-start.14 = (bf16[256,512]{1,0:T(8,128)(2,1)S(1)}, bf16[256,512]{1,0:T(8,128)(2,1)S(1)}, u32[]{:S(2)}, u32[]{:S(2)}) collective-permute-start(bf16[256,512]{1,0:T(8,128)(2,1)S(1)} %slice.98), channel_id=1, source_target_pairs={{0,1},{1,2},{2,3},{3,4},{4,5},{5,6},{6,7},{7,0},{8,9},{9,10},{10,1... | collective-permute-start | bytes 786440 | tf_op jit(solution)/shard_map/ppermute | solution.py:322
  98.3 8.5 %collective-permute-start.15 = (bf16[256,512]{1,0:T(8,128)(2,1)S(1)}, bf16[256,512]{1,0:T(8,128)(2,1)S(1)}, u32[]{:S(2)}, u32[]{:S(2)}) collective-permute-start(bf16[256,512]{1,0:T(8,128)(2,1)S(1)} %slice.99), channel_id=1, source_target_pairs={{0,7},{1,0},{2,1},{3,2},{4,3},{5,4},{6,5},{7,6},{8,15},{9,8},{10,9... | collective-permute-start | bytes 786440 | tf_op jit(solution)/shard_map/ppermute | solution.py:323
  102.5 4.2 %copy-start.20 = (bf16[512,512]{1,0:T(8,128)(2,1)S(1)}, bf16[512,512]{1,0:T(8,128)(2,1)}, u32[]{:S(2)}) copy-start(bf16[512,512]{1,0:T(8,128)(2,1)} %constant_dynamic-slice_fusion.refs_4_) | copy-start | bytes 1572868
  102.5 4.2 %copy-start.26 = (bf16[2,4,64,256]{3,2,1,0:T(8,128)(2,1)S(1)}, bf16[2,4,64,256]{3,2,1,0:T(8,128)(2,1)}, u32[]{:S(2)}) copy-start(bf16[2,4,64,256]{3,2,1,0:T(8,128)(2,1)} %get-tuple-element.72.refs_5_) | copy-start | bytes 786436
  102.5 5.7 %copy-start.18 = (bf16[4,4,128,128]{3,2,1,0:T(8,128)(2,1)S(1)}, bf16[4,4,128,128]{3,2,1,0:T(8,128)(2,1)}, u32[]{:S(2)}) copy-start(bf16[4,4,128,128]{3,2,1,0:T(8,128)(2,1)} %pad.10.spad_ref) | copy-start | bytes 1572868
  104.0 4.2 %copy-start.2 = (bf16[4,4,256,256]{3,2,1,0:T(8,128)(2,1)S(1)}, bf16[4,4,256,256]{3,2,1,0:T(8,128)(2,1)}, u32[]{:S(2)}) copy-start(bf16[4,4,256,256]{3,2,1,0:T(8,128)(2,1)} %copy-done.1) | copy-start | bytes 6291460
  104.0 4.2 %copy-start.5 = (bf16[4,4,256,256]{3,2,1,0:T(8,128)(2,1)S(1)}, bf16[4,4,256,256]{3,2,1,0:T(8,128)(2,1)}, u32[]{:S(2)}) copy-start(bf16[4,4,256,256]{3,2,1,0:T(8,128)(2,1)} %copy-done.4) | copy-start | bytes 6291460
  104.0 4.2 %copy-start.11 = (bf16[1024,512]{1,0:T(8,128)(2,1)S(1)}, bf16[1024,512]{1,0:T(8,128)(2,1)}, u32[]{:S(2)}) copy-start(bf16[1024,512]{1,0:T(8,128)(2,1)} %refs_7_.1) | copy-start | bytes 3145732
  104.0 4.2 %copy-start.14 = (bf16[1024,512]{1,0:T(8,128)(2,1)S(1)}, bf16[1024,512]{1,0:T(8,128)(2,1)}, u32[]{:S(2)}) copy-start(bf16[1024,512]{1,0:T(8,128)(2,1)} %copy.85.refs_1_.sw_ref) | copy-start | bytes 3145732
  104.0 4.2 %copy-start.27 = (f32[4]{0:T(128)S(1)}, f32[4]{0:T(128)}, u32[]{:S(2)}) copy-start(f32[4]{0:T(128)} %param.15) | copy-start | bytes 52
  112.5 1.4 copy-start.7
  113.9 1.4 copy-start.9
  116.2 11.6 %copy-start.3 = (bf16[4,4,256,256]{3,2,1,0:T(8,128)(2,1)S(1)}, bf16[4,4,256,256]{3,2,1,0:T(8,128)(2,1)}, u32[]{:S(2)}) copy-start(bf16[4,4,256,256]{3,2,1,0:T(8,128)(2,1)} %copy-done.1) | copy-start | bytes 6291460
  121.7 1.3 collective-permute-start.16
  123.1 15.3 %collective-permute-start.19 = (bf16[4,64,128]{2,1,0:T(8,128)(2,1)S(1)}, bf16[4,64,128]{2,1,0:T(8,128)(2,1)S(1)}, u32[]{:S(2)}, u32[]{:S(2)}) collective-permute-start(bf16[4,64,128]{2,1,0:T(8,128)(2,1)S(1)} %add_convert_fusion.1), channel_id=1, source_target_pairs={{0,48},{8,56},{16,0},{24,8},{32,16},{40,24},{48,32},{56,40},{64,11... | collective-permute-start | bytes 196616 | tf_op jit(solution)/shard_map/ppermute | solution.py:385
  126.2 12.2 %collective-permute-start.18 = (bf16[4,64,128]{2,1,0:T(8,128)(2,1)S(1)}, bf16[4,64,128]{2,1,0:T(8,128)(2,1)S(1)}, u32[]{:S(2)}, u32[]{:S(2)}) collective-permute-start(bf16[4,64,128]{2,1,0:T(8,128)(2,1)S(1)} %add_convert_fusion.1), channel_id=1, source_target_pairs={{0,32},{8,40},{16,48},{24,56},{32,0},{40,8},{48,16},{56,24},{64,96... | collective-permute-start | bytes 196616 | tf_op jit(solution)/shard_map/ppermute | solution.py:385
  126.8 11.6 %collective-permute-start.17 = (bf16[4,64,128]{2,1,0:T(8,128)(2,1)S(1)}, bf16[4,64,128]{2,1,0:T(8,128)(2,1)S(1)}, u32[]{:S(2)}, u32[]{:S(2)}) collective-permute-start(bf16[4,64,128]{2,1,0:T(8,128)(2,1)S(1)} %add_convert_fusion.1), channel_id=1, source_target_pairs={{0,16},{8,24},{16,32},{24,40},{32,48},{40,56},{48,0},{56,8},{64,80... | collective-permute-start | bytes 196616 | tf_op jit(solution)/shard_map/ppermute | solution.py:385
  127.8 1.6 %copy-start.6 = (bf16[4,4,256,256]{3,2,1,0:T(8,128)(2,1)S(1)}, bf16[4,4,256,256]{3,2,1,0:T(8,128)(2,1)}, u32[]{:S(2)}) copy-start(bf16[4,4,256,256]{3,2,1,0:T(8,128)(2,1)} %copy-done.4) | copy-start | bytes 6291460
  129.4 1.6 %copy-start.8 = (f32[1024,512]{1,0:T(8,128)S(1)}, f32[1024,512]{1,0:T(8,128)}, u32[]{:S(2)}) copy-start(f32[1024,512]{1,0:T(8,128)} %copy-done.7) | copy-start | bytes 6291460
  131.0 1.6 %copy-start.10 = (f32[1024,512]{1,0:T(8,128)S(1)}, f32[1024,512]{1,0:T(8,128)}, u32[]{:S(2)}) copy-start(f32[1024,512]{1,0:T(8,128)} %copy-done.9) | copy-start | bytes 6291460
  132.6 1.2 copy-start.12
  138.5 7.2 %collective-permute-start.22 = (bf16[4,64,128]{2,1,0:T(8,128)(2,1)S(1)}, bf16[4,64,128]{2,1,0:T(8,128)(2,1)S(1)}, u32[]{:S(2)}, u32[]{:S(2)}) collective-permute-start(bf16[4,64,128]{2,1,0:T(8,128)(2,1)S(1)} %add_convert_fusion), channel_id=1, source_target_pairs={{0,192},{8,200},{16,208},{24,216},{32,224},{40,232},{48,240},{56,2... | collective-permute-start | bytes 196616 | tf_op jit(solution)/shard_map/ppermute | solution.py:392
  139.2 6.6 %collective-permute-start.21 = (bf16[4,64,128]{2,1,0:T(8,128)(2,1)S(1)}, bf16[4,64,128]{2,1,0:T(8,128)(2,1)S(1)}, u32[]{:S(2)}, u32[]{:S(2)}) collective-permute-start(bf16[4,64,128]{2,1,0:T(8,128)(2,1)S(1)} %add_convert_fusion), channel_id=1, source_target_pairs={{0,128},{8,136},{16,144},{24,152},{32,160},{40,168},{48,176},{56,1... | collective-permute-start | bytes 196616 | tf_op jit(solution)/shard_map/ppermute | solution.py:392
  141.6 4.3 %collective-permute-start.20 = (bf16[4,64,128]{2,1,0:T(8,128)(2,1)S(1)}, bf16[4,64,128]{2,1,0:T(8,128)(2,1)S(1)}, u32[]{:S(2)}, u32[]{:S(2)}) collective-permute-start(bf16[4,64,128]{2,1,0:T(8,128)(2,1)S(1)} %add_convert_fusion), channel_id=1, source_target_pairs={{0,64},{8,72},{16,80},{24,88},{32,96},{40,104},{48,112},{56,120},{... | collective-permute-start | bytes 196616 | tf_op jit(solution)/shard_map/ppermute | solution.py:392
  143.4 2.4 %copy-start.17 = (f32[4,4,2,128]{0,3,2,1:T(8,128)S(1)}, f32[4,4,2,128]{0,3,2,1:T(8,128)}, u32[]{:S(2)}) copy-start(f32[4,4,2,128]{0,3,2,1:T(8,128)} %copy-done.16) | copy-start | bytes 49156
  143.4 2.4 %copy-start.24 = (f32[4,4,64,128]{3,2,1,0:T(8,128)S(1)}, f32[4,4,64,128]{3,2,1,0:T(8,128)}, u32[]{:S(2)}) copy-start(f32[4,4,64,128]{3,2,1,0:T(8,128)} %refs_12_.1) | copy-start | bytes 1572868
  (5 other events, 5.6 us)
Sparse Core Ops, SparseCore 0:
  27.4 46.5 all-gather.1

commit v3 on v2

--- a/solution.py
+++ b/solution.py
@@ -10,7 +10,7 @@
 BLOCK = 256
 F32 = jnp.float32
 BF16 = jnp.bfloat16
-VMEM_LIMIT = 20 << 20
+VMEM_LIMIT = 60 << 20
 
 
 def dot(a, b, dims):
@@ -26,73 +26,72 @@
     return lax.broadcasted_iota(jnp.int32, shape, len(shape) - 1) < STATE
 
 
-def prepare_kernel(heads, bc_ref, sw_ref, arow_ref, acol_ref, dec_ref, sct_ref, wct_ref):
-    rows = lax.broadcasted_iota(jnp.int32, (BLOCK, BLOCK), 0)
-    cols = lax.broadcasted_iota(jnp.int32, (BLOCK, BLOCK), 1)
-    low = low_lanes((BLOCK, HEAD_DIM))
-    for h in range(heads):
-        lanes = slice(h * HEAD_DIM, (h + 1) * HEAD_DIM)
-        row = arow_ref[h : h + 1, :]
-        col1 = acol_ref[:, lanes]
-        col = jnp.concatenate([col1, col1], axis=1)
-        gap = col - row
-        dec_ref[0, h] = jnp.where(rows >= cols, jnp.exp(jnp.minimum(gap, 0.0)), 0.0).astype(BF16)
-        bc = bc_ref[:, lanes]
-        sw = sw_ref[:, lanes]
-        zero = jnp.zeros_like(bc)
-        c_low = jnp.where(low, sw, zero)
-        b_low = jnp.where(low, bc, zero)
-        scores = dot(b_low, c_low, NT)
-        back = jnp.where(cols >= rows, jnp.exp(jnp.minimum(-gap, 0.0)), 0.0)
-        sct_ref[0, h] = (scores * back).astype(BF16)
-        weighted = c_low.astype(F32) * jnp.exp(col1)
-        wct_ref[0, h] = weighted.T[:STATE, :].astype(BF16)
-
-
-def prepare_body(heads):
-    def body(*refs):
-        prepare_kernel(heads, *refs)
-
-    return body
-
-
-def prepare(bc, sw, arow, acol):
+def prepare(bc, arow, aline, states):
     tokens, width = bc.shape
     heads = width // HEAD_DIM
     blocks = tokens // BLOCK
+
+    def body(bc_ref, arow_ref, aline_ref, states_ref, sw_ref, dec_ref, sct_ref, wct_ref, spad_ref):
+        rows = lax.broadcasted_iota(jnp.int32, (BLOCK, BLOCK), 0)
+        cols = lax.broadcasted_iota(jnp.int32, (BLOCK, BLOCK), 1)
+        low = low_lanes((BLOCK, HEAD_DIM))
+        for h in range(heads):
+            lanes = slice(h * HEAD_DIM, (h + 1) * HEAD_DIM)
+            gap = aline_ref[:, h : h + 1] - arow_ref[h : h + 1, :]
+            dec_ref[0, h] = jnp.where(rows >= cols, jnp.exp(jnp.minimum(gap, 0.0)), 0.0).astype(BF16)
+            bc = bc_ref[:, lanes].astype(F32)
+            swapped = pltpu.roll(bc, STATE, 1)
+            sw_ref[:, lanes] = swapped.astype(BF16)
+            c_low = jnp.where(low, swapped, 0.0)
+            b_low = jnp.where(low, bc, 0.0)
+            scores = dot(b_low.astype(BF16), c_low.astype(BF16), NT)
+            back = jnp.where(cols >= rows, jnp.exp(jnp.minimum(-gap, 0.0)), 0.0)
+            sct_ref[0, h] = (scores * back).astype(BF16)
+            weighted = c_low * jnp.exp(aline_ref[:, h : h + 1])
+            wct_ref[0, h] = weighted.T[:STATE, :].astype(BF16)
+            state = states_ref[0, h].astype(BF16)
+            spad_ref[0, h] = jnp.concatenate([jnp.zeros_like(state), state], axis=0)
+
     wide = pl.BlockSpec((BLOCK, width), lambda b: (b, 0))
-    square = pl.BlockSpec((1, heads, BLOCK, BLOCK), lambda b: (b, 0, 0, 0))
+
+    def block4(*dims):
+        return pl.BlockSpec((1, heads) + dims, lambda b: (b, 0, 0, 0))
+
     return pl.pallas_call(
-        prepare_body(heads),
+        body,
         name="prepare",
         grid=(blocks,),
         in_specs=[
             wide,
-            wide,
             pl.BlockSpec((heads, BLOCK), lambda b: (0, b)),
-            wide,
+            pl.BlockSpec((BLOCK, heads), lambda b: (b, 0)),
+            block4(STATE, HEAD_DIM),
         ],
         out_specs=[
-            square,
-            square,
-            pl.BlockSpec((1, heads, STATE, BLOCK), lambda b: (b, 0, 0, 0)),
+            wide,
+            block4(BLOCK, BLOCK),
+            block4(BLOCK, BLOCK),
+            block4(STATE, BLOCK),
+            block4(HEAD_DIM, HEAD_DIM),
         ],
         out_shape=[
+            jax.ShapeDtypeStruct((tokens, width), BF16),
             jax.ShapeDtypeStruct((blocks, heads, BLOCK, BLOCK), BF16),
             jax.ShapeDtypeStruct((blocks, heads, BLOCK, BLOCK), BF16),
             jax.ShapeDtypeStruct((blocks, heads, STATE, BLOCK), BF16),
+            jax.ShapeDtypeStruct((blocks, heads, HEAD_DIM, HEAD_DIM), BF16),
         ],
         cost_estimate=pl.CostEstimate(flops=4_000_000_000, bytes_accessed=9_000_000, transcendentals=0),
         compiler_params=pltpu.CompilerParams(vmem_limit_bytes=VMEM_LIMIT),
-    )(bc, sw, arow, acol)
-
-
-def close_chunk(first, acc, up, down, weight, wct, scale, earlier):
+    )(bc, arow, aline, states)
+
+
+def close_chunk(first, source, acc, up, down, weight, wct, scale, earlier):
     tokens, width = acc.shape
     heads = width // HEAD_DIM
     last = earlier is not None
 
-    def body(*refs):
+    def body(source_ref, *refs):
         scale_ref, acc_ref, up_ref, down_ref, weight_ref, wct_ref = refs[:6]
         if last:
             earlier_ref, dy_ref, terms_ref, part_ref = refs[6:]
@@ -116,35 +115,44 @@
             for h in range(heads):
                 part_ref[h] = sums[h]
 
-    vmem = pl.BlockSpec(memory_space=pltpu.VMEM)
-    wct = wct[first : first + 2]
-    out_shape = [
-        jax.ShapeDtypeStruct((tokens, width), BF16),
-        jax.ShapeDtypeStruct((2, heads, STATE, HEAD_DIM), F32),
+    def whole(*dims):
+        return pl.BlockSpec(dims, lambda i, source: (0,) * len(dims))
+
+    terms_shape = (2, heads, STATE, HEAD_DIM)
+    out_shape = [jax.ShapeDtypeStruct((tokens, width), BF16), jax.ShapeDtypeStruct(terms_shape, F32)]
+    out_specs = [whole(tokens, width), whole(*terms_shape)]
+    in_specs = [
+        pl.BlockSpec(memory_space=pltpu.SMEM),
+        whole(tokens, width),
+        whole(*up.shape),
+        whole(*down.shape),
+        pl.BlockSpec((width, up.shape[1]), lambda i, source: (0, source[0])),
+        pl.BlockSpec((2, heads, STATE, BLOCK), lambda i, source: (first // 2, 0, 0, 0)),
     ]
-    in_specs = [pl.BlockSpec(memory_space=pltpu.SMEM)] + [vmem] * 5
     operands = [scale, acc, up, down, weight, wct]
     if last:
         out_shape.append(jax.ShapeDtypeStruct((heads, STATE, HEAD_DIM), F32))
-        in_specs.append(vmem)
+        out_specs.append(whole(heads, STATE, HEAD_DIM))
+        in_specs.append(whole(*terms_shape))
         operands.append(earlier)
     return pl.pallas_call(
         body,
         name="close_chunk",
-        in_specs=in_specs,
-        out_specs=[vmem] * len(out_shape),
+        grid_spec=pltpu.PrefetchScalarGridSpec(
+            num_scalar_prefetch=1, grid=(1,), in_specs=in_specs, out_specs=out_specs
+        ),
         out_shape=out_shape,
         cost_estimate=pl.CostEstimate(flops=600_000_000, bytes_accessed=4_000_000, transcendentals=0),
         compiler_params=pltpu.CompilerParams(vmem_limit_bytes=VMEM_LIMIT),
-    )(*operands)
-
-
-def inside(first, count, dy_first, dy, skip, x, bc, sw, acol, dec, sct, spad, before):
+    )(source, *operands)
+
+
+def inside(first, count, dy_first, dy, skip, x, bc, sw, aline, dec, sct, spad, before):
     tokens, width = x.shape
     heads = width // HEAD_DIM
     group = heads // 2
 
-    def body(skip_ref, dy_ref, x_ref, bc_ref, sw_ref, acol_ref, dec_ref, sct_ref, spad_ref, *rest):
+    def body(skip_ref, dy_ref, x_ref, bc_ref, sw_ref, aline_ref, dec_ref, sct_ref, spad_ref, *rest):
         dx_ref, dbc_ref, dlog_ref = rest[-3:]
         base = pl.program_id(1) * group
         rows = lax.broadcasted_iota(jnp.int32, (BLOCK, BLOCK), 0)
@@ -162,7 +170,7 @@
             dx_ref[:, lanes] = dot(sct_ref[0, h], dy_h, NN) + skip_ref[0, base + h] * dy_h.astype(F32)
             grad = dot(mixed, jnp.where(low, zero, sw_h), NN)
             grad = grad + dot(mixed, jnp.where(low, sw_h, zero), TN)
-            grad = grad + jnp.exp(acol_ref[:, lanes]) * dot(dy_h, spad_ref[0, h], NT)
+            grad = grad + jnp.exp(aline_ref[0][:, h : h + 1]) * dot(dy_h, spad_ref[0, h], NT)
             dbc_ref[:, lanes] = grad
             signed = grad * bc_h.astype(F32)
             moved = jnp.sum(jnp.where(low, -signed, signed), axis=1, keepdims=True)
@@ -176,12 +184,12 @@
         wide,
         wide,
         wide,
-        wide,
+        pl.BlockSpec((1, BLOCK, group), lambda b, g: (g, b + first, 0)),
         square,
         square,
         pl.BlockSpec((1, group, HEAD_DIM, HEAD_DIM), lambda b, g: (b + first, g, 0, 0)),
     ]
-    operands = [skip, dy, x, bc, sw, acol, dec, sct, spad]
+    operands = [skip, dy, x, bc, sw, jnp.stack([aline[:, :group], aline[:, group:]]), dec, sct, spad]
     aliases = {}
     if before is not None:
         for place, array in enumerate(before):
@@ -298,98 +306,108 @@
     feats = upstream.shape[1]
     px, py, pc = ctx // 8, (ctx // 2) % 4, ctx % 2
 
-    logs = log_decay.reshape(heads, blocks, BLOCK)
-    cum = jnp.cumsum(logs, axis=-1)
-    last = cum[:, :, -1].T
-    total = jnp.sum(last, axis=0)
-    all_logs = lax.all_gather(jnp.zeros((64, 128), F32).at[0, :heads].set(total), "ctx")[:, 0, :heads]
+    places = [(x, y, c) for x in range(4) for y in range(4) for c in range(2)]
+
+    def perm(dx, dy, dc):
+        return [(x * 8 + y * 2 + c, ((x + dx) % 4) * 8 + ((y + dy) % 4) * 2 + (c ^ dc)) for x, y, c in places]
+
+    def from_core(a):
+        return lax.ppermute(a, "ctx", perm(0, 0, 1))
+
+    def from_y(a):
+        return [lax.ppermute(a, "ctx", perm(0, s, 0)) for s in (1, 2, 3)]
+
+    def from_x(a):
+        return [lax.ppermute(a, "ctx", perm(s, 0, 0)) for s in (1, 2, 3)]
 
     def weight_of(source):
         return lax.dynamic_slice_in_dim(out_weight, (source % tp) * feats, feats, 1)
 
     half = tokens // 2
-    accs, lasts = [], []
+    accs, lasts, firsts, seconds = [], [], [], []
     for c in range(2):
         own = upstream[c * half : (c + 1) * half]
-        if c == 0:
-            upstream, _ = lax.optimization_barrier((upstream, own))
         right = left = own
         acc = dot(own, weight_of(me), NT)
         for k in range(1, tp // 2):
             right = lax.ppermute(right, "tp", shift(tp, 1))
             left = lax.ppermute(left, "tp", shift(tp, -1))
+            if k == 1:
+                firsts.append(right)
+            if k == 2:
+                seconds.append(right)
             acc = acc + dot(right, weight_of(me - k + tp), NT) + dot(left, weight_of(me + k), NT)
         up = lax.ppermute(right[:BLOCK], "tp", shift(tp, 1))
         down = lax.ppermute(left[BLOCK:], "tp", shift(tp, -1))
         accs.append(acc)
         lasts.append((up, down))
-    weight_last = weight_of(me + tp // 2)
-
+
+    triangle = (jnp.arange(BLOCK)[:, None] <= jnp.arange(BLOCK)[None, :]).astype(F32)
+    cum = jnp.dot(log_decay.reshape(heads * blocks, BLOCK), triangle, precision=lax.Precision.HIGHEST)
+    cum = cum.reshape(heads, blocks, BLOCK)
+    last = cum[:, :, -1].T
     arow = cum.reshape(heads, tokens)
     aline = arow.T
-    acol = jnp.repeat(aline, HEAD_DIM, axis=1)
-    swapped = head_bc.reshape(tokens, heads, 2, STATE)[:, :, ::-1, :].reshape(tokens, width)
-    dec, sct, wct = prepare(head_bc, swapped, arow, acol)
-    spad = jnp.pad(states, ((0, 0), (0, 0), (STATE, 0), (0, 0))).astype(BF16)
+    bc_then, _ = lax.optimization_barrier((head_bc, firsts[0]))
+    sw, dec, sct, wct, spad = prepare(bc_then, arow, aline, states)
     ahead = jnp.exp(jnp.cumsum(last, axis=0) - last)
 
-    ids = jnp.arange(32)
-    ix, iy, ic = ids // 8, (ids // 2) % 4, ids % 2
-    row = ix == px
-    chip = row & (iy == py)
-    none = ids < 0
-    after_core = chip & (ic > pc)
-    after_y = row & (iy > py)
-    yes = jnp.bool_(True)
-    entries = [(chip & (ic == 0) & (pc == 1), yes), (chip & (ic == 0) & (pc == 0), yes)]
-    entries.append((row & (iy < py), yes))
-    for s in (1, 2, 3):
-        sy = (py - s) % 4
-        entries.append((row & (iy < sy), yes))
-    finals = [(none, pc == 0)]
-    for s in (1, 2, 3):
-        sy = (py - s) % 4
-        finals.append((after_core | (row & (iy > py) & (iy < sy)), sy > py))
-    for s in (1, 2, 3):
-        sx = (px - s) % 4
-        finals.append((after_core | after_y | ((ix > px) & (ix < sx)), sx > px))
-    entries = entries + finals
-    masks = jnp.stack([m for m, _ in entries])
-    valid = jnp.stack([v for _, v in entries])
-    sums = jnp.sum(jnp.where(masks[:, :, None], all_logs[None], 0.0), axis=1)
-    coefs = jnp.where(valid[:, None], jnp.exp(sums), 0.0)
+    own_log, _ = lax.optimization_barrier((jnp.sum(last, axis=0), firsts[1]))
+    other_log = from_core(own_log)
+    chip_log = own_log + other_log
+    y_logs = jnp.stack([chip_log] + from_y(chip_log))
+    row_log, _ = lax.optimization_barrier((jnp.sum(y_logs, axis=0), seconds[0]))
+    x_logs = jnp.stack([row_log] + from_x(row_log))
+    at_y = (py - jnp.arange(4)) % 4
+    at_x = (px - jnp.arange(4)) % 4
+
+    def masked(mask, logs):
+        return jnp.sum(jnp.where(mask[:, :, None], logs[None], 0.0), axis=1)
+
+    none = jnp.zeros_like(own_log)
+    first_core = pc == 0
+    after_core = jnp.where(first_core, other_log, none)
+    after_y = jnp.sum(jnp.where((at_y > py)[:, None], y_logs, 0.0), axis=0)
+    over_y = masked((at_y[None] > py) & (at_y[None] < at_y[:, None]), y_logs)
+    over_x = masked((at_x[None] > px) & (at_x[None] < at_x[:, None]), x_logs)
+    rows_y = masked(at_y[None] < at_y[:, None], y_logs)
+    chips = jnp.stack([jnp.where(first_core, none, other_log), jnp.where(first_core, own_log, none)])
+    finals = jnp.concatenate(
+        [
+            jnp.where(first_core, jnp.ones_like(own_log), none)[None],
+            jnp.where((at_y > py)[:, None], jnp.exp(after_core + over_y), 0.0)[1:],
+            jnp.where((at_x > px)[:, None], jnp.exp(after_core + after_y + over_x), 0.0)[1:],
+        ]
+    )
+    coefs = jnp.concatenate([jnp.exp(chips), jnp.exp(rows_y), finals])
 
     skips = skip[None]
 
     def within(first, count, dy_first, dy, before):
         return inside(
-            first, count, dy_first, dy, skips, inner_act, head_bc, swapped, acol, dec, sct, spad, before
+            first, count, dy_first, dy, skips, inner_act, head_bc, sw, aline, dec, sct, spad, before
         )
 
-    dy0, terms0 = close_chunk(0, accs[0], *lasts[0], weight_last, wct, ahead, None)
+    source = ((me + tp // 2) % tp).astype(jnp.int32)[None]
+    dy0, terms0 = close_chunk(0, source, accs[0], *lasts[0], out_weight, wct, ahead, None)
     grads = within(0, 2, 0, dy0, None)
     lasts[1], coefs, grads = lax.optimization_barrier((lasts[1], coefs, grads))
-    dy1, terms1, part = close_chunk(2, accs[1], *lasts[1], weight_last, wct, ahead, terms0)
+    dy1, terms1, part = close_chunk(2, source, accs[1], *lasts[1], out_weight, wct, ahead, terms0)
 
     def by(i):
         return coefs[i][:, None, None]
 
-    places = [(x, y, c) for x in range(4) for y in range(4) for c in range(2)]
-
-    def perm(dx, dy, dc):
-        return [(x * 8 + y * 2 + c, ((x + dx) % 4) * 8 + ((y + dy) % 4) * 2 + (c ^ dc)) for x, y, c in places]
-
     part16 = part.astype(BF16)
-    other = lax.ppermute(part16, "ctx", perm(0, 0, 1))
+    other = from_core(part16)
     chip_sum = (by(0) * part + by(1) * other.astype(F32)).astype(BF16)
-    ys = [lax.ppermute(chip_sum, "ctx", perm(0, s, 0)) for s in (1, 2, 3)]
+    ys = from_y(chip_sum)
     dy1, chip_sum = lax.optimization_barrier((dy1, chip_sum))
     grads = within(2, 1, 0, dy1, grads)
     row_sum = by(2) * chip_sum.astype(F32)
     for s in range(3):
         row_sum = row_sum + by(3 + s) * ys[s].astype(F32)
     row_sum = row_sum.astype(BF16)
-    xs = [lax.ppermute(row_sum, "ctx", perm(s, 0, 0)) for s in (1, 2, 3)]
+    xs = from_x(row_sum)
     dy1, row_sum = lax.optimization_barrier((dy1, row_sum))
     dx, dbc, dlog = within(3, 1, 1, dy1, grads)
     return finish(

time: 160 us -> 150 us (0.938); the launches traced: 157 us -> 149 us
  local copies, waits for them, and re-layouts: 35 us -> 12 us
  between operations: 14.9 us -> 1.37 us
  Pallas kernels: 18.7 us -> 31.7 us
  matrix products: 14.5 us -> 25.4 us
  starting transfers between devices: 37.3 us -> 47.3 us
  waiting for transfers between devices: 30.9 us -> 26.1 us
    unnamed x60 -> x30, local copies, waits for them, and re-layouts: 18.5 us -> 2.2 us
    ppermute x7 -> x14, waiting for transfers between devices: 1.32 us -> 14.5 us  [the longest x6 7.59 us: from_y(): return [lax.ppermute(a, 'ctx', perm(0, s, 0)) for s in (1, 2, 3)]]
    ppermute x7 -> x14, starting transfers between devices: 9.66 us -> 20.5 us  [the longest x6 11 us: from_y(): return [lax.ppermute(a, 'ctx', perm(0, s, 0)) for s in (1, 2, 3)]]
    dot_general x14, matrix products: 14.5 us -> 25.2 us  [dot(): return lax.dot_general(a, b, (dims, ((), ())), preferred_element_type=F32)]
    ppermute x6, waiting for transfers between devices: 21 us -> 11.6 us  [per_device(): right = lax.ppermute(right, 'tp', shift(tp, 1))]
    pallas_call x3, Pallas kernels: 5.64 us -> 12.4 us  [the longest x2 6.52 us: close_chunk(): pl.pallas_call(body, name='close_chunk', grid_spec=pltpu.PrefetchScalarGr...]
    ppermute x6, waiting for transfers between devices: 6.35 us -> 0.02 us  [per_device(): left = lax.ppermute(left, 'tp', shift(tp, -1))]
    ppermute x6, starting transfers between devices: 20.9 us -> 15.8 us  [per_device(): left = lax.ppermute(left, 'tp', shift(tp, -1))]
  transfers between devices with their start and end apart: 24 -> 30, of which waited for: 7 -> 10; matrix products, arithmetic and copies ran while one was open for 22% -> 24% of each run, Pallas kernels for 8% -> 15%
where the time goes in v3:
time: 150 us; the launch traced here: 149 us
  starting transfers between devices  47.3 us (32%)
  Pallas kernels  31.7 us (21%)
  waiting for transfers between devices  26.1 us (17%)
  matrix products  25.4 us (17%)
  local copies, waits for them, and re-layouts  12 us (8%)
  other arithmetic  5.48 us (4%)
    dot_general x14, matrix products, dot(): return lax.dot_general(a, b, (dims, ((), ())), preferred_element_type=F32)  25.2 us
    ppermute x6, starting transfers between devices, per_device(): left = lax.ppermute(left, 'tp', shift(tp, -1))  15.8 us
    pallas_call x3, Pallas kernels, inside(): pl.pallas_call(body, name='inside', grid=(count, 2), in_specs=in_specs, o...  12.7 us
    ppermute x6, waiting for transfers between devices, per_device(): right = lax.ppermute(right, 'tp', shift(tp, 1))  11.6 us
    ppermute x6, starting transfers between devices, from_y(): return [lax.ppermute(a, 'ctx', perm(0, s, 0)) for s in (1, 2, 3)]  11 us
    ppermute x6, starting transfers between devices, from_x(): return [lax.ppermute(a, 'ctx', perm(s, 0, 0)) for s in (1, 2, 3)]  9.4 us
    ppermute x6, waiting for transfers between devices, from_y(): return [lax.ppermute(a, 'ctx', perm(0, s, 0)) for s in (1, 2, 3)]  7.59 us
    ppermute x2, starting transfers between devices, per_device(): down = lax.ppermute(left[BLOCK:], 'tp', shift(tp, -1))  6.8 us
  transfers between devices with their start and end apart: 30, of which 10 were waited for; matrix products, arithmetic and copies ran while one was open for 24% of the time, Pallas kernels for 15%

profile of v3, /device:TPU:2, one launch (start us, length us, event | category | flops | bytes accessed | tf_op | source)
XLA Modules:
  0.0 149.3 jit_solution(17764715472357940801)
XLA Ops:
  0.6 2.3 %fusion.47 = (bf16[512,512]{1,0:T(8,128)(2,1)}, bf16[512,512]{1,0:T(8,128)(2,1)}) fusion(bf16[1024,512]{1,0:T(8,128)(2,1)} %param.7), kind=kLoop, calls=%fused_computation.94 | loop fusion | bytes 2097152 | tf_op jit(solution)/shard_map/slice | solution.py:329
  3.0 1.9 %collective-permute-start.12 = (bf16[512,512]{1,0:T(8,128)(2,1)}, bf16[512,512]{1,0:T(8,128)(2,1)}, u32[]{:S(2)}, u32[]{:S(2)}) collective-permute-start(bf16[512,512]{1,0:T(8,128)(2,1)} %get-tuple-element.75), channel_id=1, source_target_pairs={{0,1},{1,2},{2,3},{3,4},{4,5},{5,6},{6,7},{7,0},{8,9},{9,10},{10,1... | collective-permute-start | bytes 1572872 | tf_op jit(solution)/shard_map/ppermute | solution.py:333
  4.9 3.9 %collective-permute-start.17 = (bf16[512,512]{1,0:T(8,128)(2,1)}, bf16[512,512]{1,0:T(8,128)(2,1)}, u32[]{:S(2)}, u32[]{:S(2)}) collective-permute-start(bf16[512,512]{1,0:T(8,128)(2,1)} %get-tuple-element.75), channel_id=1, source_target_pairs={{0,7},{1,0},{2,1},{3,2},{4,3},{5,4},{6,5},{7,6},{8,15},{9,8},{10,9... | collective-permute-start | bytes 1572872 | tf_op jit(solution)/shard_map/ppermute | solution.py:334
  8.8 3.2 %collective-permute-start.4 = (bf16[512,512]{1,0:T(8,128)(2,1)}, bf16[512,512]{1,0:T(8,128)(2,1)}, u32[]{:S(2)}, u32[]{:S(2)}) collective-permute-start(bf16[512,512]{1,0:T(8,128)(2,1)} %get-tuple-element.76), channel_id=1, source_target_pairs={{0,7},{1,0},{2,1},{3,2},{4,3},{5,4},{6,5},{7,6},{8,15},{9,8},{10,9... | collective-permute-start | bytes 1572872 | tf_op jit(solution)/shard_map/ppermute | solution.py:334
  13.1 1.7 %fusion.24 = f32[512,512]{0,1:T(8,128)S(1)} fusion(bf16[512,4096]{1,0:T(8,128)(2,1)} %refs_4_.3, s32[]{:T(128)S(6)} %select_n.190, bf16[1024,512]{1,0:T(8,128)(2,1)} %param.7), kind=kOutput, calls=%fused_computation.36 | convolution fusion | flops 268435456 | bytes 2097156 | tf_op jit(solution)/shard_map/dot_general | solution.py:17
  14.8 1.5 %fusion.22 = f32[512,512]{0,1:T(8,128)S(1)} fusion(bf16[512,4096]{1,0:T(8,128)(2,1)} %refs_4_.3, s32[]{:T(128)S(6)} %select_n.190, bf16[1024,512]{1,0:T(8,128)(2,1)S(1)} %copy-done.1), kind=kOutput, calls=%fused_computation.34 | convolution fusion | flops 268435456 | bytes 2097156 | tf_op jit(solution)/shard_map/dot_general | solution.py:17
  17.4 1.0 slice_bitcast_fusion.1
  18.7 2.1 %pad_maximum_fusion.aline_ref = f32[2,1024,2]{2,1,0:T(8,128)} fusion(f32[1,1024,2]{2,1,0:T(8,128)} %get-tuple-element.78, f32[1,1024,2]{2,1,0:T(8,128)S(1)} %get-tuple-element.77), kind=kLoop, calls=%fused_computation.15 | loop fusion | flops 4096 | bytes 32768 | tf_op jit(solution)/shard_map/stack | solution.py:192
  20.7 1.1 collective-permute-done.12
  21.9 10.4 %collective-permute-done = bf16[512,512]{1,0:T(8,128)(2,1)} collective-permute-done((bf16[512,512]{1,0:T(8,128)(2,1)}, bf16[512,512]{1,0:T(8,128)(2,1)}, u32[]{:S(2)}, u32[]{:S(2)}) %collective-permute-start) | collective-permute-done | bytes 524320 | tf_op jit(solution)/shard_map/ppermute | solution.py:333
  32.3 3.3 %collective-permute-start.18 = (bf16[512,512]{1,0:T(8,128)(2,1)}, bf16[512,512]{1,0:T(8,128)(2,1)}, u32[]{:S(2)}, u32[]{:S(2)}) collective-permute-start(bf16[512,512]{1,0:T(8,128)(2,1)} %collective-permute-done.17), channel_id=1, source_target_pairs={{0,7},{1,0},{2,1},{3,2},{4,3},{5,4},{6,5},{7,6},{8,15},{9,8},{10,9... | collective-permute-start | bytes 1572872 | tf_op jit(solution)/shard_map/ppermute | solution.py:334
  35.6 5.8 %prepare.1 = (bf16[1024,512]{1,0:T(8,128)(2,1)}, bf16[4,4,256,256]{3,2,1,0:T(8,128)(2,1)}, bf16[4,4,256,256]{3,2,1,0:T(8,128)(2,1)}, bf16[4,4,64,256]{3,2,1,0:T(8,128)(2,1)}, bf16[4,4,128,128]{3,2,1,0:T(8,128)(2,1)}) custom-call(bf16[1024,512]{1,0:T(8,128)(2,1)} %refs_8_.1, f32[4,1024]{1,0:T(4,128)} %copy-done.13, f32[1024,4]{1,0:T(8,128)} %bitcast.44, ...), custom_call_target="tpu_custom_call" | custom-call | flops 4000000000 | bytes 9000000 | tf_op jit(solution)/shard_map/prepare/pallas_call | solution.py:60
  41.4 2.1 %collective-permute-start.5 = (bf16[512,512]{1,0:T(8,128)(2,1)}, bf16[512,512]{1,0:T(8,128)(2,1)}, u32[]{:S(2)}, u32[]{:S(2)}) collective-permute-start(bf16[512,512]{1,0:T(8,128)(2,1)} %collective-permute-done.4), channel_id=1, source_target_pairs={{0,7},{1,0},{2,1},{3,2},{4,3},{5,4},{6,5},{7,6},{8,15},{9,8},{10,9... | collective-permute-start | bytes 1572872 | tf_op jit(solution)/shard_map/ppermute | solution.py:334
  43.5 1.7 %convolution_add_fusion.7 = f32[512,512]{0,1:T(8,128)S(1)} fusion(f32[512,512]{0,1:T(8,128)S(1)} %fusion.24, bf16[512,512]{1,0:T(8,128)(2,1)} %collective-permute-done.12, bf16[512,4096]{1,0:T(8,128)(2,1)} %refs_4_.3, s32[]{:T(128)S(6)} %select_n.192), kind=kOutput, calls=%fused_computation.13 | convolution fusion | flops 268697600 | bytes 3145732 | tf_op jit(solution)/shard_map/dot_general | solution.py:17
  45.2 1.7 %convolution_add_fusion.3 = f32[512,512]{0,1:T(8,128)S(1)} fusion(f32[512,512]{0,1:T(8,128)S(1)} %fusion.22, bf16[512,512]{1,0:T(8,128)(2,1)} %collective-permute-done, bf16[512,4096]{1,0:T(8,128)(2,1)} %refs_4_.3, s32[]{:T(128)S(6)} %select_n.192), kind=kOutput, calls=%fused_computation.6 | convolution fusion | flops 268697600 | bytes 3145732 | tf_op jit(solution)/shard_map/dot_general | solution.py:17
  46.9 1.7 %convolution_add_fusion.6 = f32[512,512]{0,1:T(8,128)S(1)} fusion(f32[512,512]{0,1:T(8,128)S(1)} %convolution_add_fusion.7, bf16[512,512]{1,0:T(8,128)(2,1)} %collective-permute-done.17, bf16[512,4096]{1,0:T(8,128)(2,1)} %refs_4_.3, s32[]{:T(128)S(6)} %select_n.194), kind=kOutput, calls=%fused_computation.12 | convolution fusion | flops 268697600 | bytes 3145732 | tf_op jit(solution)/shard_map/dot_general | solution.py:17
  48.5 1.7 %convolution_add_fusion.2 = f32[512,512]{0,1:T(8,128)S(1)} fusion(f32[512,512]{0,1:T(8,128)S(1)} %convolution_add_fusion.3, bf16[512,512]{1,0:T(8,128)(2,1)} %collective-permute-done.4, bf16[512,4096]{1,0:T(8,128)(2,1)} %refs_4_.3, s32[]{:T(128)S(6)} %select_n.194), kind=kOutput, calls=%fused_computation.5 | convolution fusion | flops 268697600 | bytes 3145732 | tf_op jit(solution)/shard_map/dot_general | solution.py:17
  50.2 3.3 %collective-permute-start.10 = (f32[4]{0:T(128)S(1)}, f32[4]{0:T(128)S(1)}, u32[]{:S(2)}, u32[]{:S(2)}) collective-permute-start(f32[4]{0:T(128)S(1)} %get-tuple-element.86), channel_id=1, source_target_pairs={{0,32},{8,40},{16,48},{24,56},{32,0},{40,8},{48,16},{56,24},{64,96... | collective-permute-start | bytes 56 | tf_op jit(solution)/shard_map/ppermute | solution.py:318
  53.5 1.8 %collective-permute-done.10 = f32[4]{0:T(128)S(1)} collective-permute-done((f32[4]{0:T(128)S(1)}, f32[4]{0:T(128)S(1)}, u32[]{:S(2)}, u32[]{:S(2)}) %collective-permute-start.10) | collective-permute-done | bytes 48 | tf_op jit(solution)/shard_map/ppermute | solution.py:318
  55.4 3.0 %collective-permute-start.11 = (f32[4]{0:T(128)S(1)}, f32[4]{0:T(128)S(1)}, u32[]{:S(2)}, u32[]{:S(2)}) collective-permute-start(f32[4]{0:T(128)S(1)} %get-tuple-element.86), channel_id=1, source_target_pairs={{0,48},{8,56},{16,0},{24,8},{32,16},{40,24},{48,32},{56,40},{64,11... | collective-permute-start | bytes 56 | tf_op jit(solution)/shard_map/ppermute | solution.py:318
  58.4 1.3 collective-permute-done.11
  60.5 4.2 %collective-permute-done.9 = f32[4]{0:T(128)S(1)} collective-permute-done((f32[4]{0:T(128)S(1)}, f32[4]{0:T(128)S(1)}, u32[]{:S(2)}, u32[]{:S(2)}) %collective-permute-start.9) | collective-permute-done | bytes 48 | tf_op jit(solution)/shard_map/ppermute | solution.py:318
  65.7 3.2 %collective-permute-start.20 = (bf16[512,512]{1,0:T(8,128)(2,1)}, bf16[512,512]{1,0:T(8,128)(2,1)}, u32[]{:S(2)}, u32[]{:S(2)}) collective-permute-start(bf16[512,512]{1,0:T(8,128)(2,1)} %collective-permute-done.18), channel_id=1, source_target_pairs={{0,7},{1,0},{2,1},{3,2},{4,3},{5,4},{6,5},{7,6},{8,15},{9,8},{10,9... | collective-permute-start | bytes 1572872 | tf_op jit(solution)/shard_map/ppermute | solution.py:334
  69.0 1.7 %fusion.14 = f32[512,512]{0,1:T(8,128)S(1)} fusion(bf16[512,512]{1,0:T(8,128)(2,1)} %collective-permute-done.18, bf16[512,4096]{1,0:T(8,128)(2,1)} %refs_4_.3, s32[]{:T(128)S(6)} %select_n.198), kind=kOutput, calls=%fused_computation.26 | convolution fusion | flops 268435456 | bytes 2097156 | tf_op jit(solution)/shard_map/dot_general | solution.py:17
  70.7 1.7 %fusion.12 = f32[512,512]{0,1:T(8,128)S(1)} fusion(bf16[512,512]{1,0:T(8,128)(2,1)} %collective-permute-done.5, bf16[512,4096]{1,0:T(8,128)(2,1)} %refs_4_.3, s32[]{:T(128)S(6)} %select_n.198), kind=kOutput, calls=%fused_computation.24 | convolution fusion | flops 268435456 | bytes 2097156 | tf_op jit(solution)/shard_map/dot_general | solution.py:17
  72.4 2.0 %collective-permute-start.2 = (bf16[512,512]{1,0:T(8,128)(2,1)}, bf16[512,512]{1,0:T(8,128)(2,1)}, u32[]{:S(2)}, u32[]{:S(2)}) collective-permute-start(bf16[512,512]{1,0:T(8,128)(2,1)} %collective-permute-done.1), channel_id=1, source_target_pairs={{0,1},{1,2},{2,3},{3,4},{4,5},{5,6},{6,7},{7,0},{8,9},{9,10},{10,1... | collective-permute-start | bytes 1572872 | tf_op jit(solution)/shard_map/ppermute | solution.py:333
  74.4 1.7 %fusion.5 = f32[512,512]{0,1:T(8,128)S(1)} fusion(f32[512,512]{0,1:T(8,128)S(1)} %fusion.14, f32[512,512]{0,1:T(8,128)S(1)} %convolution_add_fusion.6, bf16[512,512]{1,0:T(8,128)(2,1)} %collective-permute-done.13, bf16[512,4096]{1,0:T(8,128)(2,1)} %refs_4_.3, s32[]{:T(128)S(6)} %select_n.196), kind=kOutput, calls=%fused_computation.11 | convolution fusion | flops 268959744 | bytes 4194308 | tf_op jit(solution)/shard_map/dot_general | solution.py:17
  76.1 1.7 %fusion.2 = f32[512,512]{0,1:T(8,128)S(1)} fusion(f32[512,512]{0,1:T(8,128)S(1)} %fusion.12, f32[512,512]{0,1:T(8,128)S(1)} %convolution_add_fusion.2, bf16[512,512]{1,0:T(8,128)(2,1)} %collective-permute-done.1, bf16[512,4096]{1,0:T(8,128)(2,1)} %refs_4_.3, s32[]{:T(128)S(6)} %select_n.196), kind=kOutput, calls=%fused_computation.4 | convolution fusion | flops 268959744 | bytes 4194308 | tf_op jit(solution)/shard_map/dot_general | solution.py:17
  77.8 1.6 %collective-permute-start.14 = (f32[4]{0:T(128)S(1)}, f32[4]{0:T(128)S(1)}, u32[]{:S(2)}, u32[]{:S(2)}) collective-permute-start(f32[4]{0:T(128)S(1)} %add_add_fusion), channel_id=1, source_target_pairs={{0,64},{8,72},{16,80},{24,88},{32,96},{40,104},{48,112},{56,120},{... | collective-permute-start | bytes 56 | tf_op jit(solution)/shard_map/ppermute | solution.py:321
  79.4 2.8 %collective-permute-done.14 = f32[4]{0:T(128)S(1)} collective-permute-done((f32[4]{0:T(128)S(1)}, f32[4]{0:T(128)S(1)}, u32[]{:S(2)}, u32[]{:S(2)}) %collective-permute-start.14) | collective-permute-done | bytes 48 | tf_op jit(solution)/shard_map/ppermute | solution.py:321
  82.1 1.8 %collective-permute-start.15 = (f32[4]{0:T(128)S(1)}, f32[4]{0:T(128)S(1)}, u32[]{:S(2)}, u32[]{:S(2)}) collective-permute-start(f32[4]{0:T(128)S(1)} %add_add_fusion), channel_id=1, source_target_pairs={{0,128},{8,136},{16,144},{24,152},{32,160},{40,168},{48,176},{56,1... | collective-permute-start | bytes 56 | tf_op jit(solution)/shard_map/ppermute | solution.py:321
  84.0 3.2 %collective-permute-done.15 = f32[4]{0:T(128)S(1)} collective-permute-done((f32[4]{0:T(128)S(1)}, f32[4]{0:T(128)S(1)}, u32[]{:S(2)}, u32[]{:S(2)}) %collective-permute-start.15) | collective-permute-done | bytes 48 | tf_op jit(solution)/shard_map/ppermute | solution.py:321
  89.7 3.3 %collective-permute-start.22 = (bf16[256,512]{1,0:T(8,128)(2,1)S(1)}, bf16[256,512]{1,0:T(8,128)(2,1)S(1)}, u32[]{:S(2)}, u32[]{:S(2)}) collective-permute-start(bf16[256,512]{1,0:T(8,128)(2,1)S(1)} %slice.80), channel_id=1, source_target_pairs={{0,7},{1,0},{2,1},{3,2},{4,3},{5,4},{6,5},{7,6},{8,15},{9,8},{10,9... | collective-permute-start | bytes 786440 | tf_op jit(solution)/shard_map/ppermute | solution.py:341
  95.1 3.5 %collective-permute-start.7 = (bf16[256,512]{1,0:T(8,128)(2,1)S(1)}, bf16[256,512]{1,0:T(8,128)(2,1)S(1)}, u32[]{:S(2)}, u32[]{:S(2)}) collective-permute-start(bf16[256,512]{1,0:T(8,128)(2,1)S(1)} %slice.77), channel_id=1, source_target_pairs={{0,7},{1,0},{2,1},{3,2},{4,3},{5,4},{6,5},{7,6},{8,15},{9,8},{10,9... | collective-permute-start | bytes 786440 | tf_op jit(solution)/shard_map/ppermute | solution.py:341
  98.6 1.7 %fusion.8 = f32[512,512]{0,1:T(8,128)S(1)} fusion(bf16[512,512]{1,0:T(8,128)(2,1)} %collective-permute-done.20, bf16[512,4096]{1,0:T(8,128)(2,1)} %refs_4_.3, s32[]{:T(128)S(6)} %select_n.202), kind=kOutput, calls=%fused_computation.20 | convolution fusion | flops 268435456 | bytes 2097156 | tf_op jit(solution)/shard_map/dot_general | solution.py:17
  100.2 1.7 %fusion.6 = f32[512,512]{0,1:T(8,128)S(1)} fusion(bf16[512,512]{1,0:T(8,128)(2,1)} %collective-permute-done.6, bf16[512,4096]{1,0:T(8,128)(2,1)} %refs_4_.3, s32[]{:T(128)S(6)} %select_n.202), kind=kOutput, calls=%fused_computation.18 | convolution fusion | flops 268435456 | bytes 2097156 | tf_op jit(solution)/shard_map/dot_general | solution.py:17
  101.9 2.7 %fusion.4.refs_1_ = f32[512,512]{1,0:T(8,128)} fusion(f32[512,512]{0,1:T(8,128)S(1)} %fusion.8, f32[512,512]{0,1:T(8,128)S(1)} %fusion.5, bf16[512,512]{1,0:T(8,128)(2,1)} %collective-permute-done.19, bf16[512,4096]{1,0:T(8,128)(2,1)} %refs_4_.3, s32[]{:T(128)S(6)} %select_n.200), kind=kOutput, calls=%fused_computation.9 | convolution fusion | flops 268959744 | bytes 4194308 | tf_op jit(solution)/shard_map/dot_general | solution.py:17
  104.6 2.6 %fusion.1.refs_1_ = f32[512,512]{1,0:T(8,128)} fusion(f32[512,512]{0,1:T(8,128)S(1)} %fusion.6, f32[512,512]{0,1:T(8,128)S(1)} %fusion.2, bf16[512,512]{1,0:T(8,128)(2,1)} %collective-permute-done.2, bf16[512,4096]{1,0:T(8,128)(2,1)} %refs_4_.3, s32[]{:T(128)S(6)} %select_n.200), kind=kOutput, calls=%fused_computation.2 | convolution fusion | flops 268959744 | bytes 4194308 | tf_op jit(solution)/shard_map/dot_general | solution.py:17
  108.0 3.2 %close_chunk.2 = (bf16[512,512]{1,0:T(8,128)(2,1)}, f32[2,4,64,128]{3,2,1,0:T(8,128)}) custom-call(s32[1]{0:T(128)} %bitcast.12.source_ref, f32[4,4]{1,0:T(4,128)} %subtract_exponential_fusion.refs_0_, f32[512,512]{1,0:T(8,128)} %fusion.4.refs_1_, bf16[256,512]{1,0:T(8,128)(2,1)} %copy-done.7, bf16[256,512]{1,0:T(8,128)(2,1)} %copy-done.9, ...), custom_call_target="tpu_custom_call" | custom-call | flops 600000000 | bytes 4000000 | tf_op jit(solution)/shard_map/close_chunk/pallas_call | solution.py:138
  111.2 5.6 %inside.3 = (f32[1024,512]{1,0:T(8,128)}, f32[1024,512]{1,0:T(8,128)}, f32[4,1,1024]{2,1,0:T(1,128)}) custom-call(f32[1,4]{1,0:T(1,128)} %bitcast.48, bf16[512,512]{1,0:T(8,128)(2,1)} %get-tuple-element.38.dy_ref, bf16[1024,512]{1,0:T(8,128)(2,1)} %refs_7_.1, bf16[1024,512]{1,0:T(8,128)(2,1)} %refs_8_.1, bf16[1024,512]{1,0:T(8,128)(2,1)} %get-tuple-element.39.sw_ref, ...), custom_call_target="tpu_custom_call" | custom-call | flops 2000000000 | bytes 7000000 | tf_op jit(solution)/shard_map/inside/pallas_call | solution.py:199
  117.7 3.3 %close_chunk.3 = (bf16[512,512]{1,0:T(8,128)(2,1)}, f32[2,4,64,128]{3,2,1,0:T(8,128)}, f32[4,64,128]{2,1,0:T(8,128)}) custom-call(s32[1]{0:T(128)} %bitcast.12.source_ref, f32[4,4]{1,0:T(4,128)} %subtract_exponential_fusion.refs_0_, f32[512,512]{1,0:T(8,128)} %fusion.1.refs_1_, bf16[256,512]{1,0:T(8,128)(2,1)} %copy-done.6, bf16[256,512]{1,0:T(8,128)(2,1)} %copy-done.8, ...), custom_call_target="tpu_custom_call" | custom-call | flops 600000000 | bytes 4000000 | tf_op jit(solution)/shard_map/close_chunk/pallas_call | solution.py:138
  123.3 1.0 add_convert_fusion.1
  124.4 3.5 %collective-permute-start.25 = (bf16[4,64,128]{2,1,0:T(8,128)(2,1)S(1)}, bf16[4,64,128]{2,1,0:T(8,128)(2,1)S(1)}, u32[]{:S(2)}, u32[]{:S(2)}) collective-permute-start(bf16[4,64,128]{2,1,0:T(8,128)(2,1)S(1)} %add_convert_fusion.1), channel_id=1, source_target_pairs={{0,32},{8,40},{16,48},{24,56},{32,0},{40,8},{48,16},{56,24},{64,96... | collective-permute-start | bytes 196616 | tf_op jit(solution)/shard_map/ppermute | solution.py:318
  128.2 3.5 %inside.4 = (f32[1024,512]{1,0:T(8,128)}, f32[1024,512]{1,0:T(8,128)}, f32[4,1,1024]{2,1,0:T(1,128)}) custom-call(f32[1,4]{1,0:T(1,128)} %bitcast.49, bf16[512,512]{1,0:T(8,128)(2,1)} %get-tuple-element.55.dy_ref, bf16[1024,512]{1,0:T(8,128)(2,1)} %refs_7_.1, ...), custom_call_target="tpu_custom_call", output_to_operand_aliasing={{0}: (9, {}), {1}: (10, {}), {2}: (11, {})} | custom-call | flops 1000000000 | bytes 3500000 | tf_op jit(solution)/shard_map/inside/pallas_call | solution.py:199
  132.2 1.2 collective-permute-start.27
  133.5 4.1 %collective-permute-start.28 = (bf16[4,64,128]{2,1,0:T(8,128)(2,1)S(1)}, bf16[4,64,128]{2,1,0:T(8,128)(2,1)S(1)}, u32[]{:S(2)}, u32[]{:S(2)}) collective-permute-start(bf16[4,64,128]{2,1,0:T(8,128)(2,1)S(1)} %add_convert_fusion), channel_id=1, source_target_pairs={{0,128},{8,136},{16,144},{24,152},{32,160},{40,168},{48,176},{56,1... | collective-permute-start | bytes 196616 | tf_op jit(solution)/shard_map/ppermute | solution.py:321
  137.6 3.5 %inside.5 = (f32[1024,512]{1,0:T(8,128)}, f32[1024,512]{1,0:T(8,128)}, f32[4,1,1024]{2,1,0:T(1,128)}) custom-call(f32[1,4]{1,0:T(1,128)} %bitcast.50, bf16[512,512]{1,0:T(8,128)(2,1)} %get-tuple-element.55.dy_ref, bf16[1024,512]{1,0:T(8,128)(2,1)} %refs_7_.1, ...), custom_call_target="tpu_custom_call", output_to_operand_aliasing={{0}: (9, {}), {1}: (10, {}), {2}: (11, {})} | custom-call | flops 1000000000 | bytes 3500000 | tf_op jit(solution)/shard_map/inside/pallas_call | solution.py:199
  142.5 6.6 %finish.1 = (bf16[1024,512]{1,0:T(8,128)(2,1)}, f32[1024,512]{1,0:T(8,128)}, f32[4,1024]{1,0:T(4,128)}) custom-call(f32[7,4]{1,0:T(8,128)} %slice.83.coefs_ref, f32[4,4]{1,0:T(4,128)} %bitcast.47, bf16[4,64,128]{2,1,0:T(8,128)(2,1)} %copy-done.5, bf16[4,64,128]{2,1,0:T(8,128)(2,1)} %copy-done.2, bf16[4,64,128]{2,1,0:T(8,128)(2,1)} %copy-done.3, ...), custom_call_target="tpu_custom_call" | custom-call | flops 600000000 | bytes 11000000 | tf_op jit(solution)/shard_map/finish/pallas_call | solution.py:266
  (109 shorter events, 14.7 us)
Async XLA Ops:
  0.6 14.2 %copy-start.1 = (bf16[1024,512]{1,0:T(8,128)(2,1)S(1)}, bf16[1024,512]{1,0:T(8,128)(2,1)}, u32[]{:S(2)}) copy-start(bf16[1024,512]{1,0:T(8,128)(2,1)} %param.7) | copy-start | bytes 3145732
  3.0 18.9 %collective-permute-start.12 = (bf16[512,512]{1,0:T(8,128)(2,1)}, bf16[512,512]{1,0:T(8,128)(2,1)}, u32[]{:S(2)}, u32[]{:S(2)}) collective-permute-start(bf16[512,512]{1,0:T(8,128)(2,1)} %get-tuple-element.75), channel_id=1, source_target_pairs={{0,1},{1,2},{2,3},{3,4},{4,5},{5,6},{6,7},{7,0},{8,9},{9,10},{10,1... | collective-permute-start | bytes 1572872 | tf_op jit(solution)/shard_map/ppermute | solution.py:333
  4.9 27.4 %collective-permute-start.17 = (bf16[512,512]{1,0:T(8,128)(2,1)}, bf16[512,512]{1,0:T(8,128)(2,1)}, u32[]{:S(2)}, u32[]{:S(2)}) collective-permute-start(bf16[512,512]{1,0:T(8,128)(2,1)} %get-tuple-element.75), channel_id=1, source_target_pairs={{0,7},{1,0},{2,1},{3,2},{4,3},{5,4},{6,5},{7,6},{8,15},{9,8},{10,9... | collective-permute-start | bytes 1572872 | tf_op jit(solution)/shard_map/ppermute | solution.py:334
  8.8 23.5 %collective-permute-start = (bf16[512,512]{1,0:T(8,128)(2,1)}, bf16[512,512]{1,0:T(8,128)(2,1)}, u32[]{:S(2)}, u32[]{:S(2)}) collective-permute-start(bf16[512,512]{1,0:T(8,128)(2,1)} %get-tuple-element.76), channel_id=1, source_target_pairs={{0,1},{1,2},{2,3},{3,4},{4,5},{5,6},{6,7},{7,0},{8,9},{9,10},{10,1... | collective-permute-start | bytes 1572872 | tf_op jit(solution)/shard_map/ppermute | solution.py:333
  8.8 32.6 %collective-permute-start.4 = (bf16[512,512]{1,0:T(8,128)(2,1)}, bf16[512,512]{1,0:T(8,128)(2,1)}, u32[]{:S(2)}, u32[]{:S(2)}) collective-permute-start(bf16[512,512]{1,0:T(8,128)(2,1)} %get-tuple-element.76), channel_id=1, source_target_pairs={{0,7},{1,0},{2,1},{3,2},{4,3},{5,4},{6,5},{7,6},{8,15},{9,8},{10,9... | collective-permute-start | bytes 1572872 | tf_op jit(solution)/shard_map/ppermute | solution.py:334
  13.0 7.7 %copy-start.13 = (f32[4,1024]{1,0:T(4,128)}, f32[4,1024]{1,0:T(4,128)S(1)}, u32[]{:S(2)}) copy-start(f32[4,1024]{1,0:T(4,128)S(1)} %reshape_reshape.3.arow_ref) | copy-start | bytes 49156
  16.5 19.0 %copy-start = (f32[4,1024]{0,1:T(8,128)}, f32[4,1024]{0,1:T(8,128)S(1)}, u32[]{:S(2)}) copy-start(f32[4,1024]{0,1:T(8,128)S(1)} %copy.115) | copy-start | bytes 49156
  16.9 24.6 %copy-start.14 = (f32[4,4,1]{0,1,2:T(4,128)}, f32[4,4,1]{0,1,2:T(4,128)S(1)}, u32[]{:S(2)}) copy-start(f32[4,4,1]{0,1,2:T(4,128)S(1)} %copy.139) | copy-start | bytes 196
  32.3 17.9 %collective-permute-start.8 = (f32[4]{0:T(128)S(1)}, f32[4]{0:T(128)S(1)}, u32[]{:S(2)}, u32[]{:S(2)}) collective-permute-start(f32[4]{0:T(128)S(1)} %get-tuple-element.34), channel_id=1, source_target_pairs={{0,8},{8,0},{16,24},{24,16},{32,40},{40,32},{48,56},{56,48},{64,72... | collective-permute-start | bytes 56 | tf_op jit(solution)/shard_map/ppermute | solution.py:315
  32.3 32.8 %collective-permute-start.13 = (bf16[512,512]{1,0:T(8,128)(2,1)}, bf16[512,512]{1,0:T(8,128)(2,1)}, u32[]{:S(2)}, u32[]{:S(2)}) collective-permute-start(bf16[512,512]{1,0:T(8,128)(2,1)} %collective-permute-done.12), channel_id=1, source_target_pairs={{0,1},{1,2},{2,3},{3,4},{4,5},{5,6},{6,7},{7,0},{8,9},{9,10},{10,1... | collective-permute-start | bytes 1572872 | tf_op jit(solution)/shard_map/ppermute | solution.py:333
  32.3 40.1 %collective-permute-start.1 = (bf16[512,512]{1,0:T(8,128)(2,1)}, bf16[512,512]{1,0:T(8,128)(2,1)}, u32[]{:S(2)}, u32[]{:S(2)}) collective-permute-start(bf16[512,512]{1,0:T(8,128)(2,1)} %collective-permute-done), channel_id=1, source_target_pairs={{0,1},{1,2},{2,3},{3,4},{4,5},{5,6},{6,7},{7,0},{8,9},{9,10},{10,1... | collective-permute-start | bytes 1572872 | tf_op jit(solution)/shard_map/ppermute | solution.py:333
  32.3 33.4 %collective-permute-start.18 = (bf16[512,512]{1,0:T(8,128)(2,1)}, bf16[512,512]{1,0:T(8,128)(2,1)}, u32[]{:S(2)}, u32[]{:S(2)}) collective-permute-start(bf16[512,512]{1,0:T(8,128)(2,1)} %collective-permute-done.17), channel_id=1, source_target_pairs={{0,7},{1,0},{2,1},{3,2},{4,3},{5,4},{6,5},{7,6},{8,15},{9,8},{10,9... | collective-permute-start | bytes 1572872 | tf_op jit(solution)/shard_map/ppermute | solution.py:334
  41.4 27.5 %collective-permute-start.5 = (bf16[512,512]{1,0:T(8,128)(2,1)}, bf16[512,512]{1,0:T(8,128)(2,1)}, u32[]{:S(2)}, u32[]{:S(2)}) collective-permute-start(bf16[512,512]{1,0:T(8,128)(2,1)} %collective-permute-done.4), channel_id=1, source_target_pairs={{0,7},{1,0},{2,1},{3,2},{4,3},{5,4},{6,5},{7,6},{8,15},{9,8},{10,9... | collective-permute-start | bytes 1572872 | tf_op jit(solution)/shard_map/ppermute | solution.py:334
  50.2 5.1 %collective-permute-start.10 = (f32[4]{0:T(128)S(1)}, f32[4]{0:T(128)S(1)}, u32[]{:S(2)}, u32[]{:S(2)}) collective-permute-start(f32[4]{0:T(128)S(1)} %get-tuple-element.86), channel_id=1, source_target_pairs={{0,32},{8,40},{16,48},{24,56},{32,0},{40,8},{48,16},{56,24},{64,96... | collective-permute-start | bytes 56 | tf_op jit(solution)/shard_map/ppermute | solution.py:318
  55.4 4.3 %collective-permute-start.11 = (f32[4]{0:T(128)S(1)}, f32[4]{0:T(128)S(1)}, u32[]{:S(2)}, u32[]{:S(2)}) collective-permute-start(f32[4]{0:T(128)S(1)} %get-tuple-element.86), channel_id=1, source_target_pairs={{0,48},{8,56},{16,0},{24,8},{32,16},{40,24},{48,32},{56,40},{64,11... | collective-permute-start | bytes 56 | tf_op jit(solution)/shard_map/ppermute | solution.py:318
  59.7 5.0 %collective-permute-start.9 = (f32[4]{0:T(128)S(1)}, f32[4]{0:T(128)S(1)}, u32[]{:S(2)}, u32[]{:S(2)}) collective-permute-start(f32[4]{0:T(128)S(1)} %get-tuple-element.86), channel_id=1, source_target_pairs={{0,16},{8,24},{16,32},{24,40},{32,48},{40,56},{48,0},{56,8},{64,80... | collective-permute-start | bytes 56 | tf_op jit(solution)/shard_map/ppermute | solution.py:318
  65.1 12.7 %collective-permute-start.16 = (f32[4]{0:T(128)S(1)}, f32[4]{0:T(128)S(1)}, u32[]{:S(2)}, u32[]{:S(2)}) collective-permute-start(f32[4]{0:T(128)S(1)} %add_add_fusion), channel_id=1, source_target_pairs={{0,192},{8,200},{16,208},{24,216},{32,224},{40,232},{48,240},{56,2... | collective-permute-start | bytes 56 | tf_op jit(solution)/shard_map/ppermute | solution.py:321
  65.7 22.0 %collective-permute-start.19 = (bf16[512,512]{1,0:T(8,128)(2,1)}, bf16[512,512]{1,0:T(8,128)(2,1)}, u32[]{:S(2)}, u32[]{:S(2)}) collective-permute-start(bf16[512,512]{1,0:T(8,128)(2,1)} %collective-permute-done.13), channel_id=1, source_target_pairs={{0,1},{1,2},{2,3},{3,4},{4,5},{5,6},{6,7},{7,0},{8,9},{9,10},{10,1... | collective-permute-start | bytes 1572872 | tf_op jit(solution)/shard_map/ppermute | solution.py:333
  65.7 23.0 %collective-permute-start.20 = (bf16[512,512]{1,0:T(8,128)(2,1)}, bf16[512,512]{1,0:T(8,128)(2,1)}, u32[]{:S(2)}, u32[]{:S(2)}) collective-permute-start(bf16[512,512]{1,0:T(8,128)(2,1)} %collective-permute-done.18), channel_id=1, source_target_pairs={{0,7},{1,0},{2,1},{3,2},{4,3},{5,4},{6,5},{7,6},{8,15},{9,8},{10,9... | collective-permute-start | bytes 1572872 | tf_op jit(solution)/shard_map/ppermute | solution.py:334
  68.9 25.1 %collective-permute-start.6 = (bf16[512,512]{1,0:T(8,128)(2,1)}, bf16[512,512]{1,0:T(8,128)(2,1)}, u32[]{:S(2)}, u32[]{:S(2)}) collective-permute-start(bf16[512,512]{1,0:T(8,128)(2,1)} %collective-permute-done.5), channel_id=1, source_target_pairs={{0,7},{1,0},{2,1},{3,2},{4,3},{5,4},{6,5},{7,6},{8,15},{9,8},{10,9... | collective-permute-start | bytes 1572872 | tf_op jit(solution)/shard_map/ppermute | solution.py:334
  72.4 20.6 %collective-permute-start.2 = (bf16[512,512]{1,0:T(8,128)(2,1)}, bf16[512,512]{1,0:T(8,128)(2,1)}, u32[]{:S(2)}, u32[]{:S(2)}) collective-permute-start(bf16[512,512]{1,0:T(8,128)(2,1)} %collective-permute-done.1), channel_id=1, source_target_pairs={{0,1},{1,2},{2,3},{3,4},{4,5},{5,6},{6,7},{7,0},{8,9},{9,10},{10,1... | collective-permute-start | bytes 1572872 | tf_op jit(solution)/shard_map/ppermute | solution.py:333
  77.8 4.3 %collective-permute-start.14 = (f32[4]{0:T(128)S(1)}, f32[4]{0:T(128)S(1)}, u32[]{:S(2)}, u32[]{:S(2)}) collective-permute-start(f32[4]{0:T(128)S(1)} %add_add_fusion), channel_id=1, source_target_pairs={{0,64},{8,72},{16,80},{24,88},{32,96},{40,104},{48,112},{56,120},{... | collective-permute-start | bytes 56 | tf_op jit(solution)/shard_map/ppermute | solution.py:321
  82.1 5.0 %collective-permute-start.15 = (f32[4]{0:T(128)S(1)}, f32[4]{0:T(128)S(1)}, u32[]{:S(2)}, u32[]{:S(2)}) collective-permute-start(f32[4]{0:T(128)S(1)} %add_add_fusion), channel_id=1, source_target_pairs={{0,128},{8,136},{16,144},{24,152},{32,160},{40,168},{48,176},{56,1... | collective-permute-start | bytes 56 | tf_op jit(solution)/shard_map/ppermute | solution.py:321
  88.6 18.6 %collective-permute-start.21 = (bf16[256,512]{1,0:T(8,128)(2,1)S(1)}, bf16[256,512]{1,0:T(8,128)(2,1)S(1)}, u32[]{:S(2)}, u32[]{:S(2)}) collective-permute-start(bf16[256,512]{1,0:T(8,128)(2,1)S(1)} %slice.79), channel_id=1, source_target_pairs={{0,1},{1,2},{2,3},{3,4},{4,5},{5,6},{6,7},{7,0},{8,9},{9,10},{10,1... | collective-permute-start | bytes 786440 | tf_op jit(solution)/shard_map/ppermute | solution.py:340
  89.7 17.5 %collective-permute-start.22 = (bf16[256,512]{1,0:T(8,128)(2,1)S(1)}, bf16[256,512]{1,0:T(8,128)(2,1)S(1)}, u32[]{:S(2)}, u32[]{:S(2)}) collective-permute-start(bf16[256,512]{1,0:T(8,128)(2,1)S(1)} %slice.80), channel_id=1, source_target_pairs={{0,7},{1,0},{2,1},{3,2},{4,3},{5,4},{6,5},{7,6},{8,15},{9,8},{10,9... | collective-permute-start | bytes 786440 | tf_op jit(solution)/shard_map/ppermute | solution.py:341
  94.0 22.9 %collective-permute-start.3 = (bf16[256,512]{1,0:T(8,128)(2,1)S(1)}, bf16[256,512]{1,0:T(8,128)(2,1)S(1)}, u32[]{:S(2)}, u32[]{:S(2)}) collective-permute-start(bf16[256,512]{1,0:T(8,128)(2,1)S(1)} %slice.76), channel_id=1, source_target_pairs={{0,1},{1,2},{2,3},{3,4},{4,5},{5,6},{6,7},{7,0},{8,9},{9,10},{10,1... | collective-permute-start | bytes 786440 | tf_op jit(solution)/shard_map/ppermute | solution.py:340
  95.1 21.9 %collective-permute-start.7 = (bf16[256,512]{1,0:T(8,128)(2,1)S(1)}, bf16[256,512]{1,0:T(8,128)(2,1)S(1)}, u32[]{:S(2)}, u32[]{:S(2)}) collective-permute-start(bf16[256,512]{1,0:T(8,128)(2,1)S(1)} %slice.77), channel_id=1, source_target_pairs={{0,7},{1,0},{2,1},{3,2},{4,3},{5,4},{6,5},{7,6},{8,15},{9,8},{10,9... | collective-permute-start | bytes 786440 | tf_op jit(solution)/shard_map/ppermute | solution.py:341
  107.2 0.7 copy-start.7
  107.2 0.8 copy-start.9
  116.9 0.7 copy-start.6
  116.9 0.8 copy-start.8
  121.9 1.3 collective-permute-start.23
  123.3 8.5 %copy-start.5 = (bf16[4,64,128]{2,1,0:T(8,128)(2,1)}, bf16[4,64,128]{2,1,0:T(8,128)(2,1)S(1)}, u32[]{:S(2)}) copy-start(bf16[4,64,128]{2,1,0:T(8,128)(2,1)S(1)} %collective-permute-done.23.refs_0_) | copy-start | bytes 196612
  124.3 7.5 %collective-permute-start.24 = (bf16[4,64,128]{2,1,0:T(8,128)(2,1)S(1)}, bf16[4,64,128]{2,1,0:T(8,128)(2,1)S(1)}, u32[]{:S(2)}, u32[]{:S(2)}) collective-permute-start(bf16[4,64,128]{2,1,0:T(8,128)(2,1)S(1)} %add_convert_fusion.1), channel_id=1, source_target_pairs={{0,16},{8,24},{16,32},{24,40},{32,48},{40,56},{48,0},{56,8},{64,80... | collective-permute-start | bytes 196616 | tf_op jit(solution)/shard_map/ppermute | solution.py:318
  124.4 7.4 %collective-permute-start.25 = (bf16[4,64,128]{2,1,0:T(8,128)(2,1)S(1)}, bf16[4,64,128]{2,1,0:T(8,128)(2,1)S(1)}, u32[]{:S(2)}, u32[]{:S(2)}) collective-permute-start(bf16[4,64,128]{2,1,0:T(8,128)(2,1)S(1)} %add_convert_fusion.1), channel_id=1, source_target_pairs={{0,32},{8,40},{16,48},{24,56},{32,0},{40,8},{48,16},{56,24},{64,96... | collective-permute-start | bytes 196616 | tf_op jit(solution)/shard_map/ppermute | solution.py:318
  127.8 4.3 %collective-permute-start.26 = (bf16[4,64,128]{2,1,0:T(8,128)(2,1)S(1)}, bf16[4,64,128]{2,1,0:T(8,128)(2,1)S(1)}, u32[]{:S(2)}, u32[]{:S(2)}) collective-permute-start(bf16[4,64,128]{2,1,0:T(8,128)(2,1)S(1)} %add_convert_fusion.1), channel_id=1, source_target_pairs={{0,48},{8,56},{16,0},{24,8},{32,16},{40,24},{48,32},{56,40},{64,11... | collective-permute-start | bytes 196616 | tf_op jit(solution)/shard_map/ppermute | solution.py:318
  131.8 9.4 %copy-start.2 = (bf16[4,64,128]{2,1,0:T(8,128)(2,1)}, bf16[4,64,128]{2,1,0:T(8,128)(2,1)S(1)}, u32[]{:S(2)}) copy-start(bf16[4,64,128]{2,1,0:T(8,128)(2,1)S(1)} %collective-permute-done.24.refs_1_) | copy-start | bytes 196612
  131.8 9.3 %copy-start.3 = (bf16[4,64,128]{2,1,0:T(8,128)(2,1)}, bf16[4,64,128]{2,1,0:T(8,128)(2,1)S(1)}, u32[]{:S(2)}) copy-start(bf16[4,64,128]{2,1,0:T(8,128)(2,1)S(1)} %collective-permute-done.25.refs_2_) | copy-start | bytes 196612
  132.1 9.1 %copy-start.4 = (bf16[4,64,128]{2,1,0:T(8,128)(2,1)}, bf16[4,64,128]{2,1,0:T(8,128)(2,1)S(1)}, u32[]{:S(2)}) copy-start(bf16[4,64,128]{2,1,0:T(8,128)(2,1)S(1)} %collective-permute-done.26.refs_3_) | copy-start | bytes 196612
  132.2 8.9 %collective-permute-start.27 = (bf16[4,64,128]{2,1,0:T(8,128)(2,1)S(1)}, bf16[4,64,128]{2,1,0:T(8,128)(2,1)S(1)}, u32[]{:S(2)}, u32[]{:S(2)}) collective-permute-start(bf16[4,64,128]{2,1,0:T(8,128)(2,1)S(1)} %add_convert_fusion), channel_id=1, source_target_pairs={{0,64},{8,72},{16,80},{24,88},{32,96},{40,104},{48,112},{56,120},{... | collective-permute-start | bytes 196616 | tf_op jit(solution)/shard_map/ppermute | solution.py:321
  133.5 7.7 %collective-permute-start.28 = (bf16[4,64,128]{2,1,0:T(8,128)(2,1)S(1)}, bf16[4,64,128]{2,1,0:T(8,128)(2,1)S(1)}, u32[]{:S(2)}, u32[]{:S(2)}) collective-permute-start(bf16[4,64,128]{2,1,0:T(8,128)(2,1)S(1)} %add_convert_fusion), channel_id=1, source_target_pairs={{0,128},{8,136},{16,144},{24,152},{32,160},{40,168},{48,176},{56,1... | collective-permute-start | bytes 196616 | tf_op jit(solution)/shard_map/ppermute | solution.py:321
  137.6 4.3 %collective-permute-start.29 = (bf16[4,64,128]{2,1,0:T(8,128)(2,1)S(1)}, bf16[4,64,128]{2,1,0:T(8,128)(2,1)S(1)}, u32[]{:S(2)}, u32[]{:S(2)}) collective-permute-start(bf16[4,64,128]{2,1,0:T(8,128)(2,1)S(1)} %add_convert_fusion), channel_id=1, source_target_pairs={{0,192},{8,200},{16,208},{24,216},{32,224},{40,232},{48,240},{56,2... | collective-permute-start | bytes 196616 | tf_op jit(solution)/shard_map/ppermute | solution.py:321
  141.2 0.7 copy-start.10
  141.2 0.7 copy-start.11
  141.9 0.6 copy-start.12

commit v4 on v3

--- a/solution.py
+++ b/solution.py
@@ -10,11 +10,15 @@
 BLOCK = 256
 F32 = jnp.float32
 BF16 = jnp.bfloat16
-VMEM_LIMIT = 60 << 20
+VMEM_LIMIT = 48 << 20
 
 
 def dot(a, b, dims):
     return lax.dot_general(a, b, (dims, ((), ())), preferred_element_type=F32)
+
+
+def in_hbm(*arrays):
+    return [pltpu.with_memory_space_constraint(a, pltpu.HBM) for a in arrays]
 
 
 NN = ((1,), (0,))
@@ -24,6 +28,77 @@
 
 def low_lanes(shape):
     return lax.broadcasted_iota(jnp.int32, shape, len(shape) - 1) < STATE
+
+
+def log_rows(log):
+    high = log.astype(BF16)
+    rest = log - high.astype(F32)
+    middle = rest.astype(BF16)
+    low = (rest - middle.astype(F32)).astype(BF16)
+    return high, middle, low
+
+
+def store_message(ref, sums, logs):
+    heads = len(sums)
+    for h in range(heads):
+        ref[h * STATE : (h + 1) * STATE, :] = sums[h].astype(BF16)
+    parts = [log_rows(log) for log in logs]
+    rows = [parts[h][k].astype(F32) for k in range(3) for h in range(heads)]
+    rows = rows + [jnp.zeros_like(rows[0])] * (16 - 3 * heads)
+    ref[heads * STATE :, :] = jnp.concatenate(rows, axis=0).astype(BF16)
+
+
+def message_sum(ref, h):
+    return ref[h * STATE : (h + 1) * STATE, :].astype(F32)
+
+
+def message_log(ref, heads, h):
+    tail = ref[heads * STATE :, :].astype(F32)
+    return tail[h : h + 1] + tail[heads + h : heads + h + 1] + tail[2 * heads + h : 2 * heads + h + 1]
+
+
+def masked_total(terms):
+    total = jnp.zeros_like(terms[0][1])
+    for condition, value in terms:
+        total = total + jnp.where(condition, value, 0.0)
+    return total
+
+
+def combine(kind, place, messages):
+    rows, width = messages[0].shape
+    heads = (rows - 16) // STATE
+
+    def body(place_ref, *refs):
+        got, out_ref = refs[:-1], refs[-1]
+        sums, logs = [], []
+        for h in range(heads):
+            log = [message_log(ref, heads, h) for ref in got]
+            if kind == "core":
+                first = place_ref[2] == 0
+                own = jnp.exp(jnp.where(first, 0.0, log[1]))
+                other = jnp.exp(jnp.where(first, log[0], 0.0))
+                sums.append(own * message_sum(got[0], h) + other * message_sum(got[1], h))
+            else:
+                here = [lax.rem(place_ref[1] - s + 4, 4) for s in range(4)]
+                total = None
+                for s in range(4):
+                    ahead = masked_total([(here[t] < here[s], log[t]) for t in range(4) if t != s])
+                    term = jnp.exp(ahead) * message_sum(got[s], h)
+                    total = term if total is None else total + term
+                sums.append(total)
+            logs.append(sum(log[1:], log[0]))
+        store_message(out_ref, sums, logs)
+
+    return pl.pallas_call(
+        body,
+        name="combine_" + kind,
+        in_specs=[pl.BlockSpec(memory_space=pltpu.SMEM)]
+        + [pl.BlockSpec(memory_space=pltpu.VMEM)] * len(messages),
+        out_specs=pl.BlockSpec(memory_space=pltpu.VMEM),
+        out_shape=jax.ShapeDtypeStruct((rows, width), BF16),
+        cost_estimate=pl.CostEstimate(flops=1_000_000, bytes_accessed=500_000, transcendentals=0),
+        compiler_params=pltpu.CompilerParams(vmem_limit_bytes=16 << 20),
+    )(place, *messages)
 
 
 def prepare(bc, arow, aline, states):
@@ -75,11 +150,11 @@
             block4(HEAD_DIM, HEAD_DIM),
         ],
         out_shape=[
-            jax.ShapeDtypeStruct((tokens, width), BF16),
-            jax.ShapeDtypeStruct((blocks, heads, BLOCK, BLOCK), BF16),
-            jax.ShapeDtypeStruct((blocks, heads, BLOCK, BLOCK), BF16),
-            jax.ShapeDtypeStruct((blocks, heads, STATE, BLOCK), BF16),
-            jax.ShapeDtypeStruct((blocks, heads, HEAD_DIM, HEAD_DIM), BF16),
+            pltpu.HBM((tokens, width), BF16),
+            pltpu.HBM((blocks, heads, BLOCK, BLOCK), BF16),
+            pltpu.HBM((blocks, heads, BLOCK, BLOCK), BF16),
+            pltpu.HBM((blocks, heads, STATE, BLOCK), BF16),
+            pltpu.HBM((blocks, heads, HEAD_DIM, HEAD_DIM), BF16),
         ],
         cost_estimate=pl.CostEstimate(flops=4_000_000_000, bytes_accessed=9_000_000, transcendentals=0),
         compiler_params=pltpu.CompilerParams(vmem_limit_bytes=VMEM_LIMIT),
@@ -112,14 +187,15 @@
                 if last:
                     sums[h] = sums[h] + scale_ref[b + first, h] * term
         if last:
-            for h in range(heads):
-                part_ref[h] = sums[h]
+            store_message(
+                part_ref, sums, [jnp.full((1, HEAD_DIM), scale_ref[4, h], F32) for h in range(heads)]
+            )
 
     def whole(*dims):
         return pl.BlockSpec(dims, lambda i, source: (0,) * len(dims))
 
     terms_shape = (2, heads, STATE, HEAD_DIM)
-    out_shape = [jax.ShapeDtypeStruct((tokens, width), BF16), jax.ShapeDtypeStruct(terms_shape, F32)]
+    out_shape = [pltpu.HBM((tokens, width), BF16), pltpu.HBM(terms_shape, F32)]
     out_specs = [whole(tokens, width), whole(*terms_shape)]
     in_specs = [
         pl.BlockSpec(memory_space=pltpu.SMEM),
@@ -131,10 +207,10 @@
     ]
     operands = [scale, acc, up, down, weight, wct]
     if last:
-        out_shape.append(jax.ShapeDtypeStruct((heads, STATE, HEAD_DIM), F32))
-        out_specs.append(whole(heads, STATE, HEAD_DIM))
+        out_shape.append(jax.ShapeDtypeStruct((heads * STATE + 16, HEAD_DIM), BF16))
+        out_specs.append(whole(heads * STATE + 16, HEAD_DIM))
         in_specs.append(whole(*terms_shape))
-        operands.append(earlier)
+        operands.extend(in_hbm(earlier))
     return pl.pallas_call(
         body,
         name="close_chunk",
@@ -189,10 +265,11 @@
         square,
         pl.BlockSpec((1, group, HEAD_DIM, HEAD_DIM), lambda b, g: (b + first, g, 0, 0)),
     ]
-    operands = [skip, dy, x, bc, sw, jnp.stack([aline[:, :group], aline[:, group:]]), dec, sct, spad]
+    dy, x, bc, sw, dec, sct, spad = in_hbm(dy, x, bc, sw, dec, sct, spad)
+    operands = [skip, dy, x, bc, sw, aline, dec, sct, spad]
     aliases = {}
     if before is not None:
-        for place, array in enumerate(before):
+        for place, array in enumerate(in_hbm(*before)):
             aliases[len(operands)] = place
             operands.append(array)
             in_specs.append(pl.BlockSpec(memory_space=pl.ANY))
@@ -203,9 +280,9 @@
         in_specs=in_specs,
         out_specs=[wide, wide, pl.BlockSpec((group, 1, BLOCK), lambda b, g: (g, 0, b + first))],
         out_shape=[
-            jax.ShapeDtypeStruct((tokens, width), F32),
-            jax.ShapeDtypeStruct((tokens, width), F32),
-            jax.ShapeDtypeStruct((heads, 1, tokens), F32),
+            pltpu.HBM((tokens, width), F32),
+            pltpu.HBM((tokens, width), F32),
+            pltpu.HBM((heads, 1, tokens), F32),
         ],
         input_output_aliases=aliases,
         cost_estimate=pl.CostEstimate(
@@ -215,13 +292,13 @@
     )(*operands)
 
 
-def finish(coefs, a_last, received, x, bc, aline, terms, states, dx, dbc, dlog):
+def finish(place, a_last, received, x, bc, aline, terms, states, dx, dbc, dlog):
     tokens, width = x.shape
     heads = width // HEAD_DIM
     blocks = tokens // BLOCK
     count = len(received)
 
-    def body(coefs_ref, last_ref, *refs):
+    def body(place_ref, last_ref, *refs):
         got = refs[:count]
         (x_ref, bc_ref, aline_ref, terms0_ref, terms1_ref, states_ref, dx_ref, dbc_ref, dlog_ref, out_ref,
          outbc_ref, outlog_ref, carry_ref) = refs[count:]
@@ -230,10 +307,27 @@
 
         @pl.when(step == 0)
         def _():
+            own, other, ys, xs = got[0], got[1], got[2:6], got[6:10]
+            first = place_ref[2] == 0
+            at_y = [lax.rem(place_ref[1] - s + 4, 4) for s in range(4)]
+            at_x = [lax.rem(place_ref[0] - s + 4, 4) for s in range(4)]
             for h in range(heads):
-                total = coefs_ref[0, h] * got[0][h].astype(F32)
-                for i in range(1, count):
-                    total = total + coefs_ref[i, h] * got[i][h].astype(F32)
+                y_logs = [message_log(ref, heads, h) for ref in ys]
+                x_logs = [message_log(ref, heads, h) for ref in xs]
+                after_core = jnp.where(first, message_log(other, heads, h), 0.0)
+                after_y = after_core + masked_total([(at_y[t] > at_y[0], y_logs[t]) for t in (1, 2, 3)])
+                total = jnp.where(first, message_sum(other, h), 0.0)
+                for places, logs, items, after in ((at_y, y_logs, ys, after_core), (at_x, x_logs, xs, after_y)):
+                    for s in (1, 2, 3):
+                        between = masked_total(
+                            [
+                                ((places[t] > places[0]) & (places[t] < places[s]), logs[t])
+                                for t in (1, 2, 3)
+                                if t != s
+                            ]
+                        )
+                        factor = jnp.where(places[s] > places[0], jnp.exp(after + between), 0.0)
+                        total = total + factor * message_sum(items[s], h)
                 carry_ref[h] = total
 
         rows = lax.broadcasted_iota(jnp.int32, (BLOCK, BLOCK), 0)
@@ -259,6 +353,8 @@
             )
             carry_ref[h] = ends * carry + jnp.where(late, terms1_ref[0, h], terms0_ref[0, h])
 
+    x, bc, states, dx, dbc, dlog = in_hbm(x, bc, states, dx, dbc, dlog)
+    terms = in_hbm(*terms)
     wide = pl.BlockSpec((BLOCK, width), lambda i: (blocks - 1 - i, 0))
     smem = pl.BlockSpec(memory_space=pltpu.SMEM)
     state_block = (1, heads, STATE, HEAD_DIM)
@@ -268,7 +364,7 @@
         name="finish",
         grid=(blocks,),
         in_specs=[smem, smem]
-        + [pl.BlockSpec((heads, STATE, HEAD_DIM), lambda i: (0, 0, 0)) for _ in received]
+        + [pl.BlockSpec(message.shape, lambda i: (0, 0)) for message in received]
         + [
             wide,
             wide,
@@ -289,7 +385,7 @@
         scratch_shapes=[pltpu.VMEM((heads, STATE, HEAD_DIM), F32)],
         cost_estimate=pl.CostEstimate(flops=600_000_000, bytes_accessed=11_000_000, transcendentals=0),
         compiler_params=pltpu.CompilerParams(vmem_limit_bytes=VMEM_LIMIT),
-    )(coefs, a_last, *received, x, bc, aline, terms[0], terms[1], states, dx, dbc, dlog)
+    )(place, a_last, *received, x, bc, aline, terms[0], terms[1], states, dx, dbc, dlog)
 
 
 def shift(count, by):
@@ -324,7 +420,7 @@
         return lax.dynamic_slice_in_dim(out_weight, (source % tp) * feats, feats, 1)
 
     half = tokens // 2
-    accs, lasts, firsts, seconds = [], [], [], []
+    accs, lasts, firsts = [], [], []
     for c in range(2):
         own = upstream[c * half : (c + 1) * half]
         right = left = own
@@ -334,8 +430,6 @@
             left = lax.ppermute(left, "tp", shift(tp, -1))
             if k == 1:
                 firsts.append(right)
-            if k == 2:
-                seconds.append(right)
             acc = acc + dot(right, weight_of(me - k + tp), NT) + dot(left, weight_of(me + k), NT)
         up = lax.ppermute(right[:BLOCK], "tp", shift(tp, 1))
         down = lax.ppermute(left[BLOCK:], "tp", shift(tp, -1))
@@ -350,68 +444,33 @@
     aline = arow.T
     bc_then, _ = lax.optimization_barrier((head_bc, firsts[0]))
     sw, dec, sct, wct, spad = prepare(bc_then, arow, aline, states)
-    ahead = jnp.exp(jnp.cumsum(last, axis=0) - last)
-
-    own_log, _ = lax.optimization_barrier((jnp.sum(last, axis=0), firsts[1]))
-    other_log = from_core(own_log)
-    chip_log = own_log + other_log
-    y_logs = jnp.stack([chip_log] + from_y(chip_log))
-    row_log, _ = lax.optimization_barrier((jnp.sum(y_logs, axis=0), seconds[0]))
-    x_logs = jnp.stack([row_log] + from_x(row_log))
-    at_y = (py - jnp.arange(4)) % 4
-    at_x = (px - jnp.arange(4)) % 4
-
-    def masked(mask, logs):
-        return jnp.sum(jnp.where(mask[:, :, None], logs[None], 0.0), axis=1)
-
-    none = jnp.zeros_like(own_log)
-    first_core = pc == 0
-    after_core = jnp.where(first_core, other_log, none)
-    after_y = jnp.sum(jnp.where((at_y > py)[:, None], y_logs, 0.0), axis=0)
-    over_y = masked((at_y[None] > py) & (at_y[None] < at_y[:, None]), y_logs)
-    over_x = masked((at_x[None] > px) & (at_x[None] < at_x[:, None]), x_logs)
-    rows_y = masked(at_y[None] < at_y[:, None], y_logs)
-    chips = jnp.stack([jnp.where(first_core, none, other_log), jnp.where(first_core, own_log, none)])
-    finals = jnp.concatenate(
-        [
-            jnp.where(first_core, jnp.ones_like(own_log), none)[None],
-            jnp.where((at_y > py)[:, None], jnp.exp(after_core + over_y), 0.0)[1:],
-            jnp.where((at_x > px)[:, None], jnp.exp(after_core + after_y + over_x), 0.0)[1:],
-        ]
-    )
-    coefs = jnp.concatenate([jnp.exp(chips), jnp.exp(rows_y), finals])
+    upto = jnp.cumsum(last, axis=0)
+    scale = jnp.concatenate([jnp.exp(upto - last), upto[blocks - 1 :]])
+    place = jnp.stack([px, py, pc]).astype(jnp.int32)
 
     skips = skip[None]
+    aline2 = jnp.stack([aline[:, : heads // 2], aline[:, heads // 2 :]])
 
     def within(first, count, dy_first, dy, before):
         return inside(
-            first, count, dy_first, dy, skips, inner_act, head_bc, sw, aline, dec, sct, spad, before
+            first, count, dy_first, dy, skips, inner_act, head_bc, sw, aline2, dec, sct, spad, before
         )
 
     source = ((me + tp // 2) % tp).astype(jnp.int32)[None]
-    dy0, terms0 = close_chunk(0, source, accs[0], *lasts[0], out_weight, wct, ahead, None)
+    dy0, terms0 = close_chunk(0, source, accs[0], *lasts[0], out_weight, wct, scale, None)
+    dy1, terms1, part = close_chunk(2, source, accs[1], *lasts[1], out_weight, wct, scale, terms0)
+
+    other = from_core(part)
+    chip = combine("core", place, [part, other])
+    ys = [chip] + from_y(chip)
+    dy0, ys[0] = lax.optimization_barrier((dy0, ys[0]))
     grads = within(0, 2, 0, dy0, None)
-    lasts[1], coefs, grads = lax.optimization_barrier((lasts[1], coefs, grads))
-    dy1, terms1, part = close_chunk(2, source, accs[1], *lasts[1], out_weight, wct, ahead, terms0)
-
-    def by(i):
-        return coefs[i][:, None, None]
-
-    part16 = part.astype(BF16)
-    other = from_core(part16)
-    chip_sum = (by(0) * part + by(1) * other.astype(F32)).astype(BF16)
-    ys = from_y(chip_sum)
-    dy1, chip_sum = lax.optimization_barrier((dy1, chip_sum))
-    grads = within(2, 1, 0, dy1, grads)
-    row_sum = by(2) * chip_sum.astype(F32)
-    for s in range(3):
-        row_sum = row_sum + by(3 + s) * ys[s].astype(F32)
-    row_sum = row_sum.astype(BF16)
-    xs = from_x(row_sum)
-    dy1, row_sum = lax.optimization_barrier((dy1, row_sum))
-    dx, dbc, dlog = within(3, 1, 1, dy1, grads)
+    row = combine("row", place, ys)
+    xs = [row] + from_x(row)
+    dy1, xs[0] = lax.optimization_barrier((dy1, xs[0]))
+    dx, dbc, dlog = within(2, 2, 0, dy1, grads)
     return finish(
-        coefs[6:], last, [other] + ys + xs, inner_act, head_bc, aline, (terms0, terms1), states, dx, dbc, dlog
+        place, last, [part, other] + ys + xs, inner_act, head_bc, aline, (terms0, terms1), states, dx, dbc, dlog
     )
 
 

time: 150 us -> 124 us (0.83)
  matrix products: 25.4 us -> 11.1 us
  waiting for transfers between devices: 26.1 us -> 37.7 us
  starting transfers between devices: 47.3 us -> 39 us
  local copies, waits for them, and re-layouts: 12 us -> 4.4 us
  other arithmetic: 5.48 us -> 0.2 us
  Pallas kernels: 31.7 us -> 28.4 us
    ppermute x6, waiting for transfers between devices: 11.6 us -> 26.7 us  [per_device(): right = lax.ppermute(right, 'tp', shift(tp, 1))]
    dot_general x14, matrix products: 25.2 us -> 11 us  [dot(): return lax.dot_general(a, b, (dims, ((), ())), preferred_element_type=F32)]
    ppermute x6 -> x3, waiting for transfers between devices: 7.59 us -> 0.01 us  [from_y(): return [lax.ppermute(a, 'ctx', perm(0, s, 0)) for s in (1, 2, 3)]]
    ppermute x6, waiting for transfers between devices: 0.02 us -> 7.55 us  [per_device(): left = lax.ppermute(left, 'tp', shift(tp, -1))]
    ppermute x6 -> x3, waiting for transfers between devices: 6.65 us -> 0.01 us  [from_x(): return [lax.ppermute(a, 'ctx', perm(s, 0, 0)) for s in (1, 2, 3)]]
    ppermute x6 -> x3, starting transfers between devices: 11 us -> 5.91 us  [from_y(): return [lax.ppermute(a, 'ctx', perm(0, s, 0)) for s in (1, 2, 3)]]
    ppermute x6 -> x3, starting transfers between devices: 9.4 us -> 4.84 us  [from_x(): return [lax.ppermute(a, 'ctx', perm(s, 0, 0)) for s in (1, 2, 3)]]
    ppermute x6, starting transfers between devices: 15.8 us -> 19.2 us  [per_device(): left = lax.ppermute(left, 'tp', shift(tp, -1))]
  transfers between devices with their start and end apart: 30 -> 23, of which waited for: 10 -> 8; matrix products, arithmetic and copies ran while one was open for 24% -> 10% of each run, Pallas kernels for 15% -> 15%
where the time goes in v4:
time: 124 us; the launch traced here: 122 us
  starting transfers between devices  39 us (31%)
  waiting for transfers between devices  37.7 us (30%)
  Pallas kernels  28.4 us (23%)
  matrix products  11.1 us (9%)
  local copies, waits for them, and re-layouts  4.4 us (4%)
  between operations  1.26 us (1%)
    ppermute x6, waiting for transfers between devices, per_device(): right = lax.ppermute(right, 'tp', shift(tp, 1))  26.7 us
    ppermute x6, starting transfers between devices, per_device(): left = lax.ppermute(left, 'tp', shift(tp, -1))  19.2 us
    pallas_call x2, Pallas kernels, inside(): pl.pallas_call(body, name='inside', grid=(count, 2), in_specs=in_specs, o...  11.3 us
    dot_general x14, matrix products, dot(): return lax.dot_general(a, b, (dims, ((), ())), preferred_element_type=F32)  11 us
    ppermute x6, waiting for transfers between devices, per_device(): left = lax.ppermute(left, 'tp', shift(tp, -1))  7.55 us
    ppermute x2, starting transfers between devices, per_device(): down = lax.ppermute(left[BLOCK:], 'tp', shift(tp, -1))  6.62 us
    pallas_call x1, Pallas kernels, finish(): pl.pallas_call(body, name='finish', grid=(blocks,), in_specs=[smem, smem]...  6.17 us
    ppermute x3, starting transfers between devices, from_y(): return [lax.ppermute(a, 'ctx', perm(0, s, 0)) for s in (1, 2, 3)]  5.91 us
  transfers between devices with their start and end apart: 23, of which 8 were waited for; matrix products, arithmetic and copies ran while one was open for 10% of the time, Pallas kernels for 15%

profile of v4, /device:TPU:2, one launch (start us, length us, event | category | flops | bytes accessed | tf_op | source)
XLA Modules:
  0.0 122.1 jit_solution(9763884259599945227)
XLA Ops:
  0.6 2.3 %fusion.42 = (bf16[512,512]{1,0:T(8,128)(2,1)}, bf16[512,512]{1,0:T(8,128)(2,1)}) fusion(bf16[1024,512]{1,0:T(8,128)(2,1)} %param.7), kind=kLoop, calls=%fused_computation.58 | loop fusion | bytes 2097152 | tf_op jit(solution)/shard_map/slice | solution.py:425
  3.0 1.9 %collective-permute-start.8 = (bf16[512,512]{1,0:T(8,128)(2,1)}, bf16[512,512]{1,0:T(8,128)(2,1)}, u32[]{:S(2)}, u32[]{:S(2)}) collective-permute-start(bf16[512,512]{1,0:T(8,128)(2,1)} %get-tuple-element.45), channel_id=1, source_target_pairs={{0,1},{1,2},{2,3},{3,4},{4,5},{5,6},{6,7},{7,0},{8,9},{9,10},{10,1... | collective-permute-start | bytes 1572872 | tf_op jit(solution)/shard_map/ppermute | solution.py:429
  4.9 3.9 %collective-permute-start.9 = (bf16[512,512]{1,0:T(8,128)(2,1)}, bf16[512,512]{1,0:T(8,128)(2,1)}, u32[]{:S(2)}, u32[]{:S(2)}) collective-permute-start(bf16[512,512]{1,0:T(8,128)(2,1)} %get-tuple-element.45), channel_id=1, source_target_pairs={{0,7},{1,0},{2,1},{3,2},{4,3},{5,4},{6,5},{7,6},{8,15},{9,8},{10,9... | collective-permute-start | bytes 1572872 | tf_op jit(solution)/shard_map/ppermute | solution.py:430
  8.8 3.2 %collective-permute-start.1 = (bf16[512,512]{1,0:T(8,128)(2,1)}, bf16[512,512]{1,0:T(8,128)(2,1)}, u32[]{:S(2)}, u32[]{:S(2)}) collective-permute-start(bf16[512,512]{1,0:T(8,128)(2,1)} %get-tuple-element.46), channel_id=1, source_target_pairs={{0,7},{1,0},{2,1},{3,2},{4,3},{5,4},{6,5},{7,6},{8,15},{9,8},{10,9... | collective-permute-start | bytes 1572872 | tf_op jit(solution)/shard_map/ppermute | solution.py:430
  12.1 0.7 reshape.12
  13.3 0.2 copy.77
  13.9 1.7 %fusion.22 = f32[512,512]{0,1:T(8,128)S(1)} fusion(bf16[512,4096]{1,0:T(8,128)(2,1)} %refs_4_.3, s32[]{:T(128)S(6)} %select_n.98, bf16[1024,512]{1,0:T(8,128)(2,1)S(1)} %copy-done.5), kind=kOutput, calls=%fused_computation.34 | convolution fusion | flops 268435456 | bytes 2097156 | tf_op jit(solution)/shard_map/dot_general | solution.py:17
  15.6 0.6 copy-done.4
  16.2 0.5 fusion.24
  16.6 5.2 %collective-permute-done.8 = bf16[512,512]{1,0:T(8,128)(2,1)} collective-permute-done((bf16[512,512]{1,0:T(8,128)(2,1)}, bf16[512,512]{1,0:T(8,128)(2,1)}, u32[]{:S(2)}, u32[]{:S(2)}) %collective-permute-start.8) | collective-permute-done | bytes 524320 | tf_op jit(solution)/shard_map/ppermute | solution.py:429
  21.9 3.3 %collective-permute-start.11 = (bf16[512,512]{1,0:T(8,128)(2,1)}, bf16[512,512]{1,0:T(8,128)(2,1)S(1)}, u32[]{:S(2)}, u32[]{:S(2)}) collective-permute-start(bf16[512,512]{1,0:T(8,128)(2,1)} %collective-permute-done.9), channel_id=1, source_target_pairs={{0,7},{1,0},{2,1},{3,2},{4,3},{5,4},{6,5},{7,6},{8,15},{9,8},{10,9... | collective-permute-start | bytes 1572872 | tf_op jit(solution)/shard_map/ppermute | solution.py:430
  25.2 7.9 %collective-permute-done = bf16[512,512]{1,0:T(8,128)(2,1)S(1)} collective-permute-done((bf16[512,512]{1,0:T(8,128)(2,1)}, bf16[512,512]{1,0:T(8,128)(2,1)S(1)}, u32[]{:S(2)}, u32[]{:S(2)}) %collective-permute-start) | collective-permute-done | bytes 524320 | tf_op jit(solution)/shard_map/ppermute | solution.py:429
  33.0 1.5 %convolution_add_fusion.3 = f32[512,512]{0,1:T(8,128)S(1)} fusion(f32[512,512]{0,1:T(8,128)S(1)} %fusion.22, bf16[512,512]{1,0:T(8,128)(2,1)} %collective-permute-done.8, bf16[512,4096]{1,0:T(8,128)(2,1)S(1)} %copy-done.4, s32[]{:T(128)S(6)} %select_n.100), kind=kOutput, calls=%fused_computation.6 | convolution fusion | flops 268697600 | bytes 3145732 | tf_op jit(solution)/shard_map/dot_general | solution.py:17
  34.5 0.5 convolution_add_fusion.7
  35.0 4.2 %prepare.1 = (bf16[1024,512]{1,0:T(8,128)(2,1)}, bf16[4,4,256,256]{3,2,1,0:T(8,128)(2,1)}, bf16[4,4,256,256]{3,2,1,0:T(8,128)(2,1)}, bf16[4,4,64,256]{3,2,1,0:T(8,128)(2,1)}, bf16[4,4,128,128]{3,2,1,0:T(8,128)(2,1)}) custom-call(bf16[1024,512]{1,0:T(8,128)(2,1)S(1)} %copy-done, f32[4,1024]{1,0:T(4,128)S(1)} %reshape_reshape.3.arow_ref, ...), custom_call_target="tpu_custom_call" | custom-call | flops 4000000000 | bytes 9000000 | tf_op jit(solution)/shard_map/prepare/pallas_call | solution.py:135
  39.2 3.3 %collective-permute-start.3 = (bf16[512,512]{1,0:T(8,128)(2,1)}, bf16[512,512]{1,0:T(8,128)(2,1)S(1)}, u32[]{:S(2)}, u32[]{:S(2)}) collective-permute-start(bf16[512,512]{1,0:T(8,128)(2,1)} %collective-permute-done.1), channel_id=1, source_target_pairs={{0,7},{1,0},{2,1},{3,2},{4,3},{5,4},{6,5},{7,6},{8,15},{9,8},{10,9... | collective-permute-start | bytes 1572872 | tf_op jit(solution)/shard_map/ppermute | solution.py:430
  42.6 1.5 %convolution_add_fusion.2 = f32[512,512]{0,1:T(8,128)S(1)} fusion(f32[512,512]{0,1:T(8,128)S(1)} %convolution_add_fusion.3, bf16[512,512]{1,0:T(8,128)(2,1)} %collective-permute-done.9, bf16[512,4096]{1,0:T(8,128)(2,1)S(1)} %copy-done.4, s32[]{:T(128)S(6)} %select_n.102), kind=kOutput, calls=%fused_computation.5 | convolution fusion | flops 268697600 | bytes 3145732 | tf_op jit(solution)/shard_map/dot_general | solution.py:17
  44.1 1.5 %convolution_add_fusion.6 = f32[512,512]{0,1:T(8,128)S(1)} fusion(f32[512,512]{0,1:T(8,128)S(1)} %convolution_add_fusion.7, bf16[512,512]{1,0:T(8,128)(2,1)} %collective-permute-done.1, bf16[512,4096]{1,0:T(8,128)(2,1)S(1)} %copy-done.4, s32[]{:T(128)S(6)} %select_n.102), kind=kOutput, calls=%fused_computation.12 | convolution fusion | flops 268697600 | bytes 3145732 | tf_op jit(solution)/shard_map/dot_general | solution.py:17
  45.6 1.9 %collective-permute-start.13 = (bf16[512,512]{1,0:T(8,128)(2,1)S(1)}, bf16[512,512]{1,0:T(8,128)(2,1)S(1)}, u32[]{:S(2)}, u32[]{:S(2)}) collective-permute-start(bf16[512,512]{1,0:T(8,128)(2,1)S(1)} %collective-permute-done.11), channel_id=1, source_target_pairs={{0,7},{1,0},{2,1},{3,2},{4,3},{5,4},{6,5},{7,6},{8,15},{9,8},{10,9... | collective-permute-start | bytes 1572872 | tf_op jit(solution)/shard_map/ppermute | solution.py:430
  47.7 7.5 %collective-permute-done.3 = bf16[512,512]{1,0:T(8,128)(2,1)S(1)} collective-permute-done((bf16[512,512]{1,0:T(8,128)(2,1)}, bf16[512,512]{1,0:T(8,128)(2,1)S(1)}, u32[]{:S(2)}, u32[]{:S(2)}) %collective-permute-start.3) | collective-permute-done | bytes 524320 | tf_op jit(solution)/shard_map/ppermute | solution.py:430
  55.3 3.6 %collective-permute-start.5 = (bf16[512,512]{1,0:T(8,128)(2,1)S(1)}, bf16[512,512]{1,0:T(8,128)(2,1)S(1)}, u32[]{:S(2)}, u32[]{:S(2)}) collective-permute-start(bf16[512,512]{1,0:T(8,128)(2,1)S(1)} %collective-permute-done.3), channel_id=1, source_target_pairs={{0,7},{1,0},{2,1},{3,2},{4,3},{5,4},{6,5},{7,6},{8,15},{9,8},{10,9... | collective-permute-start | bytes 1572872 | tf_op jit(solution)/shard_map/ppermute | solution.py:430
  58.8 0.5 fusion.12
  59.4 0.5 fusion.2
  59.9 0.5 fusion.14
  60.4 0.5 fusion.5
  60.9 5.8 %collective-permute-done.12 = bf16[512,512]{1,0:T(8,128)(2,1)S(1)} collective-permute-done((bf16[512,512]{1,0:T(8,128)(2,1)S(1)}, bf16[512,512]{1,0:T(8,128)(2,1)S(1)}, u32[]{:S(2)}, u32[]{:S(2)}) %collective-permute-start.12) | collective-permute-done | bytes 524320 | tf_op jit(solution)/shard_map/ppermute | solution.py:429
  66.9 3.3 %collective-permute-start.15 = (bf16[256,512]{1,0:T(8,128)(2,1)S(1)}, bf16[256,512]{1,0:T(8,128)(2,1)S(1)}, u32[]{:S(2)}, u32[]{:S(2)}) collective-permute-start(bf16[256,512]{1,0:T(8,128)(2,1)S(1)} %slice.44), channel_id=1, source_target_pairs={{0,7},{1,0},{2,1},{3,2},{4,3},{5,4},{6,5},{7,6},{8,15},{9,8},{10,9... | collective-permute-start | bytes 786440 | tf_op jit(solution)/shard_map/ppermute | solution.py:435
  70.2 7.8 %collective-permute-done.4 = bf16[512,512]{1,0:T(8,128)(2,1)S(1)} collective-permute-done((bf16[512,512]{1,0:T(8,128)(2,1)S(1)}, bf16[512,512]{1,0:T(8,128)(2,1)S(1)}, u32[]{:S(2)}, u32[]{:S(2)}) %collective-permute-start.4) | collective-permute-done | bytes 524320 | tf_op jit(solution)/shard_map/ppermute | solution.py:429
  78.1 3.3 %collective-permute-start.7 = (bf16[256,512]{1,0:T(8,128)(2,1)S(1)}, bf16[256,512]{1,0:T(8,128)(2,1)S(1)}, u32[]{:S(2)}, u32[]{:S(2)}) collective-permute-start(bf16[256,512]{1,0:T(8,128)(2,1)S(1)} %slice.42), channel_id=1, source_target_pairs={{0,7},{1,0},{2,1},{3,2},{4,3},{5,4},{6,5},{7,6},{8,15},{9,8},{10,9... | collective-permute-start | bytes 786440 | tf_op jit(solution)/shard_map/ppermute | solution.py:435
  81.4 0.5 fusion.6
  81.9 0.5 fusion.8
  82.4 0.5 fusion.1.refs_1_
  82.9 0.5 fusion.4.refs_1_
  83.6 2.7 %close_chunk.2 = (bf16[512,512]{1,0:T(8,128)(2,1)}, f32[2,4,64,128]{3,2,1,0:T(8,128)}) custom-call(s32[1]{0:T(128)} %bitcast.6.source_ref, f32[5,4]{1,0:T(8,128)S(1)} %pad_maximum_fusion.1.refs_0_, f32[512,512]{1,0:T(8,128)S(1)} %fusion.1.refs_1_, bf16[256,512]{1,0:T(8,128)(2,1)S(1)} %collective-permute-done.14.refs_2_, ...), custom_call_target="tpu_custom_call" | custom-call | flops 600000000 | bytes 4000000 | tf_op jit(solution)/shard_map/close_chunk/pallas_call | solution.py:214
  86.3 2.1 %collective-permute-done.6.refs_2_ = bf16[256,512]{1,0:T(8,128)(2,1)S(1)} collective-permute-done((bf16[256,512]{1,0:T(8,128)(2,1)S(1)}, bf16[256,512]{1,0:T(8,128)(2,1)S(1)}, u32[]{:S(2)}, u32[]{:S(2)}) %collective-permute-start.6) | collective-permute-done | bytes 262176 | tf_op jit(solution)/shard_map/ppermute | solution.py:434
  88.4 2.7 %close_chunk.3 = (bf16[512,512]{1,0:T(8,128)(2,1)}, f32[2,4,64,128]{3,2,1,0:T(8,128)}, bf16[272,128]{1,0:T(8,128)(2,1)S(1)}) custom-call(s32[1]{0:T(128)} %bitcast.6.source_ref, f32[5,4]{1,0:T(8,128)S(1)} %pad_maximum_fusion.1.refs_0_, f32[512,512]{1,0:T(8,128)S(1)} %fusion.4.refs_1_, bf16[256,512]{1,0:T(8,128)(2,1)S(1)} %collective-permute-done.6.refs_2_, ...), custom_call_target="tpu_custom_call" | custom-call | flops 600000000 | bytes 4000000 | tf_op jit(solution)/shard_map/close_chunk/pallas_call | solution.py:214
  91.2 1.2 collective-permute-done.16.refs_1_
  92.4 0.6 combine_core.1.refs_0_.refs_2_
  92.9 1.7 %collective-permute-start.17 = (bf16[272,128]{1,0:T(8,128)(2,1)S(1)}, bf16[272,128]{1,0:T(8,128)(2,1)S(1)}, u32[]{:S(2)}, u32[]{:S(2)}) collective-permute-start(bf16[272,128]{1,0:T(8,128)(2,1)S(1)} %combine_core.1.refs_0_.refs_2_), channel_id=1, source_target_pairs={{0,16},{8,24},{16,32},{24,40},{32,48},{40,56},{48,0},{56,8},{64,80... | collective-permute-start | bytes 208904 | tf_op jit(solution)/shard_map/ppermute | solution.py:414
  94.6 2.9 %collective-permute-start.18 = (bf16[272,128]{1,0:T(8,128)(2,1)S(1)}, bf16[272,128]{1,0:T(8,128)(2,1)S(1)}, u32[]{:S(2)}, u32[]{:S(2)}) collective-permute-start(bf16[272,128]{1,0:T(8,128)(2,1)S(1)} %combine_core.1.refs_0_.refs_2_), channel_id=1, source_target_pairs={{0,32},{8,40},{16,48},{24,56},{32,0},{40,8},{48,16},{56,24},{64,96... | collective-permute-start | bytes 208904 | tf_op jit(solution)/shard_map/ppermute | solution.py:414
  97.5 1.3 %collective-permute-start.19 = (bf16[272,128]{1,0:T(8,128)(2,1)S(1)}, bf16[272,128]{1,0:T(8,128)(2,1)S(1)}, u32[]{:S(2)}, u32[]{:S(2)}) collective-permute-start(bf16[272,128]{1,0:T(8,128)(2,1)S(1)} %combine_core.1.refs_0_.refs_2_), channel_id=1, source_target_pairs={{0,48},{8,56},{16,0},{24,8},{32,16},{40,24},{48,32},{56,40},{64,11... | collective-permute-start | bytes 208904 | tf_op jit(solution)/shard_map/ppermute | solution.py:414
  98.8 5.8 %inside.2 = (f32[1024,512]{1,0:T(8,128)}, f32[1024,512]{1,0:T(8,128)}, f32[4,1,1024]{2,1,0:T(1,128)}) custom-call(f32[1,4]{1,0:T(1,128)S(1)} %bitcast.39, bf16[512,512]{1,0:T(8,128)(2,1)} %get-tuple-element.38.dy_ref, bf16[1024,512]{1,0:T(8,128)(2,1)} %refs_10_.1, bf16[1024,512]{1,0:T(8,128)(2,1)} %refs_11_.1, bf16[1024,512]{1,0:T(8,128)(2,1)} %get-tuple-element.34.sw_ref, ...), custom_call_target="tpu_custom_call" | custom-call | flops 2000000000 | bytes 7000000 | tf_op jit(solution)/shard_map/inside/pallas_call | solution.py:276
  104.7 0.6 combine_row.1.refs_6_
  105.3 1.6 %collective-permute-start.20 = (bf16[272,128]{1,0:T(8,128)(2,1)S(1)}, bf16[272,128]{1,0:T(8,128)(2,1)S(1)}, u32[]{:S(2)}, u32[]{:S(2)}) collective-permute-start(bf16[272,128]{1,0:T(8,128)(2,1)S(1)} %combine_row.1.refs_6_), channel_id=1, source_target_pairs={{0,64},{8,72},{16,80},{24,88},{32,96},{40,104},{48,112},{56,120},{... | collective-permute-start | bytes 208904 | tf_op jit(solution)/shard_map/ppermute | solution.py:417
  106.9 1.1 collective-permute-start.21
  108.0 2.2 %collective-permute-start.22 = (bf16[272,128]{1,0:T(8,128)(2,1)S(1)}, bf16[272,128]{1,0:T(8,128)(2,1)S(1)}, u32[]{:S(2)}, u32[]{:S(2)}) collective-permute-start(bf16[272,128]{1,0:T(8,128)(2,1)S(1)} %combine_row.1.refs_6_), channel_id=1, source_target_pairs={{0,192},{8,200},{16,208},{24,216},{32,224},{40,232},{48,240},{56,2... | collective-permute-start | bytes 208904 | tf_op jit(solution)/shard_map/ppermute | solution.py:417
  110.1 5.6 %inside.3 = (f32[1024,512]{1,0:T(8,128)}, f32[1024,512]{1,0:T(8,128)}, f32[4,1,1024]{2,1,0:T(1,128)}) custom-call(f32[1,4]{1,0:T(1,128)S(1)} %bitcast.40, bf16[512,512]{1,0:T(8,128)(2,1)} %get-tuple-element.33.dy_ref, bf16[1024,512]{1,0:T(8,128)(2,1)} %refs_10_.1, ...), custom_call_target="tpu_custom_call", output_to_operand_aliasing={{0}: (9, {}), {1}: (10, {}), {2}: (11, {})} | custom-call | flops 2000000000 | bytes 7000000 | tf_op jit(solution)/shard_map/inside/pallas_call | solution.py:276
  115.7 6.2 %finish.1 = (bf16[1024,512]{1,0:T(8,128)(2,1)}, f32[1024,512]{1,0:T(8,128)}, f32[4,1024]{1,0:T(4,128)}) custom-call(s32[3]{0:T(128)S(1)} %pad_add_fusion.place_ref, f32[4,4]{1,0:T(4,128)S(1)} %bitcast.38, bf16[272,128]{1,0:T(8,128)(2,1)S(1)} %get-tuple-element.27.refs_0_, bf16[272,128]{1,0:T(8,128)(2,1)S(1)} %collective-permute-done.16.refs_1_, ...), custom_call_target="tpu_custom_call" | custom-call | flops 600000000 | bytes 11000000 | tf_op jit(solution)/shard_map/finish/pallas_call | solution.py:362
  (51 shorter events, 1.6 us)
Async XLA Ops:
  0.6 13.3 %copy-start.5 = (bf16[1024,512]{1,0:T(8,128)(2,1)S(1)}, bf16[1024,512]{1,0:T(8,128)(2,1)}, u32[]{:S(2)}) copy-start(bf16[1024,512]{1,0:T(8,128)(2,1)} %param.7) | copy-start | bytes 3145732
  3.0 18.9 %collective-permute-start.8 = (bf16[512,512]{1,0:T(8,128)(2,1)}, bf16[512,512]{1,0:T(8,128)(2,1)}, u32[]{:S(2)}, u32[]{:S(2)}) collective-permute-start(bf16[512,512]{1,0:T(8,128)(2,1)} %get-tuple-element.45), channel_id=1, source_target_pairs={{0,1},{1,2},{2,3},{3,4},{4,5},{5,6},{6,7},{7,0},{8,9},{9,10},{10,1... | collective-permute-start | bytes 1572872 | tf_op jit(solution)/shard_map/ppermute | solution.py:429
  4.9 17.0 %collective-permute-start.9 = (bf16[512,512]{1,0:T(8,128)(2,1)}, bf16[512,512]{1,0:T(8,128)(2,1)}, u32[]{:S(2)}, u32[]{:S(2)}) collective-permute-start(bf16[512,512]{1,0:T(8,128)(2,1)} %get-tuple-element.45), channel_id=1, source_target_pairs={{0,7},{1,0},{2,1},{3,2},{4,3},{5,4},{6,5},{7,6},{8,15},{9,8},{10,9... | collective-permute-start | bytes 1572872 | tf_op jit(solution)/shard_map/ppermute | solution.py:430
  8.8 24.2 %collective-permute-start = (bf16[512,512]{1,0:T(8,128)(2,1)}, bf16[512,512]{1,0:T(8,128)(2,1)S(1)}, u32[]{:S(2)}, u32[]{:S(2)}) collective-permute-start(bf16[512,512]{1,0:T(8,128)(2,1)} %get-tuple-element.46), channel_id=1, source_target_pairs={{0,1},{1,2},{2,3},{3,4},{4,5},{5,6},{6,7},{7,0},{8,9},{9,10},{10,1... | collective-permute-start | bytes 1572872 | tf_op jit(solution)/shard_map/ppermute | solution.py:429
  8.8 30.4 %collective-permute-start.1 = (bf16[512,512]{1,0:T(8,128)(2,1)}, bf16[512,512]{1,0:T(8,128)(2,1)}, u32[]{:S(2)}, u32[]{:S(2)}) collective-permute-start(bf16[512,512]{1,0:T(8,128)(2,1)} %get-tuple-element.46), channel_id=1, source_target_pairs={{0,7},{1,0},{2,1},{3,2},{4,3},{5,4},{6,5},{7,6},{8,15},{9,8},{10,9... | collective-permute-start | bytes 1572872 | tf_op jit(solution)/shard_map/ppermute | solution.py:430
  13.8 2.4 %copy-start.4 = (bf16[512,4096]{1,0:T(8,128)(2,1)S(1)}, bf16[512,4096]{1,0:T(8,128)(2,1)}, u32[]{:S(2)}) copy-start(bf16[512,4096]{1,0:T(8,128)(2,1)} %refs_4_.3) | copy-start | bytes 12582916
  16.2 18.9 %copy-start = (bf16[1024,512]{1,0:T(8,128)(2,1)S(1)}, bf16[1024,512]{1,0:T(8,128)(2,1)}, u32[]{:S(2)}) copy-start(bf16[1024,512]{1,0:T(8,128)(2,1)} %refs_11_.1) | copy-start | bytes 3145732
  16.2 18.9 %copy-start.2 = (f32[4,4,64,128]{3,2,1,0:T(8,128)S(1)}, f32[4,4,64,128]{3,2,1,0:T(8,128)}, u32[]{:S(2)}) copy-start(f32[4,4,64,128]{3,2,1,0:T(8,128)} %refs_15_.1) | copy-start | bytes 1572868
  21.9 25.6 %collective-permute-start.10 = (bf16[512,512]{1,0:T(8,128)(2,1)}, bf16[512,512]{1,0:T(8,128)(2,1)S(1)}, u32[]{:S(2)}, u32[]{:S(2)}) collective-permute-start(bf16[512,512]{1,0:T(8,128)(2,1)} %collective-permute-done.8), channel_id=1, source_target_pairs={{0,1},{1,2},{2,3},{3,4},{4,5},{5,6},{6,7},{7,0},{8,9},{9,10},{10,1... | collective-permute-start | bytes 1572872 | tf_op jit(solution)/shard_map/ppermute | solution.py:429
  21.9 23.7 %collective-permute-start.11 = (bf16[512,512]{1,0:T(8,128)(2,1)}, bf16[512,512]{1,0:T(8,128)(2,1)S(1)}, u32[]{:S(2)}, u32[]{:S(2)}) collective-permute-start(bf16[512,512]{1,0:T(8,128)(2,1)} %collective-permute-done.9), channel_id=1, source_target_pairs={{0,7},{1,0},{2,1},{3,2},{4,3},{5,4},{6,5},{7,6},{8,15},{9,8},{10,9... | collective-permute-start | bytes 1572872 | tf_op jit(solution)/shard_map/ppermute | solution.py:430
  33.0 26.3 %collective-permute-start.2 = (bf16[512,512]{1,0:T(8,128)(2,1)S(1)}, bf16[512,512]{1,0:T(8,128)(2,1)S(1)}, u32[]{:S(2)}, u32[]{:S(2)}) collective-permute-start(bf16[512,512]{1,0:T(8,128)(2,1)S(1)} %collective-permute-done), channel_id=1, source_target_pairs={{0,1},{1,2},{2,3},{3,4},{4,5},{5,6},{6,7},{7,0},{8,9},{9,10},{10,1... | collective-permute-start | bytes 1572872 | tf_op jit(solution)/shard_map/ppermute | solution.py:429
  39.2 16.0 %collective-permute-start.3 = (bf16[512,512]{1,0:T(8,128)(2,1)}, bf16[512,512]{1,0:T(8,128)(2,1)S(1)}, u32[]{:S(2)}, u32[]{:S(2)}) collective-permute-start(bf16[512,512]{1,0:T(8,128)(2,1)} %collective-permute-done.1), channel_id=1, source_target_pairs={{0,7},{1,0},{2,1},{3,2},{4,3},{5,4},{6,5},{7,6},{8,15},{9,8},{10,9... | collective-permute-start | bytes 1572872 | tf_op jit(solution)/shard_map/ppermute | solution.py:430
  45.6 21.2 %collective-permute-start.13 = (bf16[512,512]{1,0:T(8,128)(2,1)S(1)}, bf16[512,512]{1,0:T(8,128)(2,1)S(1)}, u32[]{:S(2)}, u32[]{:S(2)}) collective-permute-start(bf16[512,512]{1,0:T(8,128)(2,1)S(1)} %collective-permute-done.11), channel_id=1, source_target_pairs={{0,7},{1,0},{2,1},{3,2},{4,3},{5,4},{6,5},{7,6},{8,15},{9,8},{10,9... | collective-permute-start | bytes 1572872 | tf_op jit(solution)/shard_map/ppermute | solution.py:430
  47.5 19.2 %collective-permute-start.12 = (bf16[512,512]{1,0:T(8,128)(2,1)S(1)}, bf16[512,512]{1,0:T(8,128)(2,1)S(1)}, u32[]{:S(2)}, u32[]{:S(2)}) collective-permute-start(bf16[512,512]{1,0:T(8,128)(2,1)S(1)} %collective-permute-done.10), channel_id=1, source_target_pairs={{0,1},{1,2},{2,3},{3,4},{4,5},{5,6},{6,7},{7,0},{8,9},{9,10},{10,1... | collective-permute-start | bytes 1572872 | tf_op jit(solution)/shard_map/ppermute | solution.py:429
  55.3 22.8 %collective-permute-start.5 = (bf16[512,512]{1,0:T(8,128)(2,1)S(1)}, bf16[512,512]{1,0:T(8,128)(2,1)S(1)}, u32[]{:S(2)}, u32[]{:S(2)}) collective-permute-start(bf16[512,512]{1,0:T(8,128)(2,1)S(1)} %collective-permute-done.3), channel_id=1, source_target_pairs={{0,7},{1,0},{2,1},{3,2},{4,3},{5,4},{6,5},{7,6},{8,15},{9,8},{10,9... | collective-permute-start | bytes 1572872 | tf_op jit(solution)/shard_map/ppermute | solution.py:430
  59.3 18.6 %collective-permute-start.4 = (bf16[512,512]{1,0:T(8,128)(2,1)S(1)}, bf16[512,512]{1,0:T(8,128)(2,1)S(1)}, u32[]{:S(2)}, u32[]{:S(2)}) collective-permute-start(bf16[512,512]{1,0:T(8,128)(2,1)S(1)} %collective-permute-done.2), channel_id=1, source_target_pairs={{0,1},{1,2},{2,3},{3,4},{4,5},{5,6},{6,7},{7,0},{8,9},{9,10},{10,1... | collective-permute-start | bytes 1572872 | tf_op jit(solution)/shard_map/ppermute | solution.py:429
  66.7 16.8 %collective-permute-start.14 = (bf16[256,512]{1,0:T(8,128)(2,1)S(1)}, bf16[256,512]{1,0:T(8,128)(2,1)S(1)}, u32[]{:S(2)}, u32[]{:S(2)}) collective-permute-start(bf16[256,512]{1,0:T(8,128)(2,1)S(1)} %slice.43), channel_id=1, source_target_pairs={{0,1},{1,2},{2,3},{3,4},{4,5},{5,6},{6,7},{7,0},{8,9},{9,10},{10,1... | collective-permute-start | bytes 786440 | tf_op jit(solution)/shard_map/ppermute | solution.py:434
  66.9 16.7 %collective-permute-start.15 = (bf16[256,512]{1,0:T(8,128)(2,1)S(1)}, bf16[256,512]{1,0:T(8,128)(2,1)S(1)}, u32[]{:S(2)}, u32[]{:S(2)}) collective-permute-start(bf16[256,512]{1,0:T(8,128)(2,1)S(1)} %slice.44), channel_id=1, source_target_pairs={{0,7},{1,0},{2,1},{3,2},{4,3},{5,4},{6,5},{7,6},{8,15},{9,8},{10,9... | collective-permute-start | bytes 786440 | tf_op jit(solution)/shard_map/ppermute | solution.py:435
  78.0 10.4 %collective-permute-start.6 = (bf16[256,512]{1,0:T(8,128)(2,1)S(1)}, bf16[256,512]{1,0:T(8,128)(2,1)S(1)}, u32[]{:S(2)}, u32[]{:S(2)}) collective-permute-start(bf16[256,512]{1,0:T(8,128)(2,1)S(1)} %slice.41), channel_id=1, source_target_pairs={{0,1},{1,2},{2,3},{3,4},{4,5},{5,6},{6,7},{7,0},{8,9},{9,10},{10,1... | collective-permute-start | bytes 786440 | tf_op jit(solution)/shard_map/ppermute | solution.py:434
  78.1 10.3 %collective-permute-start.7 = (bf16[256,512]{1,0:T(8,128)(2,1)S(1)}, bf16[256,512]{1,0:T(8,128)(2,1)S(1)}, u32[]{:S(2)}, u32[]{:S(2)}) collective-permute-start(bf16[256,512]{1,0:T(8,128)(2,1)S(1)} %slice.42), channel_id=1, source_target_pairs={{0,7},{1,0},{2,1},{3,2},{4,3},{5,4},{6,5},{7,6},{8,15},{9,8},{10,9... | collective-permute-start | bytes 786440 | tf_op jit(solution)/shard_map/ppermute | solution.py:435
  82.4 1.2 copy-start.1
  86.3 12.6 %copy-start.3 = (f32[4]{0:T(128)S(1)}, f32[4]{0:T(128)}, u32[]{:S(2)}) copy-start(f32[4]{0:T(128)} %param.13) | copy-start | bytes 52
  91.1 1.3 %collective-permute-start.16 = (bf16[272,128]{1,0:T(8,128)(2,1)S(1)}, bf16[272,128]{1,0:T(8,128)(2,1)S(1)}, u32[]{:S(2)}, u32[]{:S(2)}) collective-permute-start(bf16[272,128]{1,0:T(8,128)(2,1)S(1)} %get-tuple-element.27.refs_0_), channel_id=1, source_target_pairs={{0,8},{8,0},{16,24},{24,16},{32,40},{40,32},{48,56},{56,48},{64,72... | collective-permute-start | bytes 208904 | tf_op jit(solution)/shard_map/ppermute | solution.py:411
  92.9 11.7 %collective-permute-start.17 = (bf16[272,128]{1,0:T(8,128)(2,1)S(1)}, bf16[272,128]{1,0:T(8,128)(2,1)S(1)}, u32[]{:S(2)}, u32[]{:S(2)}) collective-permute-start(bf16[272,128]{1,0:T(8,128)(2,1)S(1)} %combine_core.1.refs_0_.refs_2_), channel_id=1, source_target_pairs={{0,16},{8,24},{16,32},{24,40},{32,48},{40,56},{48,0},{56,8},{64,80... | collective-permute-start | bytes 208904 | tf_op jit(solution)/shard_map/ppermute | solution.py:414
  94.6 10.0 %collective-permute-start.18 = (bf16[272,128]{1,0:T(8,128)(2,1)S(1)}, bf16[272,128]{1,0:T(8,128)(2,1)S(1)}, u32[]{:S(2)}, u32[]{:S(2)}) collective-permute-start(bf16[272,128]{1,0:T(8,128)(2,1)S(1)} %combine_core.1.refs_0_.refs_2_), channel_id=1, source_target_pairs={{0,32},{8,40},{16,48},{24,56},{32,0},{40,8},{48,16},{56,24},{64,96... | collective-permute-start | bytes 208904 | tf_op jit(solution)/shard_map/ppermute | solution.py:414
  97.5 7.1 %collective-permute-start.19 = (bf16[272,128]{1,0:T(8,128)(2,1)S(1)}, bf16[272,128]{1,0:T(8,128)(2,1)S(1)}, u32[]{:S(2)}, u32[]{:S(2)}) collective-permute-start(bf16[272,128]{1,0:T(8,128)(2,1)S(1)} %combine_core.1.refs_0_.refs_2_), channel_id=1, source_target_pairs={{0,48},{8,56},{16,0},{24,8},{32,16},{40,24},{48,32},{56,40},{64,11... | collective-permute-start | bytes 208904 | tf_op jit(solution)/shard_map/ppermute | solution.py:414
  105.3 10.4 %collective-permute-start.20 = (bf16[272,128]{1,0:T(8,128)(2,1)S(1)}, bf16[272,128]{1,0:T(8,128)(2,1)S(1)}, u32[]{:S(2)}, u32[]{:S(2)}) collective-permute-start(bf16[272,128]{1,0:T(8,128)(2,1)S(1)} %combine_row.1.refs_6_), channel_id=1, source_target_pairs={{0,64},{8,72},{16,80},{24,88},{32,96},{40,104},{48,112},{56,120},{... | collective-permute-start | bytes 208904 | tf_op jit(solution)/shard_map/ppermute | solution.py:417
  106.9 8.9 %collective-permute-start.21 = (bf16[272,128]{1,0:T(8,128)(2,1)S(1)}, bf16[272,128]{1,0:T(8,128)(2,1)S(1)}, u32[]{:S(2)}, u32[]{:S(2)}) collective-permute-start(bf16[272,128]{1,0:T(8,128)(2,1)S(1)} %combine_row.1.refs_6_), channel_id=1, source_target_pairs={{0,128},{8,136},{16,144},{24,152},{32,160},{40,168},{48,176},{56,1... | collective-permute-start | bytes 208904 | tf_op jit(solution)/shard_map/ppermute | solution.py:417
  108.0 7.7 %collective-permute-start.22 = (bf16[272,128]{1,0:T(8,128)(2,1)S(1)}, bf16[272,128]{1,0:T(8,128)(2,1)S(1)}, u32[]{:S(2)}, u32[]{:S(2)}) collective-permute-start(bf16[272,128]{1,0:T(8,128)(2,1)S(1)} %combine_row.1.refs_6_), channel_id=1, source_target_pairs={{0,192},{8,200},{16,208},{24,216},{32,224},{40,232},{48,240},{56,2... | collective-permute-start | bytes 208904 | tf_op jit(solution)/shard_map/ppermute | solution.py:417

commit v5 on v4

--- a/solution.py
+++ b/solution.py
@@ -10,7 +10,7 @@
 BLOCK = 256
 F32 = jnp.float32
 BF16 = jnp.bfloat16
-VMEM_LIMIT = 48 << 20
+VMEM_LIMIT = 40 << 20
 
 
 def dot(a, b, dims):
@@ -161,17 +161,22 @@
     )(bc, arow, aline, states)
 
 
+def resident():
+    return pl.BlockSpec(memory_space=pltpu.VMEM)
+
+
 def close_chunk(first, source, acc, up, down, weight, wct, scale, earlier):
     tokens, width = acc.shape
     heads = width // HEAD_DIM
+    feats = up.shape[1]
     last = earlier is not None
 
-    def body(source_ref, *refs):
-        scale_ref, acc_ref, up_ref, down_ref, weight_ref, wct_ref = refs[:6]
+    def body(source_ref, scale_ref, acc_ref, up_ref, down_ref, weight_ref, wct_ref, *refs):
         if last:
-            earlier_ref, dy_ref, terms_ref, part_ref = refs[6:]
+            earlier_ref, dy_ref, terms_ref, part_ref = refs
         else:
-            dy_ref, terms_ref = refs[6:]
+            dy_ref, terms_ref = refs
+        weights = weight_ref[:, pl.ds(pl.multiple_of(source_ref[0] * feats, feats), feats)]
         sums = [jnp.zeros((STATE, HEAD_DIM), F32) for _ in range(heads)]
         if last:
             for b in range(2):
@@ -179,10 +184,10 @@
                     sums[h] = sums[h] + scale_ref[b, h] * earlier_ref[b, h]
         for b, piece in enumerate((up_ref, down_ref)):
             rows = slice(b * BLOCK, (b + 1) * BLOCK)
-            dy = (acc_ref[rows, :] + dot(piece[...], weight_ref[...], NT)).astype(BF16)
+            dy = (acc_ref[rows, :] + dot(piece[...], weights, NT)).astype(BF16)
             dy_ref[rows, :] = dy
             for h in range(heads):
-                term = dot(wct_ref[b, h], dy[:, h * HEAD_DIM : (h + 1) * HEAD_DIM], NN)
+                term = dot(wct_ref[first + b, h], dy[:, h * HEAD_DIM : (h + 1) * HEAD_DIM], NN)
                 terms_ref[b, h] = term
                 if last:
                     sums[h] = sums[h] + scale_ref[b + first, h] * term
@@ -191,117 +196,99 @@
                 part_ref, sums, [jnp.full((1, HEAD_DIM), scale_ref[4, h], F32) for h in range(heads)]
             )
 
-    def whole(*dims):
-        return pl.BlockSpec(dims, lambda i, source: (0,) * len(dims))
-
-    terms_shape = (2, heads, STATE, HEAD_DIM)
-    out_shape = [pltpu.HBM((tokens, width), BF16), pltpu.HBM(terms_shape, F32)]
-    out_specs = [whole(tokens, width), whole(*terms_shape)]
-    in_specs = [
-        pl.BlockSpec(memory_space=pltpu.SMEM),
-        whole(tokens, width),
-        whole(*up.shape),
-        whole(*down.shape),
-        pl.BlockSpec((width, up.shape[1]), lambda i, source: (0, source[0])),
-        pl.BlockSpec((2, heads, STATE, BLOCK), lambda i, source: (first // 2, 0, 0, 0)),
+    smem = pl.BlockSpec(memory_space=pltpu.SMEM)
+    out_shape = [
+        jax.ShapeDtypeStruct((tokens, width), BF16),
+        jax.ShapeDtypeStruct((2, heads, STATE, HEAD_DIM), F32),
     ]
-    operands = [scale, acc, up, down, weight, wct]
+    operands = [source, scale, acc, up, down, weight, wct]
     if last:
         out_shape.append(jax.ShapeDtypeStruct((heads * STATE + 16, HEAD_DIM), BF16))
-        out_specs.append(whole(heads * STATE + 16, HEAD_DIM))
-        in_specs.append(whole(*terms_shape))
-        operands.extend(in_hbm(earlier))
+        operands.append(earlier)
     return pl.pallas_call(
         body,
         name="close_chunk",
-        grid_spec=pltpu.PrefetchScalarGridSpec(
-            num_scalar_prefetch=1, grid=(1,), in_specs=in_specs, out_specs=out_specs
-        ),
+        in_specs=[smem, smem] + [resident()] * (len(operands) - 2),
+        out_specs=[resident()] * len(out_shape),
         out_shape=out_shape,
         cost_estimate=pl.CostEstimate(flops=600_000_000, bytes_accessed=4_000_000, transcendentals=0),
         compiler_params=pltpu.CompilerParams(vmem_limit_bytes=VMEM_LIMIT),
-    )(source, *operands)
-
-
-def inside(first, count, dy_first, dy, skip, x, bc, sw, aline, dec, sct, spad, before):
-    tokens, width = x.shape
+    )(*operands)
+
+
+def inside(first, count, dy_first, dy, skip, x, bc, sw, rise, dec, sct, spad):
+    width = x.shape[1]
     heads = width // HEAD_DIM
-    group = heads // 2
-
-    def body(skip_ref, dy_ref, x_ref, bc_ref, sw_ref, aline_ref, dec_ref, sct_ref, spad_ref, *rest):
-        dx_ref, dbc_ref, dlog_ref = rest[-3:]
-        base = pl.program_id(1) * group
+
+    def body(skip_ref, dy_ref, x_ref, bc_ref, sw_ref, rise_ref, dec_ref, sct_ref, spad_ref, dx_ref, dbc_ref, dlog_ref):
+        b = pl.program_id(0)
+        here = pl.ds(pl.multiple_of((b + dy_first) * BLOCK, BLOCK), BLOCK)
+        there = pl.ds(pl.multiple_of(b * BLOCK, BLOCK), BLOCK)
         rows = lax.broadcasted_iota(jnp.int32, (BLOCK, BLOCK), 0)
         cols = lax.broadcasted_iota(jnp.int32, (BLOCK, BLOCK), 1)
         low = low_lanes((BLOCK, HEAD_DIM))
-        for h in range(group):
+        for h in range(heads):
             lanes = slice(h * HEAD_DIM, (h + 1) * HEAD_DIM)
-            dy_h = dy_ref[:, lanes]
+            dy_h = dy_ref[here, lanes]
             x_h = x_ref[:, lanes]
             bc_h = bc_ref[:, lanes]
             sw_h = sw_ref[:, lanes]
             zero = jnp.zeros_like(sw_h)
             gaps = dot(dy_h, x_h, NT)
             mixed = (gaps * dec_ref[0, h].astype(F32)).astype(BF16)
-            dx_ref[:, lanes] = dot(sct_ref[0, h], dy_h, NN) + skip_ref[0, base + h] * dy_h.astype(F32)
+            dx_ref[there, lanes] = dot(sct_ref[0, h], dy_h, NN) + skip_ref[0, h] * dy_h.astype(F32)
             grad = dot(mixed, jnp.where(low, zero, sw_h), NN)
             grad = grad + dot(mixed, jnp.where(low, sw_h, zero), TN)
-            grad = grad + jnp.exp(aline_ref[0][:, h : h + 1]) * dot(dy_h, spad_ref[0, h], NT)
-            dbc_ref[:, lanes] = grad
+            grad = grad + rise_ref[:, h : h + 1] * dot(dy_h, spad_ref[0, h], NT)
+            dbc_ref[there, lanes] = grad
             signed = grad * bc_h.astype(F32)
             moved = jnp.sum(jnp.where(low, -signed, signed), axis=1, keepdims=True)
-            dlog_ref[h] = jnp.sum(jnp.where(rows >= cols, moved, 0.0), axis=0, keepdims=True)
-
-    wide = pl.BlockSpec((BLOCK, group * HEAD_DIM), lambda b, g: (b + first, g))
-    square = pl.BlockSpec((1, group, BLOCK, BLOCK), lambda b, g: (b + first, g, 0, 0))
-    in_specs = [
-        pl.BlockSpec(memory_space=pltpu.SMEM),
-        pl.BlockSpec((BLOCK, group * HEAD_DIM), lambda b, g: (b + dy_first, g)),
-        wide,
-        wide,
-        wide,
-        pl.BlockSpec((1, BLOCK, group), lambda b, g: (g, b + first, 0)),
-        square,
-        square,
-        pl.BlockSpec((1, group, HEAD_DIM, HEAD_DIM), lambda b, g: (b + first, g, 0, 0)),
-    ]
-    dy, x, bc, sw, dec, sct, spad = in_hbm(dy, x, bc, sw, dec, sct, spad)
-    operands = [skip, dy, x, bc, sw, aline, dec, sct, spad]
-    aliases = {}
-    if before is not None:
-        for place, array in enumerate(in_hbm(*before)):
-            aliases[len(operands)] = place
-            operands.append(array)
-            in_specs.append(pl.BlockSpec(memory_space=pl.ANY))
+            dlog_ref[b, h : h + 1, :] = jnp.sum(jnp.where(rows >= cols, moved, 0.0), axis=0, keepdims=True)
+
+    wide = pl.BlockSpec((BLOCK, width), lambda b: (b + first, 0))
+    square = pl.BlockSpec((1, heads, BLOCK, BLOCK), lambda b: (b + first, 0, 0, 0))
+    x, bc, sw, dec, sct, spad = in_hbm(x, bc, sw, dec, sct, spad)
     return pl.pallas_call(
         body,
         name="inside",
-        grid=(count, 2),
-        in_specs=in_specs,
-        out_specs=[wide, wide, pl.BlockSpec((group, 1, BLOCK), lambda b, g: (g, 0, b + first))],
+        grid=(count,),
+        in_specs=[
+            pl.BlockSpec(memory_space=pltpu.SMEM),
+            resident(),
+            wide,
+            wide,
+            wide,
+            pl.BlockSpec((BLOCK, heads), lambda b: (b + first, 0)),
+            square,
+            square,
+            pl.BlockSpec((1, heads, HEAD_DIM, HEAD_DIM), lambda b: (b + first, 0, 0, 0)),
+        ],
+        out_specs=[resident()] * 3,
         out_shape=[
-            pltpu.HBM((tokens, width), F32),
-            pltpu.HBM((tokens, width), F32),
-            pltpu.HBM((heads, 1, tokens), F32),
-        ],
-        input_output_aliases=aliases,
+            jax.ShapeDtypeStruct((count * BLOCK, width), F32),
+            jax.ShapeDtypeStruct((count * BLOCK, width), F32),
+            jax.ShapeDtypeStruct((count, heads, BLOCK), F32),
+        ],
         cost_estimate=pl.CostEstimate(
             flops=1_000_000_000 * count, bytes_accessed=3_500_000 * count, transcendentals=0
         ),
         compiler_params=pltpu.CompilerParams(vmem_limit_bytes=VMEM_LIMIT),
-    )(*operands)
-
-
-def finish(place, a_last, received, x, bc, aline, terms, states, dx, dbc, dlog):
+    )(skip, dy, x, bc, sw, rise, dec, sct, spad)
+
+
+def finish(place, a_last, received, x, bc, fall, terms, states, grads):
     tokens, width = x.shape
     heads = width // HEAD_DIM
     blocks = tokens // BLOCK
     count = len(received)
+    starts = [first for first, *_ in grads] + [blocks]
+    flat = [array for _, *arrays in grads for array in arrays]
 
     def body(place_ref, last_ref, *refs):
         got = refs[:count]
-        (x_ref, bc_ref, aline_ref, terms0_ref, terms1_ref, states_ref, dx_ref, dbc_ref, dlog_ref, out_ref,
-         outbc_ref, outlog_ref, carry_ref) = refs[count:]
+        x_ref, bc_ref, fall_ref, terms0_ref, terms1_ref, states_ref = refs[count : count + 6]
+        grad_refs = refs[count + 6 : -4]
+        out_ref, outbc_ref, outlog_ref, carry_ref = refs[-4:]
         step = pl.program_id(0)
         b = blocks - 1 - step
 
@@ -332,50 +319,55 @@
 
         rows = lax.broadcasted_iota(jnp.int32, (BLOCK, BLOCK), 0)
         cols = lax.broadcasted_iota(jnp.int32, (BLOCK, BLOCK), 1)
-        late = step < blocks // 2
-        for h in range(heads):
-            lanes = slice(h * HEAD_DIM, (h + 1) * HEAD_DIM)
-            carry = carry_ref[h]
-            carry16 = carry.astype(BF16)
-            last = last_ref[b, h]
-            tail = jnp.exp(last - aline_ref[:, h : h + 1])
-            bc_h = bc_ref[:, lanes].astype(F32)
-            weighted = (bc_h * tail).astype(BF16)[:, :STATE]
-            out_ref[:, lanes] = (dx_ref[:, lanes] + dot(weighted, carry16, NN)).astype(BF16)
-            padded = jnp.concatenate([carry16, jnp.zeros_like(carry16)], axis=0)
-            extra = tail * dot(x_ref[:, lanes], padded, NT)
-            outbc_ref[:, lanes] = dbc_ref[:, lanes] + extra
-            moved = jnp.sum(extra * bc_h, axis=1, keepdims=True)
-            ends = jnp.exp(jnp.full((1, HEAD_DIM), last, F32))
-            whole = jnp.sum(jnp.sum(states_ref[0, h] * carry, axis=0, keepdims=True) * ends)
-            outlog_ref[h : h + 1, :] = (
-                dlog_ref[h] + jnp.sum(jnp.where(rows < cols, moved, 0.0), axis=0, keepdims=True) + whole
-            )
-            carry_ref[h] = ends * carry + jnp.where(late, terms1_ref[0, h], terms0_ref[0, h])
-
-    x, bc, states, dx, dbc, dlog = in_hbm(x, bc, states, dx, dbc, dlog)
-    terms = in_hbm(*terms)
+
+        def run(first, dx_ref, dbc_ref, dlog_ref):
+            here = pl.ds(pl.multiple_of((b - first) * BLOCK, BLOCK), BLOCK)
+            terms_ref = terms0_ref if first < 2 else terms1_ref
+            for h in range(heads):
+                lanes = slice(h * HEAD_DIM, (h + 1) * HEAD_DIM)
+                carry = carry_ref[h]
+                carry16 = carry.astype(BF16)
+                tail = fall_ref[:, h : h + 1]
+                bc_h = bc_ref[:, lanes].astype(F32)
+                weighted = (bc_h * tail).astype(BF16)[:, :STATE]
+                out_ref[:, lanes] = (dx_ref[here, lanes] + dot(weighted, carry16, NN)).astype(BF16)
+                padded = jnp.concatenate([carry16, jnp.zeros_like(carry16)], axis=0)
+                extra = tail * dot(x_ref[:, lanes], padded, NT)
+                outbc_ref[:, lanes] = dbc_ref[here, lanes] + extra
+                moved = jnp.sum(extra * bc_h, axis=1, keepdims=True)
+                ends = jnp.exp(jnp.full((1, HEAD_DIM), last_ref[b, h], F32))
+                whole = jnp.sum(jnp.sum(states_ref[0, h] * carry, axis=0, keepdims=True) * ends)
+                outlog_ref[h : h + 1, :] = (
+                    dlog_ref[b - first, h : h + 1, :]
+                    + jnp.sum(jnp.where(rows < cols, moved, 0.0), axis=0, keepdims=True)
+                    + whole
+                )
+                carry_ref[h] = ends * carry + terms_ref[b % 2, h]
+
+        for k in range(len(grads)):
+
+            @pl.when((b >= starts[k]) & (b < starts[k + 1]))
+            def _(k=k):
+                run(starts[k], *grad_refs[3 * k : 3 * k + 3])
+
+    x, bc, states = in_hbm(x, bc, states)
     wide = pl.BlockSpec((BLOCK, width), lambda i: (blocks - 1 - i, 0))
     smem = pl.BlockSpec(memory_space=pltpu.SMEM)
-    state_block = (1, heads, STATE, HEAD_DIM)
-    half = blocks // 2
     return pl.pallas_call(
         body,
         name="finish",
         grid=(blocks,),
         in_specs=[smem, smem]
-        + [pl.BlockSpec(message.shape, lambda i: (0, 0)) for message in received]
+        + [resident()] * count
         + [
             wide,
             wide,
             pl.BlockSpec((BLOCK, heads), lambda i: (blocks - 1 - i, 0)),
-            pl.BlockSpec(state_block, lambda i: (jnp.clip(blocks - 1 - i, 0, half - 1), 0, 0, 0)),
-            pl.BlockSpec(state_block, lambda i: (jnp.clip(half - 1 - i, 0, half - 1), 0, 0, 0)),
-            pl.BlockSpec(state_block, lambda i: (blocks - 1 - i, 0, 0, 0)),
-            wide,
-            wide,
-            pl.BlockSpec((heads, 1, BLOCK), lambda i: (0, 0, blocks - 1 - i)),
-        ],
+            resident(),
+            resident(),
+            pl.BlockSpec((1, heads, STATE, HEAD_DIM), lambda i: (blocks - 1 - i, 0, 0, 0)),
+        ]
+        + [resident()] * len(flat),
         out_specs=[wide, wide, pl.BlockSpec((heads, BLOCK), lambda i: (0, blocks - 1 - i))],
         out_shape=[
             jax.ShapeDtypeStruct((tokens, width), BF16),
@@ -385,7 +377,7 @@
         scratch_shapes=[pltpu.VMEM((heads, STATE, HEAD_DIM), F32)],
         cost_estimate=pl.CostEstimate(flops=600_000_000, bytes_accessed=11_000_000, transcendentals=0),
         compiler_params=pltpu.CompilerParams(vmem_limit_bytes=VMEM_LIMIT),
-    )(place, a_last, *received, x, bc, aline, terms[0], terms[1], states, dx, dbc, dlog)
+    )(place, a_last, *received, x, bc, fall, terms[0], terms[1], states, *flat)
 
 
 def shift(count, by):
@@ -449,28 +441,31 @@
     place = jnp.stack([px, py, pc]).astype(jnp.int32)
 
     skips = skip[None]
-    aline2 = jnp.stack([aline[:, : heads // 2], aline[:, heads // 2 :]])
-
-    def within(first, count, dy_first, dy, before):
-        return inside(
-            first, count, dy_first, dy, skips, inner_act, head_bc, sw, aline2, dec, sct, spad, before
-        )
+    rise = jnp.exp(aline)
+    fall = jnp.exp((cum[:, :, -1:] - cum).reshape(heads, tokens).T)
+
+    def within(first, count, dy_first, dy):
+        grads = inside(first, count, dy_first, dy, skips, inner_act, head_bc, sw, rise, dec, sct, spad)
+        return (first, *grads)
 
     source = ((me + tp // 2) % tp).astype(jnp.int32)[None]
     dy0, terms0 = close_chunk(0, source, accs[0], *lasts[0], out_weight, wct, scale, None)
+    grads0 = within(0, 1, 0, dy0)
+    terms0, last_grad, fall = lax.optimization_barrier((terms0, grads0[3], fall))
+    grads0 = grads0[:3] + (last_grad,)
     dy1, terms1, part = close_chunk(2, source, accs[1], *lasts[1], out_weight, wct, scale, terms0)
-
     other = from_core(part)
     chip = combine("core", place, [part, other])
     ys = [chip] + from_y(chip)
     dy0, ys[0] = lax.optimization_barrier((dy0, ys[0]))
-    grads = within(0, 2, 0, dy0, None)
+    grads1 = within(1, 1, 1, dy0)
     row = combine("row", place, ys)
     xs = [row] + from_x(row)
     dy1, xs[0] = lax.optimization_barrier((dy1, xs[0]))
-    dx, dbc, dlog = within(2, 2, 0, dy1, grads)
+    grads2 = within(2, 2, 0, dy1)
     return finish(
-        place, last, [part, other] + ys + xs, inner_act, head_bc, aline, (terms0, terms1), states, dx, dbc, dlog
+        place, last, [part, other] + ys + xs, inner_act, head_bc, fall, (terms0, terms1), states,
+        [grads0, grads1, grads2],
     )
 
 

time: 124 us -> 120 us (0.968); the launches traced: 122 us -> 120 us
  Pallas kernels: 28.4 us -> 23.8 us
  waiting for transfers between devices: 37.7 us -> 40.5 us
  matrix products: 11.1 us -> 12.4 us
    pallas_call x4 -> x5, Pallas kernels: 16.8 us -> 12.9 us  [the longest x3 9.97 us: inside(): pl.pallas_call(body, name='inside', grid=(count,), in_specs=[pl.BlockSpec...]
    ppermute x6, waiting for transfers between devices: 26.7 us -> 30.4 us  [per_device(): right = lax.ppermute(right, 'tp', shift(tp, 1))]
    ppermute x3, waiting for transfers between devices: 0.01 us -> 2.5 us  [from_y(): return [lax.ppermute(a, 'ctx', perm(0, s, 0)) for s in (1, 2, 3)]]
    ppermute x2, waiting for transfers between devices: 2.28 us -> 0.21 us  [per_device(): up = lax.ppermute(right[:BLOCK], 'tp', shift(tp, 1))]
    ppermute x6, waiting for transfers between devices: 7.55 us -> 6.21 us  [per_device(): left = lax.ppermute(left, 'tp', shift(tp, -1))]
    dot_general x14, matrix products: 11 us -> 12.2 us  [dot(): return lax.dot_general(a, b, (dims, ((), ())), preferred_element_type=F32)]
  transfers between devices with their start and end apart: 23 -> 23, of which waited for: 8 -> 10; matrix products, arithmetic and copies ran while one was open for 10% -> 12% of each run, Pallas kernels for 15% -> 13%
where the time goes in v5:
time: 120 us
  waiting for transfers between devices  40.5 us (34%)
  starting transfers between devices  38.3 us (32%)
  Pallas kernels  23.8 us (20%)
  matrix products  12.4 us (10%)
  local copies, waits for them, and re-layouts  3.73 us (3%)
    ppermute x6, waiting for transfers between devices, per_device(): right = lax.ppermute(right, 'tp', shift(tp, 1))  30.4 us
    ppermute x6, starting transfers between devices, per_device(): left = lax.ppermute(left, 'tp', shift(tp, -1))  19.4 us
    dot_general x14, matrix products, dot(): return lax.dot_general(a, b, (dims, ((), ())), preferred_element_type=F32)  12.2 us
    pallas_call x3, Pallas kernels, inside(): pl.pallas_call(body, name='inside', grid=(count,), in_specs=[pl.BlockSpec...  9.97 us
    ppermute x2, starting transfers between devices, per_device(): down = lax.ppermute(left[BLOCK:], 'tp', shift(tp, -1))  7.06 us
    ppermute x6, waiting for transfers between devices, per_device(): left = lax.ppermute(left, 'tp', shift(tp, -1))  6.21 us
    pallas_call x1, Pallas kernels, finish(): pl.pallas_call(body, name='finish', grid=(blocks,), in_specs=[smem, smem]...  5.44 us
    ppermute x3, starting transfers between devices, from_x(): return [lax.ppermute(a, 'ctx', perm(s, 0, 0)) for s in (1, 2, 3)]  4.83 us
  transfers between devices with their start and end apart: 23, of which 10 were waited for; matrix products, arithmetic and copies ran while one was open for 12% of the time, Pallas kernels for 13%

profile of v5, /device:TPU:2, one launch (start us, length us, event | category | flops | bytes accessed | tf_op | source)
XLA Modules:
  0.0 120.0 jit_solution(14968810640230525158)
XLA Ops:
  0.6 2.3 %fusion.43 = (bf16[512,512]{1,0:T(8,128)(2,1)}, bf16[512,512]{1,0:T(8,128)(2,1)}) fusion(bf16[1024,512]{1,0:T(8,128)(2,1)} %param.7), kind=kLoop, calls=%fused_computation.58 | loop fusion | bytes 2097152 | tf_op jit(solution)/shard_map/slice | solution.py:417
  3.0 5.9 %collective-permute-start.9 = (bf16[512,512]{1,0:T(8,128)(2,1)}, bf16[512,512]{1,0:T(8,128)(2,1)}, u32[]{:S(2)}, u32[]{:S(2)}) collective-permute-start(bf16[512,512]{1,0:T(8,128)(2,1)} %get-tuple-element.57), channel_id=1, source_target_pairs={{0,7},{1,0},{2,1},{3,2},{4,3},{5,4},{6,5},{7,6},{8,15},{9,8},{10,9... | collective-permute-start | bytes 1572872 | tf_op jit(solution)/shard_map/ppermute | solution.py:422
  8.8 3.3 %collective-permute-start.1 = (bf16[512,512]{1,0:T(8,128)(2,1)}, bf16[512,512]{1,0:T(8,128)(2,1)S(1)}, u32[]{:S(2)}, u32[]{:S(2)}) collective-permute-start(bf16[512,512]{1,0:T(8,128)(2,1)} %get-tuple-element.58), channel_id=1, source_target_pairs={{0,7},{1,0},{2,1},{3,2},{4,3},{5,4},{6,5},{7,6},{8,15},{9,8},{10,9... | collective-permute-start | bytes 1572872 | tf_op jit(solution)/shard_map/ppermute | solution.py:422
  12.1 0.7 reshape.15
  13.3 0.2 copy.37
  13.8 1.7 %fusion.23 = f32[512,512]{0,1:T(8,128)S(1)} fusion(bf16[512,4096]{1,0:T(8,128)(2,1)} %weight_ref.3, s32[]{:T(128)S(6)} %select_n.98, bf16[1024,512]{1,0:T(8,128)(2,1)S(1)} %copy-done.5), kind=kOutput, calls=%fused_computation.33 | convolution fusion | flops 268435456 | bytes 2097156 | tf_op jit(solution)/shard_map/dot_general | solution.py:17
  15.5 1.6 %fusion.25 = f32[512,512]{0,1:T(8,128)S(1)} fusion(bf16[512,4096]{1,0:T(8,128)(2,1)} %weight_ref.3, s32[]{:T(128)S(6)} %select_n.98, bf16[1024,512]{1,0:T(8,128)(2,1)S(1)} %copy-done.5), kind=kOutput, calls=%fused_computation.35 | convolution fusion | flops 268435456 | bytes 2097156 | tf_op jit(solution)/shard_map/dot_general | solution.py:17
  17.1 8.1 %collective-permute-done.8 = bf16[512,512]{1,0:T(8,128)(2,1)} collective-permute-done((bf16[512,512]{1,0:T(8,128)(2,1)}, bf16[512,512]{1,0:T(8,128)(2,1)}, u32[]{:S(2)}, u32[]{:S(2)}) %collective-permute-start.8) | collective-permute-done | bytes 524320 | tf_op jit(solution)/shard_map/ppermute | solution.py:421
  25.2 3.2 %collective-permute-start.11 = (bf16[512,512]{1,0:T(8,128)(2,1)}, bf16[512,512]{1,0:T(8,128)(2,1)S(1)}, u32[]{:S(2)}, u32[]{:S(2)}) collective-permute-start(bf16[512,512]{1,0:T(8,128)(2,1)} %collective-permute-done.9), channel_id=1, source_target_pairs={{0,7},{1,0},{2,1},{3,2},{4,3},{5,4},{6,5},{7,6},{8,15},{9,8},{10,9... | collective-permute-start | bytes 1572872 | tf_op jit(solution)/shard_map/ppermute | solution.py:422
  28.4 8.0 %collective-permute-done = bf16[512,512]{1,0:T(8,128)(2,1)} collective-permute-done((bf16[512,512]{1,0:T(8,128)(2,1)}, bf16[512,512]{1,0:T(8,128)(2,1)}, u32[]{:S(2)}, u32[]{:S(2)}) %collective-permute-start) | collective-permute-done | bytes 524320 | tf_op jit(solution)/shard_map/ppermute | solution.py:421
  36.4 1.5 %convolution_add_fusion.3 = f32[512,512]{0,1:T(8,128)S(1)} fusion(f32[512,512]{0,1:T(8,128)S(1)} %fusion.23, bf16[512,512]{1,0:T(8,128)(2,1)} %collective-permute-done.8, bf16[512,4096]{1,0:T(8,128)(2,1)S(1)} %copy-done, s32[]{:T(128)S(6)} %select_n.100), kind=kOutput, calls=%fused_computation.6 | convolution fusion | flops 268697600 | bytes 3145732 | tf_op jit(solution)/shard_map/dot_general | solution.py:17
  38.0 1.5 %convolution_add_fusion.7 = f32[512,512]{0,1:T(8,128)S(1)} fusion(f32[512,512]{0,1:T(8,128)S(1)} %fusion.25, bf16[512,512]{1,0:T(8,128)(2,1)} %collective-permute-done, bf16[512,4096]{1,0:T(8,128)(2,1)S(1)} %copy-done, s32[]{:T(128)S(6)} %select_n.100), kind=kOutput, calls=%fused_computation.13 | convolution fusion | flops 268697600 | bytes 3145732 | tf_op jit(solution)/shard_map/dot_general | solution.py:17
  39.5 4.2 %prepare.1 = (bf16[1024,512]{1,0:T(8,128)(2,1)}, bf16[4,4,256,256]{3,2,1,0:T(8,128)(2,1)}, bf16[4,4,256,256]{3,2,1,0:T(8,128)(2,1)}, bf16[4,4,64,256]{3,2,1,0:T(8,128)(2,1)}, bf16[4,4,128,128]{3,2,1,0:T(8,128)(2,1)}) custom-call(bf16[1024,512]{1,0:T(8,128)(2,1)S(1)} %copy-done.1, f32[4,1024]{1,0:T(4,128)S(1)} %reshape_reshape.3.arow_ref, ...), custom_call_target="tpu_custom_call" | custom-call | flops 4000000000 | bytes 9000000 | tf_op jit(solution)/shard_map/prepare/pallas_call | solution.py:135
  43.8 3.3 %collective-permute-start.3 = (bf16[512,512]{1,0:T(8,128)(2,1)S(1)}, bf16[512,512]{1,0:T(8,128)(2,1)S(1)}, u32[]{:S(2)}, u32[]{:S(2)}) collective-permute-start(bf16[512,512]{1,0:T(8,128)(2,1)S(1)} %collective-permute-done.1), channel_id=1, source_target_pairs={{0,7},{1,0},{2,1},{3,2},{4,3},{5,4},{6,5},{7,6},{8,15},{9,8},{10,9... | collective-permute-start | bytes 1572872 | tf_op jit(solution)/shard_map/ppermute | solution.py:422
  47.1 1.5 %convolution_add_fusion.2 = f32[512,512]{0,1:T(8,128)S(1)} fusion(f32[512,512]{0,1:T(8,128)S(1)} %convolution_add_fusion.3, bf16[512,512]{1,0:T(8,128)(2,1)} %collective-permute-done.9, bf16[512,4096]{1,0:T(8,128)(2,1)S(1)} %copy-done, s32[]{:T(128)S(6)} %select_n.102), kind=kOutput, calls=%fused_computation.5 | convolution fusion | flops 268697600 | bytes 3145732 | tf_op jit(solution)/shard_map/dot_general | solution.py:17
  48.6 0.5 convolution_add_fusion.6
  49.2 2.0 %collective-permute-start.12 = (bf16[512,512]{1,0:T(8,128)(2,1)S(1)}, bf16[512,512]{1,0:T(8,128)(2,1)S(1)}, u32[]{:S(2)}, u32[]{:S(2)}) collective-permute-start(bf16[512,512]{1,0:T(8,128)(2,1)S(1)} %collective-permute-done.10), channel_id=1, source_target_pairs={{0,1},{1,2},{2,3},{3,4},{4,5},{5,6},{6,7},{7,0},{8,9},{9,10},{10,1... | collective-permute-start | bytes 1572872 | tf_op jit(solution)/shard_map/ppermute | solution.py:421
  51.2 7.6 %collective-permute-done.2 = bf16[512,512]{1,0:T(8,128)(2,1)S(1)} collective-permute-done((bf16[512,512]{1,0:T(8,128)(2,1)}, bf16[512,512]{1,0:T(8,128)(2,1)S(1)}, u32[]{:S(2)}, u32[]{:S(2)}) %collective-permute-start.2) | collective-permute-done | bytes 524320 | tf_op jit(solution)/shard_map/ppermute | solution.py:421
  58.8 0.5 fusion.13
  59.4 3.7 %collective-permute-start.5 = (bf16[512,512]{1,0:T(8,128)(2,1)S(1)}, bf16[512,512]{1,0:T(8,128)(2,1)S(1)}, u32[]{:S(2)}, u32[]{:S(2)}) collective-permute-start(bf16[512,512]{1,0:T(8,128)(2,1)S(1)} %collective-permute-done.3), channel_id=1, source_target_pairs={{0,7},{1,0},{2,1},{3,2},{4,3},{5,4},{6,5},{7,6},{8,15},{9,8},{10,9... | collective-permute-start | bytes 1572872 | tf_op jit(solution)/shard_map/ppermute | solution.py:422
  63.1 0.5 fusion.2
  63.6 0.5 fusion.15
  64.1 0.5 fusion.5
  64.6 6.0 %collective-permute-done.13 = bf16[512,512]{1,0:T(8,128)(2,1)S(1)} collective-permute-done((bf16[512,512]{1,0:T(8,128)(2,1)S(1)}, bf16[512,512]{1,0:T(8,128)(2,1)S(1)}, u32[]{:S(2)}, u32[]{:S(2)}) %collective-permute-start.13) | collective-permute-done | bytes 524320 | tf_op jit(solution)/shard_map/ppermute | solution.py:422
  70.7 3.8 %collective-permute-start.15 = (bf16[256,512]{1,0:T(8,128)(2,1)S(1)}, bf16[256,512]{1,0:T(8,128)(2,1)S(1)}, u32[]{:S(2)}, u32[]{:S(2)}) collective-permute-start(bf16[256,512]{1,0:T(8,128)(2,1)S(1)} %slice.37), channel_id=1, source_target_pairs={{0,7},{1,0},{2,1},{3,2},{4,3},{5,4},{6,5},{7,6},{8,15},{9,8},{10,9... | collective-permute-start | bytes 786440 | tf_op jit(solution)/shard_map/ppermute | solution.py:427
  74.6 6.7 %collective-permute-done.4 = bf16[512,512]{1,0:T(8,128)(2,1)S(1)} collective-permute-done((bf16[512,512]{1,0:T(8,128)(2,1)S(1)}, bf16[512,512]{1,0:T(8,128)(2,1)S(1)}, u32[]{:S(2)}, u32[]{:S(2)}) %collective-permute-start.4) | collective-permute-done | bytes 524320 | tf_op jit(solution)/shard_map/ppermute | solution.py:421
  81.4 3.3 %collective-permute-start.7 = (bf16[256,512]{1,0:T(8,128)(2,1)S(1)}, bf16[256,512]{1,0:T(8,128)(2,1)S(1)}, u32[]{:S(2)}, u32[]{:S(2)}) collective-permute-start(bf16[256,512]{1,0:T(8,128)(2,1)S(1)} %slice.35), channel_id=1, source_target_pairs={{0,7},{1,0},{2,1},{3,2},{4,3},{5,4},{6,5},{7,6},{8,15},{9,8},{10,9... | collective-permute-start | bytes 786440 | tf_op jit(solution)/shard_map/ppermute | solution.py:427
  84.7 0.5 fusion.7
  85.2 0.5 fusion.9
  85.7 0.5 fusion.1.acc_ref
  86.2 0.5 fusion.4.acc_ref
  86.9 1.5 %close_chunk.2 = (bf16[512,512]{1,0:T(8,128)(2,1)S(1)}, f32[2,4,64,128]{3,2,1,0:T(8,128)S(1)}) custom-call(s32[1]{0:T(128)} %bitcast.6.source_ref, f32[5,4]{1,0:T(8,128)S(1)} %pad_maximum_fusion.scale_ref, f32[512,512]{1,0:T(8,128)S(1)} %fusion.1.acc_ref, bf16[256,512]{1,0:T(8,128)(2,1)S(1)} %collective-permute-done.14.up_ref, ...), custom_call_target="tpu_custom_call" | custom-call | flops 600000000 | bytes 4000000 | tf_op jit(solution)/shard_map/close_chunk/pallas_call | solution.py:208
  88.4 2.9 %inside.3 = (f32[256,512]{1,0:T(8,128)S(1)}, f32[256,512]{1,0:T(8,128)S(1)}, f32[1,4,256]{2,1,0:T(4,128)S(1)}) custom-call(f32[1,4]{1,0:T(1,128)S(1)} %bitcast.41, bf16[512,512]{1,0:T(8,128)(2,1)S(1)} %get-tuple-element.49.dy_ref, bf16[1024,512]{1,0:T(8,128)(2,1)} %refs_10_.1, bf16[1024,512]{1,0:T(8,128)(2,1)} %refs_11_.1, ...), custom_call_target="tpu_custom_call" | custom-call | flops 1000000000 | bytes 3500000 | tf_op jit(solution)/shard_map/inside/pallas_call | solution.py:251
  91.3 1.5 %close_chunk.3 = (bf16[512,512]{1,0:T(8,128)(2,1)S(1)}, f32[2,4,64,128]{3,2,1,0:T(8,128)S(1)}, bf16[272,128]{1,0:T(8,128)(2,1)S(1)}) custom-call(s32[1]{0:T(128)} %bitcast.6.source_ref, f32[5,4]{1,0:T(8,128)S(1)} %pad_maximum_fusion.scale_ref, f32[512,512]{1,0:T(8,128)S(1)} %fusion.4.acc_ref, bf16[256,512]{1,0:T(8,128)(2,1)S(1)} %collective-permute-done.6.up_ref, ...), custom_call_target="tpu_custom_call" | custom-call | flops 600000000 | bytes 4000000 | tf_op jit(solution)/shard_map/close_chunk/pallas_call | solution.py:208
  92.9 1.2 collective-permute-done.16.refs_1_
  94.1 0.6 combine_core.1.refs_0_.refs_2_
  94.7 3.1 %collective-permute-start.19 = (bf16[272,128]{1,0:T(8,128)(2,1)S(1)}, bf16[272,128]{1,0:T(8,128)(2,1)S(1)}, u32[]{:S(2)}, u32[]{:S(2)}) collective-permute-start(bf16[272,128]{1,0:T(8,128)(2,1)S(1)} %combine_core.1.refs_0_.refs_2_), channel_id=1, source_target_pairs={{0,48},{8,56},{16,0},{24,8},{32,16},{40,24},{48,32},{56,40},{64,11... | collective-permute-start | bytes 208904 | tf_op jit(solution)/shard_map/ppermute | solution.py:406
  97.8 0.6 collective-permute-start.18
  98.4 1.0 collective-permute-start.17
  99.4 2.8 %inside.4 = (f32[256,512]{1,0:T(8,128)S(1)}, f32[256,512]{1,0:T(8,128)S(1)}, f32[1,4,256]{2,1,0:T(4,128)S(1)}) custom-call(f32[1,4]{1,0:T(1,128)S(1)} %bitcast.42, bf16[512,512]{1,0:T(8,128)(2,1)S(1)} %get-tuple-element.49.dy_ref, bf16[1024,512]{1,0:T(8,128)(2,1)} %refs_10_.1, bf16[1024,512]{1,0:T(8,128)(2,1)} %refs_11_.1, ...), custom_call_target="tpu_custom_call" | custom-call | flops 1000000000 | bytes 3500000 | tf_op jit(solution)/shard_map/inside/pallas_call | solution.py:251
  102.2 1.8 %collective-permute-done.18.refs_2_.refs_4_ = bf16[272,128]{1,0:T(8,128)(2,1)S(1)} collective-permute-done((bf16[272,128]{1,0:T(8,128)(2,1)S(1)}, bf16[272,128]{1,0:T(8,128)(2,1)S(1)}, u32[]{:S(2)}, u32[]{:S(2)}) %collective-permute-start.18) | collective-permute-done | bytes 69664 | tf_op jit(solution)/shard_map/ppermute | solution.py:406
  104.0 0.7 collective-permute-done.17.refs_1_.refs_3_
  104.7 0.6 combine_row.1.refs_6_
  105.4 0.6 collective-permute-start.22
  106.0 2.4 %collective-permute-start.21 = (bf16[272,128]{1,0:T(8,128)(2,1)S(1)}, bf16[272,128]{1,0:T(8,128)(2,1)S(1)}, u32[]{:S(2)}, u32[]{:S(2)}) collective-permute-start(bf16[272,128]{1,0:T(8,128)(2,1)S(1)} %combine_row.1.refs_6_), channel_id=1, source_target_pairs={{0,128},{8,136},{16,144},{24,152},{32,160},{40,168},{48,176},{56,1... | collective-permute-start | bytes 208904 | tf_op jit(solution)/shard_map/ppermute | solution.py:409
  108.4 1.8 %collective-permute-start.20 = (bf16[272,128]{1,0:T(8,128)(2,1)S(1)}, bf16[272,128]{1,0:T(8,128)(2,1)S(1)}, u32[]{:S(2)}, u32[]{:S(2)}) collective-permute-start(bf16[272,128]{1,0:T(8,128)(2,1)S(1)} %combine_row.1.refs_6_), channel_id=1, source_target_pairs={{0,64},{8,72},{16,80},{24,88},{32,96},{40,104},{48,112},{56,120},{... | collective-permute-start | bytes 208904 | tf_op jit(solution)/shard_map/ppermute | solution.py:409
  110.2 4.3 %inside.5 = (f32[512,512]{1,0:T(8,128)S(1)}, f32[512,512]{1,0:T(8,128)S(1)}, f32[2,4,256]{2,1,0:T(4,128)S(1)}) custom-call(f32[1,4]{1,0:T(1,128)S(1)} %bitcast.43, bf16[512,512]{1,0:T(8,128)(2,1)S(1)} %get-tuple-element.53.dy_ref, bf16[1024,512]{1,0:T(8,128)(2,1)} %refs_10_.1, bf16[1024,512]{1,0:T(8,128)(2,1)} %refs_11_.1, ...), custom_call_target="tpu_custom_call" | custom-call | flops 2000000000 | bytes 7000000 | tf_op jit(solution)/shard_map/inside/pallas_call | solution.py:251
  114.5 5.4 %finish.1 = (bf16[1024,512]{1,0:T(8,128)(2,1)}, f32[1024,512]{1,0:T(8,128)}, f32[4,1024]{1,0:T(4,128)}) custom-call(s32[3]{0:T(128)S(1)} %pad_add_fusion.place_ref, f32[4,4]{1,0:T(4,128)S(1)} %bitcast.40, bf16[272,128]{1,0:T(8,128)(2,1)S(1)} %get-tuple-element.40.refs_0_, bf16[272,128]{1,0:T(8,128)(2,1)S(1)} %collective-permute-done.16.refs_1_, ...), custom_call_target="tpu_custom_call" | custom-call | flops 600000000 | bytes 11000000 | tf_op jit(solution)/shard_map/finish/pallas_call | solution.py:356
  (52 shorter events, 1.6 us)
Async XLA Ops:
  0.6 13.2 %copy-start.5 = (bf16[1024,512]{1,0:T(8,128)(2,1)S(1)}, bf16[1024,512]{1,0:T(8,128)(2,1)}, u32[]{:S(2)}) copy-start(bf16[1024,512]{1,0:T(8,128)(2,1)} %param.7) | copy-start | bytes 3145732
  3.0 22.2 %collective-permute-start.9 = (bf16[512,512]{1,0:T(8,128)(2,1)}, bf16[512,512]{1,0:T(8,128)(2,1)}, u32[]{:S(2)}, u32[]{:S(2)}) collective-permute-start(bf16[512,512]{1,0:T(8,128)(2,1)} %get-tuple-element.57), channel_id=1, source_target_pairs={{0,7},{1,0},{2,1},{3,2},{4,3},{5,4},{6,5},{7,6},{8,15},{9,8},{10,9... | collective-permute-start | bytes 1572872 | tf_op jit(solution)/shard_map/ppermute | solution.py:422
  8.8 16.4 %collective-permute-start.8 = (bf16[512,512]{1,0:T(8,128)(2,1)}, bf16[512,512]{1,0:T(8,128)(2,1)}, u32[]{:S(2)}, u32[]{:S(2)}) collective-permute-start(bf16[512,512]{1,0:T(8,128)(2,1)} %get-tuple-element.57), channel_id=1, source_target_pairs={{0,1},{1,2},{2,3},{3,4},{4,5},{5,6},{6,7},{7,0},{8,9},{9,10},{10,1... | collective-permute-start | bytes 1572872 | tf_op jit(solution)/shard_map/ppermute | solution.py:421
  8.8 27.6 %collective-permute-start = (bf16[512,512]{1,0:T(8,128)(2,1)}, bf16[512,512]{1,0:T(8,128)(2,1)}, u32[]{:S(2)}, u32[]{:S(2)}) collective-permute-start(bf16[512,512]{1,0:T(8,128)(2,1)} %get-tuple-element.58), channel_id=1, source_target_pairs={{0,1},{1,2},{2,3},{3,4},{4,5},{5,6},{6,7},{7,0},{8,9},{9,10},{10,1... | collective-permute-start | bytes 1572872 | tf_op jit(solution)/shard_map/ppermute | solution.py:421
  8.8 34.9 %collective-permute-start.1 = (bf16[512,512]{1,0:T(8,128)(2,1)}, bf16[512,512]{1,0:T(8,128)(2,1)S(1)}, u32[]{:S(2)}, u32[]{:S(2)}) collective-permute-start(bf16[512,512]{1,0:T(8,128)(2,1)} %get-tuple-element.58), channel_id=1, source_target_pairs={{0,7},{1,0},{2,1},{3,2},{4,3},{5,4},{6,5},{7,6},{8,15},{9,8},{10,9... | collective-permute-start | bytes 1572872 | tf_op jit(solution)/shard_map/ppermute | solution.py:422
  13.8 22.7 %copy-start = (bf16[512,4096]{1,0:T(8,128)(2,1)S(1)}, bf16[512,4096]{1,0:T(8,128)(2,1)}, u32[]{:S(2)}) copy-start(bf16[512,4096]{1,0:T(8,128)(2,1)} %weight_ref.3) | copy-start | bytes 12582916
  15.5 24.0 %copy-start.1 = (bf16[1024,512]{1,0:T(8,128)(2,1)S(1)}, bf16[1024,512]{1,0:T(8,128)(2,1)}, u32[]{:S(2)}) copy-start(bf16[1024,512]{1,0:T(8,128)(2,1)} %refs_11_.1) | copy-start | bytes 3145732
  15.5 24.0 %copy-start.3 = (f32[4,4,64,128]{3,2,1,0:T(8,128)S(1)}, f32[4,4,64,128]{3,2,1,0:T(8,128)}, u32[]{:S(2)}) copy-start(f32[4,4,64,128]{3,2,1,0:T(8,128)} %refs_15_.1) | copy-start | bytes 1572868
  25.2 24.0 %collective-permute-start.10 = (bf16[512,512]{1,0:T(8,128)(2,1)}, bf16[512,512]{1,0:T(8,128)(2,1)S(1)}, u32[]{:S(2)}, u32[]{:S(2)}) collective-permute-start(bf16[512,512]{1,0:T(8,128)(2,1)} %collective-permute-done.8), channel_id=1, source_target_pairs={{0,1},{1,2},{2,3},{3,4},{4,5},{5,6},{6,7},{7,0},{8,9},{9,10},{10,1... | collective-permute-start | bytes 1572872 | tf_op jit(solution)/shard_map/ppermute | solution.py:421
  25.2 23.9 %collective-permute-start.11 = (bf16[512,512]{1,0:T(8,128)(2,1)}, bf16[512,512]{1,0:T(8,128)(2,1)S(1)}, u32[]{:S(2)}, u32[]{:S(2)}) collective-permute-start(bf16[512,512]{1,0:T(8,128)(2,1)} %collective-permute-done.9), channel_id=1, source_target_pairs={{0,7},{1,0},{2,1},{3,2},{4,3},{5,4},{6,5},{7,6},{8,15},{9,8},{10,9... | collective-permute-start | bytes 1572872 | tf_op jit(solution)/shard_map/ppermute | solution.py:422
  36.4 22.4 %collective-permute-start.2 = (bf16[512,512]{1,0:T(8,128)(2,1)}, bf16[512,512]{1,0:T(8,128)(2,1)S(1)}, u32[]{:S(2)}, u32[]{:S(2)}) collective-permute-start(bf16[512,512]{1,0:T(8,128)(2,1)} %collective-permute-done), channel_id=1, source_target_pairs={{0,1},{1,2},{2,3},{3,4},{4,5},{5,6},{6,7},{7,0},{8,9},{9,10},{10,1... | collective-permute-start | bytes 1572872 | tf_op jit(solution)/shard_map/ppermute | solution.py:421
  43.8 15.7 %collective-permute-start.3 = (bf16[512,512]{1,0:T(8,128)(2,1)S(1)}, bf16[512,512]{1,0:T(8,128)(2,1)S(1)}, u32[]{:S(2)}, u32[]{:S(2)}) collective-permute-start(bf16[512,512]{1,0:T(8,128)(2,1)S(1)} %collective-permute-done.1), channel_id=1, source_target_pairs={{0,7},{1,0},{2,1},{3,2},{4,3},{5,4},{6,5},{7,6},{8,15},{9,8},{10,9... | collective-permute-start | bytes 1572872 | tf_op jit(solution)/shard_map/ppermute | solution.py:422
  49.1 21.6 %collective-permute-start.13 = (bf16[512,512]{1,0:T(8,128)(2,1)S(1)}, bf16[512,512]{1,0:T(8,128)(2,1)S(1)}, u32[]{:S(2)}, u32[]{:S(2)}) collective-permute-start(bf16[512,512]{1,0:T(8,128)(2,1)S(1)} %collective-permute-done.11), channel_id=1, source_target_pairs={{0,7},{1,0},{2,1},{3,2},{4,3},{5,4},{6,5},{7,6},{8,15},{9,8},{10,9... | collective-permute-start | bytes 1572872 | tf_op jit(solution)/shard_map/ppermute | solution.py:422
  49.2 25.3 %collective-permute-start.12 = (bf16[512,512]{1,0:T(8,128)(2,1)S(1)}, bf16[512,512]{1,0:T(8,128)(2,1)S(1)}, u32[]{:S(2)}, u32[]{:S(2)}) collective-permute-start(bf16[512,512]{1,0:T(8,128)(2,1)S(1)} %collective-permute-done.10), channel_id=1, source_target_pairs={{0,1},{1,2},{2,3},{3,4},{4,5},{5,6},{6,7},{7,0},{8,9},{9,10},{10,1... | collective-permute-start | bytes 1572872 | tf_op jit(solution)/shard_map/ppermute | solution.py:421
  58.8 22.5 %collective-permute-start.4 = (bf16[512,512]{1,0:T(8,128)(2,1)S(1)}, bf16[512,512]{1,0:T(8,128)(2,1)S(1)}, u32[]{:S(2)}, u32[]{:S(2)}) collective-permute-start(bf16[512,512]{1,0:T(8,128)(2,1)S(1)} %collective-permute-done.2), channel_id=1, source_target_pairs={{0,1},{1,2},{2,3},{3,4},{4,5},{5,6},{6,7},{7,0},{8,9},{9,10},{10,1... | collective-permute-start | bytes 1572872 | tf_op jit(solution)/shard_map/ppermute | solution.py:421
  59.4 22.0 %collective-permute-start.5 = (bf16[512,512]{1,0:T(8,128)(2,1)S(1)}, bf16[512,512]{1,0:T(8,128)(2,1)S(1)}, u32[]{:S(2)}, u32[]{:S(2)}) collective-permute-start(bf16[512,512]{1,0:T(8,128)(2,1)S(1)} %collective-permute-done.3), channel_id=1, source_target_pairs={{0,7},{1,0},{2,1},{3,2},{4,3},{5,4},{6,5},{7,6},{8,15},{9,8},{10,9... | collective-permute-start | bytes 1572872 | tf_op jit(solution)/shard_map/ppermute | solution.py:422
  70.7 16.0 %collective-permute-start.15 = (bf16[256,512]{1,0:T(8,128)(2,1)S(1)}, bf16[256,512]{1,0:T(8,128)(2,1)S(1)}, u32[]{:S(2)}, u32[]{:S(2)}) collective-permute-start(bf16[256,512]{1,0:T(8,128)(2,1)S(1)} %slice.37), channel_id=1, source_target_pairs={{0,7},{1,0},{2,1},{3,2},{4,3},{5,4},{6,5},{7,6},{8,15},{9,8},{10,9... | collective-permute-start | bytes 786440 | tf_op jit(solution)/shard_map/ppermute | solution.py:427
  74.5 12.4 %collective-permute-start.14 = (bf16[256,512]{1,0:T(8,128)(2,1)S(1)}, bf16[256,512]{1,0:T(8,128)(2,1)S(1)}, u32[]{:S(2)}, u32[]{:S(2)}) collective-permute-start(bf16[256,512]{1,0:T(8,128)(2,1)S(1)} %slice.36), channel_id=1, source_target_pairs={{0,1},{1,2},{2,3},{3,4},{4,5},{5,6},{6,7},{7,0},{8,9},{9,10},{10,1... | collective-permute-start | bytes 786440 | tf_op jit(solution)/shard_map/ppermute | solution.py:426
  81.3 10.0 %collective-permute-start.6 = (bf16[256,512]{1,0:T(8,128)(2,1)S(1)}, bf16[256,512]{1,0:T(8,128)(2,1)S(1)}, u32[]{:S(2)}, u32[]{:S(2)}) collective-permute-start(bf16[256,512]{1,0:T(8,128)(2,1)S(1)} %slice.34), channel_id=1, source_target_pairs={{0,1},{1,2},{2,3},{3,4},{4,5},{5,6},{6,7},{7,0},{8,9},{9,10},{10,1... | collective-permute-start | bytes 786440 | tf_op jit(solution)/shard_map/ppermute | solution.py:426
  81.4 9.8 %collective-permute-start.7 = (bf16[256,512]{1,0:T(8,128)(2,1)S(1)}, bf16[256,512]{1,0:T(8,128)(2,1)S(1)}, u32[]{:S(2)}, u32[]{:S(2)}) collective-permute-start(bf16[256,512]{1,0:T(8,128)(2,1)S(1)} %slice.35), channel_id=1, source_target_pairs={{0,7},{1,0},{2,1},{3,2},{4,3},{5,4},{6,5},{7,6},{8,15},{9,8},{10,9... | collective-permute-start | bytes 786440 | tf_op jit(solution)/shard_map/ppermute | solution.py:427
  85.7 1.2 %copy-start.2 = (bf16[4,4,64,256]{3,2,1,0:T(8,128)(2,1)S(1)}, bf16[4,4,64,256]{3,2,1,0:T(8,128)(2,1)}, u32[]{:S(2)}) copy-start(bf16[4,4,64,256]{3,2,1,0:T(8,128)(2,1)} %get-tuple-element.31.wct_ref) | copy-start | bytes 1572868
  86.7 1.7 %copy-start.4 = (f32[4]{0:T(128)S(1)}, f32[4]{0:T(128)}, u32[]{:S(2)}) copy-start(f32[4]{0:T(128)} %param.13) | copy-start | bytes 52
  92.8 1.3 %collective-permute-start.16 = (bf16[272,128]{1,0:T(8,128)(2,1)S(1)}, bf16[272,128]{1,0:T(8,128)(2,1)S(1)}, u32[]{:S(2)}, u32[]{:S(2)}) collective-permute-start(bf16[272,128]{1,0:T(8,128)(2,1)S(1)} %get-tuple-element.40.refs_0_), channel_id=1, source_target_pairs={{0,8},{8,0},{16,24},{24,16},{32,40},{40,32},{48,56},{56,48},{64,72... | collective-permute-start | bytes 208904 | tf_op jit(solution)/shard_map/ppermute | solution.py:403
  94.7 7.5 %collective-permute-start.19 = (bf16[272,128]{1,0:T(8,128)(2,1)S(1)}, bf16[272,128]{1,0:T(8,128)(2,1)S(1)}, u32[]{:S(2)}, u32[]{:S(2)}) collective-permute-start(bf16[272,128]{1,0:T(8,128)(2,1)S(1)} %combine_core.1.refs_0_.refs_2_), channel_id=1, source_target_pairs={{0,48},{8,56},{16,0},{24,8},{32,16},{40,24},{48,32},{56,40},{64,11... | collective-permute-start | bytes 208904 | tf_op jit(solution)/shard_map/ppermute | solution.py:406
  97.8 6.3 %collective-permute-start.18 = (bf16[272,128]{1,0:T(8,128)(2,1)S(1)}, bf16[272,128]{1,0:T(8,128)(2,1)S(1)}, u32[]{:S(2)}, u32[]{:S(2)}) collective-permute-start(bf16[272,128]{1,0:T(8,128)(2,1)S(1)} %combine_core.1.refs_0_.refs_2_), channel_id=1, source_target_pairs={{0,32},{8,40},{16,48},{24,56},{32,0},{40,8},{48,16},{56,24},{64,96... | collective-permute-start | bytes 208904 | tf_op jit(solution)/shard_map/ppermute | solution.py:406
  98.4 6.3 %collective-permute-start.17 = (bf16[272,128]{1,0:T(8,128)(2,1)S(1)}, bf16[272,128]{1,0:T(8,128)(2,1)S(1)}, u32[]{:S(2)}, u32[]{:S(2)}) collective-permute-start(bf16[272,128]{1,0:T(8,128)(2,1)S(1)} %combine_core.1.refs_0_.refs_2_), channel_id=1, source_target_pairs={{0,16},{8,24},{16,32},{24,40},{32,48},{40,56},{48,0},{56,8},{64,80... | collective-permute-start | bytes 208904 | tf_op jit(solution)/shard_map/ppermute | solution.py:406
  105.4 9.1 %collective-permute-start.22 = (bf16[272,128]{1,0:T(8,128)(2,1)S(1)}, bf16[272,128]{1,0:T(8,128)(2,1)S(1)}, u32[]{:S(2)}, u32[]{:S(2)}) collective-permute-start(bf16[272,128]{1,0:T(8,128)(2,1)S(1)} %combine_row.1.refs_6_), channel_id=1, source_target_pairs={{0,192},{8,200},{16,208},{24,216},{32,224},{40,232},{48,240},{56,2... | collective-permute-start | bytes 208904 | tf_op jit(solution)/shard_map/ppermute | solution.py:409
  106.0 8.5 %collective-permute-start.21 = (bf16[272,128]{1,0:T(8,128)(2,1)S(1)}, bf16[272,128]{1,0:T(8,128)(2,1)S(1)}, u32[]{:S(2)}, u32[]{:S(2)}) collective-permute-start(bf16[272,128]{1,0:T(8,128)(2,1)S(1)} %combine_row.1.refs_6_), channel_id=1, source_target_pairs={{0,128},{8,136},{16,144},{24,152},{32,160},{40,168},{48,176},{56,1... | collective-permute-start | bytes 208904 | tf_op jit(solution)/shard_map/ppermute | solution.py:409
  108.4 6.1 %collective-permute-start.20 = (bf16[272,128]{1,0:T(8,128)(2,1)S(1)}, bf16[272,128]{1,0:T(8,128)(2,1)S(1)}, u32[]{:S(2)}, u32[]{:S(2)}) collective-permute-start(bf16[272,128]{1,0:T(8,128)(2,1)S(1)} %combine_row.1.refs_6_), channel_id=1, source_target_pairs={{0,64},{8,72},{16,80},{24,88},{32,96},{40,104},{48,112},{56,120},{... | collective-permute-start | bytes 208904 | tf_op jit(solution)/shard_map/ppermute | solution.py:409

commit v6 on v5

--- a/solution.py
+++ b/solution.py
@@ -163,6 +163,33 @@
 
 def resident():
     return pl.BlockSpec(memory_space=pltpu.VMEM)
+
+
+def split_rows(array, count):
+    rows, width = array.shape
+    part = rows // count
+
+    def body(source_ref, *refs):
+        outs, sem = refs[:-1], refs[-1]
+        copies = [
+            pltpu.make_async_copy(source_ref.at[i * part : (i + 1) * part], out, sem.at[i])
+            for i, out in enumerate(outs)
+        ]
+        for copy in copies:
+            copy.start()
+        for copy in copies:
+            copy.wait()
+
+    return pl.pallas_call(
+        body,
+        name="split_rows",
+        in_specs=[pl.BlockSpec(memory_space=pltpu.HBM)],
+        out_specs=[resident()] * count,
+        out_shape=[jax.ShapeDtypeStruct((part, width), array.dtype)] * count,
+        scratch_shapes=[pltpu.SemaphoreType.DMA((count,))],
+        cost_estimate=pl.CostEstimate(flops=0, bytes_accessed=2 * rows * width * 2, transcendentals=0),
+        compiler_params=pltpu.CompilerParams(vmem_limit_bytes=16 << 20),
+    )(*in_hbm(array))
 
 
 def close_chunk(first, source, acc, up, down, weight, wct, scale, earlier):
@@ -413,8 +440,9 @@
 
     half = tokens // 2
     accs, lasts, firsts = [], [], []
+    owns = split_rows(upstream, 2)
     for c in range(2):
-        own = upstream[c * half : (c + 1) * half]
+        own = owns[c]
         right = left = own
         acc = dot(own, weight_of(me), NT)
         for k in range(1, tp // 2):

time: 120 us -> 116 us (0.967); the launches traced: 120 us -> 115 us
  waiting for transfers between devices: 40.5 us -> 35.1 us
  local copies, waits for them, and re-layouts: 3.73 us -> 1.39 us
    ppermute x6, waiting for transfers between devices: 30.4 us -> 25.8 us  [per_device(): right = lax.ppermute(right, 'tp', shift(tp, 1))]
    ppermute x3, waiting for transfers between devices: 2.5 us -> 0.1 us  [from_y(): return [lax.ppermute(a, 'ctx', perm(0, s, 0)) for s in (1, 2, 3)]]
    slice x1 -> x0, local copies, waits for them, and re-layouts: 2.33 us -> none  [per_device(): own = upstream[c * half:(c + 1) * half]]
    ppermute x6, waiting for transfers between devices: 6.21 us -> 7.48 us  [per_device(): left = lax.ppermute(left, 'tp', shift(tp, -1))]
    pallas_call x0 -> x1, Pallas kernels: none -> 1.22 us  [split_rows(): pl.pallas_call(body, name='split_rows', in_specs=[pl.BlockSpec(memory_spa...]
    ppermute x3, starting transfers between devices: 4.69 us -> 5.9 us  [from_y(): return [lax.ppermute(a, 'ctx', perm(0, s, 0)) for s in (1, 2, 3)]]
  transfers between devices with their start and end apart: 23 -> 23, of which waited for: 10 -> 9; matrix products, arithmetic and copies ran while one was open for 12% -> 12% of each run, Pallas kernels for 13% -> 14%
where the time goes in v6:
time: 116 us; the launch traced here: 115 us
  starting transfers between devices  39.3 us (34%)
  waiting for transfers between devices  35.1 us (30%)
  Pallas kernels  25 us (22%)
  matrix products  12.4 us (11%)
  local copies, waits for them, and re-layouts  1.39 us (1%)
    ppermute x6, waiting for transfers between devices, per_device(): right = lax.ppermute(right, 'tp', shift(tp, 1))  25.8 us
    ppermute x6, starting transfers between devices, per_device(): left = lax.ppermute(left, 'tp', shift(tp, -1))  19.4 us
    dot_general x14, matrix products, dot(): return lax.dot_general(a, b, (dims, ((), ())), preferred_element_type=F32)  12.3 us
    pallas_call x3, Pallas kernels, inside(): pl.pallas_call(body, name='inside', grid=(count,), in_specs=[pl.BlockSpec...  9.97 us
    ppermute x6, waiting for transfers between devices, per_device(): left = lax.ppermute(left, 'tp', shift(tp, -1))  7.48 us
    ppermute x2, starting transfers between devices, per_device(): down = lax.ppermute(left[BLOCK:], 'tp', shift(tp, -1))  6.61 us
    ppermute x3, starting transfers between devices, from_y(): return [lax.ppermute(a, 'ctx', perm(0, s, 0)) for s in (1, 2, 3)]  5.9 us
    pallas_call x1, Pallas kernels, finish(): pl.pallas_call(body, name='finish', grid=(blocks,), in_specs=[smem, smem]...  5.44 us
  transfers between devices with their start and end apart: 23, of which 9 were waited for; matrix products, arithmetic and copies ran while one was open for 12% of the time, Pallas kernels for 14%

profile of v6, /device:TPU:2, one launch (start us, length us, event | category | flops | bytes accessed | tf_op | source)
XLA Modules:
  0.0 114.6 jit_solution(1495070339461297386)
XLA Ops:
  0.6 1.2 %split_rows.1 = (bf16[512,512]{1,0:T(8,128)(2,1)S(1)}, bf16[512,512]{1,0:T(8,128)(2,1)S(1)}) custom-call(bf16[1024,512]{1,0:T(8,128)(2,1)} %source_ref.1), custom_call_target="tpu_custom_call" | custom-call | bytes 2097152 | tf_op jit(solution)/shard_map/split_rows/pallas_call | solution.py:183
  1.9 2.0 %collective-permute-start.8 = (bf16[512,512]{1,0:T(8,128)(2,1)S(1)}, bf16[512,512]{1,0:T(8,128)(2,1)}, u32[]{:S(2)}, u32[]{:S(2)}) collective-permute-start(bf16[512,512]{1,0:T(8,128)(2,1)S(1)} %get-tuple-element.33), channel_id=1, source_target_pairs={{0,1},{1,2},{2,3},{3,4},{4,5},{5,6},{6,7},{7,0},{8,9},{9,10},{10,1... | collective-permute-start | bytes 1572872 | tf_op jit(solution)/shard_map/ppermute | solution.py:449
  3.8 4.0 %collective-permute-start.9 = (bf16[512,512]{1,0:T(8,128)(2,1)S(1)}, bf16[512,512]{1,0:T(8,128)(2,1)}, u32[]{:S(2)}, u32[]{:S(2)}) collective-permute-start(bf16[512,512]{1,0:T(8,128)(2,1)S(1)} %get-tuple-element.33), channel_id=1, source_target_pairs={{0,7},{1,0},{2,1},{3,2},{4,3},{5,4},{6,5},{7,6},{8,15},{9,8},{10,9... | collective-permute-start | bytes 1572872 | tf_op jit(solution)/shard_map/ppermute | solution.py:450
  7.9 3.2 %collective-permute-start.1 = (bf16[512,512]{1,0:T(8,128)(2,1)S(1)}, bf16[512,512]{1,0:T(8,128)(2,1)}, u32[]{:S(2)}, u32[]{:S(2)}) collective-permute-start(bf16[512,512]{1,0:T(8,128)(2,1)S(1)} %get-tuple-element.32), channel_id=1, source_target_pairs={{0,7},{1,0},{2,1},{3,2},{4,3},{5,4},{6,5},{7,6},{8,15},{9,8},{10,9... | collective-permute-start | bytes 1572872 | tf_op jit(solution)/shard_map/ppermute | solution.py:450
  11.1 0.7 reshape.15
  12.3 0.2 copy.37
  12.9 1.7 %fusion.23 = f32[512,512]{0,1:T(8,128)S(1)} fusion(bf16[512,512]{1,0:T(8,128)(2,1)S(1)} %get-tuple-element.33, bf16[512,4096]{1,0:T(8,128)(2,1)} %weight_ref.3, s32[]{:T(128)S(6)} %select_n.98), kind=kOutput, calls=%fused_computation.33 | convolution fusion | flops 268435456 | bytes 2097156 | tf_op jit(solution)/shard_map/dot_general | solution.py:17
  14.5 1.6 %fusion.25 = f32[512,512]{0,1:T(8,128)S(1)} fusion(bf16[512,512]{1,0:T(8,128)(2,1)S(1)} %get-tuple-element.32, bf16[512,4096]{1,0:T(8,128)(2,1)} %weight_ref.3, s32[]{:T(128)S(6)} %select_n.98), kind=kOutput, calls=%fused_computation.35 | convolution fusion | flops 268435456 | bytes 2097156 | tf_op jit(solution)/shard_map/dot_general | solution.py:17
  16.2 4.5 %collective-permute-done.8 = bf16[512,512]{1,0:T(8,128)(2,1)} collective-permute-done((bf16[512,512]{1,0:T(8,128)(2,1)S(1)}, bf16[512,512]{1,0:T(8,128)(2,1)}, u32[]{:S(2)}, u32[]{:S(2)}) %collective-permute-start.8) | collective-permute-done | bytes 524320 | tf_op jit(solution)/shard_map/ppermute | solution.py:449
  20.7 3.4 %collective-permute-start.11 = (bf16[512,512]{1,0:T(8,128)(2,1)}, bf16[512,512]{1,0:T(8,128)(2,1)S(1)}, u32[]{:S(2)}, u32[]{:S(2)}) collective-permute-start(bf16[512,512]{1,0:T(8,128)(2,1)} %collective-permute-done.9), channel_id=1, source_target_pairs={{0,7},{1,0},{2,1},{3,2},{4,3},{5,4},{6,5},{7,6},{8,15},{9,8},{10,9... | collective-permute-start | bytes 1572872 | tf_op jit(solution)/shard_map/ppermute | solution.py:450
  24.0 7.8 %collective-permute-done = bf16[512,512]{1,0:T(8,128)(2,1)S(1)} collective-permute-done((bf16[512,512]{1,0:T(8,128)(2,1)S(1)}, bf16[512,512]{1,0:T(8,128)(2,1)S(1)}, u32[]{:S(2)}, u32[]{:S(2)}) %collective-permute-start) | collective-permute-done | bytes 524320 | tf_op jit(solution)/shard_map/ppermute | solution.py:449
  31.8 1.5 %convolution_add_fusion.3 = f32[512,512]{0,1:T(8,128)S(1)} fusion(f32[512,512]{0,1:T(8,128)S(1)} %fusion.23, bf16[512,512]{1,0:T(8,128)(2,1)} %collective-permute-done.8, bf16[512,4096]{1,0:T(8,128)(2,1)S(1)} %copy-done, s32[]{:T(128)S(6)} %select_n.100), kind=kOutput, calls=%fused_computation.6 | convolution fusion | flops 268697600 | bytes 3145732 | tf_op jit(solution)/shard_map/dot_general | solution.py:17
  33.3 0.5 convolution_add_fusion.7
  33.8 4.2 %prepare.1 = (bf16[1024,512]{1,0:T(8,128)(2,1)}, bf16[4,4,256,256]{3,2,1,0:T(8,128)(2,1)}, bf16[4,4,256,256]{3,2,1,0:T(8,128)(2,1)}, bf16[4,4,64,256]{3,2,1,0:T(8,128)(2,1)}, bf16[4,4,128,128]{3,2,1,0:T(8,128)(2,1)}) custom-call(bf16[1024,512]{1,0:T(8,128)(2,1)S(1)} %copy-done.1, f32[4,1024]{1,0:T(4,128)S(1)} %reshape_reshape.3.arow_ref, ...), custom_call_target="tpu_custom_call" | custom-call | flops 4000000000 | bytes 9000000 | tf_op jit(solution)/shard_map/prepare/pallas_call | solution.py:135
  38.1 3.3 %collective-permute-start.3 = (bf16[512,512]{1,0:T(8,128)(2,1)}, bf16[512,512]{1,0:T(8,128)(2,1)S(1)}, u32[]{:S(2)}, u32[]{:S(2)}) collective-permute-start(bf16[512,512]{1,0:T(8,128)(2,1)} %collective-permute-done.1), channel_id=1, source_target_pairs={{0,7},{1,0},{2,1},{3,2},{4,3},{5,4},{6,5},{7,6},{8,15},{9,8},{10,9... | collective-permute-start | bytes 1572872 | tf_op jit(solution)/shard_map/ppermute | solution.py:450
  41.4 1.5 %convolution_add_fusion.2 = f32[512,512]{0,1:T(8,128)S(1)} fusion(f32[512,512]{0,1:T(8,128)S(1)} %convolution_add_fusion.3, bf16[512,512]{1,0:T(8,128)(2,1)} %collective-permute-done.9, bf16[512,4096]{1,0:T(8,128)(2,1)S(1)} %copy-done, s32[]{:T(128)S(6)} %select_n.102), kind=kOutput, calls=%fused_computation.5 | convolution fusion | flops 268697600 | bytes 3145732 | tf_op jit(solution)/shard_map/dot_general | solution.py:17
  42.9 1.5 %convolution_add_fusion.6 = f32[512,512]{0,1:T(8,128)S(1)} fusion(f32[512,512]{0,1:T(8,128)S(1)} %convolution_add_fusion.7, bf16[512,512]{1,0:T(8,128)(2,1)} %collective-permute-done.1, bf16[512,4096]{1,0:T(8,128)(2,1)S(1)} %copy-done, s32[]{:T(128)S(6)} %select_n.102), kind=kOutput, calls=%fused_computation.12 | convolution fusion | flops 268697600 | bytes 3145732 | tf_op jit(solution)/shard_map/dot_general | solution.py:17
  44.4 1.9 %collective-permute-start.13 = (bf16[512,512]{1,0:T(8,128)(2,1)S(1)}, bf16[512,512]{1,0:T(8,128)(2,1)S(1)}, u32[]{:S(2)}, u32[]{:S(2)}) collective-permute-start(bf16[512,512]{1,0:T(8,128)(2,1)S(1)} %collective-permute-done.11), channel_id=1, source_target_pairs={{0,7},{1,0},{2,1},{3,2},{4,3},{5,4},{6,5},{7,6},{8,15},{9,8},{10,9... | collective-permute-start | bytes 1572872 | tf_op jit(solution)/shard_map/ppermute | solution.py:450
  46.6 7.5 %collective-permute-done.3 = bf16[512,512]{1,0:T(8,128)(2,1)S(1)} collective-permute-done((bf16[512,512]{1,0:T(8,128)(2,1)}, bf16[512,512]{1,0:T(8,128)(2,1)S(1)}, u32[]{:S(2)}, u32[]{:S(2)}) %collective-permute-start.3) | collective-permute-done | bytes 524320 | tf_op jit(solution)/shard_map/ppermute | solution.py:450
  54.0 3.6 %collective-permute-start.5 = (bf16[512,512]{1,0:T(8,128)(2,1)S(1)}, bf16[512,512]{1,0:T(8,128)(2,1)S(1)}, u32[]{:S(2)}, u32[]{:S(2)}) collective-permute-start(bf16[512,512]{1,0:T(8,128)(2,1)S(1)} %collective-permute-done.3), channel_id=1, source_target_pairs={{0,7},{1,0},{2,1},{3,2},{4,3},{5,4},{6,5},{7,6},{8,15},{9,8},{10,9... | collective-permute-start | bytes 1572872 | tf_op jit(solution)/shard_map/ppermute | solution.py:450
  57.6 0.5 fusion.13
  58.2 0.5 fusion.2
  58.7 0.5 fusion.15
  59.2 0.5 fusion.5
  59.7 5.8 %collective-permute-done.12 = bf16[512,512]{1,0:T(8,128)(2,1)S(1)} collective-permute-done((bf16[512,512]{1,0:T(8,128)(2,1)S(1)}, bf16[512,512]{1,0:T(8,128)(2,1)S(1)}, u32[]{:S(2)}, u32[]{:S(2)}) %collective-permute-start.12) | collective-permute-done | bytes 524320 | tf_op jit(solution)/shard_map/ppermute | solution.py:449
  65.6 3.3 %collective-permute-start.15 = (bf16[256,512]{1,0:T(8,128)(2,1)S(1)}, bf16[256,512]{1,0:T(8,128)(2,1)S(1)}, u32[]{:S(2)}, u32[]{:S(2)}) collective-permute-start(bf16[256,512]{1,0:T(8,128)(2,1)S(1)} %slice.29), channel_id=1, source_target_pairs={{0,7},{1,0},{2,1},{3,2},{4,3},{5,4},{6,5},{7,6},{8,15},{9,8},{10,9... | collective-permute-start | bytes 786440 | tf_op jit(solution)/shard_map/ppermute | solution.py:455
  68.9 7.8 %collective-permute-done.4 = bf16[512,512]{1,0:T(8,128)(2,1)S(1)} collective-permute-done((bf16[512,512]{1,0:T(8,128)(2,1)S(1)}, bf16[512,512]{1,0:T(8,128)(2,1)S(1)}, u32[]{:S(2)}, u32[]{:S(2)}) %collective-permute-start.4) | collective-permute-done | bytes 524320 | tf_op jit(solution)/shard_map/ppermute | solution.py:449
  76.9 3.3 %collective-permute-start.7 = (bf16[256,512]{1,0:T(8,128)(2,1)S(1)}, bf16[256,512]{1,0:T(8,128)(2,1)S(1)}, u32[]{:S(2)}, u32[]{:S(2)}) collective-permute-start(bf16[256,512]{1,0:T(8,128)(2,1)S(1)} %slice.27), channel_id=1, source_target_pairs={{0,7},{1,0},{2,1},{3,2},{4,3},{5,4},{6,5},{7,6},{8,15},{9,8},{10,9... | collective-permute-start | bytes 786440 | tf_op jit(solution)/shard_map/ppermute | solution.py:455
  80.2 0.5 fusion.7
  80.7 0.5 fusion.9
  81.2 0.5 fusion.1.acc_ref
  81.7 0.5 fusion.4.acc_ref
  82.3 1.5 %close_chunk.2 = (bf16[512,512]{1,0:T(8,128)(2,1)S(1)}, f32[2,4,64,128]{3,2,1,0:T(8,128)S(1)}) custom-call(s32[1]{0:T(128)} %bitcast.6.source_ref, f32[5,4]{1,0:T(8,128)S(1)} %pad_maximum_fusion.scale_ref, f32[512,512]{1,0:T(8,128)S(1)} %fusion.1.acc_ref, bf16[256,512]{1,0:T(8,128)(2,1)S(1)} %collective-permute-done.14.up_ref, ...), custom_call_target="tpu_custom_call" | custom-call | flops 600000000 | bytes 4000000 | tf_op jit(solution)/shard_map/close_chunk/pallas_call | solution.py:235
  83.8 2.9 %inside.3 = (f32[256,512]{1,0:T(8,128)S(1)}, f32[256,512]{1,0:T(8,128)S(1)}, f32[1,4,256]{2,1,0:T(4,128)S(1)}) custom-call(f32[1,4]{1,0:T(1,128)S(1)} %bitcast.43, bf16[512,512]{1,0:T(8,128)(2,1)S(1)} %get-tuple-element.53.dy_ref, bf16[1024,512]{1,0:T(8,128)(2,1)} %refs_10_.1, bf16[1024,512]{1,0:T(8,128)(2,1)} %refs_11_.1, ...), custom_call_target="tpu_custom_call" | custom-call | flops 1000000000 | bytes 3500000 | tf_op jit(solution)/shard_map/inside/pallas_call | solution.py:278
  86.7 0.4 collective-permute-done.6.up_ref
  87.1 1.5 %close_chunk.3 = (bf16[512,512]{1,0:T(8,128)(2,1)S(1)}, f32[2,4,64,128]{3,2,1,0:T(8,128)S(1)}, bf16[272,128]{1,0:T(8,128)(2,1)S(1)}) custom-call(s32[1]{0:T(128)} %bitcast.6.source_ref, f32[5,4]{1,0:T(8,128)S(1)} %pad_maximum_fusion.scale_ref, f32[512,512]{1,0:T(8,128)S(1)} %fusion.4.acc_ref, bf16[256,512]{1,0:T(8,128)(2,1)S(1)} %collective-permute-done.6.up_ref, ...), custom_call_target="tpu_custom_call" | custom-call | flops 600000000 | bytes 4000000 | tf_op jit(solution)/shard_map/close_chunk/pallas_call | solution.py:235
  88.8 1.2 %collective-permute-done.16.refs_1_ = bf16[272,128]{1,0:T(8,128)(2,1)S(1)} collective-permute-done((bf16[272,128]{1,0:T(8,128)(2,1)S(1)}, bf16[272,128]{1,0:T(8,128)(2,1)S(1)}, u32[]{:S(2)}, u32[]{:S(2)}) %collective-permute-start.16) | collective-permute-done | bytes 69664 | tf_op jit(solution)/shard_map/ppermute | solution.py:430
  90.0 0.6 combine_core.1.refs_0_.refs_2_
  90.5 1.7 %collective-permute-start.17 = (bf16[272,128]{1,0:T(8,128)(2,1)S(1)}, bf16[272,128]{1,0:T(8,128)(2,1)S(1)}, u32[]{:S(2)}, u32[]{:S(2)}) collective-permute-start(bf16[272,128]{1,0:T(8,128)(2,1)S(1)} %combine_core.1.refs_0_.refs_2_), channel_id=1, source_target_pairs={{0,16},{8,24},{16,32},{24,40},{32,48},{40,56},{48,0},{56,8},{64,80... | collective-permute-start | bytes 208904 | tf_op jit(solution)/shard_map/ppermute | solution.py:433
  92.2 2.9 %collective-permute-start.18 = (bf16[272,128]{1,0:T(8,128)(2,1)S(1)}, bf16[272,128]{1,0:T(8,128)(2,1)S(1)}, u32[]{:S(2)}, u32[]{:S(2)}) collective-permute-start(bf16[272,128]{1,0:T(8,128)(2,1)S(1)} %combine_core.1.refs_0_.refs_2_), channel_id=1, source_target_pairs={{0,32},{8,40},{16,48},{24,56},{32,0},{40,8},{48,16},{56,24},{64,96... | collective-permute-start | bytes 208904 | tf_op jit(solution)/shard_map/ppermute | solution.py:433
  95.1 1.3 %collective-permute-start.19 = (bf16[272,128]{1,0:T(8,128)(2,1)S(1)}, bf16[272,128]{1,0:T(8,128)(2,1)S(1)}, u32[]{:S(2)}, u32[]{:S(2)}) collective-permute-start(bf16[272,128]{1,0:T(8,128)(2,1)S(1)} %combine_core.1.refs_0_.refs_2_), channel_id=1, source_target_pairs={{0,48},{8,56},{16,0},{24,8},{32,16},{40,24},{48,32},{56,40},{64,11... | collective-permute-start | bytes 208904 | tf_op jit(solution)/shard_map/ppermute | solution.py:433
  96.5 2.8 %inside.4 = (f32[256,512]{1,0:T(8,128)S(1)}, f32[256,512]{1,0:T(8,128)S(1)}, f32[1,4,256]{2,1,0:T(4,128)S(1)}) custom-call(f32[1,4]{1,0:T(1,128)S(1)} %bitcast.44, bf16[512,512]{1,0:T(8,128)(2,1)S(1)} %get-tuple-element.53.dy_ref, bf16[1024,512]{1,0:T(8,128)(2,1)} %refs_10_.1, bf16[1024,512]{1,0:T(8,128)(2,1)} %refs_11_.1, ...), custom_call_target="tpu_custom_call" | custom-call | flops 1000000000 | bytes 3500000 | tf_op jit(solution)/shard_map/inside/pallas_call | solution.py:278
  99.4 0.6 combine_row.1.refs_6_
  100.0 1.6 %collective-permute-start.20 = (bf16[272,128]{1,0:T(8,128)(2,1)S(1)}, bf16[272,128]{1,0:T(8,128)(2,1)S(1)}, u32[]{:S(2)}, u32[]{:S(2)}) collective-permute-start(bf16[272,128]{1,0:T(8,128)(2,1)S(1)} %combine_row.1.refs_6_), channel_id=1, source_target_pairs={{0,64},{8,72},{16,80},{24,88},{32,96},{40,104},{48,112},{56,120},{... | collective-permute-start | bytes 208904 | tf_op jit(solution)/shard_map/ppermute | solution.py:436
  101.6 1.1 collective-permute-start.21
  102.7 2.2 %collective-permute-start.22 = (bf16[272,128]{1,0:T(8,128)(2,1)S(1)}, bf16[272,128]{1,0:T(8,128)(2,1)S(1)}, u32[]{:S(2)}, u32[]{:S(2)}) collective-permute-start(bf16[272,128]{1,0:T(8,128)(2,1)S(1)} %combine_row.1.refs_6_), channel_id=1, source_target_pairs={{0,192},{8,200},{16,208},{24,216},{32,224},{40,232},{48,240},{56,2... | collective-permute-start | bytes 208904 | tf_op jit(solution)/shard_map/ppermute | solution.py:436
  104.9 4.3 %inside.5 = (f32[512,512]{1,0:T(8,128)S(1)}, f32[512,512]{1,0:T(8,128)S(1)}, f32[2,4,256]{2,1,0:T(4,128)S(1)}) custom-call(f32[1,4]{1,0:T(1,128)S(1)} %bitcast.45, bf16[512,512]{1,0:T(8,128)(2,1)S(1)} %get-tuple-element.57.dy_ref, bf16[1024,512]{1,0:T(8,128)(2,1)} %refs_10_.1, bf16[1024,512]{1,0:T(8,128)(2,1)} %refs_11_.1, ...), custom_call_target="tpu_custom_call" | custom-call | flops 2000000000 | bytes 7000000 | tf_op jit(solution)/shard_map/inside/pallas_call | solution.py:278
  109.2 5.4 %finish.1 = (bf16[1024,512]{1,0:T(8,128)(2,1)}, f32[1024,512]{1,0:T(8,128)}, f32[4,1024]{1,0:T(4,128)}) custom-call(s32[3]{0:T(128)S(1)} %pad_add_fusion.place_ref, f32[4,4]{1,0:T(4,128)S(1)} %bitcast.42, bf16[272,128]{1,0:T(8,128)(2,1)S(1)} %get-tuple-element.44.refs_0_, bf16[272,128]{1,0:T(8,128)(2,1)S(1)} %collective-permute-done.16.refs_1_, ...), custom_call_target="tpu_custom_call" | custom-call | flops 600000000 | bytes 11000000 | tf_op jit(solution)/shard_map/finish/pallas_call | solution.py:383
  (50 shorter events, 1.6 us)
Async XLA Ops:
  1.9 18.8 %collective-permute-start.8 = (bf16[512,512]{1,0:T(8,128)(2,1)S(1)}, bf16[512,512]{1,0:T(8,128)(2,1)}, u32[]{:S(2)}, u32[]{:S(2)}) collective-permute-start(bf16[512,512]{1,0:T(8,128)(2,1)S(1)} %get-tuple-element.33), channel_id=1, source_target_pairs={{0,1},{1,2},{2,3},{3,4},{4,5},{5,6},{6,7},{7,0},{8,9},{9,10},{10,1... | collective-permute-start | bytes 1572872 | tf_op jit(solution)/shard_map/ppermute | solution.py:449
  3.8 16.8 %collective-permute-start.9 = (bf16[512,512]{1,0:T(8,128)(2,1)S(1)}, bf16[512,512]{1,0:T(8,128)(2,1)}, u32[]{:S(2)}, u32[]{:S(2)}) collective-permute-start(bf16[512,512]{1,0:T(8,128)(2,1)S(1)} %get-tuple-element.33), channel_id=1, source_target_pairs={{0,7},{1,0},{2,1},{3,2},{4,3},{5,4},{6,5},{7,6},{8,15},{9,8},{10,9... | collective-permute-start | bytes 1572872 | tf_op jit(solution)/shard_map/ppermute | solution.py:450
  7.9 23.9 %collective-permute-start = (bf16[512,512]{1,0:T(8,128)(2,1)S(1)}, bf16[512,512]{1,0:T(8,128)(2,1)S(1)}, u32[]{:S(2)}, u32[]{:S(2)}) collective-permute-start(bf16[512,512]{1,0:T(8,128)(2,1)S(1)} %get-tuple-element.32), channel_id=1, source_target_pairs={{0,1},{1,2},{2,3},{3,4},{4,5},{5,6},{6,7},{7,0},{8,9},{9,10},{10,1... | collective-permute-start | bytes 1572872 | tf_op jit(solution)/shard_map/ppermute | solution.py:449
  7.9 30.2 %collective-permute-start.1 = (bf16[512,512]{1,0:T(8,128)(2,1)S(1)}, bf16[512,512]{1,0:T(8,128)(2,1)}, u32[]{:S(2)}, u32[]{:S(2)}) collective-permute-start(bf16[512,512]{1,0:T(8,128)(2,1)S(1)} %get-tuple-element.32), channel_id=1, source_target_pairs={{0,7},{1,0},{2,1},{3,2},{4,3},{5,4},{6,5},{7,6},{8,15},{9,8},{10,9... | collective-permute-start | bytes 1572872 | tf_op jit(solution)/shard_map/ppermute | solution.py:450
  12.8 18.9 %copy-start = (bf16[512,4096]{1,0:T(8,128)(2,1)S(1)}, bf16[512,4096]{1,0:T(8,128)(2,1)}, u32[]{:S(2)}) copy-start(bf16[512,4096]{1,0:T(8,128)(2,1)} %weight_ref.3) | copy-start | bytes 12582916
  14.5 19.3 %copy-start.1 = (bf16[1024,512]{1,0:T(8,128)(2,1)S(1)}, bf16[1024,512]{1,0:T(8,128)(2,1)}, u32[]{:S(2)}) copy-start(bf16[1024,512]{1,0:T(8,128)(2,1)} %refs_11_.1) | copy-start | bytes 3145732
  14.5 19.3 %copy-start.3 = (f32[4,4,64,128]{3,2,1,0:T(8,128)S(1)}, f32[4,4,64,128]{3,2,1,0:T(8,128)}, u32[]{:S(2)}) copy-start(f32[4,4,64,128]{3,2,1,0:T(8,128)} %refs_15_.1) | copy-start | bytes 1572868
  20.6 25.7 %collective-permute-start.10 = (bf16[512,512]{1,0:T(8,128)(2,1)}, bf16[512,512]{1,0:T(8,128)(2,1)S(1)}, u32[]{:S(2)}, u32[]{:S(2)}) collective-permute-start(bf16[512,512]{1,0:T(8,128)(2,1)} %collective-permute-done.8), channel_id=1, source_target_pairs={{0,1},{1,2},{2,3},{3,4},{4,5},{5,6},{6,7},{7,0},{8,9},{9,10},{10,1... | collective-permute-start | bytes 1572872 | tf_op jit(solution)/shard_map/ppermute | solution.py:449
  20.7 23.8 %collective-permute-start.11 = (bf16[512,512]{1,0:T(8,128)(2,1)}, bf16[512,512]{1,0:T(8,128)(2,1)S(1)}, u32[]{:S(2)}, u32[]{:S(2)}) collective-permute-start(bf16[512,512]{1,0:T(8,128)(2,1)} %collective-permute-done.9), channel_id=1, source_target_pairs={{0,7},{1,0},{2,1},{3,2},{4,3},{5,4},{6,5},{7,6},{8,15},{9,8},{10,9... | collective-permute-start | bytes 1572872 | tf_op jit(solution)/shard_map/ppermute | solution.py:450
  31.8 26.3 %collective-permute-start.2 = (bf16[512,512]{1,0:T(8,128)(2,1)S(1)}, bf16[512,512]{1,0:T(8,128)(2,1)S(1)}, u32[]{:S(2)}, u32[]{:S(2)}) collective-permute-start(bf16[512,512]{1,0:T(8,128)(2,1)S(1)} %collective-permute-done), channel_id=1, source_target_pairs={{0,1},{1,2},{2,3},{3,4},{4,5},{5,6},{6,7},{7,0},{8,9},{9,10},{10,1... | collective-permute-start | bytes 1572872 | tf_op jit(solution)/shard_map/ppermute | solution.py:449
  38.1 16.0 %collective-permute-start.3 = (bf16[512,512]{1,0:T(8,128)(2,1)}, bf16[512,512]{1,0:T(8,128)(2,1)S(1)}, u32[]{:S(2)}, u32[]{:S(2)}) collective-permute-start(bf16[512,512]{1,0:T(8,128)(2,1)} %collective-permute-done.1), channel_id=1, source_target_pairs={{0,7},{1,0},{2,1},{3,2},{4,3},{5,4},{6,5},{7,6},{8,15},{9,8},{10,9... | collective-permute-start | bytes 1572872 | tf_op jit(solution)/shard_map/ppermute | solution.py:450
  44.4 21.1 %collective-permute-start.13 = (bf16[512,512]{1,0:T(8,128)(2,1)S(1)}, bf16[512,512]{1,0:T(8,128)(2,1)S(1)}, u32[]{:S(2)}, u32[]{:S(2)}) collective-permute-start(bf16[512,512]{1,0:T(8,128)(2,1)S(1)} %collective-permute-done.11), channel_id=1, source_target_pairs={{0,7},{1,0},{2,1},{3,2},{4,3},{5,4},{6,5},{7,6},{8,15},{9,8},{10,9... | collective-permute-start | bytes 1572872 | tf_op jit(solution)/shard_map/ppermute | solution.py:450
  46.4 19.1 %collective-permute-start.12 = (bf16[512,512]{1,0:T(8,128)(2,1)S(1)}, bf16[512,512]{1,0:T(8,128)(2,1)S(1)}, u32[]{:S(2)}, u32[]{:S(2)}) collective-permute-start(bf16[512,512]{1,0:T(8,128)(2,1)S(1)} %collective-permute-done.10), channel_id=1, source_target_pairs={{0,1},{1,2},{2,3},{3,4},{4,5},{5,6},{6,7},{7,0},{8,9},{9,10},{10,1... | collective-permute-start | bytes 1572872 | tf_op jit(solution)/shard_map/ppermute | solution.py:449
  54.0 22.8 %collective-permute-start.5 = (bf16[512,512]{1,0:T(8,128)(2,1)S(1)}, bf16[512,512]{1,0:T(8,128)(2,1)S(1)}, u32[]{:S(2)}, u32[]{:S(2)}) collective-permute-start(bf16[512,512]{1,0:T(8,128)(2,1)S(1)} %collective-permute-done.3), channel_id=1, source_target_pairs={{0,7},{1,0},{2,1},{3,2},{4,3},{5,4},{6,5},{7,6},{8,15},{9,8},{10,9... | collective-permute-start | bytes 1572872 | tf_op jit(solution)/shard_map/ppermute | solution.py:450
  58.1 18.6 %collective-permute-start.4 = (bf16[512,512]{1,0:T(8,128)(2,1)S(1)}, bf16[512,512]{1,0:T(8,128)(2,1)S(1)}, u32[]{:S(2)}, u32[]{:S(2)}) collective-permute-start(bf16[512,512]{1,0:T(8,128)(2,1)S(1)} %collective-permute-done.2), channel_id=1, source_target_pairs={{0,1},{1,2},{2,3},{3,4},{4,5},{5,6},{6,7},{7,0},{8,9},{9,10},{10,1... | collective-permute-start | bytes 1572872 | tf_op jit(solution)/shard_map/ppermute | solution.py:449
  65.5 16.8 %collective-permute-start.14 = (bf16[256,512]{1,0:T(8,128)(2,1)S(1)}, bf16[256,512]{1,0:T(8,128)(2,1)S(1)}, u32[]{:S(2)}, u32[]{:S(2)}) collective-permute-start(bf16[256,512]{1,0:T(8,128)(2,1)S(1)} %slice.28), channel_id=1, source_target_pairs={{0,1},{1,2},{2,3},{3,4},{4,5},{5,6},{6,7},{7,0},{8,9},{9,10},{10,1... | collective-permute-start | bytes 786440 | tf_op jit(solution)/shard_map/ppermute | solution.py:454
  65.6 16.7 %collective-permute-start.15 = (bf16[256,512]{1,0:T(8,128)(2,1)S(1)}, bf16[256,512]{1,0:T(8,128)(2,1)S(1)}, u32[]{:S(2)}, u32[]{:S(2)}) collective-permute-start(bf16[256,512]{1,0:T(8,128)(2,1)S(1)} %slice.29), channel_id=1, source_target_pairs={{0,7},{1,0},{2,1},{3,2},{4,3},{5,4},{6,5},{7,6},{8,15},{9,8},{10,9... | collective-permute-start | bytes 786440 | tf_op jit(solution)/shard_map/ppermute | solution.py:455
  76.7 10.4 %collective-permute-start.6 = (bf16[256,512]{1,0:T(8,128)(2,1)S(1)}, bf16[256,512]{1,0:T(8,128)(2,1)S(1)}, u32[]{:S(2)}, u32[]{:S(2)}) collective-permute-start(bf16[256,512]{1,0:T(8,128)(2,1)S(1)} %slice.26), channel_id=1, source_target_pairs={{0,1},{1,2},{2,3},{3,4},{4,5},{5,6},{6,7},{7,0},{8,9},{9,10},{10,1... | collective-permute-start | bytes 786440 | tf_op jit(solution)/shard_map/ppermute | solution.py:454
  76.9 10.3 %collective-permute-start.7 = (bf16[256,512]{1,0:T(8,128)(2,1)S(1)}, bf16[256,512]{1,0:T(8,128)(2,1)S(1)}, u32[]{:S(2)}, u32[]{:S(2)}) collective-permute-start(bf16[256,512]{1,0:T(8,128)(2,1)S(1)} %slice.27), channel_id=1, source_target_pairs={{0,7},{1,0},{2,1},{3,2},{4,3},{5,4},{6,5},{7,6},{8,15},{9,8},{10,9... | collective-permute-start | bytes 786440 | tf_op jit(solution)/shard_map/ppermute | solution.py:455
  81.2 1.2 %copy-start.2 = (bf16[4,4,64,256]{3,2,1,0:T(8,128)(2,1)S(1)}, bf16[4,4,64,256]{3,2,1,0:T(8,128)(2,1)}, u32[]{:S(2)}) copy-start(bf16[4,4,64,256]{3,2,1,0:T(8,128)(2,1)} %get-tuple-element.35.wct_ref) | copy-start | bytes 1572868
  82.2 1.6 %copy-start.4 = (f32[4]{0:T(128)S(1)}, f32[4]{0:T(128)}, u32[]{:S(2)}) copy-start(f32[4]{0:T(128)} %param.13) | copy-start | bytes 52
  88.6 1.3 %collective-permute-start.16 = (bf16[272,128]{1,0:T(8,128)(2,1)S(1)}, bf16[272,128]{1,0:T(8,128)(2,1)S(1)}, u32[]{:S(2)}, u32[]{:S(2)}) collective-permute-start(bf16[272,128]{1,0:T(8,128)(2,1)S(1)} %get-tuple-element.44.refs_0_), channel_id=1, source_target_pairs={{0,8},{8,0},{16,24},{24,16},{32,40},{40,32},{48,56},{56,48},{64,72... | collective-permute-start | bytes 208904 | tf_op jit(solution)/shard_map/ppermute | solution.py:430
  90.5 8.8 %collective-permute-start.17 = (bf16[272,128]{1,0:T(8,128)(2,1)S(1)}, bf16[272,128]{1,0:T(8,128)(2,1)S(1)}, u32[]{:S(2)}, u32[]{:S(2)}) collective-permute-start(bf16[272,128]{1,0:T(8,128)(2,1)S(1)} %combine_core.1.refs_0_.refs_2_), channel_id=1, source_target_pairs={{0,16},{8,24},{16,32},{24,40},{32,48},{40,56},{48,0},{56,8},{64,80... | collective-permute-start | bytes 208904 | tf_op jit(solution)/shard_map/ppermute | solution.py:433
  92.2 7.1 %collective-permute-start.18 = (bf16[272,128]{1,0:T(8,128)(2,1)S(1)}, bf16[272,128]{1,0:T(8,128)(2,1)S(1)}, u32[]{:S(2)}, u32[]{:S(2)}) collective-permute-start(bf16[272,128]{1,0:T(8,128)(2,1)S(1)} %combine_core.1.refs_0_.refs_2_), channel_id=1, source_target_pairs={{0,32},{8,40},{16,48},{24,56},{32,0},{40,8},{48,16},{56,24},{64,96... | collective-permute-start | bytes 208904 | tf_op jit(solution)/shard_map/ppermute | solution.py:433
  95.1 4.3 %collective-permute-start.19 = (bf16[272,128]{1,0:T(8,128)(2,1)S(1)}, bf16[272,128]{1,0:T(8,128)(2,1)S(1)}, u32[]{:S(2)}, u32[]{:S(2)}) collective-permute-start(bf16[272,128]{1,0:T(8,128)(2,1)S(1)} %combine_core.1.refs_0_.refs_2_), channel_id=1, source_target_pairs={{0,48},{8,56},{16,0},{24,8},{32,16},{40,24},{48,32},{56,40},{64,11... | collective-permute-start | bytes 208904 | tf_op jit(solution)/shard_map/ppermute | solution.py:433
  100.0 9.1 %collective-permute-start.20 = (bf16[272,128]{1,0:T(8,128)(2,1)S(1)}, bf16[272,128]{1,0:T(8,128)(2,1)S(1)}, u32[]{:S(2)}, u32[]{:S(2)}) collective-permute-start(bf16[272,128]{1,0:T(8,128)(2,1)S(1)} %combine_row.1.refs_6_), channel_id=1, source_target_pairs={{0,64},{8,72},{16,80},{24,88},{32,96},{40,104},{48,112},{56,120},{... | collective-permute-start | bytes 208904 | tf_op jit(solution)/shard_map/ppermute | solution.py:436
  101.6 7.6 %collective-permute-start.21 = (bf16[272,128]{1,0:T(8,128)(2,1)S(1)}, bf16[272,128]{1,0:T(8,128)(2,1)S(1)}, u32[]{:S(2)}, u32[]{:S(2)}) collective-permute-start(bf16[272,128]{1,0:T(8,128)(2,1)S(1)} %combine_row.1.refs_6_), channel_id=1, source_target_pairs={{0,128},{8,136},{16,144},{24,152},{32,160},{40,168},{48,176},{56,1... | collective-permute-start | bytes 208904 | tf_op jit(solution)/shard_map/ppermute | solution.py:436
  102.7 6.5 %collective-permute-start.22 = (bf16[272,128]{1,0:T(8,128)(2,1)S(1)}, bf16[272,128]{1,0:T(8,128)(2,1)S(1)}, u32[]{:S(2)}, u32[]{:S(2)}) collective-permute-start(bf16[272,128]{1,0:T(8,128)(2,1)S(1)} %combine_row.1.refs_6_), channel_id=1, source_target_pairs={{0,192},{8,200},{16,208},{24,216},{32,224},{40,232},{48,240},{56,2... | collective-permute-start | bytes 208904 | tf_op jit(solution)/shard_map/ppermute | solution.py:436

commit v7 on v6

--- a/solution.py
+++ b/solution.py
@@ -356,12 +356,14 @@
                 carry16 = carry.astype(BF16)
                 tail = fall_ref[:, h : h + 1]
                 bc_h = bc_ref[:, lanes].astype(F32)
-                weighted = (bc_h * tail).astype(BF16)[:, :STATE]
+                fallen = bc_h * tail
+                weighted = fallen.astype(BF16)[:, :STATE]
                 out_ref[:, lanes] = (dx_ref[here, lanes] + dot(weighted, carry16, NN)).astype(BF16)
                 padded = jnp.concatenate([carry16, jnp.zeros_like(carry16)], axis=0)
-                extra = tail * dot(x_ref[:, lanes], padded, NT)
+                reached = dot(x_ref[:, lanes], padded, NT)
+                extra = tail * reached
                 outbc_ref[:, lanes] = dbc_ref[here, lanes] + extra
-                moved = jnp.sum(extra * bc_h, axis=1, keepdims=True)
+                moved = jnp.sum(reached * fallen, axis=1, keepdims=True)
                 ends = jnp.exp(jnp.full((1, HEAD_DIM), last_ref[b, h], F32))
                 whole = jnp.sum(jnp.sum(states_ref[0, h] * carry, axis=0, keepdims=True) * ends)
                 outlog_ref[h : h + 1, :] = (

time: 116 us -> 116 us (level)
  no operation moved by 1% of the time
where the time goes in v7:
time: 116 us; the launch traced here: 115 us
  starting transfers between devices  39.3 us (34%)
  waiting for transfers between devices  35.1 us (30%)
  Pallas kernels  25 us (22%)
  matrix products  12.4 us (11%)
  local copies, waits for them, and re-layouts  1.39 us (1%)
    ppermute x6, waiting for transfers between devices, per_device(): right = lax.ppermute(right, 'tp', shift(tp, 1))  25.8 us
    ppermute x6, starting transfers between devices, per_device(): left = lax.ppermute(left, 'tp', shift(tp, -1))  19.4 us
    dot_general x14, matrix products, dot(): return lax.dot_general(a, b, (dims, ((), ())), preferred_element_type=F32)  12.3 us
    pallas_call x3, Pallas kernels, inside(): pl.pallas_call(body, name='inside', grid=(count,), in_specs=[pl.BlockSpec...  9.97 us
    ppermute x6, waiting for transfers between devices, per_device(): left = lax.ppermute(left, 'tp', shift(tp, -1))  7.48 us
    ppermute x2, starting transfers between devices, per_device(): down = lax.ppermute(left[BLOCK:], 'tp', shift(tp, -1))  6.61 us
    ppermute x3, starting transfers between devices, from_y(): return [lax.ppermute(a, 'ctx', perm(0, s, 0)) for s in (1, 2, 3)]  5.9 us
    pallas_call x1, Pallas kernels, finish(): pl.pallas_call(body, name='finish', grid=(blocks,), in_specs=[smem, smem]...  5.42 us
  transfers between devices with their start and end apart: 23, of which 9 were waited for; matrix products, arithmetic and copies ran while one was open for 12% of the time, Pallas kernels for 14%

profile of v7, /device:TPU:2, one launch (start us, length us, event | category | flops | bytes accessed | tf_op | source)
XLA Modules:
  0.0 114.6 jit_solution(18046075666756472120)
XLA Ops:
  0.6 1.2 %split_rows.1 = (bf16[512,512]{1,0:T(8,128)(2,1)S(1)}, bf16[512,512]{1,0:T(8,128)(2,1)S(1)}) custom-call(bf16[1024,512]{1,0:T(8,128)(2,1)} %source_ref.1), custom_call_target="tpu_custom_call" | custom-call | bytes 2097152 | tf_op jit(solution)/shard_map/split_rows/pallas_call | solution.py:183
  1.9 2.0 %collective-permute-start.8 = (bf16[512,512]{1,0:T(8,128)(2,1)S(1)}, bf16[512,512]{1,0:T(8,128)(2,1)}, u32[]{:S(2)}, u32[]{:S(2)}) collective-permute-start(bf16[512,512]{1,0:T(8,128)(2,1)S(1)} %get-tuple-element.33), channel_id=1, source_target_pairs={{0,1},{1,2},{2,3},{3,4},{4,5},{5,6},{6,7},{7,0},{8,9},{9,10},{10,1... | collective-permute-start | bytes 1572872 | tf_op jit(solution)/shard_map/ppermute | solution.py:451
  3.8 4.0 %collective-permute-start.9 = (bf16[512,512]{1,0:T(8,128)(2,1)S(1)}, bf16[512,512]{1,0:T(8,128)(2,1)}, u32[]{:S(2)}, u32[]{:S(2)}) collective-permute-start(bf16[512,512]{1,0:T(8,128)(2,1)S(1)} %get-tuple-element.33), channel_id=1, source_target_pairs={{0,7},{1,0},{2,1},{3,2},{4,3},{5,4},{6,5},{7,6},{8,15},{9,8},{10,9... | collective-permute-start | bytes 1572872 | tf_op jit(solution)/shard_map/ppermute | solution.py:452
  7.9 3.2 %collective-permute-start.1 = (bf16[512,512]{1,0:T(8,128)(2,1)S(1)}, bf16[512,512]{1,0:T(8,128)(2,1)}, u32[]{:S(2)}, u32[]{:S(2)}) collective-permute-start(bf16[512,512]{1,0:T(8,128)(2,1)S(1)} %get-tuple-element.32), channel_id=1, source_target_pairs={{0,7},{1,0},{2,1},{3,2},{4,3},{5,4},{6,5},{7,6},{8,15},{9,8},{10,9... | collective-permute-start | bytes 1572872 | tf_op jit(solution)/shard_map/ppermute | solution.py:452
  11.1 0.7 reshape.15
  12.3 0.2 copy.37
  12.9 1.7 %fusion.23 = f32[512,512]{0,1:T(8,128)S(1)} fusion(bf16[512,512]{1,0:T(8,128)(2,1)S(1)} %get-tuple-element.33, bf16[512,4096]{1,0:T(8,128)(2,1)} %weight_ref.3, s32[]{:T(128)S(6)} %select_n.98), kind=kOutput, calls=%fused_computation.33 | convolution fusion | flops 268435456 | bytes 2097156 | tf_op jit(solution)/shard_map/dot_general | solution.py:17
  14.5 1.6 %fusion.25 = f32[512,512]{0,1:T(8,128)S(1)} fusion(bf16[512,512]{1,0:T(8,128)(2,1)S(1)} %get-tuple-element.32, bf16[512,4096]{1,0:T(8,128)(2,1)} %weight_ref.3, s32[]{:T(128)S(6)} %select_n.98), kind=kOutput, calls=%fused_computation.35 | convolution fusion | flops 268435456 | bytes 2097156 | tf_op jit(solution)/shard_map/dot_general | solution.py:17
  16.2 4.5 %collective-permute-done.8 = bf16[512,512]{1,0:T(8,128)(2,1)} collective-permute-done((bf16[512,512]{1,0:T(8,128)(2,1)S(1)}, bf16[512,512]{1,0:T(8,128)(2,1)}, u32[]{:S(2)}, u32[]{:S(2)}) %collective-permute-start.8) | collective-permute-done | bytes 524320 | tf_op jit(solution)/shard_map/ppermute | solution.py:451
  20.7 3.4 %collective-permute-start.11 = (bf16[512,512]{1,0:T(8,128)(2,1)}, bf16[512,512]{1,0:T(8,128)(2,1)S(1)}, u32[]{:S(2)}, u32[]{:S(2)}) collective-permute-start(bf16[512,512]{1,0:T(8,128)(2,1)} %collective-permute-done.9), channel_id=1, source_target_pairs={{0,7},{1,0},{2,1},{3,2},{4,3},{5,4},{6,5},{7,6},{8,15},{9,8},{10,9... | collective-permute-start | bytes 1572872 | tf_op jit(solution)/shard_map/ppermute | solution.py:452
  24.0 7.8 %collective-permute-done = bf16[512,512]{1,0:T(8,128)(2,1)S(1)} collective-permute-done((bf16[512,512]{1,0:T(8,128)(2,1)S(1)}, bf16[512,512]{1,0:T(8,128)(2,1)S(1)}, u32[]{:S(2)}, u32[]{:S(2)}) %collective-permute-start) | collective-permute-done | bytes 524320 | tf_op jit(solution)/shard_map/ppermute | solution.py:451
  31.8 1.5 %convolution_add_fusion.3 = f32[512,512]{0,1:T(8,128)S(1)} fusion(f32[512,512]{0,1:T(8,128)S(1)} %fusion.23, bf16[512,512]{1,0:T(8,128)(2,1)} %collective-permute-done.8, bf16[512,4096]{1,0:T(8,128)(2,1)S(1)} %copy-done, s32[]{:T(128)S(6)} %select_n.100), kind=kOutput, calls=%fused_computation.6 | convolution fusion | flops 268697600 | bytes 3145732 | tf_op jit(solution)/shard_map/dot_general | solution.py:17
  33.3 0.5 convolution_add_fusion.7
  33.8 4.2 %prepare.1 = (bf16[1024,512]{1,0:T(8,128)(2,1)}, bf16[4,4,256,256]{3,2,1,0:T(8,128)(2,1)}, bf16[4,4,256,256]{3,2,1,0:T(8,128)(2,1)}, bf16[4,4,64,256]{3,2,1,0:T(8,128)(2,1)}, bf16[4,4,128,128]{3,2,1,0:T(8,128)(2,1)}) custom-call(bf16[1024,512]{1,0:T(8,128)(2,1)S(1)} %copy-done.1, f32[4,1024]{1,0:T(4,128)S(1)} %reshape_reshape.3.arow_ref, ...), custom_call_target="tpu_custom_call" | custom-call | flops 4000000000 | bytes 9000000 | tf_op jit(solution)/shard_map/prepare/pallas_call | solution.py:135
  38.1 3.3 %collective-permute-start.3 = (bf16[512,512]{1,0:T(8,128)(2,1)}, bf16[512,512]{1,0:T(8,128)(2,1)S(1)}, u32[]{:S(2)}, u32[]{:S(2)}) collective-permute-start(bf16[512,512]{1,0:T(8,128)(2,1)} %collective-permute-done.1), channel_id=1, source_target_pairs={{0,7},{1,0},{2,1},{3,2},{4,3},{5,4},{6,5},{7,6},{8,15},{9,8},{10,9... | collective-permute-start | bytes 1572872 | tf_op jit(solution)/shard_map/ppermute | solution.py:452
  41.4 1.5 %convolution_add_fusion.2 = f32[512,512]{0,1:T(8,128)S(1)} fusion(f32[512,512]{0,1:T(8,128)S(1)} %convolution_add_fusion.3, bf16[512,512]{1,0:T(8,128)(2,1)} %collective-permute-done.9, bf16[512,4096]{1,0:T(8,128)(2,1)S(1)} %copy-done, s32[]{:T(128)S(6)} %select_n.102), kind=kOutput, calls=%fused_computation.5 | convolution fusion | flops 268697600 | bytes 3145732 | tf_op jit(solution)/shard_map/dot_general | solution.py:17
  42.9 1.5 %convolution_add_fusion.6 = f32[512,512]{0,1:T(8,128)S(1)} fusion(f32[512,512]{0,1:T(8,128)S(1)} %convolution_add_fusion.7, bf16[512,512]{1,0:T(8,128)(2,1)} %collective-permute-done.1, bf16[512,4096]{1,0:T(8,128)(2,1)S(1)} %copy-done, s32[]{:T(128)S(6)} %select_n.102), kind=kOutput, calls=%fused_computation.12 | convolution fusion | flops 268697600 | bytes 3145732 | tf_op jit(solution)/shard_map/dot_general | solution.py:17
  44.4 1.9 %collective-permute-start.13 = (bf16[512,512]{1,0:T(8,128)(2,1)S(1)}, bf16[512,512]{1,0:T(8,128)(2,1)S(1)}, u32[]{:S(2)}, u32[]{:S(2)}) collective-permute-start(bf16[512,512]{1,0:T(8,128)(2,1)S(1)} %collective-permute-done.11), channel_id=1, source_target_pairs={{0,7},{1,0},{2,1},{3,2},{4,3},{5,4},{6,5},{7,6},{8,15},{9,8},{10,9... | collective-permute-start | bytes 1572872 | tf_op jit(solution)/shard_map/ppermute | solution.py:452
  46.6 7.5 %collective-permute-done.3 = bf16[512,512]{1,0:T(8,128)(2,1)S(1)} collective-permute-done((bf16[512,512]{1,0:T(8,128)(2,1)}, bf16[512,512]{1,0:T(8,128)(2,1)S(1)}, u32[]{:S(2)}, u32[]{:S(2)}) %collective-permute-start.3) | collective-permute-done | bytes 524320 | tf_op jit(solution)/shard_map/ppermute | solution.py:452
  54.0 3.6 %collective-permute-start.5 = (bf16[512,512]{1,0:T(8,128)(2,1)S(1)}, bf16[512,512]{1,0:T(8,128)(2,1)S(1)}, u32[]{:S(2)}, u32[]{:S(2)}) collective-permute-start(bf16[512,512]{1,0:T(8,128)(2,1)S(1)} %collective-permute-done.3), channel_id=1, source_target_pairs={{0,7},{1,0},{2,1},{3,2},{4,3},{5,4},{6,5},{7,6},{8,15},{9,8},{10,9... | collective-permute-start | bytes 1572872 | tf_op jit(solution)/shard_map/ppermute | solution.py:452
  57.6 0.5 fusion.13
  58.2 0.5 fusion.2
  58.7 0.5 fusion.15
  59.2 0.5 fusion.5
  59.7 5.8 %collective-permute-done.12 = bf16[512,512]{1,0:T(8,128)(2,1)S(1)} collective-permute-done((bf16[512,512]{1,0:T(8,128)(2,1)S(1)}, bf16[512,512]{1,0:T(8,128)(2,1)S(1)}, u32[]{:S(2)}, u32[]{:S(2)}) %collective-permute-start.12) | collective-permute-done | bytes 524320 | tf_op jit(solution)/shard_map/ppermute | solution.py:451
  65.6 3.3 %collective-permute-start.15 = (bf16[256,512]{1,0:T(8,128)(2,1)S(1)}, bf16[256,512]{1,0:T(8,128)(2,1)S(1)}, u32[]{:S(2)}, u32[]{:S(2)}) collective-permute-start(bf16[256,512]{1,0:T(8,128)(2,1)S(1)} %slice.29), channel_id=1, source_target_pairs={{0,7},{1,0},{2,1},{3,2},{4,3},{5,4},{6,5},{7,6},{8,15},{9,8},{10,9... | collective-permute-start | bytes 786440 | tf_op jit(solution)/shard_map/ppermute | solution.py:457
  68.9 7.8 %collective-permute-done.4 = bf16[512,512]{1,0:T(8,128)(2,1)S(1)} collective-permute-done((bf16[512,512]{1,0:T(8,128)(2,1)S(1)}, bf16[512,512]{1,0:T(8,128)(2,1)S(1)}, u32[]{:S(2)}, u32[]{:S(2)}) %collective-permute-start.4) | collective-permute-done | bytes 524320 | tf_op jit(solution)/shard_map/ppermute | solution.py:451
  76.9 3.3 %collective-permute-start.7 = (bf16[256,512]{1,0:T(8,128)(2,1)S(1)}, bf16[256,512]{1,0:T(8,128)(2,1)S(1)}, u32[]{:S(2)}, u32[]{:S(2)}) collective-permute-start(bf16[256,512]{1,0:T(8,128)(2,1)S(1)} %slice.27), channel_id=1, source_target_pairs={{0,7},{1,0},{2,1},{3,2},{4,3},{5,4},{6,5},{7,6},{8,15},{9,8},{10,9... | collective-permute-start | bytes 786440 | tf_op jit(solution)/shard_map/ppermute | solution.py:457
  80.2 0.5 fusion.7
  80.7 0.5 fusion.9
  81.2 0.5 fusion.1.acc_ref
  81.7 0.5 fusion.4.acc_ref
  82.3 1.5 %close_chunk.2 = (bf16[512,512]{1,0:T(8,128)(2,1)S(1)}, f32[2,4,64,128]{3,2,1,0:T(8,128)S(1)}) custom-call(s32[1]{0:T(128)} %bitcast.6.source_ref, f32[5,4]{1,0:T(8,128)S(1)} %pad_maximum_fusion.scale_ref, f32[512,512]{1,0:T(8,128)S(1)} %fusion.1.acc_ref, bf16[256,512]{1,0:T(8,128)(2,1)S(1)} %collective-permute-done.14.up_ref, ...), custom_call_target="tpu_custom_call" | custom-call | flops 600000000 | bytes 4000000 | tf_op jit(solution)/shard_map/close_chunk/pallas_call | solution.py:235
  83.8 2.9 %inside.3 = (f32[256,512]{1,0:T(8,128)S(1)}, f32[256,512]{1,0:T(8,128)S(1)}, f32[1,4,256]{2,1,0:T(4,128)S(1)}) custom-call(f32[1,4]{1,0:T(1,128)S(1)} %bitcast.43, bf16[512,512]{1,0:T(8,128)(2,1)S(1)} %get-tuple-element.53.dy_ref, bf16[1024,512]{1,0:T(8,128)(2,1)} %refs_10_.1, bf16[1024,512]{1,0:T(8,128)(2,1)} %refs_11_.1, ...), custom_call_target="tpu_custom_call" | custom-call | flops 1000000000 | bytes 3500000 | tf_op jit(solution)/shard_map/inside/pallas_call | solution.py:278
  86.7 0.4 collective-permute-done.6.up_ref
  87.1 1.5 %close_chunk.3 = (bf16[512,512]{1,0:T(8,128)(2,1)S(1)}, f32[2,4,64,128]{3,2,1,0:T(8,128)S(1)}, bf16[272,128]{1,0:T(8,128)(2,1)S(1)}) custom-call(s32[1]{0:T(128)} %bitcast.6.source_ref, f32[5,4]{1,0:T(8,128)S(1)} %pad_maximum_fusion.scale_ref, f32[512,512]{1,0:T(8,128)S(1)} %fusion.4.acc_ref, bf16[256,512]{1,0:T(8,128)(2,1)S(1)} %collective-permute-done.6.up_ref, ...), custom_call_target="tpu_custom_call" | custom-call | flops 600000000 | bytes 4000000 | tf_op jit(solution)/shard_map/close_chunk/pallas_call | solution.py:235
  88.8 1.2 %collective-permute-done.16.refs_1_ = bf16[272,128]{1,0:T(8,128)(2,1)S(1)} collective-permute-done((bf16[272,128]{1,0:T(8,128)(2,1)S(1)}, bf16[272,128]{1,0:T(8,128)(2,1)S(1)}, u32[]{:S(2)}, u32[]{:S(2)}) %collective-permute-start.16) | collective-permute-done | bytes 69664 | tf_op jit(solution)/shard_map/ppermute | solution.py:432
  90.0 0.6 combine_core.1.refs_0_.refs_2_
  90.5 1.7 %collective-permute-start.17 = (bf16[272,128]{1,0:T(8,128)(2,1)S(1)}, bf16[272,128]{1,0:T(8,128)(2,1)S(1)}, u32[]{:S(2)}, u32[]{:S(2)}) collective-permute-start(bf16[272,128]{1,0:T(8,128)(2,1)S(1)} %combine_core.1.refs_0_.refs_2_), channel_id=1, source_target_pairs={{0,16},{8,24},{16,32},{24,40},{32,48},{40,56},{48,0},{56,8},{64,80... | collective-permute-start | bytes 208904 | tf_op jit(solution)/shard_map/ppermute | solution.py:435
  92.2 2.9 %collective-permute-start.18 = (bf16[272,128]{1,0:T(8,128)(2,1)S(1)}, bf16[272,128]{1,0:T(8,128)(2,1)S(1)}, u32[]{:S(2)}, u32[]{:S(2)}) collective-permute-start(bf16[272,128]{1,0:T(8,128)(2,1)S(1)} %combine_core.1.refs_0_.refs_2_), channel_id=1, source_target_pairs={{0,32},{8,40},{16,48},{24,56},{32,0},{40,8},{48,16},{56,24},{64,96... | collective-permute-start | bytes 208904 | tf_op jit(solution)/shard_map/ppermute | solution.py:435
  95.1 1.3 %collective-permute-start.19 = (bf16[272,128]{1,0:T(8,128)(2,1)S(1)}, bf16[272,128]{1,0:T(8,128)(2,1)S(1)}, u32[]{:S(2)}, u32[]{:S(2)}) collective-permute-start(bf16[272,128]{1,0:T(8,128)(2,1)S(1)} %combine_core.1.refs_0_.refs_2_), channel_id=1, source_target_pairs={{0,48},{8,56},{16,0},{24,8},{32,16},{40,24},{48,32},{56,40},{64,11... | collective-permute-start | bytes 208904 | tf_op jit(solution)/shard_map/ppermute | solution.py:435
  96.5 2.8 %inside.4 = (f32[256,512]{1,0:T(8,128)S(1)}, f32[256,512]{1,0:T(8,128)S(1)}, f32[1,4,256]{2,1,0:T(4,128)S(1)}) custom-call(f32[1,4]{1,0:T(1,128)S(1)} %bitcast.44, bf16[512,512]{1,0:T(8,128)(2,1)S(1)} %get-tuple-element.53.dy_ref, bf16[1024,512]{1,0:T(8,128)(2,1)} %refs_10_.1, bf16[1024,512]{1,0:T(8,128)(2,1)} %refs_11_.1, ...), custom_call_target="tpu_custom_call" | custom-call | flops 1000000000 | bytes 3500000 | tf_op jit(solution)/shard_map/inside/pallas_call | solution.py:278
  99.4 0.6 combine_row.1.refs_6_
  100.0 1.6 %collective-permute-start.20 = (bf16[272,128]{1,0:T(8,128)(2,1)S(1)}, bf16[272,128]{1,0:T(8,128)(2,1)S(1)}, u32[]{:S(2)}, u32[]{:S(2)}) collective-permute-start(bf16[272,128]{1,0:T(8,128)(2,1)S(1)} %combine_row.1.refs_6_), channel_id=1, source_target_pairs={{0,64},{8,72},{16,80},{24,88},{32,96},{40,104},{48,112},{56,120},{... | collective-permute-start | bytes 208904 | tf_op jit(solution)/shard_map/ppermute | solution.py:438
  101.6 1.1 collective-permute-start.21
  102.7 2.2 %collective-permute-start.22 = (bf16[272,128]{1,0:T(8,128)(2,1)S(1)}, bf16[272,128]{1,0:T(8,128)(2,1)S(1)}, u32[]{:S(2)}, u32[]{:S(2)}) collective-permute-start(bf16[272,128]{1,0:T(8,128)(2,1)S(1)} %combine_row.1.refs_6_), channel_id=1, source_target_pairs={{0,192},{8,200},{16,208},{24,216},{32,224},{40,232},{48,240},{56,2... | collective-permute-start | bytes 208904 | tf_op jit(solution)/shard_map/ppermute | solution.py:438
  104.9 4.3 %inside.5 = (f32[512,512]{1,0:T(8,128)S(1)}, f32[512,512]{1,0:T(8,128)S(1)}, f32[2,4,256]{2,1,0:T(4,128)S(1)}) custom-call(f32[1,4]{1,0:T(1,128)S(1)} %bitcast.45, bf16[512,512]{1,0:T(8,128)(2,1)S(1)} %get-tuple-element.57.dy_ref, bf16[1024,512]{1,0:T(8,128)(2,1)} %refs_10_.1, bf16[1024,512]{1,0:T(8,128)(2,1)} %refs_11_.1, ...), custom_call_target="tpu_custom_call" | custom-call | flops 2000000000 | bytes 7000000 | tf_op jit(solution)/shard_map/inside/pallas_call | solution.py:278
  109.2 5.4 %finish.1 = (bf16[1024,512]{1,0:T(8,128)(2,1)}, f32[1024,512]{1,0:T(8,128)}, f32[4,1024]{1,0:T(4,128)}) custom-call(s32[3]{0:T(128)S(1)} %pad_add_fusion.place_ref, f32[4,4]{1,0:T(4,128)S(1)} %bitcast.42, bf16[272,128]{1,0:T(8,128)(2,1)S(1)} %get-tuple-element.44.refs_0_, bf16[272,128]{1,0:T(8,128)(2,1)S(1)} %collective-permute-done.16.refs_1_, ...), custom_call_target="tpu_custom_call" | custom-call | flops 600000000 | bytes 11000000 | tf_op jit(solution)/shard_map/finish/pallas_call | solution.py:385
  (50 shorter events, 1.6 us)
Async XLA Ops:
  1.9 18.8 %collective-permute-start.8 = (bf16[512,512]{1,0:T(8,128)(2,1)S(1)}, bf16[512,512]{1,0:T(8,128)(2,1)}, u32[]{:S(2)}, u32[]{:S(2)}) collective-permute-start(bf16[512,512]{1,0:T(8,128)(2,1)S(1)} %get-tuple-element.33), channel_id=1, source_target_pairs={{0,1},{1,2},{2,3},{3,4},{4,5},{5,6},{6,7},{7,0},{8,9},{9,10},{10,1... | collective-permute-start | bytes 1572872 | tf_op jit(solution)/shard_map/ppermute | solution.py:451
  3.8 16.8 %collective-permute-start.9 = (bf16[512,512]{1,0:T(8,128)(2,1)S(1)}, bf16[512,512]{1,0:T(8,128)(2,1)}, u32[]{:S(2)}, u32[]{:S(2)}) collective-permute-start(bf16[512,512]{1,0:T(8,128)(2,1)S(1)} %get-tuple-element.33), channel_id=1, source_target_pairs={{0,7},{1,0},{2,1},{3,2},{4,3},{5,4},{6,5},{7,6},{8,15},{9,8},{10,9... | collective-permute-start | bytes 1572872 | tf_op jit(solution)/shard_map/ppermute | solution.py:452
  7.9 23.9 %collective-permute-start = (bf16[512,512]{1,0:T(8,128)(2,1)S(1)}, bf16[512,512]{1,0:T(8,128)(2,1)S(1)}, u32[]{:S(2)}, u32[]{:S(2)}) collective-permute-start(bf16[512,512]{1,0:T(8,128)(2,1)S(1)} %get-tuple-element.32), channel_id=1, source_target_pairs={{0,1},{1,2},{2,3},{3,4},{4,5},{5,6},{6,7},{7,0},{8,9},{9,10},{10,1... | collective-permute-start | bytes 1572872 | tf_op jit(solution)/shard_map/ppermute | solution.py:451
  7.9 30.2 %collective-permute-start.1 = (bf16[512,512]{1,0:T(8,128)(2,1)S(1)}, bf16[512,512]{1,0:T(8,128)(2,1)}, u32[]{:S(2)}, u32[]{:S(2)}) collective-permute-start(bf16[512,512]{1,0:T(8,128)(2,1)S(1)} %get-tuple-element.32), channel_id=1, source_target_pairs={{0,7},{1,0},{2,1},{3,2},{4,3},{5,4},{6,5},{7,6},{8,15},{9,8},{10,9... | collective-permute-start | bytes 1572872 | tf_op jit(solution)/shard_map/ppermute | solution.py:452
  12.8 18.9 %copy-start = (bf16[512,4096]{1,0:T(8,128)(2,1)S(1)}, bf16[512,4096]{1,0:T(8,128)(2,1)}, u32[]{:S(2)}) copy-start(bf16[512,4096]{1,0:T(8,128)(2,1)} %weight_ref.3) | copy-start | bytes 12582916
  14.5 19.3 %copy-start.1 = (bf16[1024,512]{1,0:T(8,128)(2,1)S(1)}, bf16[1024,512]{1,0:T(8,128)(2,1)}, u32[]{:S(2)}) copy-start(bf16[1024,512]{1,0:T(8,128)(2,1)} %refs_11_.1) | copy-start | bytes 3145732
  14.5 19.3 %copy-start.3 = (f32[4,4,64,128]{3,2,1,0:T(8,128)S(1)}, f32[4,4,64,128]{3,2,1,0:T(8,128)}, u32[]{:S(2)}) copy-start(f32[4,4,64,128]{3,2,1,0:T(8,128)} %refs_15_.1) | copy-start | bytes 1572868
  20.6 25.7 %collective-permute-start.10 = (bf16[512,512]{1,0:T(8,128)(2,1)}, bf16[512,512]{1,0:T(8,128)(2,1)S(1)}, u32[]{:S(2)}, u32[]{:S(2)}) collective-permute-start(bf16[512,512]{1,0:T(8,128)(2,1)} %collective-permute-done.8), channel_id=1, source_target_pairs={{0,1},{1,2},{2,3},{3,4},{4,5},{5,6},{6,7},{7,0},{8,9},{9,10},{10,1... | collective-permute-start | bytes 1572872 | tf_op jit(solution)/shard_map/ppermute | solution.py:451
  20.7 23.8 %collective-permute-start.11 = (bf16[512,512]{1,0:T(8,128)(2,1)}, bf16[512,512]{1,0:T(8,128)(2,1)S(1)}, u32[]{:S(2)}, u32[]{:S(2)}) collective-permute-start(bf16[512,512]{1,0:T(8,128)(2,1)} %collective-permute-done.9), channel_id=1, source_target_pairs={{0,7},{1,0},{2,1},{3,2},{4,3},{5,4},{6,5},{7,6},{8,15},{9,8},{10,9... | collective-permute-start | bytes 1572872 | tf_op jit(solution)/shard_map/ppermute | solution.py:452
  31.8 26.3 %collective-permute-start.2 = (bf16[512,512]{1,0:T(8,128)(2,1)S(1)}, bf16[512,512]{1,0:T(8,128)(2,1)S(1)}, u32[]{:S(2)}, u32[]{:S(2)}) collective-permute-start(bf16[512,512]{1,0:T(8,128)(2,1)S(1)} %collective-permute-done), channel_id=1, source_target_pairs={{0,1},{1,2},{2,3},{3,4},{4,5},{5,6},{6,7},{7,0},{8,9},{9,10},{10,1... | collective-permute-start | bytes 1572872 | tf_op jit(solution)/shard_map/ppermute | solution.py:451
  38.1 16.0 %collective-permute-start.3 = (bf16[512,512]{1,0:T(8,128)(2,1)}, bf16[512,512]{1,0:T(8,128)(2,1)S(1)}, u32[]{:S(2)}, u32[]{:S(2)}) collective-permute-start(bf16[512,512]{1,0:T(8,128)(2,1)} %collective-permute-done.1), channel_id=1, source_target_pairs={{0,7},{1,0},{2,1},{3,2},{4,3},{5,4},{6,5},{7,6},{8,15},{9,8},{10,9... | collective-permute-start | bytes 1572872 | tf_op jit(solution)/shard_map/ppermute | solution.py:452
  44.4 21.1 %collective-permute-start.13 = (bf16[512,512]{1,0:T(8,128)(2,1)S(1)}, bf16[512,512]{1,0:T(8,128)(2,1)S(1)}, u32[]{:S(2)}, u32[]{:S(2)}) collective-permute-start(bf16[512,512]{1,0:T(8,128)(2,1)S(1)} %collective-permute-done.11), channel_id=1, source_target_pairs={{0,7},{1,0},{2,1},{3,2},{4,3},{5,4},{6,5},{7,6},{8,15},{9,8},{10,9... | collective-permute-start | bytes 1572872 | tf_op jit(solution)/shard_map/ppermute | solution.py:452
  46.4 19.1 %collective-permute-start.12 = (bf16[512,512]{1,0:T(8,128)(2,1)S(1)}, bf16[512,512]{1,0:T(8,128)(2,1)S(1)}, u32[]{:S(2)}, u32[]{:S(2)}) collective-permute-start(bf16[512,512]{1,0:T(8,128)(2,1)S(1)} %collective-permute-done.10), channel_id=1, source_target_pairs={{0,1},{1,2},{2,3},{3,4},{4,5},{5,6},{6,7},{7,0},{8,9},{9,10},{10,1... | collective-permute-start | bytes 1572872 | tf_op jit(solution)/shard_map/ppermute | solution.py:451
  54.0 22.8 %collective-permute-start.5 = (bf16[512,512]{1,0:T(8,128)(2,1)S(1)}, bf16[512,512]{1,0:T(8,128)(2,1)S(1)}, u32[]{:S(2)}, u32[]{:S(2)}) collective-permute-start(bf16[512,512]{1,0:T(8,128)(2,1)S(1)} %collective-permute-done.3), channel_id=1, source_target_pairs={{0,7},{1,0},{2,1},{3,2},{4,3},{5,4},{6,5},{7,6},{8,15},{9,8},{10,9... | collective-permute-start | bytes 1572872 | tf_op jit(solution)/shard_map/ppermute | solution.py:452
  58.1 18.6 %collective-permute-start.4 = (bf16[512,512]{1,0:T(8,128)(2,1)S(1)}, bf16[512,512]{1,0:T(8,128)(2,1)S(1)}, u32[]{:S(2)}, u32[]{:S(2)}) collective-permute-start(bf16[512,512]{1,0:T(8,128)(2,1)S(1)} %collective-permute-done.2), channel_id=1, source_target_pairs={{0,1},{1,2},{2,3},{3,4},{4,5},{5,6},{6,7},{7,0},{8,9},{9,10},{10,1... | collective-permute-start | bytes 1572872 | tf_op jit(solution)/shard_map/ppermute | solution.py:451
  65.5 16.8 %collective-permute-start.14 = (bf16[256,512]{1,0:T(8,128)(2,1)S(1)}, bf16[256,512]{1,0:T(8,128)(2,1)S(1)}, u32[]{:S(2)}, u32[]{:S(2)}) collective-permute-start(bf16[256,512]{1,0:T(8,128)(2,1)S(1)} %slice.28), channel_id=1, source_target_pairs={{0,1},{1,2},{2,3},{3,4},{4,5},{5,6},{6,7},{7,0},{8,9},{9,10},{10,1... | collective-permute-start | bytes 786440 | tf_op jit(solution)/shard_map/ppermute | solution.py:456
  65.6 16.7 %collective-permute-start.15 = (bf16[256,512]{1,0:T(8,128)(2,1)S(1)}, bf16[256,512]{1,0:T(8,128)(2,1)S(1)}, u32[]{:S(2)}, u32[]{:S(2)}) collective-permute-start(bf16[256,512]{1,0:T(8,128)(2,1)S(1)} %slice.29), channel_id=1, source_target_pairs={{0,7},{1,0},{2,1},{3,2},{4,3},{5,4},{6,5},{7,6},{8,15},{9,8},{10,9... | collective-permute-start | bytes 786440 | tf_op jit(solution)/shard_map/ppermute | solution.py:457
  76.7 10.4 %collective-permute-start.6 = (bf16[256,512]{1,0:T(8,128)(2,1)S(1)}, bf16[256,512]{1,0:T(8,128)(2,1)S(1)}, u32[]{:S(2)}, u32[]{:S(2)}) collective-permute-start(bf16[256,512]{1,0:T(8,128)(2,1)S(1)} %slice.26), channel_id=1, source_target_pairs={{0,1},{1,2},{2,3},{3,4},{4,5},{5,6},{6,7},{7,0},{8,9},{9,10},{10,1... | collective-permute-start | bytes 786440 | tf_op jit(solution)/shard_map/ppermute | solution.py:456
  76.9 10.3 %collective-permute-start.7 = (bf16[256,512]{1,0:T(8,128)(2,1)S(1)}, bf16[256,512]{1,0:T(8,128)(2,1)S(1)}, u32[]{:S(2)}, u32[]{:S(2)}) collective-permute-start(bf16[256,512]{1,0:T(8,128)(2,1)S(1)} %slice.27), channel_id=1, source_target_pairs={{0,7},{1,0},{2,1},{3,2},{4,3},{5,4},{6,5},{7,6},{8,15},{9,8},{10,9... | collective-permute-start | bytes 786440 | tf_op jit(solution)/shard_map/ppermute | solution.py:457
  81.2 1.2 %copy-start.2 = (bf16[4,4,64,256]{3,2,1,0:T(8,128)(2,1)S(1)}, bf16[4,4,64,256]{3,2,1,0:T(8,128)(2,1)}, u32[]{:S(2)}) copy-start(bf16[4,4,64,256]{3,2,1,0:T(8,128)(2,1)} %get-tuple-element.35.wct_ref) | copy-start | bytes 1572868
  82.2 1.6 %copy-start.4 = (f32[4]{0:T(128)S(1)}, f32[4]{0:T(128)}, u32[]{:S(2)}) copy-start(f32[4]{0:T(128)} %param.13) | copy-start | bytes 52
  88.6 1.3 %collective-permute-start.16 = (bf16[272,128]{1,0:T(8,128)(2,1)S(1)}, bf16[272,128]{1,0:T(8,128)(2,1)S(1)}, u32[]{:S(2)}, u32[]{:S(2)}) collective-permute-start(bf16[272,128]{1,0:T(8,128)(2,1)S(1)} %get-tuple-element.44.refs_0_), channel_id=1, source_target_pairs={{0,8},{8,0},{16,24},{24,16},{32,40},{40,32},{48,56},{56,48},{64,72... | collective-permute-start | bytes 208904 | tf_op jit(solution)/shard_map/ppermute | solution.py:432
  90.5 8.8 %collective-permute-start.17 = (bf16[272,128]{1,0:T(8,128)(2,1)S(1)}, bf16[272,128]{1,0:T(8,128)(2,1)S(1)}, u32[]{:S(2)}, u32[]{:S(2)}) collective-permute-start(bf16[272,128]{1,0:T(8,128)(2,1)S(1)} %combine_core.1.refs_0_.refs_2_), channel_id=1, source_target_pairs={{0,16},{8,24},{16,32},{24,40},{32,48},{40,56},{48,0},{56,8},{64,80... | collective-permute-start | bytes 208904 | tf_op jit(solution)/shard_map/ppermute | solution.py:435
  92.2 7.1 %collective-permute-start.18 = (bf16[272,128]{1,0:T(8,128)(2,1)S(1)}, bf16[272,128]{1,0:T(8,128)(2,1)S(1)}, u32[]{:S(2)}, u32[]{:S(2)}) collective-permute-start(bf16[272,128]{1,0:T(8,128)(2,1)S(1)} %combine_core.1.refs_0_.refs_2_), channel_id=1, source_target_pairs={{0,32},{8,40},{16,48},{24,56},{32,0},{40,8},{48,16},{56,24},{64,96... | collective-permute-start | bytes 208904 | tf_op jit(solution)/shard_map/ppermute | solution.py:435
  95.1 4.3 %collective-permute-start.19 = (bf16[272,128]{1,0:T(8,128)(2,1)S(1)}, bf16[272,128]{1,0:T(8,128)(2,1)S(1)}, u32[]{:S(2)}, u32[]{:S(2)}) collective-permute-start(bf16[272,128]{1,0:T(8,128)(2,1)S(1)} %combine_core.1.refs_0_.refs_2_), channel_id=1, source_target_pairs={{0,48},{8,56},{16,0},{24,8},{32,16},{40,24},{48,32},{56,40},{64,11... | collective-permute-start | bytes 208904 | tf_op jit(solution)/shard_map/ppermute | solution.py:435
  100.0 9.1 %collective-permute-start.20 = (bf16[272,128]{1,0:T(8,128)(2,1)S(1)}, bf16[272,128]{1,0:T(8,128)(2,1)S(1)}, u32[]{:S(2)}, u32[]{:S(2)}) collective-permute-start(bf16[272,128]{1,0:T(8,128)(2,1)S(1)} %combine_row.1.refs_6_), channel_id=1, source_target_pairs={{0,64},{8,72},{16,80},{24,88},{32,96},{40,104},{48,112},{56,120},{... | collective-permute-start | bytes 208904 | tf_op jit(solution)/shard_map/ppermute | solution.py:438
  101.6 7.6 %collective-permute-start.21 = (bf16[272,128]{1,0:T(8,128)(2,1)S(1)}, bf16[272,128]{1,0:T(8,128)(2,1)S(1)}, u32[]{:S(2)}, u32[]{:S(2)}) collective-permute-start(bf16[272,128]{1,0:T(8,128)(2,1)S(1)} %combine_row.1.refs_6_), channel_id=1, source_target_pairs={{0,128},{8,136},{16,144},{24,152},{32,160},{40,168},{48,176},{56,1... | collective-permute-start | bytes 208904 | tf_op jit(solution)/shard_map/ppermute | solution.py:438
  102.7 6.5 %collective-permute-start.22 = (bf16[272,128]{1,0:T(8,128)(2,1)S(1)}, bf16[272,128]{1,0:T(8,128)(2,1)S(1)}, u32[]{:S(2)}, u32[]{:S(2)}) collective-permute-start(bf16[272,128]{1,0:T(8,128)(2,1)S(1)} %combine_row.1.refs_6_), channel_id=1, source_target_pairs={{0,192},{8,200},{16,208},{24,216},{32,224},{40,232},{48,240},{56,2... | collective-permute-start | bytes 208904 | tf_op jit(solution)/shard_map/ppermute | solution.py:438
